TPU v7x, 256 devices: a whole 4x4x8 slice. The times are simulated.
256 devices in a mesh: seq: 32 (over z_hi, y, core), tp: 8 (over z_lo, x).
Axes of the slice: x: 4, y: 4, z: 8 (z_hi: 4, z_lo: 2; z = z_hi * 2 + z_lo), core: 2. Of those that a mesh axis runs over, the one named last changes fastest.
Arguments:
- hidden_sel: bfloat16 [8192, 7168], P('seq', 'tp'), may hold values from -6 to 6
- w_query: bfloat16 [7168, 4096], P(None, 'tp'), may hold values from -0.0625 to 0.0625
- w_key: bfloat16 [7168, 1024], P(None, 'tp'), may hold values from -0.0625 to 0.0625
- w_value: bfloat16 [7168, 1024], P(None, 'tp'), may hold values from -0.0625 to 0.0625
- key_cache: bfloat16 [65536, 1024], P('seq', 'tp')
- value_cache: bfloat16 [65536, 1024], P('seq', 'tp'), may hold values from -6 to 6
- span_count: int32 [8], replicated, may hold values from 1 to 8, 32 in all
- span_key: int32 [8, 8], replicated, may hold values from 0 to 7, each once within a row
- cache_offset: int32 [64], P('seq'), may hold values from 0 to 8191
- sel_index: int32 [64, 128], P('seq'), may hold values from 0 to 1023, as said below
Outputs:
- attn_out: bfloat16 [8192, 4096], P('seq', 'tp')
Inputs may be any that keep to these rules, and one draw needn't show every extreme that they name: `sel_index`: each row holds 128 different positions in rising order. `span_count`: the counts sum to 32, and the largest is exactly 8. `span_key`: each row is a permutation of 0 to 7.
All inputs are finite; a program needn't handle non-finite values.
Results may differ from a plain program's by a relative error of at most 0.023.
Values may be sent and summed in bfloat16 or wider, within the bound.
No kernel may reach another device: no remote copies, remote signals or barrier semaphores. Data moves between devices by JAX's collectives and lax.ppermute only.
A program may use at most 128 MiB of HBM per device.

v0:
```python
import functools
import math

import jax
import jax.numpy as jnp
from jax import lax
from jax.experimental import pallas as pl
from jax.experimental.pallas import tpu as pltpu
from jax.sharding import Mesh, PartitionSpec as P

HD = 128
HG = 4
R = 8
MAXCH = 8
SPAN = 1024
SEL = 128
SLOTS = 2
ROWS = SLOTS * SEL
QW = HG * HD
PACK = SEL + 16
DK = 896
PROJ = 56

rope_base = 5000000.0
low = -1.0e30
SCALE2 = math.log2(math.e) / math.sqrt(HD)

vmem = pl.BlockSpec(memory_space=pltpu.VMEM)
smem = pl.BlockSpec(memory_space=pltpu.SMEM)
hbm = pl.BlockSpec(memory_space=pltpu.HBM)
tiny = pl.CostEstimate(flops=1, bytes_accessed=1, transcendentals=0)
AXES = ("zh", "yh", "yp", "c", "zl", "x")


def px(v, s):
    return lax.ppermute(v, "x", [(i, (i + s) % 4) for i in range(4)])


def pz(v):
    return lax.ppermute(v, "zl", [(0, 1), (1, 0)])


def py(v):
    return lax.ppermute(v, "yh", [(0, 1), (1, 0)])


def ph(v, s):
    return lax.ppermute(v, "zh", [(i, (i + s) % 4) for i in range(4)])


def span_ranks(span_count, span_key):
    column = jnp.arange(MAXCH, dtype=jnp.int32)
    filled = column[None, :] < span_count[:, None]
    earlier = span_key[:, :, None] < span_key[:, None, :]
    ranks = jnp.sum((earlier & filled[:, :, None]).astype(jnp.int32), axis=1, dtype=jnp.int32)
    return filled.T.reshape(-1), ranks.T.reshape(-1)


def tables(position):
    freq = rope_base ** (-(jnp.arange(HD // 2, dtype=jnp.float32) * 2.0) / HD)
    angle = position.astype(jnp.float32)[:, None] * freq
    cosine, sine = jnp.cos(angle), jnp.sin(angle)
    return jnp.concatenate([cosine, cosine], -1), jnp.concatenate([-sine, sine], -1)


def turned(v, cosine, sine):
    return v * cosine + pltpu.roll(v, HD // 2, 1) * sine


def project_kernel(count, carried, last, idx_ref, *refs):
    refs = list(refs)
    pieces = [refs.pop(0) for _ in range(count)]
    sources = [refs.pop(0) for _ in range(3)]
    acc_ref = refs.pop(0) if carried else None
    if last:
        cos_ref, sin_ref, q_ref, n_ref = (refs.pop(0) for _ in range(4))
    else:
        out_ref = refs.pop(0)
    held, weight, sem = refs
    widths = (QW, HD, HD)

    def copies(i):
        at = pl.ds(pl.multiple_of(idx_ref[i] * DK, DK), DK)
        start = 0
        for j, (w, width) in enumerate(zip(sources, widths)):
            to = weight.at[i, :, start : start + width]
            yield pltpu.make_async_copy(w.at[at, :], to, sem.at[i, j])
            start += width

    for i in range(count):
        for copy in copies(i):
            copy.start()
    for i in range(count):
        held[i] = pieces[i][...]

    def add(i, acc):
        for copy in copies(i):
            copy.wait()
        return acc + jnp.dot(held[i], weight[i], preferred_element_type=jnp.float32)

    begin = acc_ref[...] if carried else jnp.zeros((ROWS, QW + 2 * HD), jnp.float32)
    acc = lax.fori_loop(0, count, add, begin)
    if not last:
        out_ref[...] = acc
        return
    cosine, sine = cos_ref[...], sin_ref[...]
    for g in range(HG):
        at = slice(g * HD, (g + 1) * HD)
        q_ref[:, at] = turned(acc[:, at], cosine, sine).astype(jnp.bfloat16)
    n_ref[:ROWS, :] = turned(acc[:, QW : QW + HD], cosine, sine).astype(jnp.bfloat16)
    n_ref[ROWS:, :] = acc[:, QW + HD :].astype(jnp.bfloat16)


def project(idx, pieces, weights, acc=None, rot=None):
    if rot is None:
        out = jax.ShapeDtypeStruct((ROWS, QW + 2 * HD), jnp.float32)
    else:
        out = (
            jax.ShapeDtypeStruct((ROWS, QW), jnp.bfloat16),
            jax.ShapeDtypeStruct((2 * ROWS, HD), jnp.bfloat16),
        )
    extra = ([] if acc is None else [acc]) + ([] if rot is None else list(rot))
    n = len(pieces)
    return pl.pallas_call(
        functools.partial(project_kernel, n, acc is not None, rot is not None),
        out_shape=out,
        in_specs=[smem] + [vmem] * n + [hbm] * 3 + [vmem] * len(extra),
        out_specs=vmem if rot is None else (vmem, vmem),
        scratch_shapes=[
            pltpu.VMEM((n, ROWS, DK), jnp.bfloat16),
            pltpu.VMEM((n, DK, QW + 2 * HD), jnp.bfloat16),
            pltpu.SemaphoreType.DMA((n, 3)),
        ],
        compiler_params=pltpu.CompilerParams(vmem_limit_bytes=PROJ << 20),
        cost_estimate=tiny,
        name="project",
    )(idx, *pieces, *weights, *extra)


def attend_block(at, q_ref, keys, vals, limit, m_ref, l_ref, acc_ref):
    s = lax.dot_general(
        q_ref[at, :], keys, (((1,), (1,)), ((), ())), preferred_element_type=jnp.float32
    )
    if limit is not None:
        col = lax.broadcasted_iota(jnp.int32, s.shape, 1)
        s = jnp.where(col <= limit, s, low)
    old = m_ref[at, :]
    new = jnp.maximum(old, jnp.max(s, axis=1, keepdims=True))
    factor = jnp.exp2((old - new) * SCALE2)
    weight = jnp.exp2((s - new) * SCALE2)
    l_ref[at, :] = l_ref[at, :] * factor + jnp.sum(weight, axis=1, keepdims=True)
    acc_ref[at, :] = acc_ref[at, :] * factor + jnp.dot(
        weight.astype(jnp.bfloat16), vals, preferred_element_type=jnp.float32
    )
    m_ref[at, :] = new


def attend_source(rows_ref, i, jk_ref, jv_ref, r, valid_ref, first, o_ref, state, limit_ref=None):
    m_ref, l_ref, acc_ref = state
    m_ref[...] = jnp.full_like(m_ref, low)
    l_ref[...] = jnp.zeros_like(l_ref)
    acc_ref[...] = jnp.zeros_like(acc_ref)

    def span(step, _):
        sp = step // 2

        @pl.when(valid_ref[first + sp] != 0)
        def _():
            at = pl.ds(pl.multiple_of((step % 2) * 2 * SEL, 2 * SEL), 2 * SEL)
            limit = None if limit_ref is None else jnp.where(sp == 0, limit_ref[at, :], SPAN)
            attend_block(
                at, rows_ref.at[i], jk_ref[r * 2 + sp], jv_ref[r * 2 + sp], limit,
                m_ref, l_ref, acc_ref,
            )

        return 0

    lax.fori_loop(0, 4, span, 0)
    l = l_ref[...]
    some = l > 0.0
    mixed = acc_ref[...] / jnp.where(some, l, 1.0)
    lse = jnp.where(some, m_ref[...] * SCALE2 + jnp.log2(jnp.where(some, l, 1.0)), low)
    lane = lax.broadcasted_iota(jnp.int32, (SEL, HD), 1)
    stat = jnp.zeros((SEL, HD), jnp.float32)
    for g in range(HG):
        o_ref[i, :SEL, g * HD : (g + 1) * HD] = mixed[g * SEL : (g + 1) * SEL].astype(jnp.bfloat16)
        rest = lse[g * SEL : (g + 1) * SEL]
        for k in range(3):
            part = rest.astype(jnp.bfloat16).astype(jnp.float32)
            stat = jnp.where(lane == k * HG + g, part, stat)
            rest = rest - part
    o_ref[i, SEL:, :HD] = stat.T[:16].astype(jnp.bfloat16)
    o_ref[i, SEL:, HD:] = jnp.zeros((16, QW - HD), jnp.bfloat16)


def spread(rows_ref, i, q):
    for g in range(HG):
        rows_ref[i, g * SEL : (g + 1) * SEL, :] = q[:, g * HD : (g + 1) * HD]


def own_kernel(
    valid_ref, q_ref, k0, v0, k1, v1, n0, n1, selr_ref, rot_ref,
    jk_ref, jv_ref, oa_ref, ob_ref, rows_ref, out_ref, limit_ref, *state,
):
    spread(rows_ref, 0, q_ref[:SEL, :])
    spread(rows_ref, 1, q_ref[SEL:, :])

    def request(r, _):
        base = pl.ds(pl.multiple_of(r * SPAN, SPAN), SPAN)
        fresh_k = pl.ds(pl.multiple_of(r * SEL, SEL), SEL)
        fresh_v = pl.ds(pl.multiple_of(ROWS + r * SEL, SEL), SEL)
        for sp, (kr, vr, nr) in enumerate(((k0, v0, n0), (k1, v1, n1))):
            cached = turned(
                kr[base, :].astype(jnp.float32),
                rot_ref[r, sp : sp + 1, :],
                rot_ref[r, sp + 2 : sp + 3, :],
            )
            at = lax.broadcasted_iota(jnp.int32, (SPAN, SEL), 0)
            pick = (at == selr_ref[r, sp : sp + 1, :]).astype(jnp.float32).astype(jnp.bfloat16)
            ones = jnp.ones((SEL, HD), jnp.bfloat16)
            hit = jnp.dot(pick, ones, preferred_element_type=jnp.float32) > 0.5
            put_k = jnp.dot(pick, nr[fresh_k, :], preferred_element_type=jnp.float32)
            put_v = jnp.dot(pick, nr[fresh_v, :], preferred_element_type=jnp.float32)
            vals = vr[base, :].astype(jnp.float32)
            jk_ref[r * 2 + sp] = jnp.where(hit, put_k, cached).astype(jnp.bfloat16)
            jv_ref[r * 2 + sp] = jnp.where(hit, put_v, vals).astype(jnp.bfloat16)
        sel = selr_ref[r, 0:1, :].astype(jnp.float32)
        column = jnp.broadcast_to(sel, (SEL, SEL)).T[:, :1].astype(jnp.int32)
        limit_ref[...] = jnp.concatenate([column] * HG, axis=0)
        attend_source(
            rows_ref, r, jk_ref, jv_ref, r, valid_ref, r * 2, out_ref, state, limit_ref
        )
        return 0

    lax.fori_loop(0, SLOTS, request, 0)
    oa_ref[...] = out_ref[0]
    ob_ref[...] = out_ref[1]


def other_kernel(sources, shifts, valid_ref, *refs):
    queries, refs = refs[:sources], refs[sources:]
    jk_ref, jv_ref = refs[:2]
    outs, refs = refs[2 : 2 + 2 * len(shifts)], refs[2 + 2 * len(shifts) :]
    rows_ref, out_ref, state = refs[0], refs[1], refs[2:]
    i = 0
    for q_ref in queries:
        for start in range(0, q_ref.shape[0], SEL):
            spread(rows_ref, i, q_ref[start : start + SEL, :])
            i += 1
    first = shifts[0] * 4
    step = (shifts[-1] - shifts[0]) * 4

    def source(i, _):
        r = i % 2
        attend_source(
            rows_ref, i, jk_ref, jv_ref, r, valid_ref, first + (i // 2) * step + r * 2,
            out_ref, state,
        )
        return 0

    lax.fori_loop(0, len(outs), source, 0)
    for i, o in enumerate(outs):
        o[...] = out_ref[i]


joined_shape = jax.ShapeDtypeStruct((SLOTS * 2, SPAN, HD), jnp.bfloat16)
packed_shape = jax.ShapeDtypeStruct((PACK, QW), jnp.bfloat16)
state_scratch = [
    pltpu.VMEM((HG * SEL, 1), jnp.float32),
    pltpu.VMEM((HG * SEL, 1), jnp.float32),
    pltpu.VMEM((HG * SEL, HD), jnp.float32),
]


def attend_own(*args):
    return pl.pallas_call(
        own_kernel,
        out_shape=(joined_shape, joined_shape, packed_shape, packed_shape),
        in_specs=[smem] + [vmem] * 9,
        out_specs=(vmem,) * 4,
        scratch_shapes=[
            pltpu.VMEM((2, HG * SEL, HD), jnp.bfloat16),
            pltpu.VMEM((2, PACK, QW), jnp.bfloat16),
            pltpu.VMEM((HG * SEL, 1), jnp.int32),
        ]
        + state_scratch,
        compiler_params=pltpu.CompilerParams(vmem_limit_bytes=20 << 20),
        cost_estimate=tiny,
        name="attend_own",
    )(*args)


def attend_other(shifts, valid, queries, jk, jv):
    n = 2 * len(shifts)
    return pl.pallas_call(
        functools.partial(other_kernel, len(queries), shifts),
        out_shape=(packed_shape,) * n,
        in_specs=[smem] + [vmem] * (len(queries) + 2),
        out_specs=(vmem,) * n,
        scratch_shapes=[
            pltpu.VMEM((n, HG * SEL, HD), jnp.bfloat16),
            pltpu.VMEM((n, PACK, QW), jnp.bfloat16),
        ]
        + state_scratch,
        compiler_params=pltpu.CompilerParams(vmem_limit_bytes=20 << 20),
        cost_estimate=tiny,
        name="attend_other",
    )(valid, *queries, jk, jv)


def merge_parts(parts, put, stat_put=None):
    lse = []
    for p in parts:
        stat = p[SEL:, :HD].astype(jnp.float32)
        lse.append(stat[0:4] + stat[4:8] + stat[8:12])
    top = functools.reduce(jnp.maximum, lse)
    weight = [jnp.exp2(v - top) for v in lse]
    total = functools.reduce(jnp.add, weight)
    pad = jnp.zeros((HD - HG, SEL), jnp.float32)
    weight = [jnp.concatenate([w / total, pad], axis=0).T for w in weight]
    for g in range(HG):
        at = slice(g * HD, (g + 1) * HD)
        mixed = jnp.zeros((SEL, HD), jnp.float32)
        for w, p in zip(weight, parts):
            mixed += w[:, g : g + 1] * p[:SEL, at].astype(jnp.float32)
        put(at, mixed.astype(jnp.bfloat16))
    if stat_put is not None:
        rest = top + jnp.log2(total)
        rows = []
        for _ in range(3):
            part = rest.astype(jnp.bfloat16).astype(jnp.float32)
            rows.append(part)
            rest = rest - part
        stat_put(jnp.concatenate(rows + [jnp.zeros_like(top)], axis=0).astype(jnp.bfloat16))


def between_kernel(a0, a1, b0, b1, oa_ref, ob_ref):
    for parts, o_ref in (((a0, a1), oa_ref), ((b0, b1), ob_ref)):

        def put(at, value, o_ref=o_ref):
            o_ref[:SEL, at] = value

        def stat_put(value, o_ref=o_ref):
            o_ref[SEL:, :HD] = value
            o_ref[SEL:, HD:] = jnp.zeros((16, QW - HD), jnp.bfloat16)

        merge_parts(parts, put, stat_put)


def between(*parts):
    return pl.pallas_call(
        between_kernel,
        out_shape=(packed_shape, packed_shape),
        in_specs=[vmem] * 4,
        out_specs=(vmem, vmem),
        compiler_params=pltpu.CompilerParams(vmem_limit_bytes=8 << 20),
        cost_estimate=tiny,
        name="merge_between",
    )(*parts)


def merge_kernel(*refs):
    o_ref = refs[-1]
    for r in range(SLOTS):

        def put(at, value, r=r):
            o_ref[r * SEL : (r + 1) * SEL, at] = value

        merge_parts(refs[3 * r : 3 * r + 3], put)


def merge(*parts):
    return pl.pallas_call(
        merge_kernel,
        out_shape=jax.ShapeDtypeStruct((ROWS, QW), jnp.bfloat16),
        in_specs=[vmem] * 6,
        out_specs=vmem,
        compiler_params=pltpu.CompilerParams(vmem_limit_bytes=8 << 20),
        cost_estimate=tiny,
        name="merge",
    )(*parts)


def after(value, *others):
    return lax.optimization_barrier((value, *others))[0]


def shards(
    hidden, w_query, w_key, w_value, key_cache, value_cache,
    span_count, span_key, cache_offset, sel_index,
):
    zh, yh, yp, c = (lax.axis_index(a) for a in ("zh", "yh", "yp", "c"))
    zl, x = lax.axis_index("zl"), lax.axis_index("x")
    weights = (w_query, w_key, w_value)
    z = pz(hidden)
    right, left = px(hidden, 1), px(hidden, -1)
    k1, v1 = py(key_cache), py(value_cache)
    far = px(right, 1)
    zleft = px(z, -1)
    zright = px(after(z, left), 1)
    zfar = px(zleft, -1)
    mine = jnp.concatenate(
        [sel_index, jnp.broadcast_to(cache_offset[:, None], (SLOTS, SEL))], axis=0
    )
    theirs = py(mine)
    other = 1 - zl
    near_idx = jnp.stack(
        [zl * 4 + x, other * 4 + x, zl * 4 + (x + 3) % 4, zl * 4 + (x + 1) % 4]
    ).astype(jnp.int32)
    mid_idx = jnp.stack([zl * 4 + (x + 2) % 4, other * 4 + (x + 1) % 4]).astype(jnp.int32)
    far_idx = jnp.stack([other * 4 + (x + 3) % 4, other * 4 + (x + 2) % 4]).astype(jnp.int32)

    filled_all, rank_all = span_ranks(span_count, span_key)

    def lookup(h, half):
        start = (((h * 2 + half) * 2 + yp) * 2 + c) * SLOTS
        return (
            lax.dynamic_slice_in_dim(filled_all, start, SLOTS),
            lax.dynamic_slice_in_dim(rank_all, start, SLOTS),
        )

    span_f, span_r = zip(lookup(zh, yh), lookup(zh, 1 - yh))

    def validity(shift):
        qf, qr = lookup((zh - shift) % 4, yh)
        table = [qf & kf & (kr <= qr) for kf, kr in zip(span_f, span_r)]
        return jnp.stack(table, axis=1).astype(jnp.int32)

    position = (span_r[0][:, None] * SPAN + sel_index).reshape(-1)
    cosine, sine = tables(position)
    delta = jnp.stack(
        [span_r[0] * SPAN - cache_offset, span_r[1] * SPAN - theirs[SLOTS:, 0]], axis=1
    ).reshape(-1)
    turn_c, turn_s = tables(delta)
    rot = jnp.concatenate(
        [turn_c.reshape(SLOTS, 2, HD), turn_s.reshape(SLOTS, 2, HD)], axis=1
    )
    sel_rows = jnp.stack([sel_index, theirs[:SLOTS]], axis=1)
    valid = jnp.concatenate([validity(s) for s in range(4)], axis=0).reshape(-1)

    acc = project(near_idx, (hidden, z, right, left), weights)
    acc = project(mid_idx, (far, zleft), weights, acc)
    acc = after(acc, k1, v1)
    query, fresh = project(far_idx, (zright, zfar), weights, acc, (cosine, sine))
    minus_q, plus_q = ph(query, 1), ph(query, -1)
    fresh1 = py(fresh)
    far_a = ph(minus_q[:SEL], 1)
    far_b = ph(plus_q[SEL:], -1)
    jk, jv, own_a, own_b = attend_own(
        valid, query, key_cache, value_cache, k1, v1, fresh, fresh1, sel_rows, rot
    )
    ma, mb, pa, pb = attend_other((1, 3), valid, (minus_q, plus_q), jk, jv)
    near_a, near_b = ph(pa, 1), ph(mb, -1)
    fa, fb = attend_other((2,), valid, (far_a, far_b), jk, jv)
    back_a, back_b = ph(fa, -1), ph(fb, 1)
    both_a, both_b = between(ma, back_a, pb, back_b)
    return merge(own_a, near_a, ph(both_a, -1), own_b, near_b, ph(both_b, 1))


def solution(mesh):
    split = Mesh(mesh.devices.reshape(4, 2, 2, 2, 2, 4), AXES)
    seq, tp = AXES[:4], AXES[4:]
    placed = (
        P(seq, tp),
        P(None, tp),
        P(None, tp),
        P(None, tp),
        P(seq, tp),
        P(seq, tp),
        P(),
        P(),
        P(seq),
        P(seq, None),
    )
    return jax.shard_map(
        shards, mesh=split, in_specs=placed, out_specs=P(seq, tp), check_vma=False
    )
```

profile of v0, /device:TPU:32, one launch (start us, length us, event | category | flops | bytes accessed | tf_op | source)
XLA Modules:
  0.0 119.1 jit_solution(17656823112860038117)
XLA Ops:
  0.0 1.8 %collective-permute-start = (bf16[256,896]{1,0:T(8,128)(2,1)}, bf16[256,896]{1,0:T(8,128)(2,1)S(1)}, u32[]{:S(2)}, u32[]{:S(2)}) collective-permute-start(bf16[256,896]{1,0:T(8,128)(2,1)} %refs_0_.1), channel_id=1, source_target_pairs={{0,4},{4,0},{1,5},{5,1},{2,6},{6,2},{3,7},{7,3},{8,12},{12,8},{9,1... | collective-permute-start | bytes 1376264 | tf_op jit(solution)/shard_map/ppermute | solution.py:40
  1.8 1.0 collective-permute-start.1
  2.9 1.0 collective-permute-start.5
  3.9 2.2 %collective-permute-start.7 = (bf16[2048,128]{1,0:T(8,128)(2,1)}, bf16[2048,128]{1,0:T(8,128)(2,1)S(1)}, u32[]{:S(2)}, u32[]{:S(2)}) collective-permute-start(bf16[2048,128]{1,0:T(8,128)(2,1)} %k0.1), channel_id=1, source_target_pairs={{0,32},{32,0},{1,33},{33,1},{2,34},{34,2},{3,35},{35,3},{4,36},{36... | collective-permute-start | bytes 1572872 | tf_op jit(solution)/shard_map/ppermute | solution.py:44
  6.1 0.7 pad.9.clone
  6.8 0.7 pad_add_fusion
  7.5 1.3 %collective-permute-start.10 = (s32[4,128]{1,0:T(4,128)S(1)}, s32[4,128]{1,0:T(4,128)S(1)}, u32[]{:S(2)}, u32[]{:S(2)}) collective-permute-start(s32[4,128]{1,0:T(4,128)S(1)} %pad_add_fusion), channel_id=1, source_target_pairs={{0,32},{32,0},{1,33},{33,1},{2,34},{34,2},{3,35},{35,3},{4,36},{36... | collective-permute-start | bytes 6152 | tf_op jit(solution)/shard_map/ppermute | solution.py:44
  8.9 0.8 iota_compare_fusion.1
  9.7 0.6 pad_add_fusion.3.idx_ref
  10.3 0.9 convert_reduce_fusion
  11.2 0.6 pad_add_fusion.2.idx_ref
  11.8 0.6 pad_add_fusion.4.idx_ref
  12.6 5.3 %collective-permute-done.10 = s32[4,128]{1,0:T(4,128)S(1)} collective-permute-done((s32[4,128]{1,0:T(4,128)S(1)}, s32[4,128]{1,0:T(4,128)S(1)}, u32[]{:S(2)}, u32[]{:S(2)}) %collective-permute-start.10) | collective-permute-done | bytes 2080 | tf_op jit(solution)/shard_map/ppermute | solution.py:44
  17.9 3.2 %collective-permute-start.8 = (bf16[2048,128]{1,0:T(8,128)(2,1)}, bf16[2048,128]{1,0:T(8,128)(2,1)S(1)}, u32[]{:S(2)}, u32[]{:S(2)}) collective-permute-start(bf16[2048,128]{1,0:T(8,128)(2,1)} %v0.1), channel_id=1, source_target_pairs={{0,32},{32,0},{1,33},{33,1},{2,34},{34,2},{3,35},{35,3},{4,36},{36... | collective-permute-start | bytes 1572872 | tf_op jit(solution)/shard_map/ppermute | solution.py:44
  21.2 0.7 subtract_bitcast_fusion.1
  22.0 3.0 %collective-permute-start.3 = (bf16[256,896]{1,0:T(8,128)(2,1)S(1)}, bf16[256,896]{1,0:T(8,128)(2,1)S(1)}, u32[]{:S(2)}, u32[]{:S(2)}) collective-permute-start(bf16[256,896]{1,0:T(8,128)(2,1)S(1)} %collective-permute-done.refs_1_), channel_id=1, source_target_pairs={{0,3},{1,0},{2,1},{3,2},{4,7},{5,4},{6,5},{7,6},{8,11},{9,8},{10,9... | collective-permute-start | bytes 1376264 | tf_op jit(solution)/shard_map/ppermute | solution.py:36
  25.0 0.7 convert_bitcast_fusion
  25.8 0.5 fusion
  26.3 0.8 pad_maximum_fusion
  27.3 5.6 %collective-permute-done.3.refs_1_ = bf16[256,896]{1,0:T(8,128)(2,1)S(1)} collective-permute-done((bf16[256,896]{1,0:T(8,128)(2,1)S(1)}, bf16[256,896]{1,0:T(8,128)(2,1)S(1)}, u32[]{:S(2)}, u32[]{:S(2)}) %collective-permute-start.3) | collective-permute-done | bytes 458784 | tf_op jit(solution)/shard_map/ppermute | solution.py:36
  32.9 3.7 %collective-permute-start.4 = (bf16[256,896]{1,0:T(8,128)(2,1)S(1)}, bf16[256,896]{1,0:T(8,128)(2,1)S(1)}, u32[]{:S(2)}, u32[]{:S(2)}) collective-permute-start(bf16[256,896]{1,0:T(8,128)(2,1)S(1)} %collective-permute-done.3.refs_1_), channel_id=1, source_target_pairs={{0,3},{1,0},{2,1},{3,2},{4,7},{5,4},{6,5},{7,6},{8,11},{9,8},{10,9... | collective-permute-start | bytes 1376264 | tf_op jit(solution)/shard_map/ppermute | solution.py:36
  36.6 0.7 pad_add_fusion.1.selr_ref
  37.5 6.4 %project.3.refs_5_ = f32[256,768]{1,0:T(8,128)} custom-call(s32[4]{0:T(128)} %pad_add_fusion.4.idx_ref, bf16[256,896]{1,0:T(8,128)(2,1)} %refs_0_.1, bf16[256,896]{1,0:T(8,128)(2,1)} %copy-done.6, bf16[256,896]{1,0:T(8,128)(2,1)} %copy-done.8, bf16[256,896]{1,0:T(8,128)(2,1)} %copy-done.7, bf16[7168,512]{1,0:T(8,128)(2,1)} %refs_2_.3, ...), custom_call_target="tpu_custom_call" | custom-call | flops 1 | bytes 1 | tf_op jit(solution)/shard_map/project/pallas_call | solution.py:124
  43.9 4.4 %collective-permute-done.6.refs_0_ = bf16[256,896]{1,0:T(8,128)(2,1)S(1)} collective-permute-done((bf16[256,896]{1,0:T(8,128)(2,1)S(1)}, bf16[256,896]{1,0:T(8,128)(2,1)S(1)}, u32[]{:S(2)}, u32[]{:S(2)}) %collective-permute-start.6) | collective-permute-done | bytes 458784 | tf_op jit(solution)/shard_map/ppermute | solution.py:36
  48.3 0.8 copy-done.10
  49.1 5.0 %project.4.refs_5_ = f32[256,768]{1,0:T(8,128)} custom-call(s32[2]{0:T(128)} %pad_add_fusion.3.idx_ref, bf16[256,896]{1,0:T(8,128)(2,1)} %copy-done.10, bf16[256,896]{1,0:T(8,128)(2,1)} %copy-done.9, bf16[7168,512]{1,0:T(8,128)(2,1)} %refs_2_.3, bf16[7168,128]{1,0:T(8,128)(2,1)} %refs_3_.3, bf16[7168,128]{1,0:T(8,128)(2,1)} %refs_4_.5, ...), custom_call_target="tpu_custom_call" | custom-call | flops 1 | bytes 1 | tf_op jit(solution)/shard_map/project/pallas_call | solution.py:124
  54.1 0.8 copy-done.4
  54.9 0.1 copy-done.5
  55.0 5.1 %project.5 = (bf16[256,512]{1,0:T(8,128)(2,1)}, bf16[512,128]{1,0:T(8,128)(2,1)}) custom-call(s32[2]{0:T(128)} %pad_add_fusion.2.idx_ref, bf16[256,896]{1,0:T(8,128)(2,1)} %copy-done.4, bf16[256,896]{1,0:T(8,128)(2,1)} %copy-done.5, bf16[7168,512]{1,0:T(8,128)(2,1)} %refs_2_.3, bf16[7168,128]{1,0:T(8,128)(2,1)} %refs_3_.3, bf16[7168,128]{1,0:T(8,128)(2,1)} %refs_4_.5, ...), custom_call_target="tpu_custom_call" | custom-call | flops 1 | bytes 1 | tf_op jit(solution)/shard_map/project/pallas_call | solution.py:124
  60.2 3.3 %collective-permute-start.11 = (bf16[256,512]{1,0:T(8,128)(2,1)}, bf16[256,512]{1,0:T(8,128)(2,1)S(1)}, u32[]{:S(2)}, u32[]{:S(2)}) collective-permute-start(bf16[256,512]{1,0:T(8,128)(2,1)} %get-tuple-element.23.q_ref), channel_id=1, source_target_pairs={{0,64},{64,128},{128,192},{192,0},{1,65},{65,129},{129,193},{193,1... | collective-permute-start | bytes 786440 | tf_op jit(solution)/shard_map/ppermute | solution.py:48
  63.5 2.8 %collective-permute-start.12 = (bf16[256,512]{1,0:T(8,128)(2,1)}, bf16[256,512]{1,0:T(8,128)(2,1)S(1)}, u32[]{:S(2)}, u32[]{:S(2)}) collective-permute-start(bf16[256,512]{1,0:T(8,128)(2,1)} %get-tuple-element.23.q_ref), channel_id=1, source_target_pairs={{0,192},{64,0},{128,64},{192,128},{1,193},{65,1},{129,65},{193,129... | collective-permute-start | bytes 786440 | tf_op jit(solution)/shard_map/ppermute | solution.py:48
  66.5 0.6 collective-permute-start.9
  67.1 8.4 %collective-permute-done.11.refs_0_ = bf16[256,512]{1,0:T(8,128)(2,1)S(1)} collective-permute-done((bf16[256,512]{1,0:T(8,128)(2,1)}, bf16[256,512]{1,0:T(8,128)(2,1)S(1)}, u32[]{:S(2)}, u32[]{:S(2)}) %collective-permute-start.11) | collective-permute-done | bytes 262176 | tf_op jit(solution)/shard_map/ppermute | solution.py:48
  75.5 2.0 %collective-permute-start.14 = (bf16[128,512]{1,0:T(8,128)(2,1)S(1)}, bf16[128,512]{1,0:T(8,128)(2,1)S(1)}, u32[]{:S(2)}, u32[]{:S(2)}) collective-permute-start(bf16[128,512]{1,0:T(8,128)(2,1)S(1)} %slice.16), channel_id=1, source_target_pairs={{0,64},{64,128},{128,192},{192,0},{1,65},{65,129},{129,193},{193,1... | collective-permute-start | bytes 393224 | tf_op jit(solution)/shard_map/ppermute | solution.py:48
  77.5 2.3 %collective-permute-start.15 = (bf16[128,512]{1,0:T(8,128)(2,1)S(1)}, bf16[128,512]{1,0:T(8,128)(2,1)S(1)}, u32[]{:S(2)}, u32[]{:S(2)}) collective-permute-start(bf16[128,512]{1,0:T(8,128)(2,1)S(1)} %slice.17), channel_id=1, source_target_pairs={{0,192},{64,0},{128,64},{192,128},{1,193},{65,1},{129,65},{193,129... | collective-permute-start | bytes 393224 | tf_op jit(solution)/shard_map/ppermute | solution.py:48
  80.2 0.9 copy-done.2
  81.1 0.9 copy-done.3
  82.0 7.8 %attend_own.1 = (bf16[4,1024,128]{2,1,0:T(8,128)(2,1)S(1)}, bf16[4,1024,128]{2,1,0:T(8,128)(2,1)S(1)}, bf16[144,512]{1,0:T(8,128)(2,1)S(1)}, bf16[144,512]{1,0:T(8,128)(2,1)S(1)}) custom-call(s32[16]{0:T(128)S(1)} %reshape.106.valid_ref, bf16[256,512]{1,0:T(8,128)(2,1)S(1)} %copy-done.2, bf16[2048,128]{1,0:T(8,128)(2,1)S(1)} %copy-done, ...), custom_call_target="tpu_custom_call" | custom-call | flops 1 | bytes 1 | tf_op jit(solution)/shard_map/attend_own/pallas_call | solution.py:276
  89.8 3.1 %attend_other.3 = (bf16[144,512]{1,0:T(8,128)(2,1)S(1)}, bf16[144,512]{1,0:T(8,128)(2,1)S(1)}) custom-call(s32[16]{0:T(128)S(1)} %reshape.106.valid_ref, bf16[128,512]{1,0:T(8,128)(2,1)S(1)} %collective-permute-done.14.refs_0_, bf16[128,512]{1,0:T(8,128)(2,1)S(1)} %collective-permute-done.15.refs_1_, bf16[4,1024,128]{2,1,0:T(8,128)(2,1)S(1)} %get-tuple-element.26.refs_2_, ...), custom_call_target="tpu_custom_call" | custom-call | flops 1 | bytes 1 | tf_op jit(solution)/shard_map/attend_other/pallas_call | solution.py:295
  93.0 2.9 %collective-permute-start.17 = (bf16[144,512]{1,0:T(8,128)(2,1)S(1)}, bf16[144,512]{1,0:T(8,128)(2,1)S(1)}, u32[]{:S(2)}, u32[]{:S(2)}) collective-permute-start(bf16[144,512]{1,0:T(8,128)(2,1)S(1)} %get-tuple-element.32), channel_id=1, source_target_pairs={{0,64},{64,128},{128,192},{192,0},{1,65},{65,129},{129,193},{193,1... | collective-permute-start | bytes 442376 | tf_op jit(solution)/shard_map/ppermute | solution.py:48
  95.9 8.8 %attend_other.2 = (bf16[144,512]{1,0:T(8,128)(2,1)S(1)}, bf16[144,512]{1,0:T(8,128)(2,1)S(1)}, bf16[144,512]{1,0:T(8,128)(2,1)S(1)}, bf16[144,512]{1,0:T(8,128)(2,1)S(1)}) custom-call(s32[16]{0:T(128)S(1)} %reshape.106.valid_ref, bf16[256,512]{1,0:T(8,128)(2,1)S(1)} %collective-permute-done.11.refs_0_, bf16[256,512]{1,0:T(8,128)(2,1)S(1)} %collective-permute-done.12.refs_1_, ...), custom_call_target="tpu_custom_call" | custom-call | flops 1 | bytes 1 | tf_op jit(solution)/shard_map/attend_other/pallas_call | solution.py:295
  104.7 3.8 %collective-permute-start.13 = (bf16[144,512]{1,0:T(8,128)(2,1)S(1)}, bf16[144,512]{1,0:T(8,128)(2,1)S(1)}, u32[]{:S(2)}, u32[]{:S(2)}) collective-permute-start(bf16[144,512]{1,0:T(8,128)(2,1)S(1)} %get-tuple-element.28), channel_id=1, source_target_pairs={{0,64},{64,128},{128,192},{192,0},{1,65},{65,129},{129,193},{193,1... | collective-permute-start | bytes 442376 | tf_op jit(solution)/shard_map/ppermute | solution.py:48
  108.4 0.4 collective-permute-start.19
  108.9 0.6 merge_between.1
  109.5 2.9 %collective-permute-start.20 = (bf16[144,512]{1,0:T(8,128)(2,1)S(1)}, bf16[144,512]{1,0:T(8,128)(2,1)S(1)}, u32[]{:S(2)}, u32[]{:S(2)}) collective-permute-start(bf16[144,512]{1,0:T(8,128)(2,1)S(1)} %get-tuple-element.36), channel_id=1, source_target_pairs={{0,64},{64,128},{128,192},{192,0},{1,65},{65,129},{129,193},{193,1... | collective-permute-start | bytes 442376 | tf_op jit(solution)/shard_map/ppermute | solution.py:48
  112.4 2.0 %collective-permute-done.13.refs_1_ = bf16[144,512]{1,0:T(8,128)(2,1)S(1)} collective-permute-done((bf16[144,512]{1,0:T(8,128)(2,1)S(1)}, bf16[144,512]{1,0:T(8,128)(2,1)S(1)}, u32[]{:S(2)}, u32[]{:S(2)}) %collective-permute-start.13) | collective-permute-done | bytes 147488 | tf_op jit(solution)/shard_map/ppermute | solution.py:48
  114.5 3.2 %collective-permute-done.18.refs_2_ = bf16[144,512]{1,0:T(8,128)(2,1)S(1)} collective-permute-done((bf16[144,512]{1,0:T(8,128)(2,1)S(1)}, bf16[144,512]{1,0:T(8,128)(2,1)S(1)}, u32[]{:S(2)}, u32[]{:S(2)}) %collective-permute-start.18) | collective-permute-done | bytes 147488 | tf_op jit(solution)/shard_map/ppermute | solution.py:48
  117.7 1.4 %merge.1 = bf16[256,512]{1,0:T(8,128)(2,1)} custom-call(bf16[144,512]{1,0:T(8,128)(2,1)S(1)} %get-tuple-element.25.refs_0_, bf16[144,512]{1,0:T(8,128)(2,1)S(1)} %collective-permute-done.13.refs_1_, bf16[144,512]{1,0:T(8,128)(2,1)S(1)} %collective-permute-done.18.refs_2_, bf16[144,512]{1,0:T(8,128)(2,1)S(1)} %get-tuple-element.34.refs_3_, ...), custom_call_target="tpu_custom_call" | custom-call | flops 1 | bytes 1 | tf_op jit(solution)/shard_map/merge/pallas_call | solution.py:373
  (54 shorter events, 1.4 us)
Async XLA Ops:
  0.0 22.0 %collective-permute-start = (bf16[256,896]{1,0:T(8,128)(2,1)}, bf16[256,896]{1,0:T(8,128)(2,1)S(1)}, u32[]{:S(2)}, u32[]{:S(2)}) collective-permute-start(bf16[256,896]{1,0:T(8,128)(2,1)} %refs_0_.1), channel_id=1, source_target_pairs={{0,4},{4,0},{1,5},{5,1},{2,6},{6,2},{3,7},{7,3},{8,12},{12,8},{9,1... | collective-permute-start | bytes 1376264 | tf_op jit(solution)/shard_map/ppermute | solution.py:40
  1.8 25.3 %collective-permute-start.1 = (bf16[256,896]{1,0:T(8,128)(2,1)}, bf16[256,896]{1,0:T(8,128)(2,1)S(1)}, u32[]{:S(2)}, u32[]{:S(2)}) collective-permute-start(bf16[256,896]{1,0:T(8,128)(2,1)} %refs_0_.1), channel_id=1, source_target_pairs={{0,3},{1,0},{2,1},{3,2},{4,7},{5,4},{6,5},{7,6},{8,11},{9,8},{10,9... | collective-permute-start | bytes 1376264 | tf_op jit(solution)/shard_map/ppermute | solution.py:36
  2.9 24.3 %collective-permute-start.5 = (bf16[256,896]{1,0:T(8,128)(2,1)}, bf16[256,896]{1,0:T(8,128)(2,1)S(1)}, u32[]{:S(2)}, u32[]{:S(2)}) collective-permute-start(bf16[256,896]{1,0:T(8,128)(2,1)} %refs_0_.1), channel_id=1, source_target_pairs={{0,1},{1,2},{2,3},{3,0},{4,5},{5,6},{6,7},{7,4},{8,9},{9,10},{10,1... | collective-permute-start | bytes 1376264 | tf_op jit(solution)/shard_map/ppermute | solution.py:36
  3.9 50.2 %collective-permute-start.7 = (bf16[2048,128]{1,0:T(8,128)(2,1)}, bf16[2048,128]{1,0:T(8,128)(2,1)S(1)}, u32[]{:S(2)}, u32[]{:S(2)}) collective-permute-start(bf16[2048,128]{1,0:T(8,128)(2,1)} %k0.1), channel_id=1, source_target_pairs={{0,32},{32,0},{1,33},{33,1},{2,34},{34,2},{3,35},{35,3},{4,36},{36... | collective-permute-start | bytes 1572872 | tf_op jit(solution)/shard_map/ppermute | solution.py:44
  7.5 10.4 %collective-permute-start.10 = (s32[4,128]{1,0:T(4,128)S(1)}, s32[4,128]{1,0:T(4,128)S(1)}, u32[]{:S(2)}, u32[]{:S(2)}) collective-permute-start(s32[4,128]{1,0:T(4,128)S(1)} %pad_add_fusion), channel_id=1, source_target_pairs={{0,32},{32,0},{1,33},{33,1},{2,34},{34,2},{3,35},{35,3},{4,36},{36... | collective-permute-start | bytes 6152 | tf_op jit(solution)/shard_map/ppermute | solution.py:44
  17.9 36.2 %collective-permute-start.8 = (bf16[2048,128]{1,0:T(8,128)(2,1)}, bf16[2048,128]{1,0:T(8,128)(2,1)S(1)}, u32[]{:S(2)}, u32[]{:S(2)}) collective-permute-start(bf16[2048,128]{1,0:T(8,128)(2,1)} %v0.1), channel_id=1, source_target_pairs={{0,32},{32,0},{1,33},{33,1},{2,34},{34,2},{3,35},{35,3},{4,36},{36... | collective-permute-start | bytes 1572872 | tf_op jit(solution)/shard_map/ppermute | solution.py:44
  22.0 15.5 %copy-start.6 = (bf16[256,896]{1,0:T(8,128)(2,1)}, bf16[256,896]{1,0:T(8,128)(2,1)S(1)}, u32[]{:S(2)}) copy-start(bf16[256,896]{1,0:T(8,128)(2,1)S(1)} %collective-permute-done.refs_1_) | copy-start | bytes 1376260
  22.0 10.9 %collective-permute-start.3 = (bf16[256,896]{1,0:T(8,128)(2,1)S(1)}, bf16[256,896]{1,0:T(8,128)(2,1)S(1)}, u32[]{:S(2)}, u32[]{:S(2)}) collective-permute-start(bf16[256,896]{1,0:T(8,128)(2,1)S(1)} %collective-permute-done.refs_1_), channel_id=1, source_target_pairs={{0,3},{1,0},{2,1},{3,2},{4,7},{5,4},{6,5},{7,6},{8,11},{9,8},{10,9... | collective-permute-start | bytes 1376264 | tf_op jit(solution)/shard_map/ppermute | solution.py:36
  27.1 10.3 %copy-start.7 = (bf16[256,896]{1,0:T(8,128)(2,1)}, bf16[256,896]{1,0:T(8,128)(2,1)S(1)}, u32[]{:S(2)}) copy-start(bf16[256,896]{1,0:T(8,128)(2,1)S(1)} %collective-permute-done.1.refs_3_) | copy-start | bytes 1376260
  27.1 26.9 %collective-permute-start.2 = (bf16[256,896]{1,0:T(8,128)(2,1)S(1)}, bf16[256,896]{1,0:T(8,128)(2,1)S(1)}, u32[]{:S(2)}, u32[]{:S(2)}) collective-permute-start(bf16[256,896]{1,0:T(8,128)(2,1)S(1)} %collective-permute-done.refs_1_), channel_id=1, source_target_pairs={{0,1},{1,2},{2,3},{3,0},{4,5},{5,6},{6,7},{7,4},{8,9},{9,10},{10,1... | collective-permute-start | bytes 1376264 | tf_op jit(solution)/shard_map/ppermute | solution.py:36
  27.2 10.3 %copy-start.8 = (bf16[256,896]{1,0:T(8,128)(2,1)}, bf16[256,896]{1,0:T(8,128)(2,1)S(1)}, u32[]{:S(2)}) copy-start(bf16[256,896]{1,0:T(8,128)(2,1)S(1)} %collective-permute-done.5.refs_2_) | copy-start | bytes 1376260
  27.2 21.1 %collective-permute-start.6 = (bf16[256,896]{1,0:T(8,128)(2,1)S(1)}, bf16[256,896]{1,0:T(8,128)(2,1)S(1)}, u32[]{:S(2)}, u32[]{:S(2)}) collective-permute-start(bf16[256,896]{1,0:T(8,128)(2,1)S(1)} %collective-permute-done.5.refs_2_), channel_id=1, source_target_pairs={{0,1},{1,2},{2,3},{3,0},{4,5},{5,6},{6,7},{7,4},{8,9},{9,10},{10,1... | collective-permute-start | bytes 1376264 | tf_op jit(solution)/shard_map/ppermute | solution.py:36
  32.9 11.0 %copy-start.9 = (bf16[256,896]{1,0:T(8,128)(2,1)}, bf16[256,896]{1,0:T(8,128)(2,1)S(1)}, u32[]{:S(2)}) copy-start(bf16[256,896]{1,0:T(8,128)(2,1)S(1)} %collective-permute-done.3.refs_1_) | copy-start | bytes 1376260
  32.9 21.2 %collective-permute-start.4 = (bf16[256,896]{1,0:T(8,128)(2,1)S(1)}, bf16[256,896]{1,0:T(8,128)(2,1)S(1)}, u32[]{:S(2)}, u32[]{:S(2)}) collective-permute-start(bf16[256,896]{1,0:T(8,128)(2,1)S(1)} %collective-permute-done.3.refs_1_), channel_id=1, source_target_pairs={{0,3},{1,0},{2,1},{3,2},{4,7},{5,4},{6,5},{7,6},{8,11},{9,8},{10,9... | collective-permute-start | bytes 1376264 | tf_op jit(solution)/shard_map/ppermute | solution.py:36
  48.3 0.8 copy-start.10
  54.1 0.8 copy-start.4
  54.1 0.9 copy-start.5
  55.0 25.1 %copy-start = (bf16[2048,128]{1,0:T(8,128)(2,1)S(1)}, bf16[2048,128]{1,0:T(8,128)(2,1)}, u32[]{:S(2)}) copy-start(bf16[2048,128]{1,0:T(8,128)(2,1)} %k0.1) | copy-start | bytes 1572868
  55.0 25.1 %copy-start.1 = (bf16[2048,128]{1,0:T(8,128)(2,1)S(1)}, bf16[2048,128]{1,0:T(8,128)(2,1)}, u32[]{:S(2)}) copy-start(bf16[2048,128]{1,0:T(8,128)(2,1)} %v0.1) | copy-start | bytes 1572868
  60.2 15.3 %collective-permute-start.11 = (bf16[256,512]{1,0:T(8,128)(2,1)}, bf16[256,512]{1,0:T(8,128)(2,1)S(1)}, u32[]{:S(2)}, u32[]{:S(2)}) collective-permute-start(bf16[256,512]{1,0:T(8,128)(2,1)} %get-tuple-element.23.q_ref), channel_id=1, source_target_pairs={{0,64},{64,128},{128,192},{192,0},{1,65},{65,129},{129,193},{193,1... | collective-permute-start | bytes 786440 | tf_op jit(solution)/shard_map/ppermute | solution.py:48
  63.5 14.0 %collective-permute-start.12 = (bf16[256,512]{1,0:T(8,128)(2,1)}, bf16[256,512]{1,0:T(8,128)(2,1)S(1)}, u32[]{:S(2)}, u32[]{:S(2)}) collective-permute-start(bf16[256,512]{1,0:T(8,128)(2,1)} %get-tuple-element.23.q_ref), channel_id=1, source_target_pairs={{0,192},{64,0},{128,64},{192,128},{1,193},{65,1},{129,65},{193,129... | collective-permute-start | bytes 786440 | tf_op jit(solution)/shard_map/ppermute | solution.py:48
  66.5 13.6 %collective-permute-start.9 = (bf16[512,128]{1,0:T(8,128)(2,1)}, bf16[512,128]{1,0:T(8,128)(2,1)S(1)}, u32[]{:S(2)}, u32[]{:S(2)}) collective-permute-start(bf16[512,128]{1,0:T(8,128)(2,1)} %get-tuple-element.24.n0), channel_id=1, source_target_pairs={{0,32},{32,0},{1,33},{33,1},{2,34},{34,2},{3,35},{35,3},{4,36},{36... | collective-permute-start | bytes 393224 | tf_op jit(solution)/shard_map/ppermute | solution.py:44
  75.5 14.3 %collective-permute-start.14 = (bf16[128,512]{1,0:T(8,128)(2,1)S(1)}, bf16[128,512]{1,0:T(8,128)(2,1)S(1)}, u32[]{:S(2)}, u32[]{:S(2)}) collective-permute-start(bf16[128,512]{1,0:T(8,128)(2,1)S(1)} %slice.16), channel_id=1, source_target_pairs={{0,64},{64,128},{128,192},{192,0},{1,65},{65,129},{129,193},{193,1... | collective-permute-start | bytes 393224 | tf_op jit(solution)/shard_map/ppermute | solution.py:48
  77.5 12.3 %collective-permute-start.15 = (bf16[128,512]{1,0:T(8,128)(2,1)S(1)}, bf16[128,512]{1,0:T(8,128)(2,1)S(1)}, u32[]{:S(2)}, u32[]{:S(2)}) collective-permute-start(bf16[128,512]{1,0:T(8,128)(2,1)S(1)} %slice.17), channel_id=1, source_target_pairs={{0,192},{64,0},{128,64},{192,128},{1,193},{65,1},{129,65},{193,129... | collective-permute-start | bytes 393224 | tf_op jit(solution)/shard_map/ppermute | solution.py:48
  80.2 1.0 copy-start.2
  81.1 0.9 copy-start.3
  92.9 16.0 %collective-permute-start.16 = (bf16[144,512]{1,0:T(8,128)(2,1)S(1)}, bf16[144,512]{1,0:T(8,128)(2,1)S(1)}, u32[]{:S(2)}, u32[]{:S(2)}) collective-permute-start(bf16[144,512]{1,0:T(8,128)(2,1)S(1)} %get-tuple-element.30), channel_id=1, source_target_pairs={{0,192},{64,0},{128,64},{192,128},{1,193},{65,1},{129,65},{193,129... | collective-permute-start | bytes 442376 | tf_op jit(solution)/shard_map/ppermute | solution.py:48
  93.0 15.9 %collective-permute-start.17 = (bf16[144,512]{1,0:T(8,128)(2,1)S(1)}, bf16[144,512]{1,0:T(8,128)(2,1)S(1)}, u32[]{:S(2)}, u32[]{:S(2)}) collective-permute-start(bf16[144,512]{1,0:T(8,128)(2,1)S(1)} %get-tuple-element.32), channel_id=1, source_target_pairs={{0,64},{64,128},{128,192},{192,0},{1,65},{65,129},{129,193},{193,1... | collective-permute-start | bytes 442376 | tf_op jit(solution)/shard_map/ppermute | solution.py:48
  104.7 9.8 %collective-permute-start.13 = (bf16[144,512]{1,0:T(8,128)(2,1)S(1)}, bf16[144,512]{1,0:T(8,128)(2,1)S(1)}, u32[]{:S(2)}, u32[]{:S(2)}) collective-permute-start(bf16[144,512]{1,0:T(8,128)(2,1)S(1)} %get-tuple-element.28), channel_id=1, source_target_pairs={{0,64},{64,128},{128,192},{192,0},{1,65},{65,129},{129,193},{193,1... | collective-permute-start | bytes 442376 | tf_op jit(solution)/shard_map/ppermute | solution.py:48
  108.4 6.0 %collective-permute-start.19 = (bf16[144,512]{1,0:T(8,128)(2,1)S(1)}, bf16[144,512]{1,0:T(8,128)(2,1)S(1)}, u32[]{:S(2)}, u32[]{:S(2)}) collective-permute-start(bf16[144,512]{1,0:T(8,128)(2,1)S(1)} %get-tuple-element.35), channel_id=1, source_target_pairs={{0,192},{64,0},{128,64},{192,128},{1,193},{65,1},{129,65},{193,129... | collective-permute-start | bytes 442376 | tf_op jit(solution)/shard_map/ppermute | solution.py:48
  109.4 8.3 %collective-permute-start.18 = (bf16[144,512]{1,0:T(8,128)(2,1)S(1)}, bf16[144,512]{1,0:T(8,128)(2,1)S(1)}, u32[]{:S(2)}, u32[]{:S(2)}) collective-permute-start(bf16[144,512]{1,0:T(8,128)(2,1)S(1)} %get-tuple-element.33), channel_id=1, source_target_pairs={{0,192},{64,0},{128,64},{192,128},{1,193},{65,1},{129,65},{193,129... | collective-permute-start | bytes 442376 | tf_op jit(solution)/shard_map/ppermute | solution.py:48
  109.5 8.2 %collective-permute-start.20 = (bf16[144,512]{1,0:T(8,128)(2,1)S(1)}, bf16[144,512]{1,0:T(8,128)(2,1)S(1)}, u32[]{:S(2)}, u32[]{:S(2)}) collective-permute-start(bf16[144,512]{1,0:T(8,128)(2,1)S(1)} %get-tuple-element.36), channel_id=1, source_target_pairs={{0,64},{64,128},{128,192},{192,0},{1,65},{65,129},{129,193},{193,1... | collective-permute-start | bytes 442376 | tf_op jit(solution)/shard_map/ppermute | solution.py:48
where the time goes:
time: 121 us; the launch traced here: 119 us
  starting transfers between devices  38.6 us (32%)
  Pallas kernels  38 us (31%)
  waiting for transfers between devices  29.1 us (24%)
  other arithmetic  8.21 us (7%)
  local copies, waits for them, and re-layouts  4.93 us (4%)
    ppermute x10, starting transfers between devices, ph(): return lax.ppermute(v, 'zh', [(i, (i + s) % 4) for i in range(4)])  20.6 us
    pallas_call x3, Pallas kernels, project(): pl.pallas_call(functools.partial(project_kernel, n, acc is not None, rot...  16.5 us
    ppermute x10, waiting for transfers between devices, ph(): return lax.ppermute(v, 'zh', [(i, (i + s) % 4) for i in range(4)])  13.7 us
    pallas_call x2, Pallas kernels, attend_other(): pl.pallas_call(functools.partial(other_kernel, len(queries), shifts), out...  11.8 us
    ppermute x6, waiting for transfers between devices, px(): return lax.ppermute(v, 'x', [(i, (i + s) % 4) for i in range(4)])  10.1 us
    ppermute x6, starting transfers between devices, px(): return lax.ppermute(v, 'x', [(i, (i + s) % 4) for i in range(4)])  8.83 us
    pallas_call x1, Pallas kernels, attend_own(): pl.pallas_call(own_kernel, out_shape=(joined_shape, joined_shape, packed_...  7.76 us
    ppermute x4, starting transfers between devices, py(): return lax.ppermute(v, 'yh', [(0, 1), (1, 0)])  7.33 us
  transfers between devices with their start and end apart: 21, of which 6 were waited for; matrix products, arithmetic and copies ran while one was open for 8% of the time, Pallas kernels for 24%

commit v1 on v0

v1 whole, which is shorter than its diff:
```python
import functools
import math

import jax
import jax.numpy as jnp
from jax import lax
from jax.experimental import pallas as pl
from jax.experimental.pallas import tpu as pltpu
from jax.sharding import Mesh, PartitionSpec as P

HD = 128
HG = 4
R = 8
MAXCH = 8
SPAN = 1024
SEL = 128
SLOTS = 2
ROWS = SLOTS * SEL
QW = HG * HD
PACK = SEL + 16
DK = 896
PROJ = 16

rope_base = 5000000.0
low = -1.0e30
SCALE2 = math.log2(math.e) / math.sqrt(HD)

vmem = pl.BlockSpec(memory_space=pltpu.VMEM)
smem = pl.BlockSpec(memory_space=pltpu.SMEM)
hbm = pl.BlockSpec(memory_space=pltpu.HBM)
tiny = pl.CostEstimate(flops=1, bytes_accessed=1, transcendentals=0)


def work(microseconds):
    return pl.CostEstimate(
        flops=microseconds * 1000000000, bytes_accessed=1, transcendentals=0
    )


AXES = ("zh", "yh", "yp", "c", "zl", "x")


def opposite_ways(n):
    plus = [(i, (i + 1) % n) for i in range(n)]
    minus = [(n + i, n + (i - 1) % n) for i in range(n)]
    return plus + minus


def ring_x(v):
    return lax.ppermute(v, ("c", "x"), opposite_ways(4))


def ring_z(v):
    pairs = [(2 * i + c, 2 * ((i + 1 - 2 * c) % 4) + c) for i in range(4) for c in range(2)]
    return lax.ppermute(v, ("zh", "c"), pairs)


def pz(v):
    return lax.ppermute(v, "zl", [(0, 1), (1, 0)])


def py(v):
    return lax.ppermute(v, "yh", [(0, 1), (1, 0)])


def span_ranks(span_count, span_key):
    column = jnp.arange(MAXCH, dtype=jnp.int32)
    filled = column[None, :] < span_count[:, None]
    earlier = span_key[:, :, None] < span_key[:, None, :]
    ranks = jnp.sum((earlier & filled[:, :, None]).astype(jnp.int32), axis=1, dtype=jnp.int32)
    return filled.T.reshape(-1), ranks.T.reshape(-1)


def tables(position):
    freq = rope_base ** (-(jnp.arange(HD // 2, dtype=jnp.float32) * 2.0) / HD)
    angle = position.astype(jnp.float32)[:, None] * freq
    cosine, sine = jnp.cos(angle), jnp.sin(angle)
    return jnp.concatenate([cosine, cosine], -1), jnp.concatenate([-sine, sine], -1)


def turned(v, cosine, sine):
    return v * cosine + pltpu.roll(v, HD // 2, 1) * sine


def weight_copies(sources, idx_ref, i, to_ref, slot, sem):
    at = pl.ds(pl.multiple_of(idx_ref[i] * DK, DK), DK)
    start = 0
    for j, (w, width) in enumerate(zip(sources, (QW, HD, HD))):
        to = to_ref.at[slot, :, start : start + width]
        yield pltpu.make_async_copy(w.at[at, :], to, sem.at[i, j])
        start += width


def partial_kernel(count, ahead, carried, idx_ref, *refs):
    pieces, refs = refs[:count], refs[count:]
    sources, refs = refs[:3], refs[3:]
    if carried:
        acc_ref, refs = refs[0], refs[1:]
    out_ref, refs = refs[0], refs[1:]
    if ahead:
        next_ref, refs = refs[0], refs[1:]
    held, weight, sem = refs
    for i in range(count + ahead):
        to, slot = (weight, i) if i < count else (next_ref, i - count)
        for copy in weight_copies(sources, idx_ref, i, to, slot, sem):
            copy.start()
    for i in range(count):
        held[i] = pieces[i][...]

    def add(i, acc):
        for copy in weight_copies(sources, idx_ref, i, weight, i, sem):
            copy.wait()
        return acc + jnp.dot(held[i], weight[i], preferred_element_type=jnp.float32)

    begin = acc_ref[...] if carried else jnp.zeros((ROWS, QW + 2 * HD), jnp.float32)
    out_ref[...] = lax.fori_loop(0, count, add, begin)
    for i in range(count, count + ahead):
        for copy in weight_copies(sources, idx_ref, i, next_ref, i - count, sem):
            copy.wait()


def partial_project(idx, pieces, weights, acc=None, ahead=0):
    n = len(pieces)
    sums = jax.ShapeDtypeStruct((ROWS, QW + 2 * HD), jnp.float32)
    kept = jax.ShapeDtypeStruct((ahead, DK, QW + 2 * HD), jnp.bfloat16)
    extra = [] if acc is None else [acc]
    weights = [pltpu.with_memory_space_constraint(w, pltpu.HBM) for w in weights]
    return pl.pallas_call(
        functools.partial(partial_kernel, n, ahead, acc is not None),
        out_shape=(sums, kept) if ahead else sums,
        in_specs=[smem] + [vmem] * n + [hbm] * 3 + [vmem] * len(extra),
        out_specs=(vmem, vmem) if ahead else vmem,
        scratch_shapes=[
            pltpu.VMEM((n, ROWS, DK), jnp.bfloat16),
            pltpu.VMEM((n, DK, QW + 2 * HD), jnp.bfloat16),
            pltpu.SemaphoreType.DMA((n + ahead, 3)),
        ],
        compiler_params=pltpu.CompilerParams(vmem_limit_bytes=16 << 20),
        cost_estimate=work(6),
        name="project",
    )(idx, *pieces, *weights, *extra)


def last_kernel(piece_ref, weight_ref, acc_ref, cos_ref, sin_ref, q_ref, n_ref):
    acc = acc_ref[...] + jnp.dot(
        piece_ref[...], weight_ref[0], preferred_element_type=jnp.float32
    )
    cosine, sine = cos_ref[...], sin_ref[...]
    for g in range(HG):
        at = slice(g * HD, (g + 1) * HD)
        q_ref[:, at] = turned(acc[:, at], cosine, sine).astype(jnp.bfloat16)
    n_ref[:ROWS, :] = turned(acc[:, QW : QW + HD], cosine, sine).astype(jnp.bfloat16)
    n_ref[ROWS:, :] = acc[:, QW + HD :].astype(jnp.bfloat16)


def last_project(*args):
    return pl.pallas_call(
        last_kernel,
        out_shape=(
            jax.ShapeDtypeStruct((ROWS, QW), jnp.bfloat16),
            jax.ShapeDtypeStruct((2 * ROWS, HD), jnp.bfloat16),
        ),
        in_specs=[vmem] * 5,
        out_specs=(vmem, vmem),
        compiler_params=pltpu.CompilerParams(vmem_limit_bytes=16 << 20),
        cost_estimate=tiny,
        name="project_last",
    )(*args)


def attend_block(at, q_ref, keys, vals, limit, m_ref, l_ref, acc_ref):
    s = lax.dot_general(
        q_ref[at, :], keys, (((1,), (1,)), ((), ())), preferred_element_type=jnp.float32
    )
    if limit is not None:
        col = lax.broadcasted_iota(jnp.int32, s.shape, 1)
        s = jnp.where(col <= limit, s, low)
    old = m_ref[at, :]
    new = jnp.maximum(old, jnp.max(s, axis=1, keepdims=True))
    factor = jnp.exp2((old - new) * SCALE2)
    weight = jnp.exp2((s - new) * SCALE2)
    l_ref[at, :] = l_ref[at, :] * factor + jnp.sum(weight, axis=1, keepdims=True)
    acc_ref[at, :] = acc_ref[at, :] * factor + jnp.dot(
        weight.astype(jnp.bfloat16), vals, preferred_element_type=jnp.float32
    )
    m_ref[at, :] = new


def attend_source(rows_ref, i, jk_ref, jv_ref, r, valid_ref, first, o_ref, state, limit_ref=None):
    m_ref, l_ref, acc_ref = state
    m_ref[...] = jnp.full_like(m_ref, low)
    l_ref[...] = jnp.zeros_like(l_ref)
    acc_ref[...] = jnp.zeros_like(acc_ref)

    def span(step, _):
        sp = step // 2

        @pl.when(valid_ref[first + sp] != 0)
        def _():
            at = pl.ds(pl.multiple_of((step % 2) * 2 * SEL, 2 * SEL), 2 * SEL)
            limit = None if limit_ref is None else jnp.where(sp == 0, limit_ref[at, :], SPAN)
            attend_block(
                at, rows_ref.at[i], jk_ref[r * 2 + sp], jv_ref[r * 2 + sp], limit,
                m_ref, l_ref, acc_ref,
            )

        return 0

    lax.fori_loop(0, 4, span, 0)
    l = l_ref[...]
    some = l > 0.0
    mixed = acc_ref[...] / jnp.where(some, l, 1.0)
    lse = jnp.where(some, m_ref[...] * SCALE2 + jnp.log2(jnp.where(some, l, 1.0)), low)
    lane = lax.broadcasted_iota(jnp.int32, (SEL, HD), 1)
    stat = jnp.zeros((SEL, HD), jnp.float32)
    for g in range(HG):
        o_ref[i, :SEL, g * HD : (g + 1) * HD] = mixed[g * SEL : (g + 1) * SEL].astype(jnp.bfloat16)
        rest = lse[g * SEL : (g + 1) * SEL]
        for k in range(3):
            part = rest.astype(jnp.bfloat16).astype(jnp.float32)
            stat = jnp.where(lane == k * HG + g, part, stat)
            rest = rest - part
    o_ref[i, SEL:, :HD] = stat.T[:16].astype(jnp.bfloat16)
    o_ref[i, SEL:, HD:] = jnp.zeros((16, QW - HD), jnp.bfloat16)


def spread(rows_ref, i, q):
    for g in range(HG):
        rows_ref[i, g * SEL : (g + 1) * SEL, :] = q[:, g * HD : (g + 1) * HD]


def join_kernel(k0, v0, k1, v1, n0, n1, selr_ref, rot_ref, jk_ref, jv_ref):
    def request(r, _):
        base = pl.ds(pl.multiple_of(r * SPAN, SPAN), SPAN)
        fresh_k = pl.ds(pl.multiple_of(r * SEL, SEL), SEL)
        fresh_v = pl.ds(pl.multiple_of(ROWS + r * SEL, SEL), SEL)
        for sp, (kr, vr, nr) in enumerate(((k0, v0, n0), (k1, v1, n1))):
            cached = turned(
                kr[base, :].astype(jnp.float32),
                rot_ref[r, sp : sp + 1, :],
                rot_ref[r, sp + 2 : sp + 3, :],
            )
            at = lax.broadcasted_iota(jnp.int32, (SPAN, SEL), 0)
            pick = (at == selr_ref[r, sp : sp + 1, :]).astype(jnp.float32).astype(jnp.bfloat16)
            ones = jnp.ones((SEL, HD), jnp.bfloat16)
            hit = jnp.dot(pick, ones, preferred_element_type=jnp.float32) > 0.5
            put_k = jnp.dot(pick, nr[fresh_k, :], preferred_element_type=jnp.float32)
            put_v = jnp.dot(pick, nr[fresh_v, :], preferred_element_type=jnp.float32)
            vals = vr[base, :].astype(jnp.float32)
            jk_ref[r * 2 + sp] = jnp.where(hit, put_k, cached).astype(jnp.bfloat16)
            jv_ref[r * 2 + sp] = jnp.where(hit, put_v, vals).astype(jnp.bfloat16)
        return 0

    lax.fori_loop(0, SLOTS, request, 0)


def attend_kernel(shift, valid_ref, q_ref, jk_ref, jv_ref, *refs):
    if shift == 0:
        selr_ref, o_ref, rows_ref, limit_ref = refs[:4]
        state = refs[4:]
    else:
        o_ref, rows_ref = refs[:2]
        limit_ref, state = None, refs[2:]
    for r in range(SLOTS):
        spread(rows_ref, r, q_ref[r * SEL : (r + 1) * SEL, :])

    def request(r, _):
        if shift == 0:
            sel = selr_ref[r, 0:1, :].astype(jnp.float32)
            column = jnp.broadcast_to(sel, (SEL, SEL)).T[:, :1].astype(jnp.int32)
            limit_ref[...] = jnp.concatenate([column] * HG, axis=0)
        attend_source(
            rows_ref, r, jk_ref, jv_ref, r, valid_ref, shift * 4 + r * 2, o_ref, state, limit_ref
        )
        return 0

    lax.fori_loop(0, SLOTS, request, 0)


joined_shape = jax.ShapeDtypeStruct((SLOTS * 2, SPAN, HD), jnp.bfloat16)
packed_shape = jax.ShapeDtypeStruct((SLOTS, PACK, QW), jnp.bfloat16)


def join(*args):
    return pl.pallas_call(
        join_kernel,
        out_shape=(joined_shape, joined_shape),
        in_specs=[vmem] * 8,
        out_specs=(vmem, vmem),
        compiler_params=pltpu.CompilerParams(vmem_limit_bytes=16 << 20),
        cost_estimate=work(3),
        name="join",
    )(*args)


def attend(shift, valid, *args):
    return pl.pallas_call(
        functools.partial(attend_kernel, shift),
        out_shape=packed_shape,
        in_specs=[smem] + [vmem] * len(args),
        out_specs=vmem,
        scratch_shapes=[pltpu.VMEM((SLOTS, HG * SEL, HD), jnp.bfloat16)]
        + ([pltpu.VMEM((HG * SEL, 1), jnp.int32)] if shift == 0 else [])
        + [
            pltpu.VMEM((HG * SEL, 1), jnp.float32),
            pltpu.VMEM((HG * SEL, 1), jnp.float32),
            pltpu.VMEM((HG * SEL, HD), jnp.float32),
        ],
        compiler_params=pltpu.CompilerParams(vmem_limit_bytes=16 << 20),
        cost_estimate=work(4),
        name="attend",
    )(valid, *args)


def merge_parts(parts, put, stat_put=None):
    lse = []
    for p in parts:
        stat = p[SEL:, :HD].astype(jnp.float32)
        lse.append(stat[0:4] + stat[4:8] + stat[8:12])
    top = functools.reduce(jnp.maximum, lse)
    weight = [jnp.exp2(v - top) for v in lse]
    total = functools.reduce(jnp.add, weight)
    pad = jnp.zeros((HD - HG, SEL), jnp.float32)
    weight = [jnp.concatenate([w / total, pad], axis=0).T for w in weight]
    for g in range(HG):
        at = slice(g * HD, (g + 1) * HD)
        mixed = jnp.zeros((SEL, HD), jnp.float32)
        for w, p in zip(weight, parts):
            mixed += w[:, g : g + 1] * p[:SEL, at].astype(jnp.float32)
        put(at, mixed.astype(jnp.bfloat16))
    if stat_put is not None:
        rest = top + jnp.log2(total)
        rows = []
        for _ in range(3):
            part = rest.astype(jnp.bfloat16).astype(jnp.float32)
            rows.append(part)
            rest = rest - part
        stat_put(jnp.concatenate(rows + [jnp.zeros_like(top)], axis=0).astype(jnp.bfloat16))


def between_kernel(a_ref, b_ref, o_ref):
    for r in range(SLOTS):

        def put(at, value, r=r):
            o_ref[r, :SEL, at] = value

        def stat_put(value, r=r):
            o_ref[r, SEL:, :HD] = value
            o_ref[r, SEL:, HD:] = jnp.zeros((16, QW - HD), jnp.bfloat16)

        merge_parts((a_ref.at[r], b_ref.at[r]), put, stat_put)


def between(*parts):
    return pl.pallas_call(
        between_kernel,
        out_shape=packed_shape,
        in_specs=[vmem] * 2,
        out_specs=vmem,
        compiler_params=pltpu.CompilerParams(vmem_limit_bytes=8 << 20),
        cost_estimate=work(1),
        name="merge_between",
    )(*parts)


def merge_kernel(a_ref, b_ref, o_ref):
    for r in range(SLOTS):

        def put(at, value, r=r):
            o_ref[r * SEL : (r + 1) * SEL, at] = value

        merge_parts((a_ref.at[r], b_ref.at[r]), put)


def merge(*parts):
    return pl.pallas_call(
        merge_kernel,
        out_shape=jax.ShapeDtypeStruct((ROWS, QW), jnp.bfloat16),
        in_specs=[vmem] * 2,
        out_specs=vmem,
        compiler_params=pltpu.CompilerParams(vmem_limit_bytes=8 << 20),
        cost_estimate=tiny,
        name="merge",
    )(*parts)


def after(value, *others):
    return lax.optimization_barrier((value, *others))[0]


def shards(
    hidden, w_query, w_key, w_value, key_cache, value_cache,
    span_count, span_key, cache_offset, sel_index,
):
    zh, yh, yp, c = (lax.axis_index(a) for a in ("zh", "yh", "yp", "c"))
    zl, x = lax.axis_index("zl"), lax.axis_index("x")
    weights = (w_query, w_key, w_value)
    way = 2 * c - 1
    mine = jnp.concatenate(
        [sel_index, jnp.broadcast_to(cache_offset[:, None], (SLOTS, SEL))], axis=0
    )
    theirs = py(mine)
    h = [hidden, ring_x(hidden)]
    z = [pz(hidden)]
    k1 = py(after(key_cache, theirs))
    v1 = py(value_cache)
    for _ in range(2):
        h.append(ring_x(h[-1]))
    for _ in range(3):
        z.append(ring_x(z[-1]))
    h_idx = [zl * 4 + (x + i * way) % 4 for i in range(4)]
    z_idx = [(1 - zl) * 4 + (x + i * way) % 4 for i in range(4)]
    table = lambda *entries: jnp.stack(entries).astype(jnp.int32)

    filled_all, rank_all = span_ranks(span_count, span_key)

    def lookup(h, half):
        start = (((h * 2 + half) * 2 + yp) * 2 + c) * SLOTS
        return (
            lax.dynamic_slice_in_dim(filled_all, start, SLOTS),
            lax.dynamic_slice_in_dim(rank_all, start, SLOTS),
        )

    span_f, span_r = zip(lookup(zh, yh), lookup(zh, 1 - yh))

    def validity(shift):
        qf, qr = lookup((zh + shift * way) % 4, yh)
        table = [qf & kf & (kr <= qr) for kf, kr in zip(span_f, span_r)]
        return jnp.stack(table, axis=1).astype(jnp.int32)

    position = (span_r[0][:, None] * SPAN + sel_index).reshape(-1)
    cosine, sine = tables(position)
    delta = jnp.stack(
        [span_r[0] * SPAN - cache_offset, span_r[1] * SPAN - theirs[SLOTS:, 0]], axis=1
    ).reshape(-1)
    turn_c, turn_s = tables(delta)
    rot = jnp.concatenate(
        [turn_c.reshape(SLOTS, 2, HD), turn_s.reshape(SLOTS, 2, HD)], axis=1
    )
    sel_rows = jnp.stack([sel_index, theirs[:SLOTS]], axis=1)
    valid = jnp.concatenate([validity(s) for s in range(4)], axis=0).reshape(-1)

    acc = partial_project(table(h_idx[0]), (hidden,), weights)
    acc = partial_project(table(h_idx[1], z_idx[0]), (h[1], z[0]), weights, acc)
    acc = partial_project(table(h_idx[2], z_idx[1]), (h[2], z[1]), weights, acc)
    acc, kept = partial_project(
        table(h_idx[3], z_idx[2], z_idx[3]), (h[3], z[2]), weights, acc, ahead=1
    )
    acc = after(acc, k1, v1)
    query, fresh = last_project(z[3], kept, acc, cosine, sine)
    ring = [query]
    for _ in range(3):
        ring.append(ring_z(ring[-1]))
    jk, jv = join(key_cache, value_cache, k1, v1, fresh, py(fresh), sel_rows, rot)
    own = attend(0, valid, query, jk, jv, sel_rows)
    out = attend(1, valid, ring[1], jk, jv)
    for i in (2, 3):
        out = between(attend(i, valid, ring[i], jk, jv), ring_z(out))
    return merge(own, ring_z(out))


def solution(mesh):
    split = Mesh(mesh.devices.reshape(4, 2, 2, 2, 2, 4), AXES)
    seq, tp = AXES[:4], AXES[4:]
    placed = (
        P(seq, tp),
        P(None, tp),
        P(None, tp),
        P(None, tp),
        P(seq, tp),
        P(seq, tp),
        P(),
        P(),
        P(seq),
        P(seq, None),
    )
    return jax.shard_map(
        shards, mesh=split, in_specs=placed, out_specs=P(seq, tp), check_vma=False
    )
```

time: 121 us -> 108 us (0.89)
  the two profiles are of different devices: /device:TPU:32 before, /device:TPU:8 now
where the time goes in v1:
time: 108 us; the launch traced here: 110 us
  waiting for transfers between devices  35.2 us (33%)
  Pallas kernels  33.1 us (31%)
  starting transfers between devices  32.9 us (30%)
  local copies, waits for them, and re-layouts  4.4 us (4%)
  other arithmetic  3.94 us (4%)
    ppermute x6, waiting for transfers between devices, ring_z(): return lax.ppermute(v, ('zh', 'c'), pairs)  18.7 us
    ppermute x6, starting transfers between devices, ring_z(): return lax.ppermute(v, ('zh', 'c'), pairs)  18.6 us
    pallas_call x4, Pallas kernels, attend(): pl.pallas_call(functools.partial(attend_kernel, shift), out_shape=packed_...  17.2 us
    ppermute x6, waiting for transfers between devices, ring_x(): return lax.ppermute(v, ('c', 'x'), opposite_ways(4))  15 us
    pallas_call x4, Pallas kernels, partial_project(): pl.pallas_call(functools.partial(partial_kernel, n, ahead, acc is not Non...  11.6 us
    ppermute x4, starting transfers between devices, py(): return lax.ppermute(v, 'yh', [(0, 1), (1, 0)])  7.23 us
    ppermute x6, starting transfers between devices, ring_x(): return lax.ppermute(v, ('c', 'x'), opposite_ways(4))  5.1 us
    unnamed x14, local copies, waits for them, and re-layouts  3.06 us
  transfers between devices with their start and end apart: 17, of which 10 were waited for; matrix products, arithmetic and copies ran while one was open for 5% of the time, Pallas kernels for 28%

profile of v1, /device:TPU:8, one launch (start us, length us, event | category | flops | bytes accessed | tf_op | source)
XLA Modules:
  0.0 109.7 jit_solution(1063586898329359922)
XLA Ops:
  0.0 1.9 %collective-permute-start = (bf16[256,896]{1,0:T(8,128)(2,1)}, bf16[256,896]{1,0:T(8,128)(2,1)S(1)}, u32[]{:S(2)}, u32[]{:S(2)}) collective-permute-start(bf16[256,896]{1,0:T(8,128)(2,1)} %refs_0_.1), channel_id=1, source_target_pairs={{0,4},{4,0},{1,5},{5,1},{2,6},{6,2},{3,7},{7,3},{8,12},{12,8},{9,1... | collective-permute-start | bytes 1376264 | tf_op jit(solution)/shard_map/ppermute | solution.py:59
  1.9 1.5 %collective-permute-start.4 = (bf16[256,896]{1,0:T(8,128)(2,1)}, bf16[256,896]{1,0:T(8,128)(2,1)S(1)}, u32[]{:S(2)}, u32[]{:S(2)}) collective-permute-start(bf16[256,896]{1,0:T(8,128)(2,1)} %refs_0_.1), channel_id=1, source_target_pairs={{0,1},{1,2},{2,3},{3,0},{8,11},{9,8},{10,9},{11,10},{4,5},{5,6},{6... | collective-permute-start | bytes 1376264 | tf_op jit(solution)/shard_map/ppermute | solution.py:50
  3.4 0.7 pad.13.clone
  4.1 0.7 pad_add_fusion
  4.9 2.3 %collective-permute-start.7 = (s32[4,128]{1,0:T(4,128)S(1)}, s32[4,128]{1,0:T(4,128)S(1)}, u32[]{:S(2)}, u32[]{:S(2)}) collective-permute-start(s32[4,128]{1,0:T(4,128)S(1)} %pad_add_fusion), channel_id=1, source_target_pairs={{0,32},{32,0},{1,33},{33,1},{2,34},{34,2},{3,35},{35,3},{4,36},{36... | collective-permute-start | bytes 6152 | tf_op jit(solution)/shard_map/ppermute | solution.py:63
  7.2 1.2 %collective-permute-start.9 = (bf16[2048,128]{1,0:T(8,128)(2,1)}, bf16[2048,128]{1,0:T(8,128)(2,1)S(1)}, u32[]{:S(2)}, u32[]{:S(2)}) collective-permute-start(bf16[2048,128]{1,0:T(8,128)(2,1)} %v0.1), channel_id=1, source_target_pairs={{0,32},{32,0},{1,33},{33,1},{2,34},{34,2},{3,35},{35,3},{4,36},{36... | collective-permute-start | bytes 1572872 | tf_op jit(solution)/shard_map/ppermute | solution.py:63
  8.4 0.8 iota_compare_fusion.1
  9.4 0.9 convert_reduce_fusion
  10.3 1.0 copy-done.2
  11.4 1.9 %project.4.refs_5_ = f32[256,768]{1,0:T(8,128)S(1)} custom-call(s32[1]{0:T(128)} %bitcast.16.idx_ref, bf16[256,896]{1,0:T(8,128)(2,1)S(1)} %copy-done.2, bf16[7168,512]{1,0:T(8,128)(2,1)} %refs_2_.7, bf16[7168,128]{1,0:T(8,128)(2,1)} %refs_3_.7, bf16[7168,128]{1,0:T(8,128)(2,1)} %refs_4_.5), custom_call_target="tpu_custom_call" | custom-call | flops 6000000000 | bytes 1 | tf_op jit(solution)/shard_map/project/pallas_call | solution.py:128
  13.3 0.9 copy-done.3
  14.5 2.4 %collective-permute-start.8 = (bf16[2048,128]{1,0:T(8,128)(2,1)S(1)}, bf16[2048,128]{1,0:T(8,128)(2,1)S(1)}, u32[]{:S(2)}, u32[]{:S(2)}) collective-permute-start(bf16[2048,128]{1,0:T(8,128)(2,1)S(1)} %copy-done), channel_id=1, source_target_pairs={{0,32},{32,0},{1,33},{33,1},{2,34},{34,2},{3,35},{35,3},{4,36},{36... | collective-permute-start | bytes 1572872 | tf_op jit(solution)/shard_map/ppermute | solution.py:63
  17.1 0.5 fusion
  17.7 0.1 pad_maximum_fusion
  18.2 1.6 %collective-permute-start.1 = (bf16[256,896]{1,0:T(8,128)(2,1)S(1)}, bf16[256,896]{1,0:T(8,128)(2,1)S(1)}, u32[]{:S(2)}, u32[]{:S(2)}) collective-permute-start(bf16[256,896]{1,0:T(8,128)(2,1)S(1)} %collective-permute-done.refs_1_), channel_id=1, source_target_pairs={{0,1},{1,2},{2,3},{3,0},{8,11},{9,8},{10,9},{11,10},{4,5},{5,6},{6... | collective-permute-start | bytes 1376264 | tf_op jit(solution)/shard_map/ppermute | solution.py:50
  19.8 1.2 %collective-permute-start.5 = (bf16[256,896]{1,0:T(8,128)(2,1)S(1)}, bf16[256,896]{1,0:T(8,128)(2,1)S(1)}, u32[]{:S(2)}, u32[]{:S(2)}) collective-permute-start(bf16[256,896]{1,0:T(8,128)(2,1)S(1)} %collective-permute-done.4.refs_0_), channel_id=1, source_target_pairs={{0,1},{1,2},{2,3},{3,0},{8,11},{9,8},{10,9},{11,10},{4,5},{5,6},{6... | collective-permute-start | bytes 1376264 | tf_op jit(solution)/shard_map/ppermute | solution.py:50
  21.0 1.1 %copy-done.4 = f32[256,768]{1,0:T(8,128)S(1)} copy-done((f32[256,768]{1,0:T(8,128)S(1)}, f32[256,768]{1,0:T(8,128)}, u32[]{:S(2)}) %copy-start.4) | copy-done | bytes 786456
  22.2 3.2 %project.5.refs_5_ = f32[256,768]{1,0:T(8,128)S(1)} custom-call(s32[2]{0:T(128)S(1)} %pad_add_fusion.4.idx_ref, bf16[256,896]{1,0:T(8,128)(2,1)S(1)} %collective-permute-done.4.refs_0_, bf16[256,896]{1,0:T(8,128)(2,1)S(1)} %collective-permute-done.refs_1_, bf16[7168,512]{1,0:T(8,128)(2,1)} %refs_2_.7, bf16[7168,128]{1,0:T(8,128)(2,1)} %refs_3_.7, ...), custom_call_target="tpu_custom_call" | custom-call | flops 6000000000 | bytes 1 | tf_op jit(solution)/shard_map/project/pallas_call | solution.py:128
  25.4 2.7 %collective-permute-done.1.refs_1_ = bf16[256,896]{1,0:T(8,128)(2,1)S(1)} collective-permute-done((bf16[256,896]{1,0:T(8,128)(2,1)S(1)}, bf16[256,896]{1,0:T(8,128)(2,1)S(1)}, u32[]{:S(2)}, u32[]{:S(2)}) %collective-permute-start.1) | collective-permute-done | bytes 458784 | tf_op jit(solution)/shard_map/ppermute | solution.py:50
  28.0 0.3 collective-permute-start.2
  28.3 4.6 %collective-permute-done.5.refs_0_ = bf16[256,896]{1,0:T(8,128)(2,1)S(1)} collective-permute-done((bf16[256,896]{1,0:T(8,128)(2,1)S(1)}, bf16[256,896]{1,0:T(8,128)(2,1)S(1)}, u32[]{:S(2)}, u32[]{:S(2)}) %collective-permute-start.5) | collective-permute-done | bytes 458784 | tf_op jit(solution)/shard_map/ppermute | solution.py:50
  32.9 0.3 collective-permute-start.6
  33.2 3.2 %project.6.refs_5_ = f32[256,768]{1,0:T(8,128)S(1)} custom-call(s32[2]{0:T(128)S(1)} %pad_add_fusion.3.idx_ref, bf16[256,896]{1,0:T(8,128)(2,1)S(1)} %collective-permute-done.5.refs_0_, bf16[256,896]{1,0:T(8,128)(2,1)S(1)} %collective-permute-done.1.refs_1_, bf16[7168,512]{1,0:T(8,128)(2,1)} %refs_2_.7, bf16[7168,128]{1,0:T(8,128)(2,1)} %refs_3_.7, ...), custom_call_target="tpu_custom_call" | custom-call | flops 6000000000 | bytes 1 | tf_op jit(solution)/shard_map/project/pallas_call | solution.py:128
  36.4 1.4 %collective-permute-done.2.refs_1_ = bf16[256,896]{1,0:T(8,128)(2,1)S(1)} collective-permute-done((bf16[256,896]{1,0:T(8,128)(2,1)S(1)}, bf16[256,896]{1,0:T(8,128)(2,1)S(1)}, u32[]{:S(2)}, u32[]{:S(2)}) %collective-permute-start.2) | collective-permute-done | bytes 458784 | tf_op jit(solution)/shard_map/ppermute | solution.py:50
  37.8 0.3 collective-permute-start.3
  38.1 4.6 %collective-permute-done.6.refs_0_ = bf16[256,896]{1,0:T(8,128)(2,1)S(1)} collective-permute-done((bf16[256,896]{1,0:T(8,128)(2,1)S(1)}, bf16[256,896]{1,0:T(8,128)(2,1)S(1)}, u32[]{:S(2)}, u32[]{:S(2)}) %collective-permute-start.6) | collective-permute-done | bytes 458784 | tf_op jit(solution)/shard_map/ppermute | solution.py:50
  42.8 3.2 %project.7 = (f32[256,768]{1,0:T(8,128)S(1)}, bf16[1,896,768]{2,1,0:T(8,128)(2,1)S(1)}) custom-call(s32[3]{0:T(128)S(1)} %pad_add_fusion.2.idx_ref, bf16[256,896]{1,0:T(8,128)(2,1)S(1)} %collective-permute-done.6.refs_0_, bf16[256,896]{1,0:T(8,128)(2,1)S(1)} %collective-permute-done.2.refs_1_, bf16[7168,512]{1,0:T(8,128)(2,1)} %refs_2_.7, ...), custom_call_target="tpu_custom_call" | custom-call | flops 6000000000 | bytes 1 | tf_op jit(solution)/shard_map/project/pallas_call | solution.py:128
  46.0 1.6 %collective-permute-done.3.piece_ref = bf16[256,896]{1,0:T(8,128)(2,1)S(1)} collective-permute-done((bf16[256,896]{1,0:T(8,128)(2,1)S(1)}, bf16[256,896]{1,0:T(8,128)(2,1)S(1)}, u32[]{:S(2)}, u32[]{:S(2)}) %collective-permute-start.3) | collective-permute-done | bytes 458784 | tf_op jit(solution)/shard_map/ppermute | solution.py:50
  47.7 0.7 project_last.1
  48.4 1.3 %collective-permute-start.10 = (bf16[512,128]{1,0:T(8,128)(2,1)S(1)}, bf16[512,128]{1,0:T(8,128)(2,1)S(1)}, u32[]{:S(2)}, u32[]{:S(2)}) collective-permute-start(bf16[512,128]{1,0:T(8,128)(2,1)S(1)} %get-tuple-element.18.n0), channel_id=1, source_target_pairs={{0,32},{32,0},{1,33},{33,1},{2,34},{34,2},{3,35},{35,3},{4,36},{36... | collective-permute-start | bytes 393224 | tf_op jit(solution)/shard_map/ppermute | solution.py:63
  50.0 3.5 %collective-permute-start.11 = (bf16[256,512]{1,0:T(8,128)(2,1)S(1)}, bf16[256,512]{1,0:T(8,128)(2,1)S(1)}, u32[]{:S(2)}, u32[]{:S(2)}) collective-permute-start(bf16[256,512]{1,0:T(8,128)(2,1)S(1)} %get-tuple-element.17.q_ref), channel_id=1, source_target_pairs={{0,64},{8,200},{64,128},{72,8},{128,192},{136,72},{192,0},{200,136... | collective-permute-start | bytes 786440 | tf_op jit(solution)/shard_map/ppermute | solution.py:55
  53.5 1.4 %collective-permute-done.10.n1 = bf16[512,128]{1,0:T(8,128)(2,1)S(1)} collective-permute-done((bf16[512,128]{1,0:T(8,128)(2,1)S(1)}, bf16[512,128]{1,0:T(8,128)(2,1)S(1)}, u32[]{:S(2)}, u32[]{:S(2)}) %collective-permute-start.10) | collective-permute-done | bytes 131104 | tf_op jit(solution)/shard_map/ppermute | solution.py:63
  54.9 1.3 %join.1 = (bf16[4,1024,128]{2,1,0:T(8,128)(2,1)S(1)}, bf16[4,1024,128]{2,1,0:T(8,128)(2,1)S(1)}) custom-call(bf16[2048,128]{1,0:T(8,128)(2,1)S(1)} %copy-done, bf16[2048,128]{1,0:T(8,128)(2,1)S(1)} %copy-done.1, bf16[2048,128]{1,0:T(8,128)(2,1)S(1)} %collective-permute-done.8.k1, bf16[2048,128]{1,0:T(8,128)(2,1)S(1)} %collective-permute-done.9.v1, ...), custom_call_target="tpu_custom_call" | custom-call | flops 3000000000 | bytes 1 | tf_op jit(solution)/shard_map/join/pallas_call | solution.py:285
  56.2 4.4 %collective-permute-done.11.q_ref = bf16[256,512]{1,0:T(8,128)(2,1)S(1)} collective-permute-done((bf16[256,512]{1,0:T(8,128)(2,1)S(1)}, bf16[256,512]{1,0:T(8,128)(2,1)S(1)}, u32[]{:S(2)}, u32[]{:S(2)}) %collective-permute-start.11) | collective-permute-done | bytes 262176 | tf_op jit(solution)/shard_map/ppermute | solution.py:55
  60.6 1.7 %collective-permute-start.12 = (bf16[256,512]{1,0:T(8,128)(2,1)S(1)}, bf16[256,512]{1,0:T(8,128)(2,1)S(1)}, u32[]{:S(2)}, u32[]{:S(2)}) collective-permute-start(bf16[256,512]{1,0:T(8,128)(2,1)S(1)} %collective-permute-done.11.q_ref), channel_id=1, source_target_pairs={{0,64},{8,200},{64,128},{72,8},{128,192},{136,72},{192,0},{200,136... | collective-permute-start | bytes 786440 | tf_op jit(solution)/shard_map/ppermute | solution.py:55
  62.3 1.4 %attend.7 = bf16[2,144,512]{2,1,0:T(8,128)(2,1)S(1)} custom-call(s32[16]{0:T(128)S(1)} %reshape.106.valid_ref, bf16[256,512]{1,0:T(8,128)(2,1)S(1)} %collective-permute-done.11.q_ref, bf16[4,1024,128]{2,1,0:T(8,128)(2,1)S(1)} %get-tuple-element.19.jk_ref, bf16[4,1024,128]{2,1,0:T(8,128)(2,1)S(1)} %get-tuple-element.20.jv_ref), custom_call_target="tpu_custom_call" | custom-call | flops 4000000000 | bytes 1 | tf_op jit(solution)/shard_map/attend/pallas_call | solution.py:297
  63.7 6.2 %collective-permute-start.14 = (bf16[2,144,512]{2,1,0:T(8,128)(2,1)S(1)}, bf16[2,144,512]{2,1,0:T(8,128)(2,1)S(1)}, u32[]{:S(2)}, u32[]{:S(2)}) collective-permute-start(bf16[2,144,512]{2,1,0:T(8,128)(2,1)S(1)} %attend.7), channel_id=1, source_target_pairs={{0,64},{8,200},{64,128},{72,8},{128,192},{136,72},{192,0},{200,136... | collective-permute-start | bytes 884744 | tf_op jit(solution)/shard_map/ppermute | solution.py:55
  70.0 3.6 %collective-permute-start.13 = (bf16[256,512]{1,0:T(8,128)(2,1)S(1)}, bf16[256,512]{1,0:T(8,128)(2,1)S(1)}, u32[]{:S(2)}, u32[]{:S(2)}) collective-permute-start(bf16[256,512]{1,0:T(8,128)(2,1)S(1)} %collective-permute-done.12.q_ref), channel_id=1, source_target_pairs={{0,64},{8,200},{64,128},{72,8},{128,192},{136,72},{192,0},{200,136... | collective-permute-start | bytes 786440 | tf_op jit(solution)/shard_map/ppermute | solution.py:55
  73.5 1.4 %attend.6.a_ref = bf16[2,144,512]{2,1,0:T(8,128)(2,1)S(1)} custom-call(s32[16]{0:T(128)S(1)} %reshape.106.valid_ref, bf16[256,512]{1,0:T(8,128)(2,1)S(1)} %collective-permute-done.12.q_ref, bf16[4,1024,128]{2,1,0:T(8,128)(2,1)S(1)} %get-tuple-element.19.jk_ref, bf16[4,1024,128]{2,1,0:T(8,128)(2,1)S(1)} %get-tuple-element.20.jv_ref), custom_call_target="tpu_custom_call" | custom-call | flops 4000000000 | bytes 1 | tf_op jit(solution)/shard_map/attend/pallas_call | solution.py:297
  75.0 4.8 %collective-permute-done.14.b_ref = bf16[2,144,512]{2,1,0:T(8,128)(2,1)S(1)} collective-permute-done((bf16[2,144,512]{2,1,0:T(8,128)(2,1)S(1)}, bf16[2,144,512]{2,1,0:T(8,128)(2,1)S(1)}, u32[]{:S(2)}, u32[]{:S(2)}) %collective-permute-start.14) | collective-permute-done | bytes 294944 | tf_op jit(solution)/shard_map/ppermute | solution.py:55
  79.8 0.6 merge_between.2
  80.3 3.5 %collective-permute-start.15 = (bf16[2,144,512]{2,1,0:T(8,128)(2,1)S(1)}, bf16[2,144,512]{2,1,0:T(8,128)(2,1)S(1)}, u32[]{:S(2)}, u32[]{:S(2)}) collective-permute-start(bf16[2,144,512]{2,1,0:T(8,128)(2,1)S(1)} %merge_between.2), channel_id=1, source_target_pairs={{0,64},{8,200},{64,128},{72,8},{128,192},{136,72},{192,0},{200,136... | collective-permute-start | bytes 884744 | tf_op jit(solution)/shard_map/ppermute | solution.py:55
  83.8 4.7 %collective-permute-done.13.q_ref = bf16[256,512]{1,0:T(8,128)(2,1)S(1)} collective-permute-done((bf16[256,512]{1,0:T(8,128)(2,1)S(1)}, bf16[256,512]{1,0:T(8,128)(2,1)S(1)}, u32[]{:S(2)}, u32[]{:S(2)}) %collective-permute-start.13) | collective-permute-done | bytes 262176 | tf_op jit(solution)/shard_map/ppermute | solution.py:55
  88.6 7.8 %attend.5.a_ref = bf16[2,144,512]{2,1,0:T(8,128)(2,1)S(1)} custom-call(s32[16]{0:T(128)S(1)} %reshape.106.valid_ref, bf16[256,512]{1,0:T(8,128)(2,1)S(1)} %collective-permute-done.13.q_ref, bf16[4,1024,128]{2,1,0:T(8,128)(2,1)S(1)} %get-tuple-element.19.jk_ref, bf16[4,1024,128]{2,1,0:T(8,128)(2,1)S(1)} %get-tuple-element.20.jv_ref), custom_call_target="tpu_custom_call" | custom-call | flops 4000000000 | bytes 1 | tf_op jit(solution)/shard_map/attend/pallas_call | solution.py:297
  96.3 0.6 merge_between.3
  97.0 6.6 %attend.4.a_ref = bf16[2,144,512]{2,1,0:T(8,128)(2,1)S(1)} custom-call(s32[16]{0:T(128)S(1)} %reshape.106.valid_ref, bf16[256,512]{1,0:T(8,128)(2,1)S(1)} %get-tuple-element.17.q_ref, bf16[4,1024,128]{2,1,0:T(8,128)(2,1)S(1)} %get-tuple-element.19.jk_ref, bf16[4,1024,128]{2,1,0:T(8,128)(2,1)S(1)} %get-tuple-element.20.jv_ref, ...), custom_call_target="tpu_custom_call" | custom-call | flops 4000000000 | bytes 1 | tf_op jit(solution)/shard_map/attend/pallas_call | solution.py:297
  103.6 4.9 %collective-permute-done.16.b_ref = bf16[2,144,512]{2,1,0:T(8,128)(2,1)S(1)} collective-permute-done((bf16[2,144,512]{2,1,0:T(8,128)(2,1)S(1)}, bf16[2,144,512]{2,1,0:T(8,128)(2,1)S(1)}, u32[]{:S(2)}, u32[]{:S(2)}) %collective-permute-start.16) | collective-permute-done | bytes 294944 | tf_op jit(solution)/shard_map/ppermute | solution.py:55
  108.5 1.3 %merge.1 = bf16[256,512]{1,0:T(8,128)(2,1)} custom-call(bf16[2,144,512]{2,1,0:T(8,128)(2,1)S(1)} %attend.4.a_ref, bf16[2,144,512]{2,1,0:T(8,128)(2,1)S(1)} %collective-permute-done.16.b_ref), custom_call_target="tpu_custom_call" | custom-call | flops 1 | bytes 1 | tf_op jit(solution)/shard_map/merge/pallas_call | solution.py:376
  (41 shorter events, 1.6 us)
Async XLA Ops:
  0.0 18.2 %collective-permute-start = (bf16[256,896]{1,0:T(8,128)(2,1)}, bf16[256,896]{1,0:T(8,128)(2,1)S(1)}, u32[]{:S(2)}, u32[]{:S(2)}) collective-permute-start(bf16[256,896]{1,0:T(8,128)(2,1)} %refs_0_.1), channel_id=1, source_target_pairs={{0,4},{4,0},{1,5},{5,1},{2,6},{6,2},{3,7},{7,3},{8,12},{12,8},{9,1... | collective-permute-start | bytes 1376264 | tf_op jit(solution)/shard_map/ppermute | solution.py:59
  1.9 17.9 %collective-permute-start.4 = (bf16[256,896]{1,0:T(8,128)(2,1)}, bf16[256,896]{1,0:T(8,128)(2,1)S(1)}, u32[]{:S(2)}, u32[]{:S(2)}) collective-permute-start(bf16[256,896]{1,0:T(8,128)(2,1)} %refs_0_.1), channel_id=1, source_target_pairs={{0,1},{1,2},{2,3},{3,0},{8,11},{9,8},{10,9},{11,10},{4,5},{5,6},{6... | collective-permute-start | bytes 1376264 | tf_op jit(solution)/shard_map/ppermute | solution.py:50
  4.9 9.6 %collective-permute-start.7 = (s32[4,128]{1,0:T(4,128)S(1)}, s32[4,128]{1,0:T(4,128)S(1)}, u32[]{:S(2)}, u32[]{:S(2)}) collective-permute-start(s32[4,128]{1,0:T(4,128)S(1)} %pad_add_fusion), channel_id=1, source_target_pairs={{0,32},{32,0},{1,33},{33,1},{2,34},{34,2},{3,35},{35,3},{4,36},{36... | collective-permute-start | bytes 6152 | tf_op jit(solution)/shard_map/ppermute | solution.py:63
  7.2 38.8 %collective-permute-start.9 = (bf16[2048,128]{1,0:T(8,128)(2,1)}, bf16[2048,128]{1,0:T(8,128)(2,1)S(1)}, u32[]{:S(2)}, u32[]{:S(2)}) collective-permute-start(bf16[2048,128]{1,0:T(8,128)(2,1)} %v0.1), channel_id=1, source_target_pairs={{0,32},{32,0},{1,33},{33,1},{2,34},{34,2},{3,35},{35,3},{4,36},{36... | collective-permute-start | bytes 1572872 | tf_op jit(solution)/shard_map/ppermute | solution.py:63
  10.3 1.0 copy-start.2
  11.3 3.1 %copy-start = (bf16[2048,128]{1,0:T(8,128)(2,1)S(1)}, bf16[2048,128]{1,0:T(8,128)(2,1)}, u32[]{:S(2)}) copy-start(bf16[2048,128]{1,0:T(8,128)(2,1)} %k0.1) | copy-start | bytes 1572868
  11.4 5.6 %copy-start.6 = (s32[2]{0:T(128)S(1)}, s32[2]{0:T(128)}, u32[]{:S(2)}) copy-start(s32[2]{0:T(128)} %param.18) | copy-start | bytes 28
  11.4 5.7 %copy-start.5 = (s32[2,128]{1,0:T(2,128)S(1)}, s32[2,128]{1,0:T(2,128)}, u32[]{:S(2)}) copy-start(s32[2,128]{1,0:T(2,128)} %param.19) | copy-start | bytes 3076
  13.3 0.9 copy-start.3
  14.5 31.6 %collective-permute-start.8 = (bf16[2048,128]{1,0:T(8,128)(2,1)S(1)}, bf16[2048,128]{1,0:T(8,128)(2,1)S(1)}, u32[]{:S(2)}, u32[]{:S(2)}) collective-permute-start(bf16[2048,128]{1,0:T(8,128)(2,1)S(1)} %copy-done), channel_id=1, source_target_pairs={{0,32},{32,0},{1,33},{33,1},{2,34},{34,2},{3,35},{35,3},{4,36},{36... | collective-permute-start | bytes 1572872 | tf_op jit(solution)/shard_map/ppermute | solution.py:63
  18.2 9.8 %collective-permute-start.1 = (bf16[256,896]{1,0:T(8,128)(2,1)S(1)}, bf16[256,896]{1,0:T(8,128)(2,1)S(1)}, u32[]{:S(2)}, u32[]{:S(2)}) collective-permute-start(bf16[256,896]{1,0:T(8,128)(2,1)S(1)} %collective-permute-done.refs_1_), channel_id=1, source_target_pairs={{0,1},{1,2},{2,3},{3,0},{8,11},{9,8},{10,9},{11,10},{4,5},{5,6},{6... | collective-permute-start | bytes 1376264 | tf_op jit(solution)/shard_map/ppermute | solution.py:50
  19.8 13.1 %collective-permute-start.5 = (bf16[256,896]{1,0:T(8,128)(2,1)S(1)}, bf16[256,896]{1,0:T(8,128)(2,1)S(1)}, u32[]{:S(2)}, u32[]{:S(2)}) collective-permute-start(bf16[256,896]{1,0:T(8,128)(2,1)S(1)} %collective-permute-done.4.refs_0_), channel_id=1, source_target_pairs={{0,1},{1,2},{2,3},{3,0},{8,11},{9,8},{10,9},{11,10},{4,5},{5,6},{6... | collective-permute-start | bytes 1376264 | tf_op jit(solution)/shard_map/ppermute | solution.py:50
  21.0 1.1 %copy-start.4 = (f32[256,768]{1,0:T(8,128)S(1)}, f32[256,768]{1,0:T(8,128)}, u32[]{:S(2)}) copy-start(f32[256,768]{1,0:T(8,128)} %copy-done.3) | copy-start | bytes 2359300
  28.0 9.8 %collective-permute-start.2 = (bf16[256,896]{1,0:T(8,128)(2,1)S(1)}, bf16[256,896]{1,0:T(8,128)(2,1)S(1)}, u32[]{:S(2)}, u32[]{:S(2)}) collective-permute-start(bf16[256,896]{1,0:T(8,128)(2,1)S(1)} %collective-permute-done.1.refs_1_), channel_id=1, source_target_pairs={{0,1},{1,2},{2,3},{3,0},{8,11},{9,8},{10,9},{11,10},{4,5},{5,6},{6... | collective-permute-start | bytes 1376264 | tf_op jit(solution)/shard_map/ppermute | solution.py:50
  32.9 9.8 %collective-permute-start.6 = (bf16[256,896]{1,0:T(8,128)(2,1)S(1)}, bf16[256,896]{1,0:T(8,128)(2,1)S(1)}, u32[]{:S(2)}, u32[]{:S(2)}) collective-permute-start(bf16[256,896]{1,0:T(8,128)(2,1)S(1)} %collective-permute-done.5.refs_0_), channel_id=1, source_target_pairs={{0,1},{1,2},{2,3},{3,0},{8,11},{9,8},{10,9},{11,10},{4,5},{5,6},{6... | collective-permute-start | bytes 1376264 | tf_op jit(solution)/shard_map/ppermute | solution.py:50
  37.8 9.8 %collective-permute-start.3 = (bf16[256,896]{1,0:T(8,128)(2,1)S(1)}, bf16[256,896]{1,0:T(8,128)(2,1)S(1)}, u32[]{:S(2)}, u32[]{:S(2)}) collective-permute-start(bf16[256,896]{1,0:T(8,128)(2,1)S(1)} %collective-permute-done.2.refs_1_), channel_id=1, source_target_pairs={{0,1},{1,2},{2,3},{3,0},{8,11},{9,8},{10,9},{11,10},{4,5},{5,6},{6... | collective-permute-start | bytes 1376264 | tf_op jit(solution)/shard_map/ppermute | solution.py:50
  46.0 8.9 %copy-start.1 = (bf16[2048,128]{1,0:T(8,128)(2,1)S(1)}, bf16[2048,128]{1,0:T(8,128)(2,1)}, u32[]{:S(2)}) copy-start(bf16[2048,128]{1,0:T(8,128)(2,1)} %v0.1) | copy-start | bytes 1572868
  48.4 6.6 %collective-permute-start.10 = (bf16[512,128]{1,0:T(8,128)(2,1)S(1)}, bf16[512,128]{1,0:T(8,128)(2,1)S(1)}, u32[]{:S(2)}, u32[]{:S(2)}) collective-permute-start(bf16[512,128]{1,0:T(8,128)(2,1)S(1)} %get-tuple-element.18.n0), channel_id=1, source_target_pairs={{0,32},{32,0},{1,33},{33,1},{2,34},{34,2},{3,35},{35,3},{4,36},{36... | collective-permute-start | bytes 393224 | tf_op jit(solution)/shard_map/ppermute | solution.py:63
  50.0 10.6 %collective-permute-start.11 = (bf16[256,512]{1,0:T(8,128)(2,1)S(1)}, bf16[256,512]{1,0:T(8,128)(2,1)S(1)}, u32[]{:S(2)}, u32[]{:S(2)}) collective-permute-start(bf16[256,512]{1,0:T(8,128)(2,1)S(1)} %get-tuple-element.17.q_ref), channel_id=1, source_target_pairs={{0,64},{8,200},{64,128},{72,8},{128,192},{136,72},{192,0},{200,136... | collective-permute-start | bytes 786440 | tf_op jit(solution)/shard_map/ppermute | solution.py:55
  60.6 9.4 %collective-permute-start.12 = (bf16[256,512]{1,0:T(8,128)(2,1)S(1)}, bf16[256,512]{1,0:T(8,128)(2,1)S(1)}, u32[]{:S(2)}, u32[]{:S(2)}) collective-permute-start(bf16[256,512]{1,0:T(8,128)(2,1)S(1)} %collective-permute-done.11.q_ref), channel_id=1, source_target_pairs={{0,64},{8,200},{64,128},{72,8},{128,192},{136,72},{192,0},{200,136... | collective-permute-start | bytes 786440 | tf_op jit(solution)/shard_map/ppermute | solution.py:55
  63.7 16.0 %collective-permute-start.14 = (bf16[2,144,512]{2,1,0:T(8,128)(2,1)S(1)}, bf16[2,144,512]{2,1,0:T(8,128)(2,1)S(1)}, u32[]{:S(2)}, u32[]{:S(2)}) collective-permute-start(bf16[2,144,512]{2,1,0:T(8,128)(2,1)S(1)} %attend.7), channel_id=1, source_target_pairs={{0,64},{8,200},{64,128},{72,8},{128,192},{136,72},{192,0},{200,136... | collective-permute-start | bytes 884744 | tf_op jit(solution)/shard_map/ppermute | solution.py:55
  70.0 18.6 %collective-permute-start.13 = (bf16[256,512]{1,0:T(8,128)(2,1)S(1)}, bf16[256,512]{1,0:T(8,128)(2,1)S(1)}, u32[]{:S(2)}, u32[]{:S(2)}) collective-permute-start(bf16[256,512]{1,0:T(8,128)(2,1)S(1)} %collective-permute-done.12.q_ref), channel_id=1, source_target_pairs={{0,64},{8,200},{64,128},{72,8},{128,192},{136,72},{192,0},{200,136... | collective-permute-start | bytes 786440 | tf_op jit(solution)/shard_map/ppermute | solution.py:55
  80.3 16.0 %collective-permute-start.15 = (bf16[2,144,512]{2,1,0:T(8,128)(2,1)S(1)}, bf16[2,144,512]{2,1,0:T(8,128)(2,1)S(1)}, u32[]{:S(2)}, u32[]{:S(2)}) collective-permute-start(bf16[2,144,512]{2,1,0:T(8,128)(2,1)S(1)} %merge_between.2), channel_id=1, source_target_pairs={{0,64},{8,200},{64,128},{72,8},{128,192},{136,72},{192,0},{200,136... | collective-permute-start | bytes 884744 | tf_op jit(solution)/shard_map/ppermute | solution.py:55
  96.9 11.5 %collective-permute-start.16 = (bf16[2,144,512]{2,1,0:T(8,128)(2,1)S(1)}, bf16[2,144,512]{2,1,0:T(8,128)(2,1)S(1)}, u32[]{:S(2)}, u32[]{:S(2)}) collective-permute-start(bf16[2,144,512]{2,1,0:T(8,128)(2,1)S(1)} %merge_between.3), channel_id=1, source_target_pairs={{0,64},{8,200},{64,128},{72,8},{128,192},{136,72},{192,0},{200,136... | collective-permute-start | bytes 884744 | tf_op jit(solution)/shard_map/ppermute | solution.py:55

commit v2 on v1

--- a/solution.py
+++ b/solution.py
@@ -3,6 +3,7 @@
 
 import jax
 import jax.numpy as jnp
+import numpy as np
 from jax import lax
 from jax.experimental import pallas as pl
 from jax.experimental.pallas import tpu as pltpu
@@ -63,27 +64,80 @@
     return lax.ppermute(v, "yh", [(0, 1), (1, 0)])
 
 
-def span_ranks(span_count, span_key):
-    column = jnp.arange(MAXCH, dtype=jnp.int32)
-    filled = column[None, :] < span_count[:, None]
-    earlier = span_key[:, :, None] < span_key[:, None, :]
-    ranks = jnp.sum((earlier & filled[:, :, None]).astype(jnp.int32), axis=1, dtype=jnp.int32)
-    return filled.T.reshape(-1), ranks.T.reshape(-1)
-
-
-def tables(position):
-    freq = rope_base ** (-(jnp.arange(HD // 2, dtype=jnp.float32) * 2.0) / HD)
-    angle = position.astype(jnp.float32)[:, None] * freq
-    cosine, sine = jnp.cos(angle), jnp.sin(angle)
-    return jnp.concatenate([cosine, cosine], -1), jnp.concatenate([-sine, sine], -1)
+H_AT, Z_AT, ZH_AT, YH_AT, WAY_AT, REQ_AT = 0, 4, 8, 9, 10, 11
+
+
+def prepare_kernel(
+    place, count, key, offset, sel_ref, theirs_ref, freq_ref,
+    cos_ref, sin_ref, rot_ref, selr_ref, valid_ref,
+):
+    freq = freq_ref[0:1, :]
+    sign = freq_ref[1:2, :]
+    zh, yh, way = place[ZH_AT], place[YH_AT], place[WAY_AT]
+    for r in range(SLOTS):
+        request = place[REQ_AT] + r
+        used = count[request]
+
+        def rank(j, request=request, used=used):
+            mine = key[request, j]
+            total = jnp.int32(0)
+            for k in range(MAXCH):
+                smaller = (key[request, k] < mine) & (k < used)
+                total += jnp.where(smaller, 1, 0)
+            return total
+
+        spans = (zh * 2 + yh, zh * 2 + 1 - yh)
+        ranks = [rank(j) for j in spans]
+        for shift in range(4):
+            j = lax.rem(zh + shift * way + 4, 4) * 2 + yh
+            mine = rank(j)
+            for sp in range(2):
+                good = (j < used) & (spans[sp] < used) & (ranks[sp] <= mine)
+                valid_ref[shift * 4 + r * 2 + sp] = jnp.where(good, 1, 0)
+        sel = sel_ref[r : r + 1, :]
+        position = (sel + ranks[0] * SPAN).astype(jnp.float32)
+        angle = jnp.broadcast_to(position, (SEL, HD)).T * freq
+        cos_ref[r * SEL : (r + 1) * SEL, :] = jnp.cos(angle)
+        sin_ref[r * SEL : (r + 1) * SEL, :] = jnp.sin(angle) * sign
+        other = ranks[1] * SPAN - theirs_ref[SLOTS + r : SLOTS + r + 1, :]
+        own = jnp.zeros((1, HD), jnp.int32) + (ranks[0] * SPAN - offset[r])
+        for sp, delta in enumerate((own, other)):
+            angle = delta.astype(jnp.float32) * freq
+            rot_ref[r, sp : sp + 1, :] = jnp.cos(angle)
+            rot_ref[r, sp + 2 : sp + 3, :] = jnp.sin(angle) * sign
+        selr_ref[r, 0:1, :] = sel
+        selr_ref[r, 1:2, :] = theirs_ref[r : r + 1, :]
+
+
+def prepare(*args):
+    half = np.arange(HD // 2) * 2.0 / HD
+    freq = np.tile(rope_base**-half, 2)
+    sign = np.repeat([-1.0, 1.0], HD // 2)
+    table = jnp.asarray(np.stack([freq, sign]), jnp.float32)
+    shape = jax.ShapeDtypeStruct
+    return pl.pallas_call(
+        prepare_kernel,
+        out_shape=(
+            shape((ROWS, HD), jnp.float32),
+            shape((ROWS, HD), jnp.float32),
+            shape((SLOTS, 4, HD), jnp.float32),
+            shape((SLOTS, 2, SEL), jnp.int32),
+            shape((16,), jnp.int32),
+        ),
+        in_specs=[smem] * 4 + [vmem] * 3,
+        out_specs=(vmem,) * 4 + (smem,),
+        compiler_params=pltpu.CompilerParams(vmem_limit_bytes=8 << 20),
+        cost_estimate=work(2),
+        name="prepare",
+    )(*args, table)
 
 
 def turned(v, cosine, sine):
     return v * cosine + pltpu.roll(v, HD // 2, 1) * sine
 
 
-def weight_copies(sources, idx_ref, i, to_ref, slot, sem):
-    at = pl.ds(pl.multiple_of(idx_ref[i] * DK, DK), DK)
+def weight_copies(sources, piece, i, to_ref, slot, sem):
+    at = pl.ds(pl.multiple_of(piece * DK, DK), DK)
     start = 0
     for j, (w, width) in enumerate(zip(sources, (QW, HD, HD))):
         to = to_ref.at[slot, :, start : start + width]
@@ -91,7 +145,8 @@
         start += width
 
 
-def partial_kernel(count, ahead, carried, idx_ref, *refs):
+def partial_kernel(which, ahead, carried, place, *refs):
+    count = len(which) - ahead
     pieces, refs = refs[:count], refs[count:]
     sources, refs = refs[:3], refs[3:]
     if carried:
@@ -99,46 +154,42 @@
     out_ref, refs = refs[0], refs[1:]
     if ahead:
         next_ref, refs = refs[0], refs[1:]
-    held, weight, sem = refs
+    weight, sem = refs
     for i in range(count + ahead):
         to, slot = (weight, i) if i < count else (next_ref, i - count)
-        for copy in weight_copies(sources, idx_ref, i, to, slot, sem):
+        for copy in weight_copies(sources, place[which[i]], i, to, slot, sem):
             copy.start()
+    acc = acc_ref[...] if carried else None
     for i in range(count):
-        held[i] = pieces[i][...]
-
-    def add(i, acc):
-        for copy in weight_copies(sources, idx_ref, i, weight, i, sem):
+        for copy in weight_copies(sources, place[which[i]], i, weight, i, sem):
             copy.wait()
-        return acc + jnp.dot(held[i], weight[i], preferred_element_type=jnp.float32)
-
-    begin = acc_ref[...] if carried else jnp.zeros((ROWS, QW + 2 * HD), jnp.float32)
-    out_ref[...] = lax.fori_loop(0, count, add, begin)
+        d = jnp.dot(pieces[i][...], weight[i], preferred_element_type=jnp.float32)
+        acc = d if acc is None else acc + d
+    out_ref[...] = acc
     for i in range(count, count + ahead):
-        for copy in weight_copies(sources, idx_ref, i, next_ref, i - count, sem):
+        for copy in weight_copies(sources, place[which[i]], i, next_ref, i - count, sem):
             copy.wait()
 
 
-def partial_project(idx, pieces, weights, acc=None, ahead=0):
+def partial_project(place, which, pieces, weights, acc=None, ahead=0):
     n = len(pieces)
     sums = jax.ShapeDtypeStruct((ROWS, QW + 2 * HD), jnp.float32)
     kept = jax.ShapeDtypeStruct((ahead, DK, QW + 2 * HD), jnp.bfloat16)
     extra = [] if acc is None else [acc]
     weights = [pltpu.with_memory_space_constraint(w, pltpu.HBM) for w in weights]
     return pl.pallas_call(
-        functools.partial(partial_kernel, n, ahead, acc is not None),
+        functools.partial(partial_kernel, which, ahead, acc is not None),
         out_shape=(sums, kept) if ahead else sums,
         in_specs=[smem] + [vmem] * n + [hbm] * 3 + [vmem] * len(extra),
         out_specs=(vmem, vmem) if ahead else vmem,
         scratch_shapes=[
-            pltpu.VMEM((n, ROWS, DK), jnp.bfloat16),
             pltpu.VMEM((n, DK, QW + 2 * HD), jnp.bfloat16),
             pltpu.SemaphoreType.DMA((n + ahead, 3)),
         ],
         compiler_params=pltpu.CompilerParams(vmem_limit_bytes=16 << 20),
         cost_estimate=work(6),
         name="project",
-    )(idx, *pieces, *weights, *extra)
+    )(place, *pieces, *weights, *extra)
 
 
 def last_kernel(piece_ref, weight_ref, acc_ref, cos_ref, sin_ref, q_ref, n_ref):
@@ -396,6 +447,10 @@
     zl, x = lax.axis_index("zl"), lax.axis_index("x")
     weights = (w_query, w_key, w_value)
     way = 2 * c - 1
+    entries = [zl * 4 + (x + i * way) % 4 for i in range(4)]
+    entries += [(1 - zl) * 4 + (x + i * way) % 4 for i in range(4)]
+    entries += [zh, yh, way, (yp * 2 + c) * SLOTS]
+    place = jnp.stack(entries).astype(jnp.int32)
     mine = jnp.concatenate(
         [sel_index, jnp.broadcast_to(cache_offset[:, None], (SLOTS, SEL))], axis=0
     )
@@ -403,49 +458,19 @@
     h = [hidden, ring_x(hidden)]
     z = [pz(hidden)]
     k1 = py(after(key_cache, theirs))
-    v1 = py(value_cache)
+    v1 = py(after(value_cache, h[1]))
     for _ in range(2):
         h.append(ring_x(h[-1]))
     for _ in range(3):
         z.append(ring_x(z[-1]))
-    h_idx = [zl * 4 + (x + i * way) % 4 for i in range(4)]
-    z_idx = [(1 - zl) * 4 + (x + i * way) % 4 for i in range(4)]
-    table = lambda *entries: jnp.stack(entries).astype(jnp.int32)
-
-    filled_all, rank_all = span_ranks(span_count, span_key)
-
-    def lookup(h, half):
-        start = (((h * 2 + half) * 2 + yp) * 2 + c) * SLOTS
-        return (
-            lax.dynamic_slice_in_dim(filled_all, start, SLOTS),
-            lax.dynamic_slice_in_dim(rank_all, start, SLOTS),
-        )
-
-    span_f, span_r = zip(lookup(zh, yh), lookup(zh, 1 - yh))
-
-    def validity(shift):
-        qf, qr = lookup((zh + shift * way) % 4, yh)
-        table = [qf & kf & (kr <= qr) for kf, kr in zip(span_f, span_r)]
-        return jnp.stack(table, axis=1).astype(jnp.int32)
-
-    position = (span_r[0][:, None] * SPAN + sel_index).reshape(-1)
-    cosine, sine = tables(position)
-    delta = jnp.stack(
-        [span_r[0] * SPAN - cache_offset, span_r[1] * SPAN - theirs[SLOTS:, 0]], axis=1
-    ).reshape(-1)
-    turn_c, turn_s = tables(delta)
-    rot = jnp.concatenate(
-        [turn_c.reshape(SLOTS, 2, HD), turn_s.reshape(SLOTS, 2, HD)], axis=1
-    )
-    sel_rows = jnp.stack([sel_index, theirs[:SLOTS]], axis=1)
-    valid = jnp.concatenate([validity(s) for s in range(4)], axis=0).reshape(-1)
-
-    acc = partial_project(table(h_idx[0]), (hidden,), weights)
-    acc = partial_project(table(h_idx[1], z_idx[0]), (h[1], z[0]), weights, acc)
-    acc = partial_project(table(h_idx[2], z_idx[1]), (h[2], z[1]), weights, acc)
-    acc, kept = partial_project(
-        table(h_idx[3], z_idx[2], z_idx[3]), (h[3], z[2]), weights, acc, ahead=1
-    )
+    cosine, sine, rot, sel_rows, valid = prepare(
+        after(place, h[2]), span_count, span_key, cache_offset, sel_index, theirs
+    )
+    project = functools.partial(partial_project, place)
+    acc = project((H_AT, H_AT + 1), (hidden, h[1]), weights)
+    acc = project((H_AT + 2, Z_AT), (h[2], z[0]), weights, acc)
+    acc = project((H_AT + 3, Z_AT + 1), (h[3], z[1]), weights, acc)
+    acc, kept = project((Z_AT + 2, Z_AT + 3), (z[2],), weights, acc, ahead=1)
     acc = after(acc, k1, v1)
     query, fresh = last_project(z[3], kept, acc, cosine, sine)
     ring = [query]

time: 108 us -> 107 us (level)
  the two profiles are of different devices: /device:TPU:8 before, /device:TPU:32 now
where the time goes in v2:
time: 107 us; the launch traced here: 105 us
  waiting for transfers between devices  46.3 us (43%)
  Pallas kernels  31.9 us (30%)
  starting transfers between devices  24.4 us (23%)
  local copies, waits for them, and re-layouts  1.87 us (2%)
    ppermute x6, waiting for transfers between devices, ring_z(): return lax.ppermute(v, ('zh', 'c'), pairs)  23.7 us
    ppermute x6, waiting for transfers between devices, ring_x(): return lax.ppermute(v, ('c', 'x'), opposite_ways(4))  17.6 us
    pallas_call x4, Pallas kernels, attend(): pl.pallas_call(functools.partial(attend_kernel, shift), out_shape=packed_...  14 us
    ppermute x6, starting transfers between devices, ring_z(): return lax.ppermute(v, ('zh', 'c'), pairs)  12.7 us
    pallas_call x4, Pallas kernels, partial_project(): pl.pallas_call(functools.partial(partial_kernel, which, ahead, acc is not...  11.9 us
    ppermute x4, starting transfers between devices, py(): return lax.ppermute(v, 'yh', [(0, 1), (1, 0)])  9.51 us
    ppermute x4, waiting for transfers between devices, py(): return lax.ppermute(v, 'yh', [(0, 1), (1, 0)])  3.43 us
  transfers between devices with their start and end apart: 17, of which 12 were waited for; matrix products, arithmetic and copies ran while one was open for 1% of the time, Pallas kernels for 28%

profile of v2, /device:TPU:32, one launch (start us, length us, event | category | flops | bytes accessed | tf_op | source)
XLA Modules:
  0.0 105.4 jit_solution(17307704619970919351)
XLA Ops:
  0.0 1.5 %collective-permute-start = (bf16[256,896]{1,0:T(8,128)(2,1)}, bf16[256,896]{1,0:T(8,128)(2,1)S(1)}, u32[]{:S(2)}, u32[]{:S(2)}) collective-permute-start(bf16[256,896]{1,0:T(8,128)(2,1)} %refs_0_.1), channel_id=1, source_target_pairs={{0,1},{1,2},{2,3},{3,0},{8,11},{9,8},{10,9},{11,10},{4,5},{5,6},{6... | collective-permute-start | bytes 1376264 | tf_op jit(solution)/shard_map/ppermute | solution.py:51
  1.5 0.4 collective-permute-start.3
  1.8 0.7 pad.1.clone
  2.6 0.7 pad_add_fusion
  3.3 2.9 %collective-permute-start.2 = (s32[4,128]{1,0:T(4,128)S(1)}, s32[4,128]{1,0:T(4,128)S(1)}, u32[]{:S(2)}, u32[]{:S(2)}) collective-permute-start(s32[4,128]{1,0:T(4,128)S(1)} %pad_add_fusion), channel_id=1, source_target_pairs={{0,32},{32,0},{1,33},{33,1},{2,34},{34,2},{3,35},{35,3},{4,36},{36... | collective-permute-start | bytes 6152 | tf_op jit(solution)/shard_map/ppermute | solution.py:64
  6.3 0.1 stack.51.place
  6.4 0.0 copy-start
  6.4 2.0 %collective-permute-done.2.theirs_ref = s32[4,128]{1,0:T(4,128)S(1)} collective-permute-done((s32[4,128]{1,0:T(4,128)S(1)}, s32[4,128]{1,0:T(4,128)S(1)}, u32[]{:S(2)}, u32[]{:S(2)}) %collective-permute-start.2) | collective-permute-done | bytes 2080 | tf_op jit(solution)/shard_map/ppermute | solution.py:64
  8.4 2.9 %collective-permute-start.8 = (bf16[2048,128]{1,0:T(8,128)(2,1)}, bf16[2048,128]{1,0:T(8,128)(2,1)S(1)}, u32[]{:S(2)}, u32[]{:S(2)}) collective-permute-start(bf16[2048,128]{1,0:T(8,128)(2,1)} %k0.1), channel_id=1, source_target_pairs={{0,32},{32,0},{1,33},{33,1},{2,34},{34,2},{3,35},{35,3},{4,36},{36... | collective-permute-start | bytes 1572872 | tf_op jit(solution)/shard_map/ppermute | solution.py:64
  11.4 0.0 collective-permute-done.refs_1_
  11.4 1.7 %collective-permute-start.9 = (bf16[2048,128]{1,0:T(8,128)(2,1)}, bf16[2048,128]{1,0:T(8,128)(2,1)S(1)}, u32[]{:S(2)}, u32[]{:S(2)}) collective-permute-start(bf16[2048,128]{1,0:T(8,128)(2,1)} %v0.1), channel_id=1, source_target_pairs={{0,32},{32,0},{1,33},{33,1},{2,34},{34,2},{3,35},{35,3},{4,36},{36... | collective-permute-start | bytes 1572872 | tf_op jit(solution)/shard_map/ppermute | solution.py:64
  13.1 0.3 collective-permute-start.1
  13.4 1.6 %collective-permute-done.3.refs_1_ = bf16[256,896]{1,0:T(8,128)(2,1)S(1)} collective-permute-done((bf16[256,896]{1,0:T(8,128)(2,1)}, bf16[256,896]{1,0:T(8,128)(2,1)S(1)}, u32[]{:S(2)}, u32[]{:S(2)}) %collective-permute-start.3) | collective-permute-done | bytes 458784 | tf_op jit(solution)/shard_map/ppermute | solution.py:60
  14.9 0.0 collective-permute-start.4
  15.0 1.0 copy-done.3
  16.0 3.3 %project.4.refs_5_ = f32[256,768]{1,0:T(8,128)S(1)} custom-call(s32[12]{0:T(128)S(1)} %stack.51.place, bf16[256,896]{1,0:T(8,128)(2,1)S(1)} %copy-done.3, bf16[256,896]{1,0:T(8,128)(2,1)S(1)} %collective-permute-done.refs_1_, bf16[7168,512]{1,0:T(8,128)(2,1)} %refs_1_.1, bf16[7168,128]{1,0:T(8,128)(2,1)} %refs_2_.7, bf16[7168,128]{1,0:T(8,128)(2,1)} %refs_3_.7), custom_call_target="tpu_custom_call" | custom-call | flops 6000000000 | bytes 1 | tf_op jit(solution)/shard_map/project/pallas_call | solution.py:180
  19.2 3.5 %collective-permute-done.1.refs_0_ = bf16[256,896]{1,0:T(8,128)(2,1)S(1)} collective-permute-done((bf16[256,896]{1,0:T(8,128)(2,1)S(1)}, bf16[256,896]{1,0:T(8,128)(2,1)S(1)}, u32[]{:S(2)}, u32[]{:S(2)}) %collective-permute-start.1) | collective-permute-done | bytes 458784 | tf_op jit(solution)/shard_map/ppermute | solution.py:51
  22.8 4.9 %collective-permute-done.4.refs_1_ = bf16[256,896]{1,0:T(8,128)(2,1)S(1)} collective-permute-done((bf16[256,896]{1,0:T(8,128)(2,1)S(1)}, bf16[256,896]{1,0:T(8,128)(2,1)S(1)}, u32[]{:S(2)}, u32[]{:S(2)}) %collective-permute-start.4) | collective-permute-done | bytes 458784 | tf_op jit(solution)/shard_map/ppermute | solution.py:51
  27.7 1.6 %prepare.1 = (f32[256,128]{1,0:T(8,128)S(1)}, f32[256,128]{1,0:T(8,128)S(1)}, f32[2,4,128]{2,1,0:T(4,128)S(1)}, s32[2,2,128]{2,1,0:T(2,128)S(1)}, s32[16]{0:T(128)S(1)}) custom-call(s32[12]{0:T(128)S(1)} %stack.51.place, s32[8]{0:T(128)S(1)} %copy-done.5, s32[8,8]{1,0:T(8,128)S(1)} %copy-done.4, s32[2]{0:T(128)S(1)} %copy-done.6, s32[2,128]{1,0:T(2,128)S(1)} %copy-done, ...), custom_call_target="tpu_custom_call" | custom-call | flops 2000000000 | bytes 1 | tf_op jit(solution)/shard_map/prepare/pallas_call | solution.py:118
  29.4 3.1 %project.5.refs_5_ = f32[256,768]{1,0:T(8,128)S(1)} custom-call(s32[12]{0:T(128)S(1)} %stack.51.place, bf16[256,896]{1,0:T(8,128)(2,1)S(1)} %collective-permute-done.1.refs_0_, bf16[256,896]{1,0:T(8,128)(2,1)S(1)} %collective-permute-done.3.refs_1_, bf16[7168,512]{1,0:T(8,128)(2,1)} %refs_1_.1, bf16[7168,128]{1,0:T(8,128)(2,1)} %refs_2_.7, ...), custom_call_target="tpu_custom_call" | custom-call | flops 6000000000 | bytes 1 | tf_op jit(solution)/shard_map/project/pallas_call | solution.py:180
  32.4 5.1 %collective-permute-done.5.refs_0_ = bf16[256,896]{1,0:T(8,128)(2,1)S(1)} collective-permute-done((bf16[256,896]{1,0:T(8,128)(2,1)S(1)}, bf16[256,896]{1,0:T(8,128)(2,1)S(1)}, u32[]{:S(2)}, u32[]{:S(2)}) %collective-permute-start.5) | collective-permute-done | bytes 458784 | tf_op jit(solution)/shard_map/ppermute | solution.py:51
  37.5 0.0 collective-permute-done.7.refs_0_
  37.5 3.1 %project.6.refs_4_ = f32[256,768]{1,0:T(8,128)S(1)} custom-call(s32[12]{0:T(128)S(1)} %stack.51.place, bf16[256,896]{1,0:T(8,128)(2,1)S(1)} %collective-permute-done.7.refs_0_, bf16[256,896]{1,0:T(8,128)(2,1)S(1)} %collective-permute-done.4.refs_1_, bf16[7168,512]{1,0:T(8,128)(2,1)} %refs_1_.1, bf16[7168,128]{1,0:T(8,128)(2,1)} %refs_2_.7, ...), custom_call_target="tpu_custom_call" | custom-call | flops 6000000000 | bytes 1 | tf_op jit(solution)/shard_map/project/pallas_call | solution.py:180
  40.6 2.5 %project.7 = (f32[256,768]{1,0:T(8,128)S(1)}, bf16[1,896,768]{2,1,0:T(8,128)(2,1)S(1)}) custom-call(s32[12]{0:T(128)S(1)} %stack.51.place, bf16[256,896]{1,0:T(8,128)(2,1)S(1)} %collective-permute-done.5.refs_0_, bf16[7168,512]{1,0:T(8,128)(2,1)} %refs_1_.1, bf16[7168,128]{1,0:T(8,128)(2,1)} %refs_2_.7, bf16[7168,128]{1,0:T(8,128)(2,1)} %refs_3_.7, ...), custom_call_target="tpu_custom_call" | custom-call | flops 6000000000 | bytes 1 | tf_op jit(solution)/shard_map/project/pallas_call | solution.py:180
  43.1 0.0 copy-start.1
  43.1 0.0 copy-start.2
  43.1 4.1 %collective-permute-done.6.piece_ref = bf16[256,896]{1,0:T(8,128)(2,1)S(1)} collective-permute-done((bf16[256,896]{1,0:T(8,128)(2,1)S(1)}, bf16[256,896]{1,0:T(8,128)(2,1)S(1)}, u32[]{:S(2)}, u32[]{:S(2)}) %collective-permute-start.6) | collective-permute-done | bytes 458784 | tf_op jit(solution)/shard_map/ppermute | solution.py:51
  47.2 0.7 project_last.1
  47.9 1.9 %collective-permute-start.10 = (bf16[512,128]{1,0:T(8,128)(2,1)S(1)}, bf16[512,128]{1,0:T(8,128)(2,1)S(1)}, u32[]{:S(2)}, u32[]{:S(2)}) collective-permute-start(bf16[512,128]{1,0:T(8,128)(2,1)S(1)} %get-tuple-element.30.n0), channel_id=1, source_target_pairs={{0,32},{32,0},{1,33},{33,1},{2,34},{34,2},{3,35},{35,3},{4,36},{36... | collective-permute-start | bytes 393224 | tf_op jit(solution)/shard_map/ppermute | solution.py:64
  49.8 3.3 %collective-permute-start.11 = (bf16[256,512]{1,0:T(8,128)(2,1)S(1)}, bf16[256,512]{1,0:T(8,128)(2,1)S(1)}, u32[]{:S(2)}, u32[]{:S(2)}) collective-permute-start(bf16[256,512]{1,0:T(8,128)(2,1)S(1)} %get-tuple-element.29.q_ref), channel_id=1, source_target_pairs={{0,64},{8,200},{64,128},{72,8},{128,192},{136,72},{192,0},{200,136... | collective-permute-start | bytes 786440 | tf_op jit(solution)/shard_map/ppermute | solution.py:56
  53.1 1.4 %collective-permute-done.10.n1 = bf16[512,128]{1,0:T(8,128)(2,1)S(1)} collective-permute-done((bf16[512,128]{1,0:T(8,128)(2,1)S(1)}, bf16[512,128]{1,0:T(8,128)(2,1)S(1)}, u32[]{:S(2)}, u32[]{:S(2)}) %collective-permute-start.10) | collective-permute-done | bytes 131104 | tf_op jit(solution)/shard_map/ppermute | solution.py:64
  54.5 1.3 %join.1 = (bf16[4,1024,128]{2,1,0:T(8,128)(2,1)S(1)}, bf16[4,1024,128]{2,1,0:T(8,128)(2,1)S(1)}) custom-call(bf16[2048,128]{1,0:T(8,128)(2,1)S(1)} %copy-done.1, bf16[2048,128]{1,0:T(8,128)(2,1)S(1)} %copy-done.2, bf16[2048,128]{1,0:T(8,128)(2,1)S(1)} %collective-permute-done.8.k1, bf16[2048,128]{1,0:T(8,128)(2,1)S(1)} %collective-permute-done.9.v1, ...), custom_call_target="tpu_custom_call" | custom-call | flops 3000000000 | bytes 1 | tf_op jit(solution)/shard_map/join/pallas_call | solution.py:336
  55.8 7.5 %collective-permute-done.11.q_ref = bf16[256,512]{1,0:T(8,128)(2,1)S(1)} collective-permute-done((bf16[256,512]{1,0:T(8,128)(2,1)S(1)}, bf16[256,512]{1,0:T(8,128)(2,1)S(1)}, u32[]{:S(2)}, u32[]{:S(2)}) %collective-permute-start.11) | collective-permute-done | bytes 262176 | tf_op jit(solution)/shard_map/ppermute | solution.py:56
  63.3 1.0 collective-permute-start.12
  64.3 1.4 %attend.7 = bf16[2,144,512]{2,1,0:T(8,128)(2,1)S(1)} custom-call(s32[16]{0:T(128)S(1)} %get-tuple-element.21.valid_ref, bf16[256,512]{1,0:T(8,128)(2,1)S(1)} %collective-permute-done.11.q_ref, bf16[4,1024,128]{2,1,0:T(8,128)(2,1)S(1)} %get-tuple-element.33.jk_ref, bf16[4,1024,128]{2,1,0:T(8,128)(2,1)S(1)} %get-tuple-element.34.jv_ref), custom_call_target="tpu_custom_call" | custom-call | flops 4000000000 | bytes 1 | tf_op jit(solution)/shard_map/attend/pallas_call | solution.py:348
  65.7 4.6 %collective-permute-start.14 = (bf16[2,144,512]{2,1,0:T(8,128)(2,1)S(1)}, bf16[2,144,512]{2,1,0:T(8,128)(2,1)S(1)}, u32[]{:S(2)}, u32[]{:S(2)}) collective-permute-start(bf16[2,144,512]{2,1,0:T(8,128)(2,1)S(1)} %attend.7), channel_id=1, source_target_pairs={{0,64},{8,200},{64,128},{72,8},{128,192},{136,72},{192,0},{200,136... | collective-permute-start | bytes 884744 | tf_op jit(solution)/shard_map/ppermute | solution.py:56
  70.3 5.7 %collective-permute-done.12.q_ref = bf16[256,512]{1,0:T(8,128)(2,1)S(1)} collective-permute-done((bf16[256,512]{1,0:T(8,128)(2,1)S(1)}, bf16[256,512]{1,0:T(8,128)(2,1)S(1)}, u32[]{:S(2)}, u32[]{:S(2)}) %collective-permute-start.12) | collective-permute-done | bytes 262176 | tf_op jit(solution)/shard_map/ppermute | solution.py:56
  76.0 1.4 %attend.6.a_ref = bf16[2,144,512]{2,1,0:T(8,128)(2,1)S(1)} custom-call(s32[16]{0:T(128)S(1)} %get-tuple-element.21.valid_ref, bf16[256,512]{1,0:T(8,128)(2,1)S(1)} %collective-permute-done.12.q_ref, bf16[4,1024,128]{2,1,0:T(8,128)(2,1)S(1)} %get-tuple-element.33.jk_ref, bf16[4,1024,128]{2,1,0:T(8,128)(2,1)S(1)} %get-tuple-element.34.jv_ref), custom_call_target="tpu_custom_call" | custom-call | flops 4000000000 | bytes 1 | tf_op jit(solution)/shard_map/attend/pallas_call | solution.py:348
  77.4 3.2 %collective-permute-done.14.b_ref = bf16[2,144,512]{2,1,0:T(8,128)(2,1)S(1)} collective-permute-done((bf16[2,144,512]{2,1,0:T(8,128)(2,1)S(1)}, bf16[2,144,512]{2,1,0:T(8,128)(2,1)S(1)}, u32[]{:S(2)}, u32[]{:S(2)}) %collective-permute-start.14) | collective-permute-done | bytes 294944 | tf_op jit(solution)/shard_map/ppermute | solution.py:56
  80.6 0.6 merge_between.2
  81.2 0.9 collective-permute-start.15
  82.1 4.7 %collective-permute-done.13.q_ref = bf16[256,512]{1,0:T(8,128)(2,1)S(1)} collective-permute-done((bf16[256,512]{1,0:T(8,128)(2,1)S(1)}, bf16[256,512]{1,0:T(8,128)(2,1)S(1)}, u32[]{:S(2)}, u32[]{:S(2)}) %collective-permute-start.13) | collective-permute-done | bytes 262176 | tf_op jit(solution)/shard_map/ppermute | solution.py:56
  86.8 4.6 %attend.5.a_ref = bf16[2,144,512]{2,1,0:T(8,128)(2,1)S(1)} custom-call(s32[16]{0:T(128)S(1)} %get-tuple-element.21.valid_ref, bf16[256,512]{1,0:T(8,128)(2,1)S(1)} %collective-permute-done.13.q_ref, bf16[4,1024,128]{2,1,0:T(8,128)(2,1)S(1)} %get-tuple-element.33.jk_ref, bf16[4,1024,128]{2,1,0:T(8,128)(2,1)S(1)} %get-tuple-element.34.jv_ref), custom_call_target="tpu_custom_call" | custom-call | flops 4000000000 | bytes 1 | tf_op jit(solution)/shard_map/attend/pallas_call | solution.py:348
  91.4 0.6 merge_between.3
  92.0 2.9 %collective-permute-start.16 = (bf16[2,144,512]{2,1,0:T(8,128)(2,1)S(1)}, bf16[2,144,512]{2,1,0:T(8,128)(2,1)S(1)}, u32[]{:S(2)}, u32[]{:S(2)}) collective-permute-start(bf16[2,144,512]{2,1,0:T(8,128)(2,1)S(1)} %merge_between.3), channel_id=1, source_target_pairs={{0,64},{8,200},{64,128},{72,8},{128,192},{136,72},{192,0},{200,136... | collective-permute-start | bytes 884744 | tf_op jit(solution)/shard_map/ppermute | solution.py:56
  94.9 6.6 %attend.4.a_ref = bf16[2,144,512]{2,1,0:T(8,128)(2,1)S(1)} custom-call(s32[16]{0:T(128)S(1)} %get-tuple-element.21.valid_ref, bf16[256,512]{1,0:T(8,128)(2,1)S(1)} %get-tuple-element.29.q_ref, bf16[4,1024,128]{2,1,0:T(8,128)(2,1)S(1)} %get-tuple-element.33.jk_ref, bf16[4,1024,128]{2,1,0:T(8,128)(2,1)S(1)} %get-tuple-element.34.jv_ref, ...), custom_call_target="tpu_custom_call" | custom-call | flops 4000000000 | bytes 1 | tf_op jit(solution)/shard_map/attend/pallas_call | solution.py:348
  101.5 2.7 %collective-permute-done.16.b_ref = bf16[2,144,512]{2,1,0:T(8,128)(2,1)S(1)} collective-permute-done((bf16[2,144,512]{2,1,0:T(8,128)(2,1)S(1)}, bf16[2,144,512]{2,1,0:T(8,128)(2,1)S(1)}, u32[]{:S(2)}, u32[]{:S(2)}) %collective-permute-start.16) | collective-permute-done | bytes 294944 | tf_op jit(solution)/shard_map/ppermute | solution.py:56
  104.1 1.3 %merge.1 = bf16[256,512]{1,0:T(8,128)(2,1)} custom-call(bf16[2,144,512]{2,1,0:T(8,128)(2,1)S(1)} %attend.4.a_ref, bf16[2,144,512]{2,1,0:T(8,128)(2,1)S(1)} %collective-permute-done.16.b_ref), custom_call_target="tpu_custom_call" | custom-call | flops 1 | bytes 1 | tf_op jit(solution)/shard_map/merge/pallas_call | solution.py:427
  (19 shorter events, 0.0 us)
Async XLA Ops:
  0.0 11.4 %collective-permute-start = (bf16[256,896]{1,0:T(8,128)(2,1)}, bf16[256,896]{1,0:T(8,128)(2,1)S(1)}, u32[]{:S(2)}, u32[]{:S(2)}) collective-permute-start(bf16[256,896]{1,0:T(8,128)(2,1)} %refs_0_.1), channel_id=1, source_target_pairs={{0,1},{1,2},{2,3},{3,0},{8,11},{9,8},{10,9},{11,10},{4,5},{5,6},{6... | collective-permute-start | bytes 1376264 | tf_op jit(solution)/shard_map/ppermute | solution.py:51
  1.5 13.5 %collective-permute-start.3 = (bf16[256,896]{1,0:T(8,128)(2,1)}, bf16[256,896]{1,0:T(8,128)(2,1)S(1)}, u32[]{:S(2)}, u32[]{:S(2)}) collective-permute-start(bf16[256,896]{1,0:T(8,128)(2,1)} %refs_0_.1), channel_id=1, source_target_pairs={{0,4},{4,0},{1,5},{5,1},{2,6},{6,2},{3,7},{7,3},{8,12},{12,8},{9,1... | collective-permute-start | bytes 1376264 | tf_op jit(solution)/shard_map/ppermute | solution.py:60
  3.3 5.1 %collective-permute-start.2 = (s32[4,128]{1,0:T(4,128)S(1)}, s32[4,128]{1,0:T(4,128)S(1)}, u32[]{:S(2)}, u32[]{:S(2)}) collective-permute-start(s32[4,128]{1,0:T(4,128)S(1)} %pad_add_fusion), channel_id=1, source_target_pairs={{0,32},{32,0},{1,33},{33,1},{2,34},{34,2},{3,35},{35,3},{4,36},{36... | collective-permute-start | bytes 6152 | tf_op jit(solution)/shard_map/ppermute | solution.py:64
  6.3 21.4 %copy-start.4 = (s32[8,8]{1,0:T(8,128)S(1)}, s32[8,8]{1,0:T(8,128)}, u32[]{:S(2)}) copy-start(s32[8,8]{1,0:T(8,128)} %key.1) | copy-start | bytes 772
  6.3 21.4 %copy-start.5 = (s32[8]{0:T(128)S(1)}, s32[8]{0:T(128)}, u32[]{:S(2)}) copy-start(s32[8]{0:T(128)} %count.1) | copy-start | bytes 100
  6.3 21.4 %copy-start.6 = (s32[2]{0:T(128)S(1)}, s32[2]{0:T(128)}, u32[]{:S(2)}) copy-start(s32[2]{0:T(128)} %offset.1) | copy-start | bytes 28
  6.3 21.4 %copy-start.7 = (f32[2,128]{1,0:T(2,128)S(1)}, f32[2,128]{1,0:T(2,128)}, u32[]{:S(2)}) copy-start(f32[2,128]{1,0:T(2,128)} %constant.66.clone.freq_ref) | copy-start | bytes 3076
  6.4 21.4 %copy-start = (s32[2,128]{1,0:T(2,128)S(1)}, s32[2,128]{1,0:T(2,128)}, u32[]{:S(2)}) copy-start(s32[2,128]{1,0:T(2,128)} %sel_ref.1) | copy-start | bytes 3076
  8.4 34.7 %collective-permute-start.8 = (bf16[2048,128]{1,0:T(8,128)(2,1)}, bf16[2048,128]{1,0:T(8,128)(2,1)S(1)}, u32[]{:S(2)}, u32[]{:S(2)}) collective-permute-start(bf16[2048,128]{1,0:T(8,128)(2,1)} %k0.1), channel_id=1, source_target_pairs={{0,32},{32,0},{1,33},{33,1},{2,34},{34,2},{3,35},{35,3},{4,36},{36... | collective-permute-start | bytes 1572872 | tf_op jit(solution)/shard_map/ppermute | solution.py:64
  11.4 31.8 %collective-permute-start.9 = (bf16[2048,128]{1,0:T(8,128)(2,1)}, bf16[2048,128]{1,0:T(8,128)(2,1)S(1)}, u32[]{:S(2)}, u32[]{:S(2)}) collective-permute-start(bf16[2048,128]{1,0:T(8,128)(2,1)} %v0.1), channel_id=1, source_target_pairs={{0,32},{32,0},{1,33},{33,1},{2,34},{34,2},{3,35},{35,3},{4,36},{36... | collective-permute-start | bytes 1572872 | tf_op jit(solution)/shard_map/ppermute | solution.py:64
  13.1 9.7 %collective-permute-start.1 = (bf16[256,896]{1,0:T(8,128)(2,1)S(1)}, bf16[256,896]{1,0:T(8,128)(2,1)S(1)}, u32[]{:S(2)}, u32[]{:S(2)}) collective-permute-start(bf16[256,896]{1,0:T(8,128)(2,1)S(1)} %collective-permute-done.refs_1_), channel_id=1, source_target_pairs={{0,1},{1,2},{2,3},{3,0},{8,11},{9,8},{10,9},{11,10},{4,5},{5,6},{6... | collective-permute-start | bytes 1376264 | tf_op jit(solution)/shard_map/ppermute | solution.py:51
  14.9 12.8 %collective-permute-start.4 = (bf16[256,896]{1,0:T(8,128)(2,1)S(1)}, bf16[256,896]{1,0:T(8,128)(2,1)S(1)}, u32[]{:S(2)}, u32[]{:S(2)}) collective-permute-start(bf16[256,896]{1,0:T(8,128)(2,1)S(1)} %collective-permute-done.3.refs_1_), channel_id=1, source_target_pairs={{0,1},{1,2},{2,3},{3,0},{8,11},{9,8},{10,9},{11,10},{4,5},{5,6},{6... | collective-permute-start | bytes 1376264 | tf_op jit(solution)/shard_map/ppermute | solution.py:51
  15.0 1.0 copy-start.3
  22.8 14.8 %collective-permute-start.7 = (bf16[256,896]{1,0:T(8,128)(2,1)S(1)}, bf16[256,896]{1,0:T(8,128)(2,1)S(1)}, u32[]{:S(2)}, u32[]{:S(2)}) collective-permute-start(bf16[256,896]{1,0:T(8,128)(2,1)S(1)} %collective-permute-done.1.refs_0_), channel_id=1, source_target_pairs={{0,1},{1,2},{2,3},{3,0},{8,11},{9,8},{10,9},{11,10},{4,5},{5,6},{6... | collective-permute-start | bytes 1376264 | tf_op jit(solution)/shard_map/ppermute | solution.py:51
  27.7 9.8 %collective-permute-start.5 = (bf16[256,896]{1,0:T(8,128)(2,1)S(1)}, bf16[256,896]{1,0:T(8,128)(2,1)S(1)}, u32[]{:S(2)}, u32[]{:S(2)}) collective-permute-start(bf16[256,896]{1,0:T(8,128)(2,1)S(1)} %collective-permute-done.4.refs_1_), channel_id=1, source_target_pairs={{0,1},{1,2},{2,3},{3,0},{8,11},{9,8},{10,9},{11,10},{4,5},{5,6},{6... | collective-permute-start | bytes 1376264 | tf_op jit(solution)/shard_map/ppermute | solution.py:51
  37.5 9.7 %collective-permute-start.6 = (bf16[256,896]{1,0:T(8,128)(2,1)S(1)}, bf16[256,896]{1,0:T(8,128)(2,1)S(1)}, u32[]{:S(2)}, u32[]{:S(2)}) collective-permute-start(bf16[256,896]{1,0:T(8,128)(2,1)S(1)} %collective-permute-done.5.refs_0_), channel_id=1, source_target_pairs={{0,1},{1,2},{2,3},{3,0},{8,11},{9,8},{10,9},{11,10},{4,5},{5,6},{6... | collective-permute-start | bytes 1376264 | tf_op jit(solution)/shard_map/ppermute | solution.py:51
  43.1 11.4 %copy-start.1 = (bf16[2048,128]{1,0:T(8,128)(2,1)S(1)}, bf16[2048,128]{1,0:T(8,128)(2,1)}, u32[]{:S(2)}) copy-start(bf16[2048,128]{1,0:T(8,128)(2,1)} %k0.1) | copy-start | bytes 1572868
  43.1 11.4 %copy-start.2 = (bf16[2048,128]{1,0:T(8,128)(2,1)S(1)}, bf16[2048,128]{1,0:T(8,128)(2,1)}, u32[]{:S(2)}) copy-start(bf16[2048,128]{1,0:T(8,128)(2,1)} %v0.1) | copy-start | bytes 1572868
  47.9 6.6 %collective-permute-start.10 = (bf16[512,128]{1,0:T(8,128)(2,1)S(1)}, bf16[512,128]{1,0:T(8,128)(2,1)S(1)}, u32[]{:S(2)}, u32[]{:S(2)}) collective-permute-start(bf16[512,128]{1,0:T(8,128)(2,1)S(1)} %get-tuple-element.30.n0), channel_id=1, source_target_pairs={{0,32},{32,0},{1,33},{33,1},{2,34},{34,2},{3,35},{35,3},{4,36},{36... | collective-permute-start | bytes 393224 | tf_op jit(solution)/shard_map/ppermute | solution.py:64
  49.8 13.5 %collective-permute-start.11 = (bf16[256,512]{1,0:T(8,128)(2,1)S(1)}, bf16[256,512]{1,0:T(8,128)(2,1)S(1)}, u32[]{:S(2)}, u32[]{:S(2)}) collective-permute-start(bf16[256,512]{1,0:T(8,128)(2,1)S(1)} %get-tuple-element.29.q_ref), channel_id=1, source_target_pairs={{0,64},{8,200},{64,128},{72,8},{128,192},{136,72},{192,0},{200,136... | collective-permute-start | bytes 786440 | tf_op jit(solution)/shard_map/ppermute | solution.py:56
  63.3 12.7 %collective-permute-start.12 = (bf16[256,512]{1,0:T(8,128)(2,1)S(1)}, bf16[256,512]{1,0:T(8,128)(2,1)S(1)}, u32[]{:S(2)}, u32[]{:S(2)}) collective-permute-start(bf16[256,512]{1,0:T(8,128)(2,1)S(1)} %collective-permute-done.11.q_ref), channel_id=1, source_target_pairs={{0,64},{8,200},{64,128},{72,8},{128,192},{136,72},{192,0},{200,136... | collective-permute-start | bytes 786440 | tf_op jit(solution)/shard_map/ppermute | solution.py:56
  65.7 14.9 %collective-permute-start.14 = (bf16[2,144,512]{2,1,0:T(8,128)(2,1)S(1)}, bf16[2,144,512]{2,1,0:T(8,128)(2,1)S(1)}, u32[]{:S(2)}, u32[]{:S(2)}) collective-permute-start(bf16[2,144,512]{2,1,0:T(8,128)(2,1)S(1)} %attend.7), channel_id=1, source_target_pairs={{0,64},{8,200},{64,128},{72,8},{128,192},{136,72},{192,0},{200,136... | collective-permute-start | bytes 884744 | tf_op jit(solution)/shard_map/ppermute | solution.py:56
  76.0 10.8 %collective-permute-start.13 = (bf16[256,512]{1,0:T(8,128)(2,1)S(1)}, bf16[256,512]{1,0:T(8,128)(2,1)S(1)}, u32[]{:S(2)}, u32[]{:S(2)}) collective-permute-start(bf16[256,512]{1,0:T(8,128)(2,1)S(1)} %collective-permute-done.12.q_ref), channel_id=1, source_target_pairs={{0,64},{8,200},{64,128},{72,8},{128,192},{136,72},{192,0},{200,136... | collective-permute-start | bytes 786440 | tf_op jit(solution)/shard_map/ppermute | solution.py:56
  81.2 10.3 %collective-permute-start.15 = (bf16[2,144,512]{2,1,0:T(8,128)(2,1)S(1)}, bf16[2,144,512]{2,1,0:T(8,128)(2,1)S(1)}, u32[]{:S(2)}, u32[]{:S(2)}) collective-permute-start(bf16[2,144,512]{2,1,0:T(8,128)(2,1)S(1)} %merge_between.2), channel_id=1, source_target_pairs={{0,64},{8,200},{64,128},{72,8},{128,192},{136,72},{192,0},{200,136... | collective-permute-start | bytes 884744 | tf_op jit(solution)/shard_map/ppermute | solution.py:56
  92.0 12.1 %collective-permute-start.16 = (bf16[2,144,512]{2,1,0:T(8,128)(2,1)S(1)}, bf16[2,144,512]{2,1,0:T(8,128)(2,1)S(1)}, u32[]{:S(2)}, u32[]{:S(2)}) collective-permute-start(bf16[2,144,512]{2,1,0:T(8,128)(2,1)S(1)} %merge_between.3), channel_id=1, source_target_pairs={{0,64},{8,200},{64,128},{72,8},{128,192},{136,72},{192,0},{200,136... | collective-permute-start | bytes 884744 | tf_op jit(solution)/shard_map/ppermute | solution.py:56

commit v3 on v2

--- a/solution.py
+++ b/solution.py
@@ -454,17 +454,18 @@
     mine = jnp.concatenate(
         [sel_index, jnp.broadcast_to(cache_offset[:, None], (SLOTS, SEL))], axis=0
     )
-    theirs = py(mine)
     h = [hidden, ring_x(hidden)]
     z = [pz(hidden)]
-    k1 = py(after(key_cache, theirs))
-    v1 = py(after(value_cache, h[1]))
+    k1 = py(key_cache)
+    theirs = py(after(mine, h[1]))
     for _ in range(2):
         h.append(ring_x(h[-1]))
-    for _ in range(3):
+    for _ in range(2):
         z.append(ring_x(z[-1]))
+    z.append(pz(h[3]))
+    v1 = py(after(value_cache, h[2]))
     cosine, sine, rot, sel_rows, valid = prepare(
-        after(place, h[2]), span_count, span_key, cache_offset, sel_index, theirs
+        after(place, h[3]), span_count, span_key, cache_offset, sel_index, theirs
     )
     project = functools.partial(partial_project, place)
     acc = project((H_AT, H_AT + 1), (hidden, h[1]), weights)

time: 107 us -> 103 us (0.963)
  the two profiles are of different devices: /device:TPU:32 before, /device:TPU:14 now
where the time goes in v3:
time: 103 us; the launch traced here: 102 us
  starting transfers between devices  42.4 us (41%)
  Pallas kernels  35 us (34%)
  waiting for transfers between devices  22.1 us (21%)
  local copies, waits for them, and re-layouts  1.87 us (2%)
    ppermute x6, starting transfers between devices, ring_z(): return lax.ppermute(v, ('zh', 'c'), pairs)  20.8 us
    pallas_call x4, Pallas kernels, attend(): pl.pallas_call(functools.partial(attend_kernel, shift), out_shape=packed_...  17.2 us
    ppermute x6, waiting for transfers between devices, ring_z(): return lax.ppermute(v, ('zh', 'c'), pairs)  14.7 us
    pallas_call x4, Pallas kernels, partial_project(): pl.pallas_call(functools.partial(partial_kernel, which, ahead, acc is not...  11.9 us
    ppermute x4, starting transfers between devices, py(): return lax.ppermute(v, 'yh', [(0, 1), (1, 0)])  9.18 us
    ppermute x5, starting transfers between devices, ring_x(): return lax.ppermute(v, ('c', 'x'), opposite_ways(4))  8.69 us
    ppermute x2, starting transfers between devices, pz(): return lax.ppermute(v, 'zl', [(0, 1), (1, 0)])  3.75 us
    ppermute x5, waiting for transfers between devices, ring_x(): return lax.ppermute(v, ('c', 'x'), opposite_ways(4))  3.6 us
  transfers between devices with their start and end apart: 17, of which 10 were waited for; matrix products, arithmetic and copies ran while one was open for 2% of the time, Pallas kernels for 32%

profile of v3, /device:TPU:14, one launch (start us, length us, event | category | flops | bytes accessed | tf_op | source)
XLA Modules:
  0.0 102.3 jit_solution(6814723694598495561)
XLA Ops:
  0.0 0.5 collective-permute-start
  0.5 1.9 %collective-permute-start.5 = (bf16[256,896]{1,0:T(8,128)(2,1)}, bf16[256,896]{1,0:T(8,128)(2,1)S(1)}, u32[]{:S(2)}, u32[]{:S(2)}) collective-permute-start(bf16[256,896]{1,0:T(8,128)(2,1)} %refs_0_.1), channel_id=1, source_target_pairs={{0,4},{4,0},{1,5},{5,1},{2,6},{6,2},{3,7},{7,3},{8,12},{12,8},{9,1... | collective-permute-start | bytes 1376264 | tf_op jit(solution)/shard_map/ppermute | solution.py:60
  2.4 2.3 %collective-permute-start.8 = (bf16[2048,128]{1,0:T(8,128)(2,1)}, bf16[2048,128]{1,0:T(8,128)(2,1)S(1)}, u32[]{:S(2)}, u32[]{:S(2)}) collective-permute-start(bf16[2048,128]{1,0:T(8,128)(2,1)} %k0.1), channel_id=1, source_target_pairs={{0,32},{32,0},{1,33},{33,1},{2,34},{34,2},{3,35},{35,3},{4,36},{36... | collective-permute-start | bytes 1572872 | tf_op jit(solution)/shard_map/ppermute | solution.py:64
  4.7 0.7 pad.1.clone
  5.4 0.1 stack.51.place
  5.5 0.8 pad_add_fusion
  6.3 2.4 %collective-permute-done.refs_1_ = bf16[256,896]{1,0:T(8,128)(2,1)S(1)} collective-permute-done((bf16[256,896]{1,0:T(8,128)(2,1)}, bf16[256,896]{1,0:T(8,128)(2,1)S(1)}, u32[]{:S(2)}, u32[]{:S(2)}) %collective-permute-start) | collective-permute-done | bytes 458784 | tf_op jit(solution)/shard_map/ppermute | solution.py:51
  8.7 2.3 %collective-permute-start.3 = (s32[4,128]{1,0:T(4,128)S(1)}, s32[4,128]{1,0:T(4,128)S(1)}, u32[]{:S(2)}, u32[]{:S(2)}) collective-permute-start(s32[4,128]{1,0:T(4,128)S(1)} %pad_add_fusion), channel_id=1, source_target_pairs={{0,32},{32,0},{1,33},{33,1},{2,34},{34,2},{3,35},{35,3},{4,36},{36... | collective-permute-start | bytes 6152 | tf_op jit(solution)/shard_map/ppermute | solution.py:64
  11.0 1.7 %collective-permute-start.1 = (bf16[256,896]{1,0:T(8,128)(2,1)S(1)}, bf16[256,896]{1,0:T(8,128)(2,1)S(1)}, u32[]{:S(2)}, u32[]{:S(2)}) collective-permute-start(bf16[256,896]{1,0:T(8,128)(2,1)S(1)} %collective-permute-done.refs_1_), channel_id=1, source_target_pairs={{0,1},{1,2},{2,3},{3,0},{8,11},{9,8},{10,9},{11,10},{4,5},{5,6},{6... | collective-permute-start | bytes 1376264 | tf_op jit(solution)/shard_map/ppermute | solution.py:51
  12.7 0.6 collective-permute-done.5.refs_1_
  13.2 2.3 %collective-permute-start.6 = (bf16[256,896]{1,0:T(8,128)(2,1)S(1)}, bf16[256,896]{1,0:T(8,128)(2,1)S(1)}, u32[]{:S(2)}, u32[]{:S(2)}) collective-permute-start(bf16[256,896]{1,0:T(8,128)(2,1)S(1)} %collective-permute-done.5.refs_1_), channel_id=1, source_target_pairs={{0,1},{1,2},{2,3},{3,0},{8,11},{9,8},{10,9},{11,10},{4,5},{5,6},{6... | collective-permute-start | bytes 1376264 | tf_op jit(solution)/shard_map/ppermute | solution.py:51
  15.5 1.0 copy-done.3
  16.5 3.3 %project.4.refs_5_ = f32[256,768]{1,0:T(8,128)S(1)} custom-call(s32[12]{0:T(128)S(1)} %stack.51.place, bf16[256,896]{1,0:T(8,128)(2,1)S(1)} %copy-done.3, bf16[256,896]{1,0:T(8,128)(2,1)S(1)} %collective-permute-done.refs_1_, bf16[7168,512]{1,0:T(8,128)(2,1)} %refs_1_.1, bf16[7168,128]{1,0:T(8,128)(2,1)} %refs_2_.7, bf16[7168,128]{1,0:T(8,128)(2,1)} %refs_3_.7), custom_call_target="tpu_custom_call" | custom-call | flops 6000000000 | bytes 1 | tf_op jit(solution)/shard_map/project/pallas_call | solution.py:180
  19.8 0.0 copy-start.5
  19.8 0.0 copy-start.6
  19.9 0.0 copy-start.7
  19.9 2.4 %collective-permute-start.9 = (bf16[2048,128]{1,0:T(8,128)(2,1)S(1)}, bf16[2048,128]{1,0:T(8,128)(2,1)S(1)}, u32[]{:S(2)}, u32[]{:S(2)}) collective-permute-start(bf16[2048,128]{1,0:T(8,128)(2,1)S(1)} %copy-done.2), channel_id=1, source_target_pairs={{0,32},{32,0},{1,33},{33,1},{2,34},{34,2},{3,35},{35,3},{4,36},{36... | collective-permute-start | bytes 1572872 | tf_op jit(solution)/shard_map/ppermute | solution.py:64
  22.3 1.3 %collective-permute-start.2 = (bf16[256,896]{1,0:T(8,128)(2,1)S(1)}, bf16[256,896]{1,0:T(8,128)(2,1)S(1)}, u32[]{:S(2)}, u32[]{:S(2)}) collective-permute-start(bf16[256,896]{1,0:T(8,128)(2,1)S(1)} %collective-permute-done.1.refs_0_), channel_id=1, source_target_pairs={{0,1},{1,2},{2,3},{3,0},{8,11},{9,8},{10,9},{11,10},{4,5},{5,6},{6... | collective-permute-start | bytes 1376264 | tf_op jit(solution)/shard_map/ppermute | solution.py:51
  23.6 0.8 collective-permute-done.6.refs_1_
  24.4 2.9 %collective-permute-start.7 = (bf16[256,896]{1,0:T(8,128)(2,1)S(1)}, bf16[256,896]{1,0:T(8,128)(2,1)S(1)}, u32[]{:S(2)}, u32[]{:S(2)}) collective-permute-start(bf16[256,896]{1,0:T(8,128)(2,1)S(1)} %collective-permute-done.6.refs_1_), channel_id=1, source_target_pairs={{0,1},{1,2},{2,3},{3,0},{8,11},{9,8},{10,9},{11,10},{4,5},{5,6},{6... | collective-permute-start | bytes 1376264 | tf_op jit(solution)/shard_map/ppermute | solution.py:51
  27.3 3.1 %project.5.refs_5_ = f32[256,768]{1,0:T(8,128)S(1)} custom-call(s32[12]{0:T(128)S(1)} %stack.51.place, bf16[256,896]{1,0:T(8,128)(2,1)S(1)} %collective-permute-done.1.refs_0_, bf16[256,896]{1,0:T(8,128)(2,1)S(1)} %collective-permute-done.5.refs_1_, bf16[7168,512]{1,0:T(8,128)(2,1)} %refs_1_.1, bf16[7168,128]{1,0:T(8,128)(2,1)} %refs_2_.7, ...), custom_call_target="tpu_custom_call" | custom-call | flops 6000000000 | bytes 1 | tf_op jit(solution)/shard_map/project/pallas_call | solution.py:180
  30.4 0.4 collective-permute-done.2.refs_0_
  30.8 1.8 %collective-permute-start.4 = (bf16[256,896]{1,0:T(8,128)(2,1)S(1)}, bf16[256,896]{1,0:T(8,128)(2,1)S(1)}, u32[]{:S(2)}, u32[]{:S(2)}) collective-permute-start(bf16[256,896]{1,0:T(8,128)(2,1)S(1)} %collective-permute-done.2.refs_0_), channel_id=1, source_target_pairs={{0,4},{4,0},{1,5},{5,1},{2,6},{6,2},{3,7},{7,3},{8,12},{12,8},{9,1... | collective-permute-start | bytes 1376264 | tf_op jit(solution)/shard_map/ppermute | solution.py:60
  32.6 1.6 %prepare.1 = (f32[256,128]{1,0:T(8,128)S(1)}, f32[256,128]{1,0:T(8,128)S(1)}, f32[2,4,128]{2,1,0:T(4,128)S(1)}, s32[2,2,128]{2,1,0:T(2,128)S(1)}, s32[16]{0:T(128)S(1)}) custom-call(s32[12]{0:T(128)S(1)} %stack.51.place, s32[8]{0:T(128)S(1)} %copy-done.5, s32[8,8]{1,0:T(8,128)S(1)} %copy-done.4, s32[2]{0:T(128)S(1)} %copy-done.6, s32[2,128]{1,0:T(2,128)S(1)} %copy-done, ...), custom_call_target="tpu_custom_call" | custom-call | flops 2000000000 | bytes 1 | tf_op jit(solution)/shard_map/prepare/pallas_call | solution.py:118
  34.2 3.1 %project.6.refs_4_ = f32[256,768]{1,0:T(8,128)S(1)} custom-call(s32[12]{0:T(128)S(1)} %stack.51.place, bf16[256,896]{1,0:T(8,128)(2,1)S(1)} %collective-permute-done.2.refs_0_, bf16[256,896]{1,0:T(8,128)(2,1)S(1)} %collective-permute-done.6.refs_1_, bf16[7168,512]{1,0:T(8,128)(2,1)} %refs_1_.1, bf16[7168,128]{1,0:T(8,128)(2,1)} %refs_2_.7, ...), custom_call_target="tpu_custom_call" | custom-call | flops 6000000000 | bytes 1 | tf_op jit(solution)/shard_map/project/pallas_call | solution.py:180
  37.3 2.5 %project.7 = (f32[256,768]{1,0:T(8,128)S(1)}, bf16[1,896,768]{2,1,0:T(8,128)(2,1)S(1)}) custom-call(s32[12]{0:T(128)S(1)} %stack.51.place, bf16[256,896]{1,0:T(8,128)(2,1)S(1)} %collective-permute-done.7.refs_0_, bf16[7168,512]{1,0:T(8,128)(2,1)} %refs_1_.1, bf16[7168,128]{1,0:T(8,128)(2,1)} %refs_2_.7, bf16[7168,128]{1,0:T(8,128)(2,1)} %refs_3_.7, ...), custom_call_target="tpu_custom_call" | custom-call | flops 6000000000 | bytes 1 | tf_op jit(solution)/shard_map/project/pallas_call | solution.py:180
  39.9 2.2 %collective-permute-done.4.piece_ref = bf16[256,896]{1,0:T(8,128)(2,1)S(1)} collective-permute-done((bf16[256,896]{1,0:T(8,128)(2,1)S(1)}, bf16[256,896]{1,0:T(8,128)(2,1)S(1)}, u32[]{:S(2)}, u32[]{:S(2)}) %collective-permute-start.4) | collective-permute-done | bytes 458784 | tf_op jit(solution)/shard_map/ppermute | solution.py:60
  42.0 0.7 project_last.1
  42.7 2.2 %collective-permute-start.10 = (bf16[512,128]{1,0:T(8,128)(2,1)S(1)}, bf16[512,128]{1,0:T(8,128)(2,1)S(1)}, u32[]{:S(2)}, u32[]{:S(2)}) collective-permute-start(bf16[512,128]{1,0:T(8,128)(2,1)S(1)} %get-tuple-element.30.n0), channel_id=1, source_target_pairs={{0,32},{32,0},{1,33},{33,1},{2,34},{34,2},{3,35},{35,3},{4,36},{36... | collective-permute-start | bytes 393224 | tf_op jit(solution)/shard_map/ppermute | solution.py:64
  44.9 3.3 %collective-permute-start.11 = (bf16[256,512]{1,0:T(8,128)(2,1)S(1)}, bf16[256,512]{1,0:T(8,128)(2,1)S(1)}, u32[]{:S(2)}, u32[]{:S(2)}) collective-permute-start(bf16[256,512]{1,0:T(8,128)(2,1)S(1)} %get-tuple-element.29.q_ref), channel_id=1, source_target_pairs={{0,64},{8,200},{64,128},{72,8},{128,192},{136,72},{192,0},{200,136... | collective-permute-start | bytes 786440 | tf_op jit(solution)/shard_map/ppermute | solution.py:56
  48.2 1.1 %collective-permute-done.10.n1 = bf16[512,128]{1,0:T(8,128)(2,1)S(1)} collective-permute-done((bf16[512,128]{1,0:T(8,128)(2,1)S(1)}, bf16[512,128]{1,0:T(8,128)(2,1)S(1)}, u32[]{:S(2)}, u32[]{:S(2)}) %collective-permute-start.10) | collective-permute-done | bytes 131104 | tf_op jit(solution)/shard_map/ppermute | solution.py:64
  49.3 1.3 %join.1 = (bf16[4,1024,128]{2,1,0:T(8,128)(2,1)S(1)}, bf16[4,1024,128]{2,1,0:T(8,128)(2,1)S(1)}) custom-call(bf16[2048,128]{1,0:T(8,128)(2,1)S(1)} %copy-done.1, bf16[2048,128]{1,0:T(8,128)(2,1)S(1)} %copy-done.2, bf16[2048,128]{1,0:T(8,128)(2,1)S(1)} %collective-permute-done.8.k1, bf16[2048,128]{1,0:T(8,128)(2,1)S(1)} %collective-permute-done.9.v1, ...), custom_call_target="tpu_custom_call" | custom-call | flops 3000000000 | bytes 1 | tf_op jit(solution)/shard_map/join/pallas_call | solution.py:336
  50.5 5.4 %collective-permute-done.11.q_ref = bf16[256,512]{1,0:T(8,128)(2,1)S(1)} collective-permute-done((bf16[256,512]{1,0:T(8,128)(2,1)S(1)}, bf16[256,512]{1,0:T(8,128)(2,1)S(1)}, u32[]{:S(2)}, u32[]{:S(2)}) %collective-permute-start.11) | collective-permute-done | bytes 262176 | tf_op jit(solution)/shard_map/ppermute | solution.py:56
  56.0 3.1 %collective-permute-start.12 = (bf16[256,512]{1,0:T(8,128)(2,1)S(1)}, bf16[256,512]{1,0:T(8,128)(2,1)S(1)}, u32[]{:S(2)}, u32[]{:S(2)}) collective-permute-start(bf16[256,512]{1,0:T(8,128)(2,1)S(1)} %collective-permute-done.11.q_ref), channel_id=1, source_target_pairs={{0,64},{8,200},{64,128},{72,8},{128,192},{136,72},{192,0},{200,136... | collective-permute-start | bytes 786440 | tf_op jit(solution)/shard_map/ppermute | solution.py:56
  59.1 1.4 %attend.7 = bf16[2,144,512]{2,1,0:T(8,128)(2,1)S(1)} custom-call(s32[16]{0:T(128)S(1)} %get-tuple-element.22.valid_ref, bf16[256,512]{1,0:T(8,128)(2,1)S(1)} %collective-permute-done.11.q_ref, bf16[4,1024,128]{2,1,0:T(8,128)(2,1)S(1)} %get-tuple-element.33.jk_ref, bf16[4,1024,128]{2,1,0:T(8,128)(2,1)S(1)} %get-tuple-element.34.jv_ref), custom_call_target="tpu_custom_call" | custom-call | flops 4000000000 | bytes 1 | tf_op jit(solution)/shard_map/attend/pallas_call | solution.py:348
  60.5 6.2 %collective-permute-start.14 = (bf16[2,144,512]{2,1,0:T(8,128)(2,1)S(1)}, bf16[2,144,512]{2,1,0:T(8,128)(2,1)S(1)}, u32[]{:S(2)}, u32[]{:S(2)}) collective-permute-start(bf16[2,144,512]{2,1,0:T(8,128)(2,1)S(1)} %attend.7), channel_id=1, source_target_pairs={{0,64},{8,200},{64,128},{72,8},{128,192},{136,72},{192,0},{200,136... | collective-permute-start | bytes 884744 | tf_op jit(solution)/shard_map/ppermute | solution.py:56
  66.7 5.4 %collective-permute-start.13 = (bf16[256,512]{1,0:T(8,128)(2,1)S(1)}, bf16[256,512]{1,0:T(8,128)(2,1)S(1)}, u32[]{:S(2)}, u32[]{:S(2)}) collective-permute-start(bf16[256,512]{1,0:T(8,128)(2,1)S(1)} %collective-permute-done.12.q_ref), channel_id=1, source_target_pairs={{0,64},{8,200},{64,128},{72,8},{128,192},{136,72},{192,0},{200,136... | collective-permute-start | bytes 786440 | tf_op jit(solution)/shard_map/ppermute | solution.py:56
  72.2 4.6 %attend.6.a_ref = bf16[2,144,512]{2,1,0:T(8,128)(2,1)S(1)} custom-call(s32[16]{0:T(128)S(1)} %get-tuple-element.22.valid_ref, bf16[256,512]{1,0:T(8,128)(2,1)S(1)} %collective-permute-done.12.q_ref, bf16[4,1024,128]{2,1,0:T(8,128)(2,1)S(1)} %get-tuple-element.33.jk_ref, bf16[4,1024,128]{2,1,0:T(8,128)(2,1)S(1)} %get-tuple-element.34.jv_ref), custom_call_target="tpu_custom_call" | custom-call | flops 4000000000 | bytes 1 | tf_op jit(solution)/shard_map/attend/pallas_call | solution.py:348
  76.7 0.6 merge_between.2
  77.3 1.5 %collective-permute-start.15 = (bf16[2,144,512]{2,1,0:T(8,128)(2,1)S(1)}, bf16[2,144,512]{2,1,0:T(8,128)(2,1)S(1)}, u32[]{:S(2)}, u32[]{:S(2)}) collective-permute-start(bf16[2,144,512]{2,1,0:T(8,128)(2,1)S(1)} %merge_between.2), channel_id=1, source_target_pairs={{0,64},{8,200},{64,128},{72,8},{128,192},{136,72},{192,0},{200,136... | collective-permute-start | bytes 884744 | tf_op jit(solution)/shard_map/ppermute | solution.py:56
  78.8 1.2 %collective-permute-done.13.q_ref = bf16[256,512]{1,0:T(8,128)(2,1)S(1)} collective-permute-done((bf16[256,512]{1,0:T(8,128)(2,1)S(1)}, bf16[256,512]{1,0:T(8,128)(2,1)S(1)}, u32[]{:S(2)}, u32[]{:S(2)}) %collective-permute-start.13) | collective-permute-done | bytes 262176 | tf_op jit(solution)/shard_map/ppermute | solution.py:56
  80.0 4.6 %attend.5.a_ref = bf16[2,144,512]{2,1,0:T(8,128)(2,1)S(1)} custom-call(s32[16]{0:T(128)S(1)} %get-tuple-element.22.valid_ref, bf16[256,512]{1,0:T(8,128)(2,1)S(1)} %collective-permute-done.13.q_ref, bf16[4,1024,128]{2,1,0:T(8,128)(2,1)S(1)} %get-tuple-element.33.jk_ref, bf16[4,1024,128]{2,1,0:T(8,128)(2,1)S(1)} %get-tuple-element.34.jv_ref), custom_call_target="tpu_custom_call" | custom-call | flops 4000000000 | bytes 1 | tf_op jit(solution)/shard_map/attend/pallas_call | solution.py:348
  84.6 3.8 %collective-permute-done.15.b_ref = bf16[2,144,512]{2,1,0:T(8,128)(2,1)S(1)} collective-permute-done((bf16[2,144,512]{2,1,0:T(8,128)(2,1)S(1)}, bf16[2,144,512]{2,1,0:T(8,128)(2,1)S(1)}, u32[]{:S(2)}, u32[]{:S(2)}) %collective-permute-start.15) | collective-permute-done | bytes 294944 | tf_op jit(solution)/shard_map/ppermute | solution.py:56
  88.4 0.6 merge_between.3
  89.0 1.3 %collective-permute-start.16 = (bf16[2,144,512]{2,1,0:T(8,128)(2,1)S(1)}, bf16[2,144,512]{2,1,0:T(8,128)(2,1)S(1)}, u32[]{:S(2)}, u32[]{:S(2)}) collective-permute-start(bf16[2,144,512]{2,1,0:T(8,128)(2,1)S(1)} %merge_between.3), channel_id=1, source_target_pairs={{0,64},{8,200},{64,128},{72,8},{128,192},{136,72},{192,0},{200,136... | collective-permute-start | bytes 884744 | tf_op jit(solution)/shard_map/ppermute | solution.py:56
  90.2 6.6 %attend.4.a_ref = bf16[2,144,512]{2,1,0:T(8,128)(2,1)S(1)} custom-call(s32[16]{0:T(128)S(1)} %get-tuple-element.22.valid_ref, bf16[256,512]{1,0:T(8,128)(2,1)S(1)} %get-tuple-element.29.q_ref, bf16[4,1024,128]{2,1,0:T(8,128)(2,1)S(1)} %get-tuple-element.33.jk_ref, bf16[4,1024,128]{2,1,0:T(8,128)(2,1)S(1)} %get-tuple-element.34.jv_ref, ...), custom_call_target="tpu_custom_call" | custom-call | flops 4000000000 | bytes 1 | tf_op jit(solution)/shard_map/attend/pallas_call | solution.py:348
  96.8 4.2 %collective-permute-done.16.b_ref = bf16[2,144,512]{2,1,0:T(8,128)(2,1)S(1)} collective-permute-done((bf16[2,144,512]{2,1,0:T(8,128)(2,1)S(1)}, bf16[2,144,512]{2,1,0:T(8,128)(2,1)S(1)}, u32[]{:S(2)}, u32[]{:S(2)}) %collective-permute-start.16) | collective-permute-done | bytes 294944 | tf_op jit(solution)/shard_map/ppermute | solution.py:56
  101.0 1.3 %merge.1 = bf16[256,512]{1,0:T(8,128)(2,1)} custom-call(bf16[2,144,512]{2,1,0:T(8,128)(2,1)S(1)} %attend.4.a_ref, bf16[2,144,512]{2,1,0:T(8,128)(2,1)S(1)} %collective-permute-done.16.b_ref), custom_call_target="tpu_custom_call" | custom-call | flops 1 | bytes 1 | tf_op jit(solution)/shard_map/merge/pallas_call | solution.py:427
  (19 shorter events, 0.0 us)
Async XLA Ops:
  0.0 8.7 %collective-permute-start = (bf16[256,896]{1,0:T(8,128)(2,1)}, bf16[256,896]{1,0:T(8,128)(2,1)S(1)}, u32[]{:S(2)}, u32[]{:S(2)}) collective-permute-start(bf16[256,896]{1,0:T(8,128)(2,1)} %refs_0_.1), channel_id=1, source_target_pairs={{0,1},{1,2},{2,3},{3,0},{8,11},{9,8},{10,9},{11,10},{4,5},{5,6},{6... | collective-permute-start | bytes 1376264 | tf_op jit(solution)/shard_map/ppermute | solution.py:51
  0.5 12.7 %collective-permute-start.5 = (bf16[256,896]{1,0:T(8,128)(2,1)}, bf16[256,896]{1,0:T(8,128)(2,1)S(1)}, u32[]{:S(2)}, u32[]{:S(2)}) collective-permute-start(bf16[256,896]{1,0:T(8,128)(2,1)} %refs_0_.1), channel_id=1, source_target_pairs={{0,4},{4,0},{1,5},{5,1},{2,6},{6,2},{3,7},{7,3},{8,12},{12,8},{9,1... | collective-permute-start | bytes 1376264 | tf_op jit(solution)/shard_map/ppermute | solution.py:60
  2.4 37.4 %collective-permute-start.8 = (bf16[2048,128]{1,0:T(8,128)(2,1)}, bf16[2048,128]{1,0:T(8,128)(2,1)S(1)}, u32[]{:S(2)}, u32[]{:S(2)}) collective-permute-start(bf16[2048,128]{1,0:T(8,128)(2,1)} %k0.1), channel_id=1, source_target_pairs={{0,32},{32,0},{1,33},{33,1},{2,34},{34,2},{3,35},{35,3},{4,36},{36... | collective-permute-start | bytes 1572872 | tf_op jit(solution)/shard_map/ppermute | solution.py:64
  6.3 13.6 %copy-start.2 = (bf16[2048,128]{1,0:T(8,128)(2,1)S(1)}, bf16[2048,128]{1,0:T(8,128)(2,1)}, u32[]{:S(2)}) copy-start(bf16[2048,128]{1,0:T(8,128)(2,1)} %v0.1) | copy-start | bytes 1572868
  8.7 23.9 %collective-permute-start.3 = (s32[4,128]{1,0:T(4,128)S(1)}, s32[4,128]{1,0:T(4,128)S(1)}, u32[]{:S(2)}, u32[]{:S(2)}) collective-permute-start(s32[4,128]{1,0:T(4,128)S(1)} %pad_add_fusion), channel_id=1, source_target_pairs={{0,32},{32,0},{1,33},{33,1},{2,34},{34,2},{3,35},{35,3},{4,36},{36... | collective-permute-start | bytes 6152 | tf_op jit(solution)/shard_map/ppermute | solution.py:64
  11.0 8.9 %collective-permute-start.1 = (bf16[256,896]{1,0:T(8,128)(2,1)S(1)}, bf16[256,896]{1,0:T(8,128)(2,1)S(1)}, u32[]{:S(2)}, u32[]{:S(2)}) collective-permute-start(bf16[256,896]{1,0:T(8,128)(2,1)S(1)} %collective-permute-done.refs_1_), channel_id=1, source_target_pairs={{0,1},{1,2},{2,3},{3,0},{8,11},{9,8},{10,9},{11,10},{4,5},{5,6},{6... | collective-permute-start | bytes 1376264 | tf_op jit(solution)/shard_map/ppermute | solution.py:51
  13.2 11.2 %collective-permute-start.6 = (bf16[256,896]{1,0:T(8,128)(2,1)S(1)}, bf16[256,896]{1,0:T(8,128)(2,1)S(1)}, u32[]{:S(2)}, u32[]{:S(2)}) collective-permute-start(bf16[256,896]{1,0:T(8,128)(2,1)S(1)} %collective-permute-done.5.refs_1_), channel_id=1, source_target_pairs={{0,1},{1,2},{2,3},{3,0},{8,11},{9,8},{10,9},{11,10},{4,5},{5,6},{6... | collective-permute-start | bytes 1376264 | tf_op jit(solution)/shard_map/ppermute | solution.py:51
  15.5 1.0 copy-start.3
  19.8 12.8 %copy-start = (s32[2,128]{1,0:T(2,128)S(1)}, s32[2,128]{1,0:T(2,128)}, u32[]{:S(2)}) copy-start(s32[2,128]{1,0:T(2,128)} %sel_ref.1) | copy-start | bytes 3076
  19.8 12.8 %copy-start.4 = (s32[8,8]{1,0:T(8,128)S(1)}, s32[8,8]{1,0:T(8,128)}, u32[]{:S(2)}) copy-start(s32[8,8]{1,0:T(8,128)} %key.1) | copy-start | bytes 772
  19.8 12.8 %copy-start.5 = (s32[8]{0:T(128)S(1)}, s32[8]{0:T(128)}, u32[]{:S(2)}) copy-start(s32[8]{0:T(128)} %count.1) | copy-start | bytes 100
  19.8 12.8 %copy-start.6 = (s32[2]{0:T(128)S(1)}, s32[2]{0:T(128)}, u32[]{:S(2)}) copy-start(s32[2]{0:T(128)} %offset.1) | copy-start | bytes 28
  19.9 12.8 %copy-start.7 = (f32[2,128]{1,0:T(2,128)S(1)}, f32[2,128]{1,0:T(2,128)}, u32[]{:S(2)}) copy-start(f32[2,128]{1,0:T(2,128)} %constant.66.clone.freq_ref) | copy-start | bytes 3076
  19.9 20.0 %collective-permute-start.9 = (bf16[2048,128]{1,0:T(8,128)(2,1)S(1)}, bf16[2048,128]{1,0:T(8,128)(2,1)S(1)}, u32[]{:S(2)}, u32[]{:S(2)}) collective-permute-start(bf16[2048,128]{1,0:T(8,128)(2,1)S(1)} %copy-done.2), channel_id=1, source_target_pairs={{0,32},{32,0},{1,33},{33,1},{2,34},{34,2},{3,35},{35,3},{4,36},{36... | collective-permute-start | bytes 1572872 | tf_op jit(solution)/shard_map/ppermute | solution.py:64
  22.3 8.5 %collective-permute-start.2 = (bf16[256,896]{1,0:T(8,128)(2,1)S(1)}, bf16[256,896]{1,0:T(8,128)(2,1)S(1)}, u32[]{:S(2)}, u32[]{:S(2)}) collective-permute-start(bf16[256,896]{1,0:T(8,128)(2,1)S(1)} %collective-permute-done.1.refs_0_), channel_id=1, source_target_pairs={{0,1},{1,2},{2,3},{3,0},{8,11},{9,8},{10,9},{11,10},{4,5},{5,6},{6... | collective-permute-start | bytes 1376264 | tf_op jit(solution)/shard_map/ppermute | solution.py:51
  24.4 13.0 %collective-permute-start.7 = (bf16[256,896]{1,0:T(8,128)(2,1)S(1)}, bf16[256,896]{1,0:T(8,128)(2,1)S(1)}, u32[]{:S(2)}, u32[]{:S(2)}) collective-permute-start(bf16[256,896]{1,0:T(8,128)(2,1)S(1)} %collective-permute-done.6.refs_1_), channel_id=1, source_target_pairs={{0,1},{1,2},{2,3},{3,0},{8,11},{9,8},{10,9},{11,10},{4,5},{5,6},{6... | collective-permute-start | bytes 1376264 | tf_op jit(solution)/shard_map/ppermute | solution.py:51
  30.8 11.3 %collective-permute-start.4 = (bf16[256,896]{1,0:T(8,128)(2,1)S(1)}, bf16[256,896]{1,0:T(8,128)(2,1)S(1)}, u32[]{:S(2)}, u32[]{:S(2)}) collective-permute-start(bf16[256,896]{1,0:T(8,128)(2,1)S(1)} %collective-permute-done.2.refs_0_), channel_id=1, source_target_pairs={{0,4},{4,0},{1,5},{5,1},{2,6},{6,2},{3,7},{7,3},{8,12},{12,8},{9,1... | collective-permute-start | bytes 1376264 | tf_op jit(solution)/shard_map/ppermute | solution.py:60
  39.8 9.5 %copy-start.1 = (bf16[2048,128]{1,0:T(8,128)(2,1)S(1)}, bf16[2048,128]{1,0:T(8,128)(2,1)}, u32[]{:S(2)}) copy-start(bf16[2048,128]{1,0:T(8,128)(2,1)} %k0.1) | copy-start | bytes 1572868
  42.7 6.6 %collective-permute-start.10 = (bf16[512,128]{1,0:T(8,128)(2,1)S(1)}, bf16[512,128]{1,0:T(8,128)(2,1)S(1)}, u32[]{:S(2)}, u32[]{:S(2)}) collective-permute-start(bf16[512,128]{1,0:T(8,128)(2,1)S(1)} %get-tuple-element.30.n0), channel_id=1, source_target_pairs={{0,32},{32,0},{1,33},{33,1},{2,34},{34,2},{3,35},{35,3},{4,36},{36... | collective-permute-start | bytes 393224 | tf_op jit(solution)/shard_map/ppermute | solution.py:64
  44.9 11.1 %collective-permute-start.11 = (bf16[256,512]{1,0:T(8,128)(2,1)S(1)}, bf16[256,512]{1,0:T(8,128)(2,1)S(1)}, u32[]{:S(2)}, u32[]{:S(2)}) collective-permute-start(bf16[256,512]{1,0:T(8,128)(2,1)S(1)} %get-tuple-element.29.q_ref), channel_id=1, source_target_pairs={{0,64},{8,200},{64,128},{72,8},{128,192},{136,72},{192,0},{200,136... | collective-permute-start | bytes 786440 | tf_op jit(solution)/shard_map/ppermute | solution.py:56
  56.0 10.8 %collective-permute-start.12 = (bf16[256,512]{1,0:T(8,128)(2,1)S(1)}, bf16[256,512]{1,0:T(8,128)(2,1)S(1)}, u32[]{:S(2)}, u32[]{:S(2)}) collective-permute-start(bf16[256,512]{1,0:T(8,128)(2,1)S(1)} %collective-permute-done.11.q_ref), channel_id=1, source_target_pairs={{0,64},{8,200},{64,128},{72,8},{128,192},{136,72},{192,0},{200,136... | collective-permute-start | bytes 786440 | tf_op jit(solution)/shard_map/ppermute | solution.py:56
  60.5 16.2 %collective-permute-start.14 = (bf16[2,144,512]{2,1,0:T(8,128)(2,1)S(1)}, bf16[2,144,512]{2,1,0:T(8,128)(2,1)S(1)}, u32[]{:S(2)}, u32[]{:S(2)}) collective-permute-start(bf16[2,144,512]{2,1,0:T(8,128)(2,1)S(1)} %attend.7), channel_id=1, source_target_pairs={{0,64},{8,200},{64,128},{72,8},{128,192},{136,72},{192,0},{200,136... | collective-permute-start | bytes 884744 | tf_op jit(solution)/shard_map/ppermute | solution.py:56
  66.7 13.3 %collective-permute-start.13 = (bf16[256,512]{1,0:T(8,128)(2,1)S(1)}, bf16[256,512]{1,0:T(8,128)(2,1)S(1)}, u32[]{:S(2)}, u32[]{:S(2)}) collective-permute-start(bf16[256,512]{1,0:T(8,128)(2,1)S(1)} %collective-permute-done.12.q_ref), channel_id=1, source_target_pairs={{0,64},{8,200},{64,128},{72,8},{128,192},{136,72},{192,0},{200,136... | collective-permute-start | bytes 786440 | tf_op jit(solution)/shard_map/ppermute | solution.py:56
  77.3 11.1 %collective-permute-start.15 = (bf16[2,144,512]{2,1,0:T(8,128)(2,1)S(1)}, bf16[2,144,512]{2,1,0:T(8,128)(2,1)S(1)}, u32[]{:S(2)}, u32[]{:S(2)}) collective-permute-start(bf16[2,144,512]{2,1,0:T(8,128)(2,1)S(1)} %merge_between.2), channel_id=1, source_target_pairs={{0,64},{8,200},{64,128},{72,8},{128,192},{136,72},{192,0},{200,136... | collective-permute-start | bytes 884744 | tf_op jit(solution)/shard_map/ppermute | solution.py:56
  89.0 12.1 %collective-permute-start.16 = (bf16[2,144,512]{2,1,0:T(8,128)(2,1)S(1)}, bf16[2,144,512]{2,1,0:T(8,128)(2,1)S(1)}, u32[]{:S(2)}, u32[]{:S(2)}) collective-permute-start(bf16[2,144,512]{2,1,0:T(8,128)(2,1)S(1)} %merge_between.3), channel_id=1, source_target_pairs={{0,64},{8,200},{64,128},{72,8},{128,192},{136,72},{192,0},{200,136... | collective-permute-start | bytes 884744 | tf_op jit(solution)/shard_map/ppermute | solution.py:56

commit v4 on v3

--- a/solution.py
+++ b/solution.py
@@ -219,22 +219,23 @@
     )(*args)
 
 
-def attend_block(at, q_ref, keys, vals, limit, m_ref, l_ref, acc_ref):
-    s = lax.dot_general(
-        q_ref[at, :], keys, (((1,), (1,)), ((), ())), preferred_element_type=jnp.float32
-    )
+def attend_block(q, keys, vals, limit, m_ref, l_ref, acc_ref):
+    s = lax.dot_general(keys, q, (((1,), (1,)), ((), ())), preferred_element_type=jnp.float32)
     if limit is not None:
-        col = lax.broadcasted_iota(jnp.int32, s.shape, 1)
-        s = jnp.where(col <= limit, s, low)
-    old = m_ref[at, :]
-    new = jnp.maximum(old, jnp.max(s, axis=1, keepdims=True))
+        at = lax.broadcasted_iota(jnp.int32, s.shape, 0)
+        s = jnp.where(at <= limit, s, low)
+    old = m_ref[...]
+    new = jnp.maximum(old, jnp.max(s, axis=0, keepdims=True))
     factor = jnp.exp2((old - new) * SCALE2)
     weight = jnp.exp2((s - new) * SCALE2)
-    l_ref[at, :] = l_ref[at, :] * factor + jnp.sum(weight, axis=1, keepdims=True)
-    acc_ref[at, :] = acc_ref[at, :] * factor + jnp.dot(
-        weight.astype(jnp.bfloat16), vals, preferred_element_type=jnp.float32
-    )
-    m_ref[at, :] = new
+    l_ref[...] = l_ref[...] * factor + jnp.sum(weight, axis=0, keepdims=True)
+    acc_ref[...] = acc_ref[...] * factor + lax.dot_general(
+        vals,
+        weight.astype(jnp.bfloat16),
+        (((0,), (0,)), ((), ())),
+        preferred_element_type=jnp.float32,
+    )
+    m_ref[...] = new
 
 
 def attend_source(rows_ref, i, jk_ref, jv_ref, r, valid_ref, first, o_ref, state, limit_ref=None):
@@ -243,35 +244,31 @@
     l_ref[...] = jnp.zeros_like(l_ref)
     acc_ref[...] = jnp.zeros_like(acc_ref)
 
-    def span(step, _):
-        sp = step // 2
-
+    def span(sp, _):
         @pl.when(valid_ref[first + sp] != 0)
         def _():
-            at = pl.ds(pl.multiple_of((step % 2) * 2 * SEL, 2 * SEL), 2 * SEL)
-            limit = None if limit_ref is None else jnp.where(sp == 0, limit_ref[at, :], SPAN)
+            limit = None if limit_ref is None else jnp.where(sp == 0, limit_ref[...], SPAN)
             attend_block(
-                at, rows_ref.at[i], jk_ref[r * 2 + sp], jv_ref[r * 2 + sp], limit,
-                m_ref, l_ref, acc_ref,
+                rows_ref[i], jk_ref[r * 2 + sp], jv_ref[r * 2 + sp], limit, m_ref, l_ref, acc_ref
             )
 
         return 0
 
-    lax.fori_loop(0, 4, span, 0)
+    lax.fori_loop(0, 2, span, 0)
     l = l_ref[...]
     some = l > 0.0
     mixed = acc_ref[...] / jnp.where(some, l, 1.0)
-    lse = jnp.where(some, m_ref[...] * SCALE2 + jnp.log2(jnp.where(some, l, 1.0)), low)
-    lane = lax.broadcasted_iota(jnp.int32, (SEL, HD), 1)
-    stat = jnp.zeros((SEL, HD), jnp.float32)
+    rest = jnp.where(some, m_ref[...] * SCALE2 + jnp.log2(jnp.where(some, l, 1.0)), low)
+    rows = []
+    for k in range(3):
+        part = rest.astype(jnp.bfloat16).astype(jnp.float32)
+        rows += [part[:, g * SEL : (g + 1) * SEL] for g in range(HG)]
+        rest = rest - part
     for g in range(HG):
-        o_ref[i, :SEL, g * HD : (g + 1) * HD] = mixed[g * SEL : (g + 1) * SEL].astype(jnp.bfloat16)
-        rest = lse[g * SEL : (g + 1) * SEL]
-        for k in range(3):
-            part = rest.astype(jnp.bfloat16).astype(jnp.float32)
-            stat = jnp.where(lane == k * HG + g, part, stat)
-            rest = rest - part
-    o_ref[i, SEL:, :HD] = stat.T[:16].astype(jnp.bfloat16)
+        at = slice(g * SEL, (g + 1) * SEL)
+        o_ref[i, :SEL, g * HD : (g + 1) * HD] = mixed[:, at].T.astype(jnp.bfloat16)
+    stat = jnp.concatenate(rows + [jnp.zeros((HG, SEL), jnp.float32)], axis=0)
+    o_ref[i, SEL:, :HD] = stat.astype(jnp.bfloat16)
     o_ref[i, SEL:, HD:] = jnp.zeros((16, QW - HD), jnp.bfloat16)
 
 
@@ -317,9 +314,7 @@
 
     def request(r, _):
         if shift == 0:
-            sel = selr_ref[r, 0:1, :].astype(jnp.float32)
-            column = jnp.broadcast_to(sel, (SEL, SEL)).T[:, :1].astype(jnp.int32)
-            limit_ref[...] = jnp.concatenate([column] * HG, axis=0)
+            limit_ref[...] = jnp.concatenate([selr_ref[r, 0:1, :]] * HG, axis=1)
         attend_source(
             rows_ref, r, jk_ref, jv_ref, r, valid_ref, shift * 4 + r * 2, o_ref, state, limit_ref
         )
@@ -351,11 +346,11 @@
         in_specs=[smem] + [vmem] * len(args),
         out_specs=vmem,
         scratch_shapes=[pltpu.VMEM((SLOTS, HG * SEL, HD), jnp.bfloat16)]
-        + ([pltpu.VMEM((HG * SEL, 1), jnp.int32)] if shift == 0 else [])
+        + ([pltpu.VMEM((1, HG * SEL), jnp.int32)] if shift == 0 else [])
         + [
-            pltpu.VMEM((HG * SEL, 1), jnp.float32),
-            pltpu.VMEM((HG * SEL, 1), jnp.float32),
-            pltpu.VMEM((HG * SEL, HD), jnp.float32),
+            pltpu.VMEM((1, HG * SEL), jnp.float32),
+            pltpu.VMEM((1, HG * SEL), jnp.float32),
+            pltpu.VMEM((HD, HG * SEL), jnp.float32),
         ],
         compiler_params=pltpu.CompilerParams(vmem_limit_bytes=16 << 20),
         cost_estimate=work(4),
@@ -457,18 +452,18 @@
     h = [hidden, ring_x(hidden)]
     z = [pz(hidden)]
     k1 = py(key_cache)
-    theirs = py(after(mine, h[1]))
+    project = functools.partial(partial_project, place)
+    acc = project((H_AT, H_AT + 1), (hidden, h[1]), weights)
     for _ in range(2):
         h.append(ring_x(h[-1]))
-    for _ in range(2):
-        z.append(ring_x(z[-1]))
+    z.append(ring_x(after(z[0], acc)))
+    z.append(ring_x(z[1]))
     z.append(pz(h[3]))
-    v1 = py(after(value_cache, h[2]))
+    theirs = py(after(mine, h[2]))
+    v1 = py(after(value_cache, k1))
     cosine, sine, rot, sel_rows, valid = prepare(
         after(place, h[3]), span_count, span_key, cache_offset, sel_index, theirs
     )
-    project = functools.partial(partial_project, place)
-    acc = project((H_AT, H_AT + 1), (hidden, h[1]), weights)
     acc = project((H_AT + 2, Z_AT), (h[2], z[0]), weights, acc)
     acc = project((H_AT + 3, Z_AT + 1), (h[3], z[1]), weights, acc)
     acc, kept = project((Z_AT + 2, Z_AT + 3), (z[2],), weights, acc, ahead=1)

time: 103 us -> 101 us (0.981)
  the two profiles are of different devices: /device:TPU:14 before, /device:TPU:168 now
where the time goes in v4:
time: 101 us; the launch traced here: 99.8 us
  waiting for transfers between devices  59.9 us (59%)
  Pallas kernels  21.4 us (21%)
  starting transfers between devices  17.1 us (17%)
  local copies, waits for them, and re-layouts  1.22 us (1%)
    ppermute x6, waiting for transfers between devices, ring_z(): return lax.ppermute(v, ('zh', 'c'), pairs)  41.4 us
    ppermute x5, waiting for transfers between devices, ring_x(): return lax.ppermute(v, ('c', 'x'), opposite_ways(4))  12.4 us
    pallas_call x4, Pallas kernels, partial_project(): pl.pallas_call(functools.partial(partial_kernel, which, ahead, acc is not...  11.9 us
    ppermute x4, starting transfers between devices, py(): return lax.ppermute(v, 'yh', [(0, 1), (1, 0)])  8.21 us
    ppermute x4, waiting for transfers between devices, py(): return lax.ppermute(v, 'yh', [(0, 1), (1, 0)])  5.09 us
    ppermute x6, starting transfers between devices, ring_z(): return lax.ppermute(v, ('zh', 'c'), pairs)  3.99 us
    pallas_call x4, Pallas kernels, attend(): pl.pallas_call(functools.partial(attend_kernel, shift), out_shape=packed_...  3.51 us
    ppermute x5, starting transfers between devices, ring_x(): return lax.ppermute(v, ('c', 'x'), opposite_ways(4))  2.88 us
  transfers between devices with their start and end apart: 17, of which 14 were waited for; matrix products, arithmetic and copies ran while one was open for 0% of the time, Pallas kernels for 19%

profile of v4, /device:TPU:168, one launch (start us, length us, event | category | flops | bytes accessed | tf_op | source)
XLA Modules:
  0.0 99.8 jit_solution(5455520692541768234)
XLA Ops:
  0.0 1.5 %collective-permute-start = (bf16[256,896]{1,0:T(8,128)(2,1)}, bf16[256,896]{1,0:T(8,128)(2,1)S(1)}, u32[]{:S(2)}, u32[]{:S(2)}) collective-permute-start(bf16[256,896]{1,0:T(8,128)(2,1)} %refs_0_.1), channel_id=1, source_target_pairs={{0,1},{1,2},{2,3},{3,0},{8,11},{9,8},{10,9},{11,10},{4,5},{5,6},{6... | collective-permute-start | bytes 1376264 | tf_op jit(solution)/shard_map/ppermute | solution.py:51
  1.5 1.0 %collective-permute-start.5 = (bf16[256,896]{1,0:T(8,128)(2,1)}, bf16[256,896]{1,0:T(8,128)(2,1)S(1)}, u32[]{:S(2)}, u32[]{:S(2)}) collective-permute-start(bf16[256,896]{1,0:T(8,128)(2,1)} %refs_0_.1), channel_id=1, source_target_pairs={{0,4},{4,0},{1,5},{5,1},{2,6},{6,2},{3,7},{7,3},{8,12},{12,8},{9,1... | collective-permute-start | bytes 1376264 | tf_op jit(solution)/shard_map/ppermute | solution.py:60
  2.5 2.3 %collective-permute-start.8 = (bf16[2048,128]{1,0:T(8,128)(2,1)}, bf16[2048,128]{1,0:T(8,128)(2,1)S(1)}, u32[]{:S(2)}, u32[]{:S(2)}) collective-permute-start(bf16[2048,128]{1,0:T(8,128)(2,1)} %k0.1), channel_id=1, source_target_pairs={{0,32},{32,0},{1,33},{33,1},{2,34},{34,2},{3,35},{35,3},{4,36},{36... | collective-permute-start | bytes 1572872 | tf_op jit(solution)/shard_map/ppermute | solution.py:64
  4.8 0.1 stack.51.place
  4.9 5.0 %collective-permute-done.refs_1_ = bf16[256,896]{1,0:T(8,128)(2,1)S(1)} collective-permute-done((bf16[256,896]{1,0:T(8,128)(2,1)}, bf16[256,896]{1,0:T(8,128)(2,1)S(1)}, u32[]{:S(2)}, u32[]{:S(2)}) %collective-permute-start) | collective-permute-done | bytes 458784 | tf_op jit(solution)/shard_map/ppermute | solution.py:51
  9.9 0.3 collective-permute-start.1
  10.2 1.0 %copy-done.3 = bf16[256,896]{1,0:T(8,128)(2,1)S(1)} copy-done((bf16[256,896]{1,0:T(8,128)(2,1)S(1)}, bf16[256,896]{1,0:T(8,128)(2,1)}, u32[]{:S(2)}) %copy-start.3) | copy-done | bytes 458776
  11.2 3.3 %project.4.refs_5_ = f32[256,768]{1,0:T(8,128)S(1)} custom-call(s32[12]{0:T(128)S(1)} %stack.51.place, bf16[256,896]{1,0:T(8,128)(2,1)S(1)} %copy-done.3, bf16[256,896]{1,0:T(8,128)(2,1)S(1)} %collective-permute-done.refs_1_, bf16[7168,512]{1,0:T(8,128)(2,1)} %refs_1_.1, bf16[7168,128]{1,0:T(8,128)(2,1)} %refs_2_.7, bf16[7168,128]{1,0:T(8,128)(2,1)} %refs_3_.7), custom_call_target="tpu_custom_call" | custom-call | flops 6000000000 | bytes 1 | tf_op jit(solution)/shard_map/project/pallas_call | solution.py:180
  14.5 0.5 collective-permute-done.5.refs_1_
  14.9 1.1 %collective-permute-start.6 = (bf16[256,896]{1,0:T(8,128)(2,1)S(1)}, bf16[256,896]{1,0:T(8,128)(2,1)S(1)}, u32[]{:S(2)}, u32[]{:S(2)}) collective-permute-start(bf16[256,896]{1,0:T(8,128)(2,1)S(1)} %collective-permute-done.5.refs_1_), channel_id=1, source_target_pairs={{0,1},{1,2},{2,3},{3,0},{8,11},{9,8},{10,9},{11,10},{4,5},{5,6},{6... | collective-permute-start | bytes 1376264 | tf_op jit(solution)/shard_map/ppermute | solution.py:51
  16.1 0.1 pad.1.clone
  16.1 0.1 pad_add_fusion
  16.2 2.4 %collective-permute-done.8.k1 = bf16[2048,128]{1,0:T(8,128)(2,1)S(1)} collective-permute-done((bf16[2048,128]{1,0:T(8,128)(2,1)}, bf16[2048,128]{1,0:T(8,128)(2,1)S(1)}, u32[]{:S(2)}, u32[]{:S(2)}) %collective-permute-start.8) | collective-permute-done | bytes 524320 | tf_op jit(solution)/shard_map/ppermute | solution.py:64
  18.6 2.3 %collective-permute-start.9 = (bf16[2048,128]{1,0:T(8,128)(2,1)S(1)}, bf16[2048,128]{1,0:T(8,128)(2,1)S(1)}, u32[]{:S(2)}, u32[]{:S(2)}) collective-permute-start(bf16[2048,128]{1,0:T(8,128)(2,1)S(1)} %copy-done.2), channel_id=1, source_target_pairs={{0,32},{32,0},{1,33},{33,1},{2,34},{34,2},{3,35},{35,3},{4,36},{36... | collective-permute-start | bytes 1572872 | tf_op jit(solution)/shard_map/ppermute | solution.py:64
  20.9 1.2 %collective-permute-start.3 = (s32[4,128]{1,0:T(4,128)S(1)}, s32[4,128]{1,0:T(4,128)S(1)}, u32[]{:S(2)}, u32[]{:S(2)}) collective-permute-start(s32[4,128]{1,0:T(4,128)S(1)} %pad_add_fusion), channel_id=1, source_target_pairs={{0,32},{32,0},{1,33},{33,1},{2,34},{34,2},{3,35},{35,3},{4,36},{36... | collective-permute-start | bytes 6152 | tf_op jit(solution)/shard_map/ppermute | solution.py:64
  22.1 2.5 %collective-permute-done.6.refs_1_ = bf16[256,896]{1,0:T(8,128)(2,1)S(1)} collective-permute-done((bf16[256,896]{1,0:T(8,128)(2,1)S(1)}, bf16[256,896]{1,0:T(8,128)(2,1)S(1)}, u32[]{:S(2)}, u32[]{:S(2)}) %collective-permute-start.6) | collective-permute-done | bytes 458784 | tf_op jit(solution)/shard_map/ppermute | solution.py:51
  24.6 3.1 %project.5.refs_5_ = f32[256,768]{1,0:T(8,128)S(1)} custom-call(s32[12]{0:T(128)S(1)} %stack.51.place, bf16[256,896]{1,0:T(8,128)(2,1)S(1)} %collective-permute-done.1.refs_0_, bf16[256,896]{1,0:T(8,128)(2,1)S(1)} %collective-permute-done.5.refs_1_, bf16[7168,512]{1,0:T(8,128)(2,1)} %refs_1_.1, bf16[7168,128]{1,0:T(8,128)(2,1)} %refs_2_.7, ...), custom_call_target="tpu_custom_call" | custom-call | flops 6000000000 | bytes 1 | tf_op jit(solution)/shard_map/project/pallas_call | solution.py:180
  27.7 4.1 %collective-permute-done.2.refs_0_ = bf16[256,896]{1,0:T(8,128)(2,1)S(1)} collective-permute-done((bf16[256,896]{1,0:T(8,128)(2,1)S(1)}, bf16[256,896]{1,0:T(8,128)(2,1)S(1)}, u32[]{:S(2)}, u32[]{:S(2)}) %collective-permute-start.2) | collective-permute-done | bytes 458784 | tf_op jit(solution)/shard_map/ppermute | solution.py:51
  31.8 1.0 %collective-permute-start.4 = (bf16[256,896]{1,0:T(8,128)(2,1)S(1)}, bf16[256,896]{1,0:T(8,128)(2,1)S(1)}, u32[]{:S(2)}, u32[]{:S(2)}) collective-permute-start(bf16[256,896]{1,0:T(8,128)(2,1)S(1)} %collective-permute-done.2.refs_0_), channel_id=1, source_target_pairs={{0,4},{4,0},{1,5},{5,1},{2,6},{6,2},{3,7},{7,3},{8,12},{12,8},{9,1... | collective-permute-start | bytes 1376264 | tf_op jit(solution)/shard_map/ppermute | solution.py:60
  32.8 3.1 %project.6.refs_4_ = f32[256,768]{1,0:T(8,128)S(1)} custom-call(s32[12]{0:T(128)S(1)} %stack.51.place, bf16[256,896]{1,0:T(8,128)(2,1)S(1)} %collective-permute-done.2.refs_0_, bf16[256,896]{1,0:T(8,128)(2,1)S(1)} %collective-permute-done.6.refs_1_, bf16[7168,512]{1,0:T(8,128)(2,1)} %refs_1_.1, bf16[7168,128]{1,0:T(8,128)(2,1)} %refs_2_.7, ...), custom_call_target="tpu_custom_call" | custom-call | flops 6000000000 | bytes 1 | tf_op jit(solution)/shard_map/project/pallas_call | solution.py:180
  35.9 0.0 copy-start.7
  36.0 0.8 collective-permute-done.7.refs_0_
  36.7 2.5 %project.7 = (f32[256,768]{1,0:T(8,128)S(1)}, bf16[1,896,768]{2,1,0:T(8,128)(2,1)S(1)}) custom-call(s32[12]{0:T(128)S(1)} %stack.51.place, bf16[256,896]{1,0:T(8,128)(2,1)S(1)} %collective-permute-done.7.refs_0_, bf16[7168,512]{1,0:T(8,128)(2,1)} %refs_1_.1, bf16[7168,128]{1,0:T(8,128)(2,1)} %refs_2_.7, bf16[7168,128]{1,0:T(8,128)(2,1)} %refs_3_.7, ...), custom_call_target="tpu_custom_call" | custom-call | flops 6000000000 | bytes 1 | tf_op jit(solution)/shard_map/project/pallas_call | solution.py:180
  39.3 1.6 %prepare.1 = (f32[256,128]{1,0:T(8,128)S(1)}, f32[256,128]{1,0:T(8,128)S(1)}, f32[2,4,128]{2,1,0:T(4,128)S(1)}, s32[2,2,128]{2,1,0:T(2,128)S(1)}, s32[16]{0:T(128)S(1)}) custom-call(s32[12]{0:T(128)S(1)} %stack.51.place, s32[8]{0:T(128)S(1)} %copy-done.5, s32[8,8]{1,0:T(8,128)S(1)} %copy-done.4, s32[2]{0:T(128)S(1)} %copy-done.6, s32[2,128]{1,0:T(2,128)S(1)} %copy-done, ...), custom_call_target="tpu_custom_call" | custom-call | flops 2000000000 | bytes 1 | tf_op jit(solution)/shard_map/prepare/pallas_call | solution.py:118
  40.9 0.5 collective-permute-done.4.piece_ref
  41.4 0.7 project_last.1
  42.1 2.4 %collective-permute-start.10 = (bf16[512,128]{1,0:T(8,128)(2,1)S(1)}, bf16[512,128]{1,0:T(8,128)(2,1)S(1)}, u32[]{:S(2)}, u32[]{:S(2)}) collective-permute-start(bf16[512,128]{1,0:T(8,128)(2,1)S(1)} %get-tuple-element.32.n0), channel_id=1, source_target_pairs={{0,32},{32,0},{1,33},{33,1},{2,34},{34,2},{3,35},{35,3},{4,36},{36... | collective-permute-start | bytes 393224 | tf_op jit(solution)/shard_map/ppermute | solution.py:64
  44.5 1.5 %collective-permute-start.11 = (bf16[256,512]{1,0:T(8,128)(2,1)S(1)}, bf16[256,512]{1,0:T(8,128)(2,1)S(1)}, u32[]{:S(2)}, u32[]{:S(2)}) collective-permute-start(bf16[256,512]{1,0:T(8,128)(2,1)S(1)} %get-tuple-element.31.q_ref), channel_id=1, source_target_pairs={{0,64},{8,200},{64,128},{72,8},{128,192},{136,72},{192,0},{200,136... | collective-permute-start | bytes 786440 | tf_op jit(solution)/shard_map/ppermute | solution.py:56
  45.9 2.7 %collective-permute-done.10.n1 = bf16[512,128]{1,0:T(8,128)(2,1)S(1)} collective-permute-done((bf16[512,128]{1,0:T(8,128)(2,1)S(1)}, bf16[512,128]{1,0:T(8,128)(2,1)S(1)}, u32[]{:S(2)}, u32[]{:S(2)}) %collective-permute-start.10) | collective-permute-done | bytes 131104 | tf_op jit(solution)/shard_map/ppermute | solution.py:64
  48.6 1.3 %join.1 = (bf16[4,1024,128]{2,1,0:T(8,128)(2,1)S(1)}, bf16[4,1024,128]{2,1,0:T(8,128)(2,1)S(1)}) custom-call(bf16[2048,128]{1,0:T(8,128)(2,1)S(1)} %copy-done.1, bf16[2048,128]{1,0:T(8,128)(2,1)S(1)} %copy-done.2, bf16[2048,128]{1,0:T(8,128)(2,1)S(1)} %collective-permute-done.8.k1, bf16[2048,128]{1,0:T(8,128)(2,1)S(1)} %collective-permute-done.9.v1, ...), custom_call_target="tpu_custom_call" | custom-call | flops 3000000000 | bytes 1 | tf_op jit(solution)/shard_map/join/pallas_call | solution.py:331
  49.9 5.8 %collective-permute-done.11.q_ref = bf16[256,512]{1,0:T(8,128)(2,1)S(1)} collective-permute-done((bf16[256,512]{1,0:T(8,128)(2,1)S(1)}, bf16[256,512]{1,0:T(8,128)(2,1)S(1)}, u32[]{:S(2)}, u32[]{:S(2)}) %collective-permute-start.11) | collective-permute-done | bytes 262176 | tf_op jit(solution)/shard_map/ppermute | solution.py:56
  55.8 0.3 collective-permute-start.12
  56.0 0.9 attend.7
  56.9 1.3 %collective-permute-start.14 = (bf16[2,144,512]{2,1,0:T(8,128)(2,1)S(1)}, bf16[2,144,512]{2,1,0:T(8,128)(2,1)S(1)}, u32[]{:S(2)}, u32[]{:S(2)}) collective-permute-start(bf16[2,144,512]{2,1,0:T(8,128)(2,1)S(1)} %attend.7), channel_id=1, source_target_pairs={{0,64},{8,200},{64,128},{72,8},{128,192},{136,72},{192,0},{200,136... | collective-permute-start | bytes 884744 | tf_op jit(solution)/shard_map/ppermute | solution.py:56
  58.2 9.1 %collective-permute-done.12.q_ref = bf16[256,512]{1,0:T(8,128)(2,1)S(1)} collective-permute-done((bf16[256,512]{1,0:T(8,128)(2,1)S(1)}, bf16[256,512]{1,0:T(8,128)(2,1)S(1)}, u32[]{:S(2)}, u32[]{:S(2)}) %collective-permute-start.12) | collective-permute-done | bytes 262176 | tf_op jit(solution)/shard_map/ppermute | solution.py:56
  67.3 0.8 collective-permute-start.13
  68.1 0.9 attend.6.a_ref
  69.0 2.6 %collective-permute-done.14.b_ref = bf16[2,144,512]{2,1,0:T(8,128)(2,1)S(1)} collective-permute-done((bf16[2,144,512]{2,1,0:T(8,128)(2,1)S(1)}, bf16[2,144,512]{2,1,0:T(8,128)(2,1)S(1)}, u32[]{:S(2)}, u32[]{:S(2)}) %collective-permute-start.14) | collective-permute-done | bytes 294944 | tf_op jit(solution)/shard_map/ppermute | solution.py:56
  71.6 0.6 merge_between.2
  72.2 0.1 collective-permute-start.15
  72.3 7.5 %collective-permute-done.13.q_ref = bf16[256,512]{1,0:T(8,128)(2,1)S(1)} collective-permute-done((bf16[256,512]{1,0:T(8,128)(2,1)S(1)}, bf16[256,512]{1,0:T(8,128)(2,1)S(1)}, u32[]{:S(2)}, u32[]{:S(2)}) %collective-permute-start.13) | collective-permute-done | bytes 262176 | tf_op jit(solution)/shard_map/ppermute | solution.py:56
  79.8 0.9 attend.5.a_ref
  80.7 5.3 %collective-permute-done.15.b_ref = bf16[2,144,512]{2,1,0:T(8,128)(2,1)S(1)} collective-permute-done((bf16[2,144,512]{2,1,0:T(8,128)(2,1)S(1)}, bf16[2,144,512]{2,1,0:T(8,128)(2,1)S(1)}, u32[]{:S(2)}, u32[]{:S(2)}) %collective-permute-start.15) | collective-permute-done | bytes 294944 | tf_op jit(solution)/shard_map/ppermute | solution.py:56
  86.0 0.6 merge_between.3
  86.6 0.1 collective-permute-start.16
  86.7 0.9 attend.4.a_ref
  87.6 11.0 %collective-permute-done.16.b_ref = bf16[2,144,512]{2,1,0:T(8,128)(2,1)S(1)} collective-permute-done((bf16[2,144,512]{2,1,0:T(8,128)(2,1)S(1)}, bf16[2,144,512]{2,1,0:T(8,128)(2,1)S(1)}, u32[]{:S(2)}, u32[]{:S(2)}) %collective-permute-start.16) | collective-permute-done | bytes 294944 | tf_op jit(solution)/shard_map/ppermute | solution.py:56
  98.6 1.3 %merge.1 = bf16[256,512]{1,0:T(8,128)(2,1)} custom-call(bf16[2,144,512]{2,1,0:T(8,128)(2,1)S(1)} %attend.4.a_ref, bf16[2,144,512]{2,1,0:T(8,128)(2,1)S(1)} %collective-permute-done.16.b_ref), custom_call_target="tpu_custom_call" | custom-call | flops 1 | bytes 1 | tf_op jit(solution)/shard_map/merge/pallas_call | solution.py:422
  (19 shorter events, 0.1 us)
Async XLA Ops:
  0.0 9.9 %collective-permute-start = (bf16[256,896]{1,0:T(8,128)(2,1)}, bf16[256,896]{1,0:T(8,128)(2,1)S(1)}, u32[]{:S(2)}, u32[]{:S(2)}) collective-permute-start(bf16[256,896]{1,0:T(8,128)(2,1)} %refs_0_.1), channel_id=1, source_target_pairs={{0,1},{1,2},{2,3},{3,0},{8,11},{9,8},{10,9},{11,10},{4,5},{5,6},{6... | collective-permute-start | bytes 1376264 | tf_op jit(solution)/shard_map/ppermute | solution.py:51
  1.5 13.5 %collective-permute-start.5 = (bf16[256,896]{1,0:T(8,128)(2,1)}, bf16[256,896]{1,0:T(8,128)(2,1)S(1)}, u32[]{:S(2)}, u32[]{:S(2)}) collective-permute-start(bf16[256,896]{1,0:T(8,128)(2,1)} %refs_0_.1), channel_id=1, source_target_pairs={{0,4},{4,0},{1,5},{5,1},{2,6},{6,2},{3,7},{7,3},{8,12},{12,8},{9,1... | collective-permute-start | bytes 1376264 | tf_op jit(solution)/shard_map/ppermute | solution.py:60
  2.5 16.1 %collective-permute-start.8 = (bf16[2048,128]{1,0:T(8,128)(2,1)}, bf16[2048,128]{1,0:T(8,128)(2,1)S(1)}, u32[]{:S(2)}, u32[]{:S(2)}) collective-permute-start(bf16[2048,128]{1,0:T(8,128)(2,1)} %k0.1), channel_id=1, source_target_pairs={{0,32},{32,0},{1,33},{33,1},{2,34},{34,2},{3,35},{35,3},{4,36},{36... | collective-permute-start | bytes 1572872 | tf_op jit(solution)/shard_map/ppermute | solution.py:64
  4.8 11.3 %copy-start.6 = (s32[2]{0:T(128)S(1)}, s32[2]{0:T(128)}, u32[]{:S(2)}) copy-start(s32[2]{0:T(128)} %offset.1) | copy-start | bytes 28
  4.9 11.2 %copy-start = (s32[2,128]{1,0:T(2,128)S(1)}, s32[2,128]{1,0:T(2,128)}, u32[]{:S(2)}) copy-start(s32[2,128]{1,0:T(2,128)} %sel_ref.1) | copy-start | bytes 3076
  4.9 13.7 %copy-start.2 = (bf16[2048,128]{1,0:T(8,128)(2,1)S(1)}, bf16[2048,128]{1,0:T(8,128)(2,1)}, u32[]{:S(2)}) copy-start(bf16[2048,128]{1,0:T(8,128)(2,1)} %v0.1) | copy-start | bytes 1572868
  9.9 11.0 %collective-permute-start.1 = (bf16[256,896]{1,0:T(8,128)(2,1)S(1)}, bf16[256,896]{1,0:T(8,128)(2,1)S(1)}, u32[]{:S(2)}, u32[]{:S(2)}) collective-permute-start(bf16[256,896]{1,0:T(8,128)(2,1)S(1)} %collective-permute-done.refs_1_), channel_id=1, source_target_pairs={{0,1},{1,2},{2,3},{3,0},{8,11},{9,8},{10,9},{11,10},{4,5},{5,6},{6... | collective-permute-start | bytes 1376264 | tf_op jit(solution)/shard_map/ppermute | solution.py:51
  10.2 1.0 %copy-start.3 = (bf16[256,896]{1,0:T(8,128)(2,1)S(1)}, bf16[256,896]{1,0:T(8,128)(2,1)}, u32[]{:S(2)}) copy-start(bf16[256,896]{1,0:T(8,128)(2,1)} %refs_0_.1) | copy-start | bytes 1376260
  14.9 9.7 %collective-permute-start.6 = (bf16[256,896]{1,0:T(8,128)(2,1)S(1)}, bf16[256,896]{1,0:T(8,128)(2,1)S(1)}, u32[]{:S(2)}, u32[]{:S(2)}) collective-permute-start(bf16[256,896]{1,0:T(8,128)(2,1)S(1)} %collective-permute-done.5.refs_1_), channel_id=1, source_target_pairs={{0,1},{1,2},{2,3},{3,0},{8,11},{9,8},{10,9},{11,10},{4,5},{5,6},{6... | collective-permute-start | bytes 1376264 | tf_op jit(solution)/shard_map/ppermute | solution.py:51
  18.6 20.6 %collective-permute-start.9 = (bf16[2048,128]{1,0:T(8,128)(2,1)S(1)}, bf16[2048,128]{1,0:T(8,128)(2,1)S(1)}, u32[]{:S(2)}, u32[]{:S(2)}) collective-permute-start(bf16[2048,128]{1,0:T(8,128)(2,1)S(1)} %copy-done.2), channel_id=1, source_target_pairs={{0,32},{32,0},{1,33},{33,1},{2,34},{34,2},{3,35},{35,3},{4,36},{36... | collective-permute-start | bytes 1572872 | tf_op jit(solution)/shard_map/ppermute | solution.py:64
  20.9 18.3 %collective-permute-start.3 = (s32[4,128]{1,0:T(4,128)S(1)}, s32[4,128]{1,0:T(4,128)S(1)}, u32[]{:S(2)}, u32[]{:S(2)}) collective-permute-start(s32[4,128]{1,0:T(4,128)S(1)} %pad_add_fusion), channel_id=1, source_target_pairs={{0,32},{32,0},{1,33},{33,1},{2,34},{34,2},{3,35},{35,3},{4,36},{36... | collective-permute-start | bytes 6152 | tf_op jit(solution)/shard_map/ppermute | solution.py:64
  22.1 9.7 %collective-permute-start.2 = (bf16[256,896]{1,0:T(8,128)(2,1)S(1)}, bf16[256,896]{1,0:T(8,128)(2,1)S(1)}, u32[]{:S(2)}, u32[]{:S(2)}) collective-permute-start(bf16[256,896]{1,0:T(8,128)(2,1)S(1)} %collective-permute-done.1.refs_0_), channel_id=1, source_target_pairs={{0,1},{1,2},{2,3},{3,0},{8,11},{9,8},{10,9},{11,10},{4,5},{5,6},{6... | collective-permute-start | bytes 1376264 | tf_op jit(solution)/shard_map/ppermute | solution.py:51
  24.6 12.1 %collective-permute-start.7 = (bf16[256,896]{1,0:T(8,128)(2,1)S(1)}, bf16[256,896]{1,0:T(8,128)(2,1)S(1)}, u32[]{:S(2)}, u32[]{:S(2)}) collective-permute-start(bf16[256,896]{1,0:T(8,128)(2,1)S(1)} %collective-permute-done.6.refs_1_), channel_id=1, source_target_pairs={{0,1},{1,2},{2,3},{3,0},{8,11},{9,8},{10,9},{11,10},{4,5},{5,6},{6... | collective-permute-start | bytes 1376264 | tf_op jit(solution)/shard_map/ppermute | solution.py:51
  31.8 9.6 %collective-permute-start.4 = (bf16[256,896]{1,0:T(8,128)(2,1)S(1)}, bf16[256,896]{1,0:T(8,128)(2,1)S(1)}, u32[]{:S(2)}, u32[]{:S(2)}) collective-permute-start(bf16[256,896]{1,0:T(8,128)(2,1)S(1)} %collective-permute-done.2.refs_0_), channel_id=1, source_target_pairs={{0,4},{4,0},{1,5},{5,1},{2,6},{6,2},{3,7},{7,3},{8,12},{12,8},{9,1... | collective-permute-start | bytes 1376264 | tf_op jit(solution)/shard_map/ppermute | solution.py:60
  35.9 3.3 %copy-start.4 = (s32[8,8]{1,0:T(8,128)S(1)}, s32[8,8]{1,0:T(8,128)}, u32[]{:S(2)}) copy-start(s32[8,8]{1,0:T(8,128)} %key.1) | copy-start | bytes 772
  35.9 3.3 %copy-start.5 = (s32[8]{0:T(128)S(1)}, s32[8]{0:T(128)}, u32[]{:S(2)}) copy-start(s32[8]{0:T(128)} %count.1) | copy-start | bytes 100
  35.9 3.3 %copy-start.7 = (f32[2,128]{1,0:T(2,128)S(1)}, f32[2,128]{1,0:T(2,128)}, u32[]{:S(2)}) copy-start(f32[2,128]{1,0:T(2,128)} %constant.66.clone.freq_ref) | copy-start | bytes 3076
  40.9 7.8 %copy-start.1 = (bf16[2048,128]{1,0:T(8,128)(2,1)S(1)}, bf16[2048,128]{1,0:T(8,128)(2,1)}, u32[]{:S(2)}) copy-start(bf16[2048,128]{1,0:T(8,128)(2,1)} %k0.1) | copy-start | bytes 1572868
  42.1 6.6 %collective-permute-start.10 = (bf16[512,128]{1,0:T(8,128)(2,1)S(1)}, bf16[512,128]{1,0:T(8,128)(2,1)S(1)}, u32[]{:S(2)}, u32[]{:S(2)}) collective-permute-start(bf16[512,128]{1,0:T(8,128)(2,1)S(1)} %get-tuple-element.32.n0), channel_id=1, source_target_pairs={{0,32},{32,0},{1,33},{33,1},{2,34},{34,2},{3,35},{35,3},{4,36},{36... | collective-permute-start | bytes 393224 | tf_op jit(solution)/shard_map/ppermute | solution.py:64
  44.5 11.3 %collective-permute-start.11 = (bf16[256,512]{1,0:T(8,128)(2,1)S(1)}, bf16[256,512]{1,0:T(8,128)(2,1)S(1)}, u32[]{:S(2)}, u32[]{:S(2)}) collective-permute-start(bf16[256,512]{1,0:T(8,128)(2,1)S(1)} %get-tuple-element.31.q_ref), channel_id=1, source_target_pairs={{0,64},{8,200},{64,128},{72,8},{128,192},{136,72},{192,0},{200,136... | collective-permute-start | bytes 786440 | tf_op jit(solution)/shard_map/ppermute | solution.py:56
  55.8 11.5 %collective-permute-start.12 = (bf16[256,512]{1,0:T(8,128)(2,1)S(1)}, bf16[256,512]{1,0:T(8,128)(2,1)S(1)}, u32[]{:S(2)}, u32[]{:S(2)}) collective-permute-start(bf16[256,512]{1,0:T(8,128)(2,1)S(1)} %collective-permute-done.11.q_ref), channel_id=1, source_target_pairs={{0,64},{8,200},{64,128},{72,8},{128,192},{136,72},{192,0},{200,136... | collective-permute-start | bytes 786440 | tf_op jit(solution)/shard_map/ppermute | solution.py:56
  56.9 14.7 %collective-permute-start.14 = (bf16[2,144,512]{2,1,0:T(8,128)(2,1)S(1)}, bf16[2,144,512]{2,1,0:T(8,128)(2,1)S(1)}, u32[]{:S(2)}, u32[]{:S(2)}) collective-permute-start(bf16[2,144,512]{2,1,0:T(8,128)(2,1)S(1)} %attend.7), channel_id=1, source_target_pairs={{0,64},{8,200},{64,128},{72,8},{128,192},{136,72},{192,0},{200,136... | collective-permute-start | bytes 884744 | tf_op jit(solution)/shard_map/ppermute | solution.py:56
  67.3 12.5 %collective-permute-start.13 = (bf16[256,512]{1,0:T(8,128)(2,1)S(1)}, bf16[256,512]{1,0:T(8,128)(2,1)S(1)}, u32[]{:S(2)}, u32[]{:S(2)}) collective-permute-start(bf16[256,512]{1,0:T(8,128)(2,1)S(1)} %collective-permute-done.12.q_ref), channel_id=1, source_target_pairs={{0,64},{8,200},{64,128},{72,8},{128,192},{136,72},{192,0},{200,136... | collective-permute-start | bytes 786440 | tf_op jit(solution)/shard_map/ppermute | solution.py:56
  72.2 13.9 %collective-permute-start.15 = (bf16[2,144,512]{2,1,0:T(8,128)(2,1)S(1)}, bf16[2,144,512]{2,1,0:T(8,128)(2,1)S(1)}, u32[]{:S(2)}, u32[]{:S(2)}) collective-permute-start(bf16[2,144,512]{2,1,0:T(8,128)(2,1)S(1)} %merge_between.2), channel_id=1, source_target_pairs={{0,64},{8,200},{64,128},{72,8},{128,192},{136,72},{192,0},{200,136... | collective-permute-start | bytes 884744 | tf_op jit(solution)/shard_map/ppermute | solution.py:56
  86.6 12.0 %collective-permute-start.16 = (bf16[2,144,512]{2,1,0:T(8,128)(2,1)S(1)}, bf16[2,144,512]{2,1,0:T(8,128)(2,1)S(1)}, u32[]{:S(2)}, u32[]{:S(2)}) collective-permute-start(bf16[2,144,512]{2,1,0:T(8,128)(2,1)S(1)} %merge_between.3), channel_id=1, source_target_pairs={{0,64},{8,200},{64,128},{72,8},{128,192},{136,72},{192,0},{200,136... | collective-permute-start | bytes 884744 | tf_op jit(solution)/shard_map/ppermute | solution.py:56

commit v5 on v4

--- a/solution.py
+++ b/solution.py
@@ -56,6 +56,15 @@
     return lax.ppermute(v, ("zh", "c"), pairs)
 
 
+def back_z(v):
+    pairs = [(2 * i + c, 2 * ((i - 1 + 2 * c) % 4) + c) for i in range(4) for c in range(2)]
+    return lax.ppermute(v, ("zh", "c"), pairs)
+
+
+def far_z(v):
+    return lax.ppermute(v, "zh", [(i, (i + 2) % 4) for i in range(4)])
+
+
 def pz(v):
     return lax.ppermute(v, "zl", [(0, 1), (1, 0)])
 
@@ -67,10 +76,7 @@
 H_AT, Z_AT, ZH_AT, YH_AT, WAY_AT, REQ_AT = 0, 4, 8, 9, 10, 11
 
 
-def prepare_kernel(
-    place, count, key, offset, sel_ref, theirs_ref, freq_ref,
-    cos_ref, sin_ref, rot_ref, selr_ref, valid_ref,
-):
+def prepare_kernel(place, count, key, sel_ref, freq_ref, cos_ref, sin_ref, rank_ref, valid_ref):
     freq = freq_ref[0:1, :]
     sign = freq_ref[1:2, :]
     zh, yh, way = place[ZH_AT], place[YH_AT], place[WAY_AT]
@@ -88,48 +94,36 @@
 
         spans = (zh * 2 + yh, zh * 2 + 1 - yh)
         ranks = [rank(j) for j in spans]
+        for sp in range(2):
+            rank_ref[r * 2 + sp] = ranks[sp]
         for shift in range(4):
             j = lax.rem(zh + shift * way + 4, 4) * 2 + yh
             mine = rank(j)
             for sp in range(2):
                 good = (j < used) & (spans[sp] < used) & (ranks[sp] <= mine)
                 valid_ref[shift * 4 + r * 2 + sp] = jnp.where(good, 1, 0)
-        sel = sel_ref[r : r + 1, :]
-        position = (sel + ranks[0] * SPAN).astype(jnp.float32)
+        position = (sel_ref[r : r + 1, :] + ranks[0] * SPAN).astype(jnp.float32)
         angle = jnp.broadcast_to(position, (SEL, HD)).T * freq
         cos_ref[r * SEL : (r + 1) * SEL, :] = jnp.cos(angle)
         sin_ref[r * SEL : (r + 1) * SEL, :] = jnp.sin(angle) * sign
-        other = ranks[1] * SPAN - theirs_ref[SLOTS + r : SLOTS + r + 1, :]
-        own = jnp.zeros((1, HD), jnp.int32) + (ranks[0] * SPAN - offset[r])
-        for sp, delta in enumerate((own, other)):
-            angle = delta.astype(jnp.float32) * freq
-            rot_ref[r, sp : sp + 1, :] = jnp.cos(angle)
-            rot_ref[r, sp + 2 : sp + 3, :] = jnp.sin(angle) * sign
-        selr_ref[r, 0:1, :] = sel
-        selr_ref[r, 1:2, :] = theirs_ref[r : r + 1, :]
 
 
 def prepare(*args):
-    half = np.arange(HD // 2) * 2.0 / HD
-    freq = np.tile(rope_base**-half, 2)
-    sign = np.repeat([-1.0, 1.0], HD // 2)
-    table = jnp.asarray(np.stack([freq, sign]), jnp.float32)
     shape = jax.ShapeDtypeStruct
     return pl.pallas_call(
         prepare_kernel,
         out_shape=(
             shape((ROWS, HD), jnp.float32),
             shape((ROWS, HD), jnp.float32),
-            shape((SLOTS, 4, HD), jnp.float32),
-            shape((SLOTS, 2, SEL), jnp.int32),
+            shape((4,), jnp.int32),
             shape((16,), jnp.int32),
         ),
-        in_specs=[smem] * 4 + [vmem] * 3,
-        out_specs=(vmem,) * 4 + (smem,),
+        in_specs=[smem] * 3 + [vmem] * 2,
+        out_specs=(vmem, vmem, smem, smem),
         compiler_params=pltpu.CompilerParams(vmem_limit_bytes=8 << 20),
         cost_estimate=work(2),
         name="prepare",
-    )(*args, table)
+    )(*args)
 
 
 def turned(v, cosine, sine):
@@ -277,34 +271,32 @@
         rows_ref[i, g * SEL : (g + 1) * SEL, :] = q[:, g * HD : (g + 1) * HD]
 
 
-def join_kernel(k0, v0, k1, v1, n0, n1, selr_ref, rot_ref, jk_ref, jv_ref):
-    def request(r, _):
-        base = pl.ds(pl.multiple_of(r * SPAN, SPAN), SPAN)
-        fresh_k = pl.ds(pl.multiple_of(r * SEL, SEL), SEL)
-        fresh_v = pl.ds(pl.multiple_of(ROWS + r * SEL, SEL), SEL)
-        for sp, (kr, vr, nr) in enumerate(((k0, v0, n0), (k1, v1, n1))):
-            cached = turned(
-                kr[base, :].astype(jnp.float32),
-                rot_ref[r, sp : sp + 1, :],
-                rot_ref[r, sp + 2 : sp + 3, :],
-            )
+def join_kernel(rank_ref, k0, v0, k1, v1, n0, n1, mine, theirs, freq_ref, jk_ref, jv_ref):
+    freq = freq_ref[0:1, :]
+    sign = freq_ref[1:2, :]
+    for r in range(SLOTS):
+        rows = slice(r * SPAN, (r + 1) * SPAN)
+        for sp, (kr, vr, nr, here) in enumerate(((k0, v0, n0, mine), (k1, v1, n1, theirs))):
+            offset = here[SLOTS + r : SLOTS + r + 1, :]
+            angle = (rank_ref[r * 2 + sp] * SPAN - offset).astype(jnp.float32) * freq
+            raw = kr[rows, :].astype(jnp.float32)
+            cached = turned(raw, jnp.cos(angle), jnp.sin(angle) * sign)
             at = lax.broadcasted_iota(jnp.int32, (SPAN, SEL), 0)
-            pick = (at == selr_ref[r, sp : sp + 1, :]).astype(jnp.float32).astype(jnp.bfloat16)
+            pick = (at == here[r : r + 1, :]).astype(jnp.float32).astype(jnp.bfloat16)
             ones = jnp.ones((SEL, HD), jnp.bfloat16)
             hit = jnp.dot(pick, ones, preferred_element_type=jnp.float32) > 0.5
-            put_k = jnp.dot(pick, nr[fresh_k, :], preferred_element_type=jnp.float32)
-            put_v = jnp.dot(pick, nr[fresh_v, :], preferred_element_type=jnp.float32)
-            vals = vr[base, :].astype(jnp.float32)
+            fresh_k = nr[r * SEL : (r + 1) * SEL, :]
+            fresh_v = nr[ROWS + r * SEL : ROWS + (r + 1) * SEL, :]
+            put_k = jnp.dot(pick, fresh_k, preferred_element_type=jnp.float32)
+            put_v = jnp.dot(pick, fresh_v, preferred_element_type=jnp.float32)
+            vals = vr[rows, :].astype(jnp.float32)
             jk_ref[r * 2 + sp] = jnp.where(hit, put_k, cached).astype(jnp.bfloat16)
             jv_ref[r * 2 + sp] = jnp.where(hit, put_v, vals).astype(jnp.bfloat16)
-        return 0
-
-    lax.fori_loop(0, SLOTS, request, 0)
 
 
 def attend_kernel(shift, valid_ref, q_ref, jk_ref, jv_ref, *refs):
     if shift == 0:
-        selr_ref, o_ref, rows_ref, limit_ref = refs[:4]
+        sel_ref, o_ref, rows_ref, limit_ref = refs[:4]
         state = refs[4:]
     else:
         o_ref, rows_ref = refs[:2]
@@ -314,7 +306,7 @@
 
     def request(r, _):
         if shift == 0:
-            limit_ref[...] = jnp.concatenate([selr_ref[r, 0:1, :]] * HG, axis=1)
+            limit_ref[...] = jnp.concatenate([sel_ref[pl.ds(r, 1), :]] * HG, axis=1)
         attend_source(
             rows_ref, r, jk_ref, jv_ref, r, valid_ref, shift * 4 + r * 2, o_ref, state, limit_ref
         )
@@ -331,7 +323,7 @@
     return pl.pallas_call(
         join_kernel,
         out_shape=(joined_shape, joined_shape),
-        in_specs=[vmem] * 8,
+        in_specs=[smem] + [vmem] * 9,
         out_specs=(vmem, vmem),
         compiler_params=pltpu.CompilerParams(vmem_limit_bytes=16 << 20),
         cost_estimate=work(3),
@@ -353,12 +345,12 @@
             pltpu.VMEM((HD, HG * SEL), jnp.float32),
         ],
         compiler_params=pltpu.CompilerParams(vmem_limit_bytes=16 << 20),
-        cost_estimate=work(4),
+        cost_estimate=work(1),
         name="attend",
     )(valid, *args)
 
 
-def merge_parts(parts, put, stat_put=None):
+def merge_parts(parts, put):
     lse = []
     for p in parts:
         stat = p[SEL:, :HD].astype(jnp.float32)
@@ -374,55 +366,23 @@
         for w, p in zip(weight, parts):
             mixed += w[:, g : g + 1] * p[:SEL, at].astype(jnp.float32)
         put(at, mixed.astype(jnp.bfloat16))
-    if stat_put is not None:
-        rest = top + jnp.log2(total)
-        rows = []
-        for _ in range(3):
-            part = rest.astype(jnp.bfloat16).astype(jnp.float32)
-            rows.append(part)
-            rest = rest - part
-        stat_put(jnp.concatenate(rows + [jnp.zeros_like(top)], axis=0).astype(jnp.bfloat16))
-
-
-def between_kernel(a_ref, b_ref, o_ref):
-    for r in range(SLOTS):
-
-        def put(at, value, r=r):
-            o_ref[r, :SEL, at] = value
-
-        def stat_put(value, r=r):
-            o_ref[r, SEL:, :HD] = value
-            o_ref[r, SEL:, HD:] = jnp.zeros((16, QW - HD), jnp.bfloat16)
-
-        merge_parts((a_ref.at[r], b_ref.at[r]), put, stat_put)
-
-
-def between(*parts):
-    return pl.pallas_call(
-        between_kernel,
-        out_shape=packed_shape,
-        in_specs=[vmem] * 2,
-        out_specs=vmem,
-        compiler_params=pltpu.CompilerParams(vmem_limit_bytes=8 << 20),
-        cost_estimate=work(1),
-        name="merge_between",
-    )(*parts)
-
-
-def merge_kernel(a_ref, b_ref, o_ref):
+
+
+def merge_kernel(*refs):
+    o_ref = refs[-1]
     for r in range(SLOTS):
 
         def put(at, value, r=r):
             o_ref[r * SEL : (r + 1) * SEL, at] = value
 
-        merge_parts((a_ref.at[r], b_ref.at[r]), put)
+        merge_parts([p.at[r] for p in refs[:-1]], put)
 
 
 def merge(*parts):
     return pl.pallas_call(
         merge_kernel,
         out_shape=jax.ShapeDtypeStruct((ROWS, QW), jnp.bfloat16),
-        in_specs=[vmem] * 2,
+        in_specs=[vmem] * len(parts),
         out_specs=vmem,
         compiler_params=pltpu.CompilerParams(vmem_limit_bytes=8 << 20),
         cost_estimate=tiny,
@@ -449,35 +409,36 @@
     mine = jnp.concatenate(
         [sel_index, jnp.broadcast_to(cache_offset[:, None], (SLOTS, SEL))], axis=0
     )
+    half = np.arange(HD // 2) * 2.0 / HD
+    freq = jnp.asarray(
+        np.stack([np.tile(rope_base**-half, 2), np.repeat([-1.0, 1.0], HD // 2)]), jnp.float32
+    )
+    cosine, sine, ranks, valid = prepare(place, span_count, span_key, sel_index, freq)
     h = [hidden, ring_x(hidden)]
     z = [pz(hidden)]
     k1 = py(key_cache)
     project = functools.partial(partial_project, place)
     acc = project((H_AT, H_AT + 1), (hidden, h[1]), weights)
-    for _ in range(2):
-        h.append(ring_x(h[-1]))
+    h.append(ring_x(after(h[1], cosine)))
+    h.append(ring_x(h[2]))
     z.append(ring_x(after(z[0], acc)))
     z.append(ring_x(z[1]))
     z.append(pz(h[3]))
-    theirs = py(after(mine, h[2]))
-    v1 = py(after(value_cache, k1))
-    cosine, sine, rot, sel_rows, valid = prepare(
-        after(place, h[3]), span_count, span_key, cache_offset, sel_index, theirs
-    )
+    theirs = py(after(mine, h[3]))
+    v1 = py(after(value_cache, k1, h[2]))
     acc = project((H_AT + 2, Z_AT), (h[2], z[0]), weights, acc)
     acc = project((H_AT + 3, Z_AT + 1), (h[3], z[1]), weights, acc)
     acc, kept = project((Z_AT + 2, Z_AT + 3), (z[2],), weights, acc, ahead=1)
-    acc = after(acc, k1, v1)
+    acc = after(acc, k1, v1, theirs)
     query, fresh = last_project(z[3], kept, acc, cosine, sine)
-    ring = [query]
-    for _ in range(3):
-        ring.append(ring_z(ring[-1]))
-    jk, jv = join(key_cache, value_cache, k1, v1, fresh, py(fresh), sel_rows, rot)
-    own = attend(0, valid, query, jk, jv, sel_rows)
-    out = attend(1, valid, ring[1], jk, jv)
-    for i in (2, 3):
-        out = between(attend(i, valid, ring[i], jk, jv), ring_z(out))
-    return merge(own, ring_z(out))
+    near, behind = ring_z(query), back_z(query)
+    far = ring_z(near)
+    jk, jv = join(ranks, key_cache, value_cache, k1, v1, fresh, py(fresh), mine, theirs, freq)
+    out_near = back_z(attend(1, valid, near, jk, jv))
+    out_behind = ring_z(attend(3, valid, behind, jk, jv))
+    out_far = far_z(attend(2, valid, far, jk, jv))
+    own = attend(0, valid, query, jk, jv, mine)
+    return merge(own, out_near, out_behind, out_far)
 
 
 def solution(mesh):

time: 101 us -> 100 us (0.990)
  the two profiles are of different devices: /device:TPU:168 before, /device:TPU:32 now
where the time goes in v5:
time: 100 us; the launch traced here: 99.9 us
  waiting for transfers between devices  37.3 us (37%)
  starting transfers between devices  34 us (34%)
  Pallas kernels  25.4 us (25%)
  local copies, waits for them, and re-layouts  2.88 us (3%)
    ppermute x3, waiting for transfers between devices, ring_z(): return lax.ppermute(v, ('zh', 'c'), pairs)  22 us
    pallas_call x4, Pallas kernels, partial_project(): pl.pallas_call(functools.partial(partial_kernel, which, ahead, acc is not...  11.9 us
    ppermute x3, starting transfers between devices, ring_z(): return lax.ppermute(v, ('zh', 'c'), pairs)  11.7 us
    ppermute x4, starting transfers between devices, py(): return lax.ppermute(v, 'yh', [(0, 1), (1, 0)])  10.5 us
    ppermute x5, waiting for transfers between devices, ring_x(): return lax.ppermute(v, ('c', 'x'), opposite_ways(4))  9.11 us
    pallas_call x4, Pallas kernels, attend(): pl.pallas_call(functools.partial(attend_kernel, shift), out_shape=packed_...  7.9 us
    ppermute x1, starting transfers between devices, far_z(): return lax.ppermute(v, 'zh', [(i, (i + 2) % 4) for i in range(4)])  6.82 us
    ppermute x2, waiting for transfers between devices, pz(): return lax.ppermute(v, 'zl', [(0, 1), (1, 0)])  3.83 us
  transfers between devices with their start and end apart: 17, of which 9 were waited for; matrix products, arithmetic and copies ran while one was open for 0% of the time, Pallas kernels for 23%

profile of v5, /device:TPU:32, one launch (start us, length us, event | category | flops | bytes accessed | tf_op | source)
XLA Modules:
  0.0 99.9 jit_solution(1487884178313816652)
XLA Ops:
  0.0 1.5 %collective-permute-start = (bf16[256,896]{1,0:T(8,128)(2,1)}, bf16[256,896]{1,0:T(8,128)(2,1)S(1)}, u32[]{:S(2)}, u32[]{:S(2)}) collective-permute-start(bf16[256,896]{1,0:T(8,128)(2,1)} %refs_0_.1), channel_id=1, source_target_pairs={{0,1},{1,2},{2,3},{3,0},{8,11},{9,8},{10,9},{11,10},{4,5},{5,6},{6... | collective-permute-start | bytes 1376264 | tf_op jit(solution)/shard_map/ppermute | solution.py:51
  1.5 0.4 collective-permute-start.4
  1.8 2.9 %collective-permute-start.7 = (bf16[2048,128]{1,0:T(8,128)(2,1)}, bf16[2048,128]{1,0:T(8,128)(2,1)S(1)}, u32[]{:S(2)}, u32[]{:S(2)}) collective-permute-start(bf16[2048,128]{1,0:T(8,128)(2,1)} %k0.1), channel_id=1, source_target_pairs={{0,32},{32,0},{1,33},{33,1},{2,34},{34,2},{3,35},{35,3},{4,36},{36... | collective-permute-start | bytes 1572872 | tf_op jit(solution)/shard_map/ppermute | solution.py:73
  4.8 0.1 stack.51.place
  4.9 0.0 copy-start
  4.9 0.7 copy-done
  5.6 0.7 copy-done.5
  6.3 0.7 copy-done.6
  6.9 0.7 copy-done.7
  7.6 1.5 %prepare.1 = (f32[256,128]{1,0:T(8,128)S(1)}, f32[256,128]{1,0:T(8,128)S(1)}, s32[4]{0:T(128)S(1)}, s32[16]{0:T(128)S(1)}) custom-call(s32[12]{0:T(128)S(1)} %stack.51.place, s32[8]{0:T(128)S(1)} %copy-done.6, s32[8,8]{1,0:T(8,128)S(1)} %copy-done.5, s32[2,128]{1,0:T(2,128)S(1)} %copy-done, f32[2,128]{1,0:T(2,128)S(1)} %copy-done.7), custom_call_target="tpu_custom_call" | custom-call | flops 2000000000 | bytes 1 | tf_op jit(solution)/shard_map/prepare/pallas_call | solution.py:113
  9.1 0.8 collective-permute-done.refs_1_
  9.9 0.8 collective-permute-start.1
  10.8 3.3 %project.4.refs_5_ = f32[256,768]{1,0:T(8,128)S(1)} custom-call(s32[12]{0:T(128)S(1)} %stack.51.place, bf16[256,896]{1,0:T(8,128)(2,1)S(1)} %copy-done.4, bf16[256,896]{1,0:T(8,128)(2,1)S(1)} %collective-permute-done.refs_1_, bf16[7168,512]{1,0:T(8,128)(2,1)} %refs_1_.1, bf16[7168,128]{1,0:T(8,128)(2,1)} %refs_2_.7, bf16[7168,128]{1,0:T(8,128)(2,1)} %refs_3_.7), custom_call_target="tpu_custom_call" | custom-call | flops 6000000000 | bytes 1 | tf_op jit(solution)/shard_map/project/pallas_call | solution.py:174
  14.0 0.9 collective-permute-done.4.refs_1_
  14.9 0.4 collective-permute-start.5
  15.3 0.1 pad.1.clone
  15.4 0.1 pad_add_fusion.mine.refs_0_
  15.5 2.4 %collective-permute-done.7.k1 = bf16[2048,128]{1,0:T(8,128)(2,1)S(1)} collective-permute-done((bf16[2048,128]{1,0:T(8,128)(2,1)}, bf16[2048,128]{1,0:T(8,128)(2,1)S(1)}, u32[]{:S(2)}, u32[]{:S(2)}) %collective-permute-start.7) | collective-permute-done | bytes 524320 | tf_op jit(solution)/shard_map/ppermute | solution.py:73
  17.9 1.7 %collective-permute-done.1.refs_0_ = bf16[256,896]{1,0:T(8,128)(2,1)S(1)} collective-permute-done((bf16[256,896]{1,0:T(8,128)(2,1)S(1)}, bf16[256,896]{1,0:T(8,128)(2,1)S(1)}, u32[]{:S(2)}, u32[]{:S(2)}) %collective-permute-start.1) | collective-permute-done | bytes 458784 | tf_op jit(solution)/shard_map/ppermute | solution.py:51
  19.6 3.2 %collective-permute-start.8 = (bf16[2048,128]{1,0:T(8,128)(2,1)S(1)}, bf16[2048,128]{1,0:T(8,128)(2,1)S(1)}, u32[]{:S(2)}, u32[]{:S(2)}) collective-permute-start(bf16[2048,128]{1,0:T(8,128)(2,1)S(1)} %copy-done.3), channel_id=1, source_target_pairs={{0,32},{32,0},{1,33},{33,1},{2,34},{34,2},{3,35},{35,3},{4,36},{36... | collective-permute-start | bytes 1572872 | tf_op jit(solution)/shard_map/ppermute | solution.py:73
  22.8 0.0 collective-permute-start.2
  22.8 1.8 %collective-permute-done.5.refs_1_ = bf16[256,896]{1,0:T(8,128)(2,1)S(1)} collective-permute-done((bf16[256,896]{1,0:T(8,128)(2,1)S(1)}, bf16[256,896]{1,0:T(8,128)(2,1)S(1)}, u32[]{:S(2)}, u32[]{:S(2)}) %collective-permute-start.5) | collective-permute-done | bytes 458784 | tf_op jit(solution)/shard_map/ppermute | solution.py:51
  24.6 0.0 collective-permute-start.6
  24.6 3.1 %project.5.refs_5_ = f32[256,768]{1,0:T(8,128)S(1)} custom-call(s32[12]{0:T(128)S(1)} %stack.51.place, bf16[256,896]{1,0:T(8,128)(2,1)S(1)} %collective-permute-done.1.refs_0_, bf16[256,896]{1,0:T(8,128)(2,1)S(1)} %collective-permute-done.4.refs_1_, bf16[7168,512]{1,0:T(8,128)(2,1)} %refs_1_.1, bf16[7168,128]{1,0:T(8,128)(2,1)} %refs_2_.7, ...), custom_call_target="tpu_custom_call" | custom-call | flops 6000000000 | bytes 1 | tf_op jit(solution)/shard_map/project/pallas_call | solution.py:174
  27.7 4.8 %collective-permute-done.2.refs_0_ = bf16[256,896]{1,0:T(8,128)(2,1)S(1)} collective-permute-done((bf16[256,896]{1,0:T(8,128)(2,1)S(1)}, bf16[256,896]{1,0:T(8,128)(2,1)S(1)}, u32[]{:S(2)}, u32[]{:S(2)}) %collective-permute-start.2) | collective-permute-done | bytes 458784 | tf_op jit(solution)/shard_map/ppermute | solution.py:51
  32.5 0.3 collective-permute-start.9
  32.8 1.8 %collective-permute-start.3 = (bf16[256,896]{1,0:T(8,128)(2,1)S(1)}, bf16[256,896]{1,0:T(8,128)(2,1)S(1)}, u32[]{:S(2)}, u32[]{:S(2)}) collective-permute-start(bf16[256,896]{1,0:T(8,128)(2,1)S(1)} %collective-permute-done.2.refs_0_), channel_id=1, source_target_pairs={{0,4},{4,0},{1,5},{5,1},{2,6},{6,2},{3,7},{7,3},{8,12},{12,8},{9,1... | collective-permute-start | bytes 1376264 | tf_op jit(solution)/shard_map/ppermute | solution.py:69
  34.7 3.1 %project.6.refs_4_ = f32[256,768]{1,0:T(8,128)S(1)} custom-call(s32[12]{0:T(128)S(1)} %stack.51.place, bf16[256,896]{1,0:T(8,128)(2,1)S(1)} %collective-permute-done.2.refs_0_, bf16[256,896]{1,0:T(8,128)(2,1)S(1)} %collective-permute-done.5.refs_1_, bf16[7168,512]{1,0:T(8,128)(2,1)} %refs_1_.1, bf16[7168,128]{1,0:T(8,128)(2,1)} %refs_2_.7, ...), custom_call_target="tpu_custom_call" | custom-call | flops 6000000000 | bytes 1 | tf_op jit(solution)/shard_map/project/pallas_call | solution.py:174
  37.8 2.5 %project.7 = (f32[256,768]{1,0:T(8,128)S(1)}, bf16[1,896,768]{2,1,0:T(8,128)(2,1)S(1)}) custom-call(s32[12]{0:T(128)S(1)} %stack.51.place, bf16[256,896]{1,0:T(8,128)(2,1)S(1)} %collective-permute-done.6.refs_0_, bf16[7168,512]{1,0:T(8,128)(2,1)} %refs_1_.1, bf16[7168,128]{1,0:T(8,128)(2,1)} %refs_2_.7, bf16[7168,128]{1,0:T(8,128)(2,1)} %refs_3_.7, ...), custom_call_target="tpu_custom_call" | custom-call | flops 6000000000 | bytes 1 | tf_op jit(solution)/shard_map/project/pallas_call | solution.py:174
  40.2 0.0 copy-start.2
  40.2 0.0 copy-start.8
  40.3 0.0 collective-permute-done.8.v1
  40.3 2.9 %collective-permute-done.3.piece_ref = bf16[256,896]{1,0:T(8,128)(2,1)S(1)} collective-permute-done((bf16[256,896]{1,0:T(8,128)(2,1)S(1)}, bf16[256,896]{1,0:T(8,128)(2,1)S(1)}, u32[]{:S(2)}, u32[]{:S(2)}) %collective-permute-start.3) | collective-permute-done | bytes 458784 | tf_op jit(solution)/shard_map/ppermute | solution.py:69
  43.2 0.7 project_last.1
  43.9 3.3 %collective-permute-start.11 = (bf16[256,512]{1,0:T(8,128)(2,1)S(1)}, bf16[256,512]{1,0:T(8,128)(2,1)S(1)}, u32[]{:S(2)}, u32[]{:S(2)}) collective-permute-start(bf16[256,512]{1,0:T(8,128)(2,1)S(1)} %get-tuple-element.30.q_ref), channel_id=1, source_target_pairs={{0,64},{8,200},{64,128},{72,8},{128,192},{136,72},{192,0},{200,136... | collective-permute-start | bytes 786440 | tf_op jit(solution)/shard_map/ppermute | solution.py:56
  47.2 4.0 %collective-permute-start.10 = (bf16[512,128]{1,0:T(8,128)(2,1)S(1)}, bf16[512,128]{1,0:T(8,128)(2,1)S(1)}, u32[]{:S(2)}, u32[]{:S(2)}) collective-permute-start(bf16[512,128]{1,0:T(8,128)(2,1)S(1)} %get-tuple-element.32.n0), channel_id=1, source_target_pairs={{0,32},{32,0},{1,33},{33,1},{2,34},{34,2},{3,35},{35,3},{4,36},{36... | collective-permute-start | bytes 393224 | tf_op jit(solution)/shard_map/ppermute | solution.py:73
  51.3 0.0 collective-permute-start.13
  51.3 10.5 %collective-permute-done.11.q_ref = bf16[256,512]{1,0:T(8,128)(2,1)S(1)} collective-permute-done((bf16[256,512]{1,0:T(8,128)(2,1)S(1)}, bf16[256,512]{1,0:T(8,128)(2,1)S(1)}, u32[]{:S(2)}, u32[]{:S(2)}) %collective-permute-start.11) | collective-permute-done | bytes 262176 | tf_op jit(solution)/shard_map/ppermute | solution.py:56
  61.8 1.8 %join.1 = (bf16[4,1024,128]{2,1,0:T(8,128)(2,1)S(1)}, bf16[4,1024,128]{2,1,0:T(8,128)(2,1)S(1)}) custom-call(s32[4]{0:T(128)S(1)} %get-tuple-element.31.rank_ref, bf16[2048,128]{1,0:T(8,128)(2,1)S(1)} %copy-done.2, bf16[2048,128]{1,0:T(8,128)(2,1)S(1)} %copy-done.3, bf16[2048,128]{1,0:T(8,128)(2,1)S(1)} %collective-permute-done.7.k1, ...), custom_call_target="tpu_custom_call" | custom-call | flops 3000000000 | bytes 1 | tf_op jit(solution)/shard_map/join/pallas_call | solution.py:323
  63.6 1.9 %attend.6 = bf16[2,144,512]{2,1,0:T(8,128)(2,1)S(1)} custom-call(s32[16]{0:T(128)S(1)} %get-tuple-element.20.valid_ref, bf16[256,512]{1,0:T(8,128)(2,1)S(1)} %collective-permute-done.13.q_ref, bf16[4,1024,128]{2,1,0:T(8,128)(2,1)S(1)} %get-tuple-element.33.jk_ref, bf16[4,1024,128]{2,1,0:T(8,128)(2,1)S(1)} %get-tuple-element.34.jv_ref), custom_call_target="tpu_custom_call" | custom-call | flops 1000000000 | bytes 1 | tf_op jit(solution)/shard_map/attend/pallas_call | solution.py:335
  65.6 8.4 %collective-permute-start.14 = (bf16[2,144,512]{2,1,0:T(8,128)(2,1)S(1)}, bf16[2,144,512]{2,1,0:T(8,128)(2,1)S(1)}, u32[]{:S(2)}, u32[]{:S(2)}) collective-permute-start(bf16[2,144,512]{2,1,0:T(8,128)(2,1)S(1)} %attend.6), channel_id=1, source_target_pairs={{0,64},{8,200},{64,128},{72,8},{128,192},{136,72},{192,0},{200,136... | collective-permute-start | bytes 884744 | tf_op jit(solution)/shard_map/ppermute | solution.py:56
  74.0 0.9 attend.5
  74.8 0.1 collective-permute-start.12
  74.9 0.9 attend.7
  75.8 6.8 %collective-permute-start.16 = (bf16[2,144,512]{2,1,0:T(8,128)(2,1)S(1)}, bf16[2,144,512]{2,1,0:T(8,128)(2,1)S(1)}, u32[]{:S(2)}, u32[]{:S(2)}) collective-permute-start(bf16[2,144,512]{2,1,0:T(8,128)(2,1)S(1)} %attend.7), channel_id=1, source_target_pairs={{0,128},{64,192},{128,0},{192,64},{1,129},{65,193},{129,1},{193,65... | collective-permute-start | bytes 884744 | tf_op jit(solution)/shard_map/ppermute | solution.py:65
  82.7 4.2 %attend.4.refs_0_ = bf16[2,144,512]{2,1,0:T(8,128)(2,1)S(1)} custom-call(s32[16]{0:T(128)S(1)} %get-tuple-element.20.valid_ref, bf16[256,512]{1,0:T(8,128)(2,1)S(1)} %get-tuple-element.30.q_ref, bf16[4,1024,128]{2,1,0:T(8,128)(2,1)S(1)} %get-tuple-element.33.jk_ref, bf16[4,1024,128]{2,1,0:T(8,128)(2,1)S(1)} %get-tuple-element.34.jv_ref, ...), custom_call_target="tpu_custom_call" | custom-call | flops 1000000000 | bytes 1 | tf_op jit(solution)/shard_map/attend/pallas_call | solution.py:335
  86.9 11.4 %collective-permute-done.14.refs_2_ = bf16[2,144,512]{2,1,0:T(8,128)(2,1)S(1)} collective-permute-done((bf16[2,144,512]{2,1,0:T(8,128)(2,1)S(1)}, bf16[2,144,512]{2,1,0:T(8,128)(2,1)S(1)}, u32[]{:S(2)}, u32[]{:S(2)}) %collective-permute-start.14) | collective-permute-done | bytes 294944 | tf_op jit(solution)/shard_map/ppermute | solution.py:56
  98.3 1.6 %merge.1 = bf16[256,512]{1,0:T(8,128)(2,1)} custom-call(bf16[2,144,512]{2,1,0:T(8,128)(2,1)S(1)} %attend.4.refs_0_, bf16[2,144,512]{2,1,0:T(8,128)(2,1)S(1)} %collective-permute-done.12.refs_1_, bf16[2,144,512]{2,1,0:T(8,128)(2,1)S(1)} %collective-permute-done.14.refs_2_, bf16[2,144,512]{2,1,0:T(8,128)(2,1)S(1)} %collective-permute-done.16.refs_3_), custom_call_target="tpu_custom_call" | custom-call | flops 1 | bytes 1 | tf_op jit(solution)/shard_map/merge/pallas_call | solution.py:382
  (21 shorter events, 0.0 us)
Async XLA Ops:
  0.0 9.9 %collective-permute-start = (bf16[256,896]{1,0:T(8,128)(2,1)}, bf16[256,896]{1,0:T(8,128)(2,1)S(1)}, u32[]{:S(2)}, u32[]{:S(2)}) collective-permute-start(bf16[256,896]{1,0:T(8,128)(2,1)} %refs_0_.1), channel_id=1, source_target_pairs={{0,1},{1,2},{2,3},{3,0},{8,11},{9,8},{10,9},{11,10},{4,5},{5,6},{6... | collective-permute-start | bytes 1376264 | tf_op jit(solution)/shard_map/ppermute | solution.py:51
  1.5 13.5 %collective-permute-start.4 = (bf16[256,896]{1,0:T(8,128)(2,1)}, bf16[256,896]{1,0:T(8,128)(2,1)S(1)}, u32[]{:S(2)}, u32[]{:S(2)}) collective-permute-start(bf16[256,896]{1,0:T(8,128)(2,1)} %refs_0_.1), channel_id=1, source_target_pairs={{0,4},{4,0},{1,5},{5,1},{2,6},{6,2},{3,7},{7,3},{8,12},{12,8},{9,1... | collective-permute-start | bytes 1376264 | tf_op jit(solution)/shard_map/ppermute | solution.py:69
  1.8 16.0 %collective-permute-start.7 = (bf16[2048,128]{1,0:T(8,128)(2,1)}, bf16[2048,128]{1,0:T(8,128)(2,1)S(1)}, u32[]{:S(2)}, u32[]{:S(2)}) collective-permute-start(bf16[2048,128]{1,0:T(8,128)(2,1)} %k0.1), channel_id=1, source_target_pairs={{0,32},{32,0},{1,33},{33,1},{2,34},{34,2},{3,35},{35,3},{4,36},{36... | collective-permute-start | bytes 1572872 | tf_op jit(solution)/shard_map/ppermute | solution.py:73
  4.9 0.7 copy-start
  5.6 0.7 copy-start.5
  6.3 0.7 copy-start.6
  6.9 0.7 copy-start.7
  7.6 3.2 %copy-start.4 = (bf16[256,896]{1,0:T(8,128)(2,1)S(1)}, bf16[256,896]{1,0:T(8,128)(2,1)}, u32[]{:S(2)}) copy-start(bf16[256,896]{1,0:T(8,128)(2,1)} %refs_0_.1) | copy-start | bytes 1376260
  9.9 5.4 %copy-start.9 = (s32[2]{0:T(128)S(1)}, s32[2]{0:T(128)}, u32[]{:S(2)}) copy-start(s32[2]{0:T(128)} %param.19) | copy-start | bytes 28
  9.9 5.5 %copy-start.1 = (s32[2,128]{1,0:T(2,128)S(1)}, s32[2,128]{1,0:T(2,128)}, u32[]{:S(2)}) copy-start(s32[2,128]{1,0:T(2,128)} %sel_ref.1) | copy-start | bytes 3076
  9.9 9.7 %copy-start.3 = (bf16[2048,128]{1,0:T(8,128)(2,1)S(1)}, bf16[2048,128]{1,0:T(8,128)(2,1)}, u32[]{:S(2)}) copy-start(bf16[2048,128]{1,0:T(8,128)(2,1)} %v0.1) | copy-start | bytes 1572868
  9.9 9.7 %collective-permute-start.1 = (bf16[256,896]{1,0:T(8,128)(2,1)S(1)}, bf16[256,896]{1,0:T(8,128)(2,1)S(1)}, u32[]{:S(2)}, u32[]{:S(2)}) collective-permute-start(bf16[256,896]{1,0:T(8,128)(2,1)S(1)} %collective-permute-done.refs_1_), channel_id=1, source_target_pairs={{0,1},{1,2},{2,3},{3,0},{8,11},{9,8},{10,9},{11,10},{4,5},{5,6},{6... | collective-permute-start | bytes 1376264 | tf_op jit(solution)/shard_map/ppermute | solution.py:51
  14.9 9.7 %collective-permute-start.5 = (bf16[256,896]{1,0:T(8,128)(2,1)S(1)}, bf16[256,896]{1,0:T(8,128)(2,1)S(1)}, u32[]{:S(2)}, u32[]{:S(2)}) collective-permute-start(bf16[256,896]{1,0:T(8,128)(2,1)S(1)} %collective-permute-done.4.refs_1_), channel_id=1, source_target_pairs={{0,1},{1,2},{2,3},{3,0},{8,11},{9,8},{10,9},{11,10},{4,5},{5,6},{6... | collective-permute-start | bytes 1376264 | tf_op jit(solution)/shard_map/ppermute | solution.py:51
  19.6 20.7 %collective-permute-start.8 = (bf16[2048,128]{1,0:T(8,128)(2,1)S(1)}, bf16[2048,128]{1,0:T(8,128)(2,1)S(1)}, u32[]{:S(2)}, u32[]{:S(2)}) collective-permute-start(bf16[2048,128]{1,0:T(8,128)(2,1)S(1)} %copy-done.3), channel_id=1, source_target_pairs={{0,32},{32,0},{1,33},{33,1},{2,34},{34,2},{3,35},{35,3},{4,36},{36... | collective-permute-start | bytes 1572872 | tf_op jit(solution)/shard_map/ppermute | solution.py:73
  22.8 9.7 %collective-permute-start.2 = (bf16[256,896]{1,0:T(8,128)(2,1)S(1)}, bf16[256,896]{1,0:T(8,128)(2,1)S(1)}, u32[]{:S(2)}, u32[]{:S(2)}) collective-permute-start(bf16[256,896]{1,0:T(8,128)(2,1)S(1)} %collective-permute-done.1.refs_0_), channel_id=1, source_target_pairs={{0,1},{1,2},{2,3},{3,0},{8,11},{9,8},{10,9},{11,10},{4,5},{5,6},{6... | collective-permute-start | bytes 1376264 | tf_op jit(solution)/shard_map/ppermute | solution.py:51
  24.6 13.1 %collective-permute-start.6 = (bf16[256,896]{1,0:T(8,128)(2,1)S(1)}, bf16[256,896]{1,0:T(8,128)(2,1)S(1)}, u32[]{:S(2)}, u32[]{:S(2)}) collective-permute-start(bf16[256,896]{1,0:T(8,128)(2,1)S(1)} %collective-permute-done.5.refs_1_), channel_id=1, source_target_pairs={{0,1},{1,2},{2,3},{3,0},{8,11},{9,8},{10,9},{11,10},{4,5},{5,6},{6... | collective-permute-start | bytes 1376264 | tf_op jit(solution)/shard_map/ppermute | solution.py:51
  32.5 7.8 %collective-permute-start.9 = (s32[4,128]{1,0:T(4,128)S(1)}, s32[4,128]{1,0:T(4,128)S(1)}, u32[]{:S(2)}, u32[]{:S(2)}) collective-permute-start(s32[4,128]{1,0:T(4,128)S(1)} %pad_add_fusion.mine.refs_0_), channel_id=1, source_target_pairs={{0,32},{32,0},{1,33},{33,1},{2,34},{34,2},{3,35},{35,3},{4,36},{36... | collective-permute-start | bytes 6152 | tf_op jit(solution)/shard_map/ppermute | solution.py:73
  32.8 10.4 %collective-permute-start.3 = (bf16[256,896]{1,0:T(8,128)(2,1)S(1)}, bf16[256,896]{1,0:T(8,128)(2,1)S(1)}, u32[]{:S(2)}, u32[]{:S(2)}) collective-permute-start(bf16[256,896]{1,0:T(8,128)(2,1)S(1)} %collective-permute-done.2.refs_0_), channel_id=1, source_target_pairs={{0,4},{4,0},{1,5},{5,1},{2,6},{6,2},{3,7},{7,3},{8,12},{12,8},{9,1... | collective-permute-start | bytes 1376264 | tf_op jit(solution)/shard_map/ppermute | solution.py:69
  40.2 21.6 %copy-start.2 = (bf16[2048,128]{1,0:T(8,128)(2,1)S(1)}, bf16[2048,128]{1,0:T(8,128)(2,1)}, u32[]{:S(2)}) copy-start(bf16[2048,128]{1,0:T(8,128)(2,1)} %k0.1) | copy-start | bytes 1572868
  40.2 21.6 %copy-start.8 = (f32[2,128]{1,0:T(2,128)S(1)}, f32[2,128]{1,0:T(2,128)}, u32[]{:S(2)}) copy-start(f32[2,128]{1,0:T(2,128)} %constant.66.clone.freq_ref) | copy-start | bytes 3076
  43.9 17.9 %collective-permute-start.11 = (bf16[256,512]{1,0:T(8,128)(2,1)S(1)}, bf16[256,512]{1,0:T(8,128)(2,1)S(1)}, u32[]{:S(2)}, u32[]{:S(2)}) collective-permute-start(bf16[256,512]{1,0:T(8,128)(2,1)S(1)} %get-tuple-element.30.q_ref), channel_id=1, source_target_pairs={{0,64},{8,200},{64,128},{72,8},{128,192},{136,72},{192,0},{200,136... | collective-permute-start | bytes 786440 | tf_op jit(solution)/shard_map/ppermute | solution.py:56
  47.2 14.6 %collective-permute-start.10 = (bf16[512,128]{1,0:T(8,128)(2,1)S(1)}, bf16[512,128]{1,0:T(8,128)(2,1)S(1)}, u32[]{:S(2)}, u32[]{:S(2)}) collective-permute-start(bf16[512,128]{1,0:T(8,128)(2,1)S(1)} %get-tuple-element.32.n0), channel_id=1, source_target_pairs={{0,32},{32,0},{1,33},{33,1},{2,34},{34,2},{3,35},{35,3},{4,36},{36... | collective-permute-start | bytes 393224 | tf_op jit(solution)/shard_map/ppermute | solution.py:73
  51.3 12.4 %collective-permute-start.13 = (bf16[256,512]{1,0:T(8,128)(2,1)S(1)}, bf16[256,512]{1,0:T(8,128)(2,1)S(1)}, u32[]{:S(2)}, u32[]{:S(2)}) collective-permute-start(bf16[256,512]{1,0:T(8,128)(2,1)S(1)} %get-tuple-element.30.q_ref), channel_id=1, source_target_pairs={{0,192},{8,72},{64,0},{72,136},{128,64},{136,200},{192,128},{200,8... | collective-permute-start | bytes 786440 | tf_op jit(solution)/shard_map/ppermute | solution.py:61
  61.8 13.2 %collective-permute-start.15 = (bf16[256,512]{1,0:T(8,128)(2,1)S(1)}, bf16[256,512]{1,0:T(8,128)(2,1)S(1)}, u32[]{:S(2)}, u32[]{:S(2)}) collective-permute-start(bf16[256,512]{1,0:T(8,128)(2,1)S(1)} %collective-permute-done.11.q_ref), channel_id=1, source_target_pairs={{0,64},{8,200},{64,128},{72,8},{128,192},{136,72},{192,0},{200,136... | collective-permute-start | bytes 786440 | tf_op jit(solution)/shard_map/ppermute | solution.py:56
  65.6 32.7 %collective-permute-start.14 = (bf16[2,144,512]{2,1,0:T(8,128)(2,1)S(1)}, bf16[2,144,512]{2,1,0:T(8,128)(2,1)S(1)}, u32[]{:S(2)}, u32[]{:S(2)}) collective-permute-start(bf16[2,144,512]{2,1,0:T(8,128)(2,1)S(1)} %attend.6), channel_id=1, source_target_pairs={{0,64},{8,200},{64,128},{72,8},{128,192},{136,72},{192,0},{200,136... | collective-permute-start | bytes 884744 | tf_op jit(solution)/shard_map/ppermute | solution.py:56
  74.8 23.5 %collective-permute-start.12 = (bf16[2,144,512]{2,1,0:T(8,128)(2,1)S(1)}, bf16[2,144,512]{2,1,0:T(8,128)(2,1)S(1)}, u32[]{:S(2)}, u32[]{:S(2)}) collective-permute-start(bf16[2,144,512]{2,1,0:T(8,128)(2,1)S(1)} %attend.5), channel_id=1, source_target_pairs={{0,192},{8,72},{64,0},{72,136},{128,64},{136,200},{192,128},{200,8... | collective-permute-start | bytes 884744 | tf_op jit(solution)/shard_map/ppermute | solution.py:61
  75.8 22.5 %collective-permute-start.16 = (bf16[2,144,512]{2,1,0:T(8,128)(2,1)S(1)}, bf16[2,144,512]{2,1,0:T(8,128)(2,1)S(1)}, u32[]{:S(2)}, u32[]{:S(2)}) collective-permute-start(bf16[2,144,512]{2,1,0:T(8,128)(2,1)S(1)} %attend.7), channel_id=1, source_target_pairs={{0,128},{64,192},{128,0},{192,64},{1,129},{65,193},{129,1},{193,65... | collective-permute-start | bytes 884744 | tf_op jit(solution)/shard_map/ppermute | solution.py:65

commit v6 on v5

--- a/solution.py
+++ b/solution.py
@@ -49,6 +49,11 @@
 
 def ring_x(v):
     return lax.ppermute(v, ("c", "x"), opposite_ways(4))
+
+
+def back_x(v):
+    pairs = [(4 * c + i, 4 * c + (i - 1 + 2 * c) % 4) for c in range(2) for i in range(4)]
+    return lax.ppermute(v, ("c", "x"), pairs)
 
 
 def ring_z(v):
@@ -186,7 +191,7 @@
     )(place, *pieces, *weights, *extra)
 
 
-def last_kernel(piece_ref, weight_ref, acc_ref, cos_ref, sin_ref, q_ref, n_ref):
+def last_kernel(piece_ref, weight_ref, acc_ref, cos_ref, sin_ref, mine_ref, q_ref, n_ref):
     acc = acc_ref[...] + jnp.dot(
         piece_ref[...], weight_ref[0], preferred_element_type=jnp.float32
     )
@@ -195,7 +200,11 @@
         at = slice(g * HD, (g + 1) * HD)
         q_ref[:, at] = turned(acc[:, at], cosine, sine).astype(jnp.bfloat16)
     n_ref[:ROWS, :] = turned(acc[:, QW : QW + HD], cosine, sine).astype(jnp.bfloat16)
-    n_ref[ROWS:, :] = acc[:, QW + HD :].astype(jnp.bfloat16)
+    n_ref[ROWS : 2 * ROWS, :] = acc[:, QW + HD :].astype(jnp.bfloat16)
+    mine = mine_ref[...]
+    high = lax.shift_right_logical(mine, 6)
+    both = jnp.concatenate([high, mine - high * 64, jnp.zeros((8, SEL), jnp.int32)], axis=0)
+    n_ref[2 * ROWS :, :] = both.astype(jnp.float32).astype(jnp.bfloat16)
 
 
 def last_project(*args):
@@ -203,9 +212,9 @@
         last_kernel,
         out_shape=(
             jax.ShapeDtypeStruct((ROWS, QW), jnp.bfloat16),
-            jax.ShapeDtypeStruct((2 * ROWS, HD), jnp.bfloat16),
+            jax.ShapeDtypeStruct((2 * ROWS + 16, HD), jnp.bfloat16),
         ),
-        in_specs=[vmem] * 5,
+        in_specs=[vmem] * 6,
         out_specs=(vmem, vmem),
         compiler_params=pltpu.CompilerParams(vmem_limit_bytes=16 << 20),
         cost_estimate=tiny,
@@ -271,9 +280,12 @@
         rows_ref[i, g * SEL : (g + 1) * SEL, :] = q[:, g * HD : (g + 1) * HD]
 
 
-def join_kernel(rank_ref, k0, v0, k1, v1, n0, n1, mine, theirs, freq_ref, jk_ref, jv_ref):
+def join_kernel(rank_ref, k0, v0, k1, v1, n0, n1, mine_ref, freq_ref, jk_ref, jv_ref):
     freq = freq_ref[0:1, :]
     sign = freq_ref[1:2, :]
+    mine = mine_ref[...]
+    both = n1[2 * ROWS :, :].astype(jnp.float32)
+    theirs = (both[0:4] * 64.0 + both[4:8]).astype(jnp.int32)
     for r in range(SLOTS):
         rows = slice(r * SPAN, (r + 1) * SPAN)
         for sp, (kr, vr, nr, here) in enumerate(((k0, v0, n0, mine), (k1, v1, n1, theirs))):
@@ -323,7 +335,7 @@
     return pl.pallas_call(
         join_kernel,
         out_shape=(joined_shape, joined_shape),
-        in_specs=[smem] + [vmem] * 9,
+        in_specs=[smem] + [vmem] * 8,
         out_specs=(vmem, vmem),
         compiler_params=pltpu.CompilerParams(vmem_limit_bytes=16 << 20),
         cost_estimate=work(3),
@@ -414,26 +426,25 @@
         np.stack([np.tile(rope_base**-half, 2), np.repeat([-1.0, 1.0], HD // 2)]), jnp.float32
     )
     cosine, sine, ranks, valid = prepare(place, span_count, span_key, sel_index, freq)
-    h = [hidden, ring_x(hidden)]
-    z = [pz(hidden)]
+    h1, h3, z0 = ring_x(hidden), back_x(hidden), pz(hidden)
     k1 = py(key_cache)
     project = functools.partial(partial_project, place)
-    acc = project((H_AT, H_AT + 1), (hidden, h[1]), weights)
-    h.append(ring_x(after(h[1], cosine)))
-    h.append(ring_x(h[2]))
-    z.append(ring_x(after(z[0], acc)))
-    z.append(ring_x(z[1]))
-    z.append(pz(h[3]))
-    theirs = py(after(mine, h[3]))
-    v1 = py(after(value_cache, k1, h[2]))
-    acc = project((H_AT + 2, Z_AT), (h[2], z[0]), weights, acc)
-    acc = project((H_AT + 3, Z_AT + 1), (h[3], z[1]), weights, acc)
-    acc, kept = project((Z_AT + 2, Z_AT + 3), (z[2],), weights, acc, ahead=1)
-    acc = after(acc, k1, v1, theirs)
-    query, fresh = last_project(z[3], kept, acc, cosine, sine)
+    acc = project((H_AT,), (hidden,), weights)
+    h2 = ring_x(after(h1, cosine, acc))
+    z1 = ring_x(z0)
+    z3 = pz(h3)
+    v1 = py(after(value_cache, k1))
+    acc = project((H_AT + 1, H_AT + 3), (h1, h3), weights, acc)
+    z2 = ring_x(z1)
+    acc = project((Z_AT, H_AT + 2), (z0, h2), weights, acc)
+    acc, kept = project(
+        (Z_AT + 3, Z_AT + 1, Z_AT + 2), (z3, z1), weights, acc, ahead=1
+    )
+    acc = after(acc, k1, v1)
+    query, fresh = last_project(z2, kept, acc, cosine, sine, mine)
     near, behind = ring_z(query), back_z(query)
     far = ring_z(near)
-    jk, jv = join(ranks, key_cache, value_cache, k1, v1, fresh, py(fresh), mine, theirs, freq)
+    jk, jv = join(ranks, key_cache, value_cache, k1, v1, fresh, py(fresh), mine, freq)
     out_near = back_z(attend(1, valid, near, jk, jv))
     out_behind = ring_z(attend(3, valid, behind, jk, jv))
     out_far = far_z(attend(2, valid, far, jk, jv))

time: 100 us -> 97.3 us (0.973)
  the two profiles are of different devices: /device:TPU:32 before, /device:TPU:36 now
where the time goes in v6:
time: 97.3 us; the launch traced here: 97.7 us
  starting transfers between devices  44.1 us (45%)
  Pallas kernels  30.6 us (31%)
  waiting for transfers between devices  18.5 us (19%)
  local copies, waits for them, and re-layouts  3.53 us (4%)
    ppermute x1, starting transfers between devices, far_z(): return lax.ppermute(v, 'zh', [(i, (i + 2) % 4) for i in range(4)])  19.3 us
    pallas_call x4, Pallas kernels, attend(): pl.pallas_call(functools.partial(attend_kernel, shift), out_shape=packed_...  13.3 us
    pallas_call x4, Pallas kernels, partial_project(): pl.pallas_call(functools.partial(partial_kernel, which, ahead, acc is not...  11.7 us
    ppermute x3, waiting for transfers between devices, ring_z(): return lax.ppermute(v, ('zh', 'c'), pairs)  10.8 us
    ppermute x4, starting transfers between devices, ring_x(): return lax.ppermute(v, ('c', 'x'), opposite_ways(4))  6.48 us
    ppermute x3, starting transfers between devices, ring_z(): return lax.ppermute(v, ('zh', 'c'), pairs)  6.14 us
    ppermute x3, starting transfers between devices, py(): return lax.ppermute(v, 'yh', [(0, 1), (1, 0)])  5.62 us
    ppermute x4, waiting for transfers between devices, ring_x(): return lax.ppermute(v, ('c', 'x'), opposite_ways(4))  5.23 us
  transfers between devices with their start and end apart: 16, of which 3 were waited for; matrix products, arithmetic and copies ran while one was open for 2% of the time, Pallas kernels for 29%

profile of v6, /device:TPU:36, one launch (start us, length us, event | category | flops | bytes accessed | tf_op | source)
XLA Modules:
  0.0 97.7 jit_solution(13477763132802968709)
XLA Ops:
  0.0 0.5 collective-permute-start.3
  0.5 1.5 %collective-permute-start.5 = (bf16[256,896]{1,0:T(8,128)(2,1)}, bf16[256,896]{1,0:T(8,128)(2,1)S(1)}, u32[]{:S(2)}, u32[]{:S(2)}) collective-permute-start(bf16[256,896]{1,0:T(8,128)(2,1)} %refs_0_.1), channel_id=1, source_target_pairs={{0,1},{1,2},{2,3},{3,0},{8,11},{9,8},{10,9},{11,10},{4,5},{5,6},{6... | collective-permute-start | bytes 1376264 | tf_op jit(solution)/shard_map/ppermute | solution.py:51
  2.0 0.1 collective-permute-start
  2.1 3.2 %collective-permute-start.7 = (bf16[2048,128]{1,0:T(8,128)(2,1)}, bf16[2048,128]{1,0:T(8,128)(2,1)S(1)}, u32[]{:S(2)}, u32[]{:S(2)}) collective-permute-start(bf16[2048,128]{1,0:T(8,128)(2,1)} %k0.1), channel_id=1, source_target_pairs={{0,32},{32,0},{1,33},{33,1},{2,34},{34,2},{3,35},{35,3},{4,36},{36... | collective-permute-start | bytes 1572872 | tf_op jit(solution)/shard_map/ppermute | solution.py:78
  5.3 0.7 pad.1.clone
  6.1 0.7 pad_add_fusion.mine_ref.refs_0_
  6.8 0.1 stack.51.place
  6.9 0.0 copy-start
  6.9 0.7 copy-done
  7.6 0.7 copy-done.4
  8.3 0.7 copy-done.5
  8.9 0.7 copy-done.6
  9.6 1.5 %prepare.1 = (f32[256,128]{1,0:T(8,128)S(1)}, f32[256,128]{1,0:T(8,128)S(1)}, s32[4]{0:T(128)S(1)}, s32[16]{0:T(128)S(1)}) custom-call(s32[12]{0:T(128)S(1)} %stack.51.place, s32[8]{0:T(128)S(1)} %copy-done.5, s32[8,8]{1,0:T(8,128)S(1)} %copy-done.4, s32[2,128]{1,0:T(2,128)S(1)} %copy-done, f32[2,128]{1,0:T(2,128)S(1)} %copy-done.6), custom_call_target="tpu_custom_call" | custom-call | flops 2000000000 | bytes 1 | tf_op jit(solution)/shard_map/prepare/pallas_call | solution.py:118
  11.2 2.4 %project.4.refs_5_ = f32[256,768]{1,0:T(8,128)S(1)} custom-call(s32[12]{0:T(128)S(1)} %stack.51.place, bf16[256,896]{1,0:T(8,128)(2,1)S(1)} %copy-done.3, bf16[7168,512]{1,0:T(8,128)(2,1)} %refs_2_.7, bf16[7168,128]{1,0:T(8,128)(2,1)} %refs_3_.7, bf16[7168,128]{1,0:T(8,128)(2,1)} %refs_4_.5), custom_call_target="tpu_custom_call" | custom-call | flops 6000000000 | bytes 1 | tf_op jit(solution)/shard_map/project/pallas_call | solution.py:179
  13.6 0.0 collective-permute-done.5.refs_0_
  13.6 0.0 copy-start.2
  13.6 2.5 %collective-permute-start.6 = (bf16[256,896]{1,0:T(8,128)(2,1)S(1)}, bf16[256,896]{1,0:T(8,128)(2,1)S(1)}, u32[]{:S(2)}, u32[]{:S(2)}) collective-permute-start(bf16[256,896]{1,0:T(8,128)(2,1)S(1)} %collective-permute-done.5.refs_0_), channel_id=1, source_target_pairs={{0,1},{1,2},{2,3},{3,0},{8,11},{9,8},{10,9},{11,10},{4,5},{5,6},{6... | collective-permute-start | bytes 1376264 | tf_op jit(solution)/shard_map/ppermute | solution.py:51
  16.1 0.0 collective-permute-done.refs_0_
  16.1 0.1 collective-permute-start.1
  16.2 0.0 collective-permute-done.3.refs_1_
  16.2 1.9 %collective-permute-start.4 = (bf16[256,896]{1,0:T(8,128)(2,1)S(1)}, bf16[256,896]{1,0:T(8,128)(2,1)S(1)}, u32[]{:S(2)}, u32[]{:S(2)}) collective-permute-start(bf16[256,896]{1,0:T(8,128)(2,1)S(1)} %collective-permute-done.3.refs_1_), channel_id=1, source_target_pairs={{0,4},{4,0},{1,5},{5,1},{2,6},{6,2},{3,7},{7,3},{8,12},{12,8},{9,1... | collective-permute-start | bytes 1376264 | tf_op jit(solution)/shard_map/ppermute | solution.py:74
  18.1 3.1 %project.5.refs_5_ = f32[256,768]{1,0:T(8,128)S(1)} custom-call(s32[12]{0:T(128)S(1)} %stack.51.place, bf16[256,896]{1,0:T(8,128)(2,1)S(1)} %collective-permute-done.5.refs_0_, bf16[256,896]{1,0:T(8,128)(2,1)S(1)} %collective-permute-done.3.refs_1_, bf16[7168,512]{1,0:T(8,128)(2,1)} %refs_2_.7, bf16[7168,128]{1,0:T(8,128)(2,1)} %refs_3_.7, ...), custom_call_target="tpu_custom_call" | custom-call | flops 6000000000 | bytes 1 | tf_op jit(solution)/shard_map/project/pallas_call | solution.py:179
  21.2 0.0 collective-permute-done.7.k1
  21.2 0.6 collective-permute-start.8
  21.9 5.2 %collective-permute-done.1.refs_1_ = bf16[256,896]{1,0:T(8,128)(2,1)S(1)} collective-permute-done((bf16[256,896]{1,0:T(8,128)(2,1)S(1)}, bf16[256,896]{1,0:T(8,128)(2,1)S(1)}, u32[]{:S(2)}, u32[]{:S(2)}) %collective-permute-start.1) | collective-permute-done | bytes 458784 | tf_op jit(solution)/shard_map/ppermute | solution.py:51
  27.1 2.4 %collective-permute-start.2 = (bf16[256,896]{1,0:T(8,128)(2,1)S(1)}, bf16[256,896]{1,0:T(8,128)(2,1)S(1)}, u32[]{:S(2)}, u32[]{:S(2)}) collective-permute-start(bf16[256,896]{1,0:T(8,128)(2,1)S(1)} %collective-permute-done.1.refs_1_), channel_id=1, source_target_pairs={{0,1},{1,2},{2,3},{3,0},{8,11},{9,8},{10,9},{11,10},{4,5},{5,6},{6... | collective-permute-start | bytes 1376264 | tf_op jit(solution)/shard_map/ppermute | solution.py:51
  29.5 3.1 %project.6.refs_5_ = f32[256,768]{1,0:T(8,128)S(1)} custom-call(s32[12]{0:T(128)S(1)} %stack.51.place, bf16[256,896]{1,0:T(8,128)(2,1)S(1)} %collective-permute-done.refs_0_, bf16[256,896]{1,0:T(8,128)(2,1)S(1)} %collective-permute-done.6.refs_1_, bf16[7168,512]{1,0:T(8,128)(2,1)} %refs_2_.7, bf16[7168,128]{1,0:T(8,128)(2,1)} %refs_3_.7, ...), custom_call_target="tpu_custom_call" | custom-call | flops 6000000000 | bytes 1 | tf_op jit(solution)/shard_map/project/pallas_call | solution.py:179
  32.6 0.0 collective-permute-done.4.refs_0_
  32.6 3.1 %project.7 = (f32[256,768]{1,0:T(8,128)S(1)}, bf16[1,896,768]{2,1,0:T(8,128)(2,1)S(1)}) custom-call(s32[12]{0:T(128)S(1)} %stack.51.place, bf16[256,896]{1,0:T(8,128)(2,1)S(1)} %collective-permute-done.4.refs_0_, bf16[256,896]{1,0:T(8,128)(2,1)S(1)} %collective-permute-done.1.refs_1_, bf16[7168,512]{1,0:T(8,128)(2,1)} %refs_2_.7, bf16[7168,128]{1,0:T(8,128)(2,1)} %refs_3_.7, ...), custom_call_target="tpu_custom_call" | custom-call | flops 6000000000 | bytes 1 | tf_op jit(solution)/shard_map/project/pallas_call | solution.py:179
  35.7 0.0 copy-start.1
  35.7 0.0 copy-start.7
  35.7 0.0 collective-permute-done.8.v1
  35.8 0.7 project_last.1
  36.5 3.3 %collective-permute-start.10 = (bf16[256,512]{1,0:T(8,128)(2,1)S(1)}, bf16[256,512]{1,0:T(8,128)(2,1)S(1)}, u32[]{:S(2)}, u32[]{:S(2)}) collective-permute-start(bf16[256,512]{1,0:T(8,128)(2,1)S(1)} %get-tuple-element.26.q_ref), channel_id=1, source_target_pairs={{0,64},{8,200},{64,128},{72,8},{128,192},{136,72},{192,0},{200,136... | collective-permute-start | bytes 786440 | tf_op jit(solution)/shard_map/ppermute | solution.py:61
  39.8 1.8 %collective-permute-start.9 = (bf16[528,128]{1,0:T(8,128)(2,1)S(1)}, bf16[528,128]{1,0:T(8,128)(2,1)S(1)}, u32[]{:S(2)}, u32[]{:S(2)}) collective-permute-start(bf16[528,128]{1,0:T(8,128)(2,1)S(1)} %get-tuple-element.28.n0), channel_id=1, source_target_pairs={{0,32},{32,0},{1,33},{33,1},{2,34},{34,2},{3,35},{35,3},{4,36},{36... | collective-permute-start | bytes 405512 | tf_op jit(solution)/shard_map/ppermute | solution.py:78
  41.6 2.2 %collective-permute-start.12 = (bf16[256,512]{1,0:T(8,128)(2,1)S(1)}, bf16[256,512]{1,0:T(8,128)(2,1)S(1)}, u32[]{:S(2)}, u32[]{:S(2)}) collective-permute-start(bf16[256,512]{1,0:T(8,128)(2,1)S(1)} %get-tuple-element.26.q_ref), channel_id=1, source_target_pairs={{0,192},{8,72},{64,0},{72,136},{128,64},{136,200},{192,128},{200,8... | collective-permute-start | bytes 786440 | tf_op jit(solution)/shard_map/ppermute | solution.py:66
  43.8 10.8 %collective-permute-done.10.q_ref = bf16[256,512]{1,0:T(8,128)(2,1)S(1)} collective-permute-done((bf16[256,512]{1,0:T(8,128)(2,1)S(1)}, bf16[256,512]{1,0:T(8,128)(2,1)S(1)}, u32[]{:S(2)}, u32[]{:S(2)}) %collective-permute-start.10) | collective-permute-done | bytes 262176 | tf_op jit(solution)/shard_map/ppermute | solution.py:61
  54.6 1.3 %collective-permute-start.14 = (bf16[256,512]{1,0:T(8,128)(2,1)S(1)}, bf16[256,512]{1,0:T(8,128)(2,1)S(1)}, u32[]{:S(2)}, u32[]{:S(2)}) collective-permute-start(bf16[256,512]{1,0:T(8,128)(2,1)S(1)} %collective-permute-done.10.q_ref), channel_id=1, source_target_pairs={{0,64},{8,200},{64,128},{72,8},{128,192},{136,72},{192,0},{200,136... | collective-permute-start | bytes 786440 | tf_op jit(solution)/shard_map/ppermute | solution.py:61
  56.0 1.8 %join.1 = (bf16[4,1024,128]{2,1,0:T(8,128)(2,1)S(1)}, bf16[4,1024,128]{2,1,0:T(8,128)(2,1)S(1)}) custom-call(s32[4]{0:T(128)S(1)} %get-tuple-element.27.rank_ref, bf16[2048,128]{1,0:T(8,128)(2,1)S(1)} %copy-done.1, bf16[2048,128]{1,0:T(8,128)(2,1)S(1)} %copy-done.2, bf16[2048,128]{1,0:T(8,128)(2,1)S(1)} %collective-permute-done.7.k1, ...), custom_call_target="tpu_custom_call" | custom-call | flops 3000000000 | bytes 1 | tf_op jit(solution)/shard_map/join/pallas_call | solution.py:335
  57.8 4.0 %attend.6 = bf16[2,144,512]{2,1,0:T(8,128)(2,1)S(1)} custom-call(s32[16]{0:T(128)S(1)} %get-tuple-element.18.valid_ref, bf16[256,512]{1,0:T(8,128)(2,1)S(1)} %collective-permute-done.12.q_ref, bf16[4,1024,128]{2,1,0:T(8,128)(2,1)S(1)} %get-tuple-element.29.jk_ref, bf16[4,1024,128]{2,1,0:T(8,128)(2,1)S(1)} %get-tuple-element.30.jv_ref), custom_call_target="tpu_custom_call" | custom-call | flops 1000000000 | bytes 1 | tf_op jit(solution)/shard_map/attend/pallas_call | solution.py:347
  61.8 1.5 %collective-permute-start.13 = (bf16[2,144,512]{2,1,0:T(8,128)(2,1)S(1)}, bf16[2,144,512]{2,1,0:T(8,128)(2,1)S(1)}, u32[]{:S(2)}, u32[]{:S(2)}) collective-permute-start(bf16[2,144,512]{2,1,0:T(8,128)(2,1)S(1)} %attend.6), channel_id=1, source_target_pairs={{0,64},{8,200},{64,128},{72,8},{128,192},{136,72},{192,0},{200,136... | collective-permute-start | bytes 884744 | tf_op jit(solution)/shard_map/ppermute | solution.py:61
  63.3 1.9 %attend.5 = bf16[2,144,512]{2,1,0:T(8,128)(2,1)S(1)} custom-call(s32[16]{0:T(128)S(1)} %get-tuple-element.18.valid_ref, bf16[256,512]{1,0:T(8,128)(2,1)S(1)} %collective-permute-done.10.q_ref, bf16[4,1024,128]{2,1,0:T(8,128)(2,1)S(1)} %get-tuple-element.29.jk_ref, bf16[4,1024,128]{2,1,0:T(8,128)(2,1)S(1)} %get-tuple-element.30.jv_ref), custom_call_target="tpu_custom_call" | custom-call | flops 1000000000 | bytes 1 | tf_op jit(solution)/shard_map/attend/pallas_call | solution.py:347
  65.2 1.8 %collective-permute-start.11 = (bf16[2,144,512]{2,1,0:T(8,128)(2,1)S(1)}, bf16[2,144,512]{2,1,0:T(8,128)(2,1)S(1)}, u32[]{:S(2)}, u32[]{:S(2)}) collective-permute-start(bf16[2,144,512]{2,1,0:T(8,128)(2,1)S(1)} %attend.5), channel_id=1, source_target_pairs={{0,192},{8,72},{64,0},{72,136},{128,64},{136,200},{192,128},{200,8... | collective-permute-start | bytes 884744 | tf_op jit(solution)/shard_map/ppermute | solution.py:66
  67.0 1.9 %attend.7 = bf16[2,144,512]{2,1,0:T(8,128)(2,1)S(1)} custom-call(s32[16]{0:T(128)S(1)} %get-tuple-element.18.valid_ref, bf16[256,512]{1,0:T(8,128)(2,1)S(1)} %collective-permute-done.14.q_ref, bf16[4,1024,128]{2,1,0:T(8,128)(2,1)S(1)} %get-tuple-element.29.jk_ref, bf16[4,1024,128]{2,1,0:T(8,128)(2,1)S(1)} %get-tuple-element.30.jv_ref), custom_call_target="tpu_custom_call" | custom-call | flops 1000000000 | bytes 1 | tf_op jit(solution)/shard_map/attend/pallas_call | solution.py:347
  68.9 19.3 %collective-permute-start.15 = (bf16[2,144,512]{2,1,0:T(8,128)(2,1)S(1)}, bf16[2,144,512]{2,1,0:T(8,128)(2,1)S(1)}, u32[]{:S(2)}, u32[]{:S(2)}) collective-permute-start(bf16[2,144,512]{2,1,0:T(8,128)(2,1)S(1)} %attend.7), channel_id=1, source_target_pairs={{0,128},{64,192},{128,0},{192,64},{1,129},{65,193},{129,1},{193,65... | collective-permute-start | bytes 884744 | tf_op jit(solution)/shard_map/ppermute | solution.py:70
  88.3 5.4 %attend.4.refs_0_ = bf16[2,144,512]{2,1,0:T(8,128)(2,1)S(1)} custom-call(s32[16]{0:T(128)S(1)} %get-tuple-element.18.valid_ref, bf16[256,512]{1,0:T(8,128)(2,1)S(1)} %get-tuple-element.26.q_ref, bf16[4,1024,128]{2,1,0:T(8,128)(2,1)S(1)} %get-tuple-element.29.jk_ref, bf16[4,1024,128]{2,1,0:T(8,128)(2,1)S(1)} %get-tuple-element.30.jv_ref, ...), custom_call_target="tpu_custom_call" | custom-call | flops 1000000000 | bytes 1 | tf_op jit(solution)/shard_map/attend/pallas_call | solution.py:347
  93.7 2.4 %collective-permute-done.15.refs_3_ = bf16[2,144,512]{2,1,0:T(8,128)(2,1)S(1)} collective-permute-done((bf16[2,144,512]{2,1,0:T(8,128)(2,1)S(1)}, bf16[2,144,512]{2,1,0:T(8,128)(2,1)S(1)}, u32[]{:S(2)}, u32[]{:S(2)}) %collective-permute-start.15) | collective-permute-done | bytes 294944 | tf_op jit(solution)/shard_map/ppermute | solution.py:70
  96.1 1.5 %merge.1 = bf16[256,512]{1,0:T(8,128)(2,1)} custom-call(bf16[2,144,512]{2,1,0:T(8,128)(2,1)S(1)} %attend.4.refs_0_, bf16[2,144,512]{2,1,0:T(8,128)(2,1)S(1)} %collective-permute-done.11.refs_1_, bf16[2,144,512]{2,1,0:T(8,128)(2,1)S(1)} %collective-permute-done.13.refs_2_, bf16[2,144,512]{2,1,0:T(8,128)(2,1)S(1)} %collective-permute-done.15.refs_3_), custom_call_target="tpu_custom_call" | custom-call | flops 1 | bytes 1 | tf_op jit(solution)/shard_map/merge/pallas_call | solution.py:394
  (15 shorter events, 0.0 us)
Async XLA Ops:
  0.0 16.2 %collective-permute-start.3 = (bf16[256,896]{1,0:T(8,128)(2,1)}, bf16[256,896]{1,0:T(8,128)(2,1)S(1)}, u32[]{:S(2)}, u32[]{:S(2)}) collective-permute-start(bf16[256,896]{1,0:T(8,128)(2,1)} %refs_0_.1), channel_id=1, source_target_pairs={{0,3},{1,0},{2,1},{3,2},{8,9},{9,10},{10,11},{11,8},{4,7},{5,4},{6... | collective-permute-start | bytes 1376264 | tf_op jit(solution)/shard_map/ppermute | solution.py:56
  0.5 13.1 %collective-permute-start.5 = (bf16[256,896]{1,0:T(8,128)(2,1)}, bf16[256,896]{1,0:T(8,128)(2,1)S(1)}, u32[]{:S(2)}, u32[]{:S(2)}) collective-permute-start(bf16[256,896]{1,0:T(8,128)(2,1)} %refs_0_.1), channel_id=1, source_target_pairs={{0,1},{1,2},{2,3},{3,0},{8,11},{9,8},{10,9},{11,10},{4,5},{5,6},{6... | collective-permute-start | bytes 1376264 | tf_op jit(solution)/shard_map/ppermute | solution.py:51
  2.0 14.1 %collective-permute-start = (bf16[256,896]{1,0:T(8,128)(2,1)}, bf16[256,896]{1,0:T(8,128)(2,1)S(1)}, u32[]{:S(2)}, u32[]{:S(2)}) collective-permute-start(bf16[256,896]{1,0:T(8,128)(2,1)} %refs_0_.1), channel_id=1, source_target_pairs={{0,4},{4,0},{1,5},{5,1},{2,6},{6,2},{3,7},{7,3},{8,12},{12,8},{9,1... | collective-permute-start | bytes 1376264 | tf_op jit(solution)/shard_map/ppermute | solution.py:74
  2.1 19.1 %collective-permute-start.7 = (bf16[2048,128]{1,0:T(8,128)(2,1)}, bf16[2048,128]{1,0:T(8,128)(2,1)S(1)}, u32[]{:S(2)}, u32[]{:S(2)}) collective-permute-start(bf16[2048,128]{1,0:T(8,128)(2,1)} %k0.1), channel_id=1, source_target_pairs={{0,32},{32,0},{1,33},{33,1},{2,34},{34,2},{3,35},{35,3},{4,36},{36... | collective-permute-start | bytes 1572872 | tf_op jit(solution)/shard_map/ppermute | solution.py:78
  6.9 0.7 copy-start
  7.6 0.7 copy-start.4
  8.3 0.7 copy-start.5
  8.9 0.7 copy-start.6
  9.6 1.5 %copy-start.3 = (bf16[256,896]{1,0:T(8,128)(2,1)S(1)}, bf16[256,896]{1,0:T(8,128)(2,1)}, u32[]{:S(2)}) copy-start(bf16[256,896]{1,0:T(8,128)(2,1)} %refs_0_.1) | copy-start | bytes 1376260
  13.6 7.6 %copy-start.2 = (bf16[2048,128]{1,0:T(8,128)(2,1)S(1)}, bf16[2048,128]{1,0:T(8,128)(2,1)}, u32[]{:S(2)}) copy-start(bf16[2048,128]{1,0:T(8,128)(2,1)} %v0.1) | copy-start | bytes 1572868
  13.6 15.9 %collective-permute-start.6 = (bf16[256,896]{1,0:T(8,128)(2,1)S(1)}, bf16[256,896]{1,0:T(8,128)(2,1)S(1)}, u32[]{:S(2)}, u32[]{:S(2)}) collective-permute-start(bf16[256,896]{1,0:T(8,128)(2,1)S(1)} %collective-permute-done.5.refs_0_), channel_id=1, source_target_pairs={{0,1},{1,2},{2,3},{3,0},{8,11},{9,8},{10,9},{11,10},{4,5},{5,6},{6... | collective-permute-start | bytes 1376264 | tf_op jit(solution)/shard_map/ppermute | solution.py:51
  16.1 11.0 %collective-permute-start.1 = (bf16[256,896]{1,0:T(8,128)(2,1)S(1)}, bf16[256,896]{1,0:T(8,128)(2,1)S(1)}, u32[]{:S(2)}, u32[]{:S(2)}) collective-permute-start(bf16[256,896]{1,0:T(8,128)(2,1)S(1)} %collective-permute-done.refs_0_), channel_id=1, source_target_pairs={{0,1},{1,2},{2,3},{3,0},{8,11},{9,8},{10,9},{11,10},{4,5},{5,6},{6... | collective-permute-start | bytes 1376264 | tf_op jit(solution)/shard_map/ppermute | solution.py:51
  16.2 16.4 %collective-permute-start.4 = (bf16[256,896]{1,0:T(8,128)(2,1)S(1)}, bf16[256,896]{1,0:T(8,128)(2,1)S(1)}, u32[]{:S(2)}, u32[]{:S(2)}) collective-permute-start(bf16[256,896]{1,0:T(8,128)(2,1)S(1)} %collective-permute-done.3.refs_1_), channel_id=1, source_target_pairs={{0,4},{4,0},{1,5},{5,1},{2,6},{6,2},{3,7},{7,3},{8,12},{12,8},{9,1... | collective-permute-start | bytes 1376264 | tf_op jit(solution)/shard_map/ppermute | solution.py:74
  21.2 14.5 %collective-permute-start.8 = (bf16[2048,128]{1,0:T(8,128)(2,1)S(1)}, bf16[2048,128]{1,0:T(8,128)(2,1)S(1)}, u32[]{:S(2)}, u32[]{:S(2)}) collective-permute-start(bf16[2048,128]{1,0:T(8,128)(2,1)S(1)} %copy-done.2), channel_id=1, source_target_pairs={{0,32},{32,0},{1,33},{33,1},{2,34},{34,2},{3,35},{35,3},{4,36},{36... | collective-permute-start | bytes 1572872 | tf_op jit(solution)/shard_map/ppermute | solution.py:78
  27.1 8.7 %collective-permute-start.2 = (bf16[256,896]{1,0:T(8,128)(2,1)S(1)}, bf16[256,896]{1,0:T(8,128)(2,1)S(1)}, u32[]{:S(2)}, u32[]{:S(2)}) collective-permute-start(bf16[256,896]{1,0:T(8,128)(2,1)S(1)} %collective-permute-done.1.refs_1_), channel_id=1, source_target_pairs={{0,1},{1,2},{2,3},{3,0},{8,11},{9,8},{10,9},{11,10},{4,5},{5,6},{6... | collective-permute-start | bytes 1376264 | tf_op jit(solution)/shard_map/ppermute | solution.py:51
  35.7 20.2 %copy-start.1 = (bf16[2048,128]{1,0:T(8,128)(2,1)S(1)}, bf16[2048,128]{1,0:T(8,128)(2,1)}, u32[]{:S(2)}) copy-start(bf16[2048,128]{1,0:T(8,128)(2,1)} %k0.1) | copy-start | bytes 1572868
  35.7 20.2 %copy-start.7 = (f32[2,128]{1,0:T(2,128)S(1)}, f32[2,128]{1,0:T(2,128)}, u32[]{:S(2)}) copy-start(f32[2,128]{1,0:T(2,128)} %constant.66.clone.freq_ref) | copy-start | bytes 3076
  36.5 18.2 %collective-permute-start.10 = (bf16[256,512]{1,0:T(8,128)(2,1)S(1)}, bf16[256,512]{1,0:T(8,128)(2,1)S(1)}, u32[]{:S(2)}, u32[]{:S(2)}) collective-permute-start(bf16[256,512]{1,0:T(8,128)(2,1)S(1)} %get-tuple-element.26.q_ref), channel_id=1, source_target_pairs={{0,64},{8,200},{64,128},{72,8},{128,192},{136,72},{192,0},{200,136... | collective-permute-start | bytes 786440 | tf_op jit(solution)/shard_map/ppermute | solution.py:61
  39.8 16.1 %collective-permute-start.9 = (bf16[528,128]{1,0:T(8,128)(2,1)S(1)}, bf16[528,128]{1,0:T(8,128)(2,1)S(1)}, u32[]{:S(2)}, u32[]{:S(2)}) collective-permute-start(bf16[528,128]{1,0:T(8,128)(2,1)S(1)} %get-tuple-element.28.n0), channel_id=1, source_target_pairs={{0,32},{32,0},{1,33},{33,1},{2,34},{34,2},{3,35},{35,3},{4,36},{36... | collective-permute-start | bytes 405512 | tf_op jit(solution)/shard_map/ppermute | solution.py:78
  41.6 16.2 %collective-permute-start.12 = (bf16[256,512]{1,0:T(8,128)(2,1)S(1)}, bf16[256,512]{1,0:T(8,128)(2,1)S(1)}, u32[]{:S(2)}, u32[]{:S(2)}) collective-permute-start(bf16[256,512]{1,0:T(8,128)(2,1)S(1)} %get-tuple-element.26.q_ref), channel_id=1, source_target_pairs={{0,192},{8,72},{64,0},{72,136},{128,64},{136,200},{192,128},{200,8... | collective-permute-start | bytes 786440 | tf_op jit(solution)/shard_map/ppermute | solution.py:66
  54.6 12.4 %collective-permute-start.14 = (bf16[256,512]{1,0:T(8,128)(2,1)S(1)}, bf16[256,512]{1,0:T(8,128)(2,1)S(1)}, u32[]{:S(2)}, u32[]{:S(2)}) collective-permute-start(bf16[256,512]{1,0:T(8,128)(2,1)S(1)} %collective-permute-done.10.q_ref), channel_id=1, source_target_pairs={{0,64},{8,200},{64,128},{72,8},{128,192},{136,72},{192,0},{200,136... | collective-permute-start | bytes 786440 | tf_op jit(solution)/shard_map/ppermute | solution.py:61
  61.8 31.9 %collective-permute-start.13 = (bf16[2,144,512]{2,1,0:T(8,128)(2,1)S(1)}, bf16[2,144,512]{2,1,0:T(8,128)(2,1)S(1)}, u32[]{:S(2)}, u32[]{:S(2)}) collective-permute-start(bf16[2,144,512]{2,1,0:T(8,128)(2,1)S(1)} %attend.6), channel_id=1, source_target_pairs={{0,64},{8,200},{64,128},{72,8},{128,192},{136,72},{192,0},{200,136... | collective-permute-start | bytes 884744 | tf_op jit(solution)/shard_map/ppermute | solution.py:61
  65.2 28.5 %collective-permute-start.11 = (bf16[2,144,512]{2,1,0:T(8,128)(2,1)S(1)}, bf16[2,144,512]{2,1,0:T(8,128)(2,1)S(1)}, u32[]{:S(2)}, u32[]{:S(2)}) collective-permute-start(bf16[2,144,512]{2,1,0:T(8,128)(2,1)S(1)} %attend.5), channel_id=1, source_target_pairs={{0,192},{8,72},{64,0},{72,136},{128,64},{136,200},{192,128},{200,8... | collective-permute-start | bytes 884744 | tf_op jit(solution)/shard_map/ppermute | solution.py:66
  68.9 27.2 %collective-permute-start.15 = (bf16[2,144,512]{2,1,0:T(8,128)(2,1)S(1)}, bf16[2,144,512]{2,1,0:T(8,128)(2,1)S(1)}, u32[]{:S(2)}, u32[]{:S(2)}) collective-permute-start(bf16[2,144,512]{2,1,0:T(8,128)(2,1)S(1)} %attend.7), channel_id=1, source_target_pairs={{0,128},{64,192},{128,0},{192,64},{1,129},{65,193},{129,1},{193,65... | collective-permute-start | bytes 884744 | tf_op jit(solution)/shard_map/ppermute | solution.py:70

commit v7 on v6

--- a/solution.py
+++ b/solution.py
@@ -191,10 +191,12 @@
     )(place, *pieces, *weights, *extra)
 
 
-def last_kernel(piece_ref, weight_ref, acc_ref, cos_ref, sin_ref, mine_ref, q_ref, n_ref):
-    acc = acc_ref[...] + jnp.dot(
-        piece_ref[...], weight_ref[0], preferred_element_type=jnp.float32
-    )
+def last_kernel(
+    first_ref, second_ref, weight_ref, acc_ref, cos_ref, sin_ref, mine_ref, q_ref, n_ref
+):
+    acc = acc_ref[...]
+    for i, piece in enumerate((first_ref, second_ref)):
+        acc += jnp.dot(piece[...], weight_ref[i], preferred_element_type=jnp.float32)
     cosine, sine = cos_ref[...], sin_ref[...]
     for g in range(HG):
         at = slice(g * HD, (g + 1) * HD)
@@ -214,7 +216,7 @@
             jax.ShapeDtypeStruct((ROWS, QW), jnp.bfloat16),
             jax.ShapeDtypeStruct((2 * ROWS + 16, HD), jnp.bfloat16),
         ),
-        in_specs=[vmem] * 6,
+        in_specs=[vmem] * 7,
         out_specs=(vmem, vmem),
         compiler_params=pltpu.CompilerParams(vmem_limit_bytes=16 << 20),
         cost_estimate=tiny,
@@ -430,18 +432,16 @@
     k1 = py(key_cache)
     project = functools.partial(partial_project, place)
     acc = project((H_AT,), (hidden,), weights)
-    h2 = ring_x(after(h1, cosine, acc))
-    z1 = ring_x(z0)
+    z1 = ring_x(after(z0, cosine, acc))
     z3 = pz(h3)
     v1 = py(after(value_cache, k1))
     acc = project((H_AT + 1, H_AT + 3), (h1, h3), weights, acc)
     z2 = ring_x(z1)
-    acc = project((Z_AT, H_AT + 2), (z0, h2), weights, acc)
-    acc, kept = project(
-        (Z_AT + 3, Z_AT + 1, Z_AT + 2), (z3, z1), weights, acc, ahead=1
-    )
+    h2 = ring_x(after(h1, z1))
+    acc = project((Z_AT, Z_AT + 1), (z0, z1), weights, acc)
+    acc, kept = project((Z_AT + 3, Z_AT + 2, H_AT + 2), (z3,), weights, acc, ahead=2)
     acc = after(acc, k1, v1)
-    query, fresh = last_project(z2, kept, acc, cosine, sine, mine)
+    query, fresh = last_project(z2, h2, kept, acc, cosine, sine, mine)
     near, behind = ring_z(query), back_z(query)
     far = ring_z(near)
     jk, jv = join(ranks, key_cache, value_cache, k1, v1, fresh, py(fresh), mine, freq)

time: 97.3 us -> 102 us (1.048)
  the two profiles are of different devices: /device:TPU:36 before, /device:TPU:34 now
where the time goes in v7:
time: 102 us
  waiting for transfers between devices  36 us (35%)
  starting transfers between devices  33.3 us (33%)
  Pallas kernels  28.2 us (28%)
  local copies, waits for them, and re-layouts  3.53 us (3%)
    ppermute x3, waiting for transfers between devices, ring_z(): return lax.ppermute(v, ('zh', 'c'), pairs)  23.7 us
    ppermute x3, starting transfers between devices, ring_z(): return lax.ppermute(v, ('zh', 'c'), pairs)  13.1 us
    pallas_call x4, Pallas kernels, partial_project(): pl.pallas_call(functools.partial(partial_kernel, which, ahead, acc is not...  11.3 us
    pallas_call x4, Pallas kernels, attend(): pl.pallas_call(functools.partial(attend_kernel, shift), out_shape=packed_...  11 us
    ppermute x4, starting transfers between devices, ring_x(): return lax.ppermute(v, ('c', 'x'), opposite_ways(4))  5.77 us
    ppermute x2, starting transfers between devices, back_z(): return lax.ppermute(v, ('zh', 'c'), pairs)  5.61 us
    ppermute x1, waiting for transfers between devices, far_z(): return lax.ppermute(v, 'zh', [(i, (i + 2) % 4) for i in range(4)])  5.03 us
    ppermute x3, starting transfers between devices, py(): return lax.ppermute(v, 'yh', [(0, 1), (1, 0)])  4.4 us
  transfers between devices with their start and end apart: 16, of which 6 were waited for; matrix products, arithmetic and copies ran while one was open for 2% of the time, Pallas kernels for 25%

profile of v7, /device:TPU:34, one launch (start us, length us, event | category | flops | bytes accessed | tf_op | source)
XLA Modules:
  0.0 102.0 jit_solution(3190543511214188903)
XLA Ops:
  0.0 0.1 collective-permute-start
  0.1 1.5 %collective-permute-start.3 = (bf16[256,896]{1,0:T(8,128)(2,1)}, bf16[256,896]{1,0:T(8,128)(2,1)S(1)}, u32[]{:S(2)}, u32[]{:S(2)}) collective-permute-start(bf16[256,896]{1,0:T(8,128)(2,1)} %refs_0_.1), channel_id=1, source_target_pairs={{0,1},{1,2},{2,3},{3,0},{8,11},{9,8},{10,9},{11,10},{4,5},{5,6},{6... | collective-permute-start | bytes 1376264 | tf_op jit(solution)/shard_map/ppermute | solution.py:51
  1.6 0.8 collective-permute-start.5
  2.4 2.9 %collective-permute-start.7 = (bf16[2048,128]{1,0:T(8,128)(2,1)}, bf16[2048,128]{1,0:T(8,128)(2,1)S(1)}, u32[]{:S(2)}, u32[]{:S(2)}) collective-permute-start(bf16[2048,128]{1,0:T(8,128)(2,1)} %k0.1), channel_id=1, source_target_pairs={{0,32},{32,0},{1,33},{33,1},{2,34},{34,2},{3,35},{35,3},{4,36},{36... | collective-permute-start | bytes 1572872 | tf_op jit(solution)/shard_map/ppermute | solution.py:78
  5.3 0.7 pad.1.clone
  6.1 0.7 pad_add_fusion.mine_ref.refs_0_
  6.8 0.1 stack.51.place
  6.9 0.0 copy-start
  6.9 0.7 copy-done
  7.6 0.7 copy-done.4
  8.3 0.7 copy-done.5
  8.9 0.7 copy-done.6
  9.6 1.5 %prepare.1 = (f32[256,128]{1,0:T(8,128)S(1)}, f32[256,128]{1,0:T(8,128)S(1)}, s32[4]{0:T(128)S(1)}, s32[16]{0:T(128)S(1)}) custom-call(s32[12]{0:T(128)S(1)} %stack.51.place, s32[8]{0:T(128)S(1)} %copy-done.5, s32[8,8]{1,0:T(8,128)S(1)} %copy-done.4, s32[2,128]{1,0:T(2,128)S(1)} %copy-done, f32[2,128]{1,0:T(2,128)S(1)} %copy-done.6), custom_call_target="tpu_custom_call" | custom-call | flops 2000000000 | bytes 1 | tf_op jit(solution)/shard_map/prepare/pallas_call | solution.py:118
  11.2 2.4 %project.4.refs_5_ = f32[256,768]{1,0:T(8,128)S(1)} custom-call(s32[12]{0:T(128)S(1)} %stack.51.place, bf16[256,896]{1,0:T(8,128)(2,1)S(1)} %copy-done.3, bf16[7168,512]{1,0:T(8,128)(2,1)} %refs_1_.3, bf16[7168,128]{1,0:T(8,128)(2,1)} %refs_2_.7, bf16[7168,128]{1,0:T(8,128)(2,1)} %refs_3_.7), custom_call_target="tpu_custom_call" | custom-call | flops 6000000000 | bytes 1 | tf_op jit(solution)/shard_map/project/pallas_call | solution.py:179
  13.6 0.0 collective-permute-done.refs_0_
  13.6 0.0 copy-start.2
  13.6 1.6 %collective-permute-start.1 = (bf16[256,896]{1,0:T(8,128)(2,1)S(1)}, bf16[256,896]{1,0:T(8,128)(2,1)S(1)}, u32[]{:S(2)}, u32[]{:S(2)}) collective-permute-start(bf16[256,896]{1,0:T(8,128)(2,1)S(1)} %collective-permute-done.refs_0_), channel_id=1, source_target_pairs={{0,1},{1,2},{2,3},{3,0},{8,11},{9,8},{10,9},{11,10},{4,5},{5,6},{6... | collective-permute-start | bytes 1376264 | tf_op jit(solution)/shard_map/ppermute | solution.py:51
  15.2 0.0 collective-permute-done.5.refs_1_
  15.2 1.9 %collective-permute-start.6 = (bf16[256,896]{1,0:T(8,128)(2,1)S(1)}, bf16[256,896]{1,0:T(8,128)(2,1)S(1)}, u32[]{:S(2)}, u32[]{:S(2)}) collective-permute-start(bf16[256,896]{1,0:T(8,128)(2,1)S(1)} %collective-permute-done.5.refs_1_), channel_id=1, source_target_pairs={{0,4},{4,0},{1,5},{5,1},{2,6},{6,2},{3,7},{7,3},{8,12},{12,8},{9,1... | collective-permute-start | bytes 1376264 | tf_op jit(solution)/shard_map/ppermute | solution.py:74
  17.1 0.0 collective-permute-done.3.refs_0_
  17.1 3.1 %project.5.refs_5_ = f32[256,768]{1,0:T(8,128)S(1)} custom-call(s32[12]{0:T(128)S(1)} %stack.51.place, bf16[256,896]{1,0:T(8,128)(2,1)S(1)} %collective-permute-done.3.refs_0_, bf16[256,896]{1,0:T(8,128)(2,1)S(1)} %collective-permute-done.5.refs_1_, bf16[7168,512]{1,0:T(8,128)(2,1)} %refs_1_.3, bf16[7168,128]{1,0:T(8,128)(2,1)} %refs_2_.7, ...), custom_call_target="tpu_custom_call" | custom-call | flops 6000000000 | bytes 1 | tf_op jit(solution)/shard_map/project/pallas_call | solution.py:179
  20.2 0.4 collective-permute-start.8
  20.6 1.5 %collective-permute-done.1.refs_1_ = bf16[256,896]{1,0:T(8,128)(2,1)S(1)} collective-permute-done((bf16[256,896]{1,0:T(8,128)(2,1)S(1)}, bf16[256,896]{1,0:T(8,128)(2,1)S(1)}, u32[]{:S(2)}, u32[]{:S(2)}) %collective-permute-start.1) | collective-permute-done | bytes 458784 | tf_op jit(solution)/shard_map/ppermute | solution.py:51
  22.2 1.5 %collective-permute-start.4 = (bf16[256,896]{1,0:T(8,128)(2,1)S(1)}, bf16[256,896]{1,0:T(8,128)(2,1)S(1)}, u32[]{:S(2)}, u32[]{:S(2)}) collective-permute-start(bf16[256,896]{1,0:T(8,128)(2,1)S(1)} %collective-permute-done.3.refs_0_), channel_id=1, source_target_pairs={{0,1},{1,2},{2,3},{3,0},{8,11},{9,8},{10,9},{11,10},{4,5},{5,6},{6... | collective-permute-start | bytes 1376264 | tf_op jit(solution)/shard_map/ppermute | solution.py:51
  23.7 1.2 %collective-permute-start.2 = (bf16[256,896]{1,0:T(8,128)(2,1)S(1)}, bf16[256,896]{1,0:T(8,128)(2,1)S(1)}, u32[]{:S(2)}, u32[]{:S(2)}) collective-permute-start(bf16[256,896]{1,0:T(8,128)(2,1)S(1)} %collective-permute-done.1.refs_1_), channel_id=1, source_target_pairs={{0,1},{1,2},{2,3},{3,0},{8,11},{9,8},{10,9},{11,10},{4,5},{5,6},{6... | collective-permute-start | bytes 1376264 | tf_op jit(solution)/shard_map/ppermute | solution.py:51
  24.9 3.1 %project.6.refs_4_ = f32[256,768]{1,0:T(8,128)S(1)} custom-call(s32[12]{0:T(128)S(1)} %stack.51.place, bf16[256,896]{1,0:T(8,128)(2,1)S(1)} %collective-permute-done.refs_0_, bf16[256,896]{1,0:T(8,128)(2,1)S(1)} %collective-permute-done.1.refs_1_, bf16[7168,512]{1,0:T(8,128)(2,1)} %refs_1_.3, bf16[7168,128]{1,0:T(8,128)(2,1)} %refs_2_.7, ...), custom_call_target="tpu_custom_call" | custom-call | flops 6000000000 | bytes 1 | tf_op jit(solution)/shard_map/project/pallas_call | solution.py:179
  28.0 2.7 %project.7 = (f32[256,768]{1,0:T(8,128)S(1)}, bf16[2,896,768]{2,1,0:T(8,128)(2,1)S(1)}) custom-call(s32[12]{0:T(128)S(1)} %stack.51.place, bf16[256,896]{1,0:T(8,128)(2,1)S(1)} %collective-permute-done.6.refs_0_, bf16[7168,512]{1,0:T(8,128)(2,1)} %refs_1_.3, bf16[7168,128]{1,0:T(8,128)(2,1)} %refs_2_.7, bf16[7168,128]{1,0:T(8,128)(2,1)} %refs_3_.7, ...), custom_call_target="tpu_custom_call" | custom-call | flops 6000000000 | bytes 1 | tf_op jit(solution)/shard_map/project/pallas_call | solution.py:179
  30.7 0.0 copy-start.1
  30.7 0.0 copy-start.7
  30.7 3.1 %collective-permute-done.8.v1 = bf16[2048,128]{1,0:T(8,128)(2,1)S(1)} collective-permute-done((bf16[2048,128]{1,0:T(8,128)(2,1)S(1)}, bf16[2048,128]{1,0:T(8,128)(2,1)S(1)}, u32[]{:S(2)}, u32[]{:S(2)}) %collective-permute-start.8) | collective-permute-done | bytes 524320 | tf_op jit(solution)/shard_map/ppermute | solution.py:78
  33.9 2.6 %collective-permute-done.2.first_ref = bf16[256,896]{1,0:T(8,128)(2,1)S(1)} collective-permute-done((bf16[256,896]{1,0:T(8,128)(2,1)S(1)}, bf16[256,896]{1,0:T(8,128)(2,1)S(1)}, u32[]{:S(2)}, u32[]{:S(2)}) %collective-permute-start.2) | collective-permute-done | bytes 458784 | tf_op jit(solution)/shard_map/ppermute | solution.py:51
  36.5 1.1 %project_last.1 = (bf16[256,512]{1,0:T(8,128)(2,1)S(1)}, bf16[528,128]{1,0:T(8,128)(2,1)S(1)}) custom-call(bf16[256,896]{1,0:T(8,128)(2,1)S(1)} %collective-permute-done.2.first_ref, bf16[256,896]{1,0:T(8,128)(2,1)S(1)} %collective-permute-done.4.second_ref, bf16[2,896,768]{2,1,0:T(8,128)(2,1)S(1)} %get-tuple-element.23.weight_ref, ...), custom_call_target="tpu_custom_call" | custom-call | flops 1 | bytes 1 | tf_op jit(solution)/shard_map/project_last/pallas_call | solution.py:213
  37.6 3.4 %collective-permute-start.10 = (bf16[256,512]{1,0:T(8,128)(2,1)S(1)}, bf16[256,512]{1,0:T(8,128)(2,1)S(1)}, u32[]{:S(2)}, u32[]{:S(2)}) collective-permute-start(bf16[256,512]{1,0:T(8,128)(2,1)S(1)} %get-tuple-element.28.q_ref), channel_id=1, source_target_pairs={{0,64},{8,200},{64,128},{72,8},{128,192},{136,72},{192,0},{200,136... | collective-permute-start | bytes 786440 | tf_op jit(solution)/shard_map/ppermute | solution.py:61
  40.9 1.0 %collective-permute-start.9 = (bf16[528,128]{1,0:T(8,128)(2,1)S(1)}, bf16[528,128]{1,0:T(8,128)(2,1)S(1)}, u32[]{:S(2)}, u32[]{:S(2)}) collective-permute-start(bf16[528,128]{1,0:T(8,128)(2,1)S(1)} %get-tuple-element.30.n0), channel_id=1, source_target_pairs={{0,32},{32,0},{1,33},{33,1},{2,34},{34,2},{3,35},{35,3},{4,36},{36... | collective-permute-start | bytes 405512 | tf_op jit(solution)/shard_map/ppermute | solution.py:78
  42.0 2.4 %collective-permute-start.12 = (bf16[256,512]{1,0:T(8,128)(2,1)S(1)}, bf16[256,512]{1,0:T(8,128)(2,1)S(1)}, u32[]{:S(2)}, u32[]{:S(2)}) collective-permute-start(bf16[256,512]{1,0:T(8,128)(2,1)S(1)} %get-tuple-element.28.q_ref), channel_id=1, source_target_pairs={{0,192},{8,72},{64,0},{72,136},{128,64},{136,200},{192,128},{200,8... | collective-permute-start | bytes 786440 | tf_op jit(solution)/shard_map/ppermute | solution.py:66
  44.4 11.6 %collective-permute-done.10.q_ref = bf16[256,512]{1,0:T(8,128)(2,1)S(1)} collective-permute-done((bf16[256,512]{1,0:T(8,128)(2,1)S(1)}, bf16[256,512]{1,0:T(8,128)(2,1)S(1)}, u32[]{:S(2)}, u32[]{:S(2)}) %collective-permute-start.10) | collective-permute-done | bytes 262176 | tf_op jit(solution)/shard_map/ppermute | solution.py:61
  56.0 1.0 %collective-permute-start.14 = (bf16[256,512]{1,0:T(8,128)(2,1)S(1)}, bf16[256,512]{1,0:T(8,128)(2,1)S(1)}, u32[]{:S(2)}, u32[]{:S(2)}) collective-permute-start(bf16[256,512]{1,0:T(8,128)(2,1)S(1)} %collective-permute-done.10.q_ref), channel_id=1, source_target_pairs={{0,64},{8,200},{64,128},{72,8},{128,192},{136,72},{192,0},{200,136... | collective-permute-start | bytes 786440 | tf_op jit(solution)/shard_map/ppermute | solution.py:61
  57.0 1.8 %join.1 = (bf16[4,1024,128]{2,1,0:T(8,128)(2,1)S(1)}, bf16[4,1024,128]{2,1,0:T(8,128)(2,1)S(1)}) custom-call(s32[4]{0:T(128)S(1)} %get-tuple-element.29.rank_ref, bf16[2048,128]{1,0:T(8,128)(2,1)S(1)} %copy-done.1, bf16[2048,128]{1,0:T(8,128)(2,1)S(1)} %copy-done.2, bf16[2048,128]{1,0:T(8,128)(2,1)S(1)} %collective-permute-done.7.k1, ...), custom_call_target="tpu_custom_call" | custom-call | flops 3000000000 | bytes 1 | tf_op jit(solution)/shard_map/join/pallas_call | solution.py:337
  58.8 0.9 attend.5
  59.7 3.2 %collective-permute-start.11 = (bf16[2,144,512]{2,1,0:T(8,128)(2,1)S(1)}, bf16[2,144,512]{2,1,0:T(8,128)(2,1)S(1)}, u32[]{:S(2)}, u32[]{:S(2)}) collective-permute-start(bf16[2,144,512]{2,1,0:T(8,128)(2,1)S(1)} %attend.5), channel_id=1, source_target_pairs={{0,192},{8,72},{64,0},{72,136},{128,64},{136,200},{192,128},{200,8... | collective-permute-start | bytes 884744 | tf_op jit(solution)/shard_map/ppermute | solution.py:66
  62.9 3.0 %attend.6 = bf16[2,144,512]{2,1,0:T(8,128)(2,1)S(1)} custom-call(s32[16]{0:T(128)S(1)} %get-tuple-element.19.valid_ref, bf16[256,512]{1,0:T(8,128)(2,1)S(1)} %collective-permute-done.12.q_ref, bf16[4,1024,128]{2,1,0:T(8,128)(2,1)S(1)} %get-tuple-element.31.jk_ref, bf16[4,1024,128]{2,1,0:T(8,128)(2,1)S(1)} %get-tuple-element.32.jv_ref), custom_call_target="tpu_custom_call" | custom-call | flops 1000000000 | bytes 1 | tf_op jit(solution)/shard_map/attend/pallas_call | solution.py:349
  65.9 8.7 %collective-permute-start.13 = (bf16[2,144,512]{2,1,0:T(8,128)(2,1)S(1)}, bf16[2,144,512]{2,1,0:T(8,128)(2,1)S(1)}, u32[]{:S(2)}, u32[]{:S(2)}) collective-permute-start(bf16[2,144,512]{2,1,0:T(8,128)(2,1)S(1)} %attend.6), channel_id=1, source_target_pairs={{0,64},{8,200},{64,128},{72,8},{128,192},{136,72},{192,0},{200,136... | collective-permute-start | bytes 884744 | tf_op jit(solution)/shard_map/ppermute | solution.py:61
  74.6 12.1 %collective-permute-done.14.q_ref = bf16[256,512]{1,0:T(8,128)(2,1)S(1)} collective-permute-done((bf16[256,512]{1,0:T(8,128)(2,1)S(1)}, bf16[256,512]{1,0:T(8,128)(2,1)S(1)}, u32[]{:S(2)}, u32[]{:S(2)}) %collective-permute-start.14) | collective-permute-done | bytes 262176 | tf_op jit(solution)/shard_map/ppermute | solution.py:61
  86.7 3.0 %attend.7 = bf16[2,144,512]{2,1,0:T(8,128)(2,1)S(1)} custom-call(s32[16]{0:T(128)S(1)} %get-tuple-element.19.valid_ref, bf16[256,512]{1,0:T(8,128)(2,1)S(1)} %collective-permute-done.14.q_ref, bf16[4,1024,128]{2,1,0:T(8,128)(2,1)S(1)} %get-tuple-element.31.jk_ref, bf16[4,1024,128]{2,1,0:T(8,128)(2,1)S(1)} %get-tuple-element.32.jv_ref), custom_call_target="tpu_custom_call" | custom-call | flops 1000000000 | bytes 1 | tf_op jit(solution)/shard_map/attend/pallas_call | solution.py:349
  89.6 1.6 %collective-permute-start.15 = (bf16[2,144,512]{2,1,0:T(8,128)(2,1)S(1)}, bf16[2,144,512]{2,1,0:T(8,128)(2,1)S(1)}, u32[]{:S(2)}, u32[]{:S(2)}) collective-permute-start(bf16[2,144,512]{2,1,0:T(8,128)(2,1)S(1)} %attend.7), channel_id=1, source_target_pairs={{0,128},{64,192},{128,0},{192,64},{1,129},{65,193},{129,1},{193,65... | collective-permute-start | bytes 884744 | tf_op jit(solution)/shard_map/ppermute | solution.py:70
  91.2 4.2 %attend.4.refs_0_ = bf16[2,144,512]{2,1,0:T(8,128)(2,1)S(1)} custom-call(s32[16]{0:T(128)S(1)} %get-tuple-element.19.valid_ref, bf16[256,512]{1,0:T(8,128)(2,1)S(1)} %get-tuple-element.28.q_ref, bf16[4,1024,128]{2,1,0:T(8,128)(2,1)S(1)} %get-tuple-element.31.jk_ref, bf16[4,1024,128]{2,1,0:T(8,128)(2,1)S(1)} %get-tuple-element.32.jv_ref, ...), custom_call_target="tpu_custom_call" | custom-call | flops 1000000000 | bytes 1 | tf_op jit(solution)/shard_map/attend/pallas_call | solution.py:349
  95.4 5.0 %collective-permute-done.15.refs_3_ = bf16[2,144,512]{2,1,0:T(8,128)(2,1)S(1)} collective-permute-done((bf16[2,144,512]{2,1,0:T(8,128)(2,1)S(1)}, bf16[2,144,512]{2,1,0:T(8,128)(2,1)S(1)}, u32[]{:S(2)}, u32[]{:S(2)}) %collective-permute-start.15) | collective-permute-done | bytes 294944 | tf_op jit(solution)/shard_map/ppermute | solution.py:70
  100.5 1.5 %merge.1 = bf16[256,512]{1,0:T(8,128)(2,1)} custom-call(bf16[2,144,512]{2,1,0:T(8,128)(2,1)S(1)} %attend.4.refs_0_, bf16[2,144,512]{2,1,0:T(8,128)(2,1)S(1)} %collective-permute-done.11.refs_1_, bf16[2,144,512]{2,1,0:T(8,128)(2,1)S(1)} %collective-permute-done.13.refs_2_, bf16[2,144,512]{2,1,0:T(8,128)(2,1)S(1)} %collective-permute-done.15.refs_3_), custom_call_target="tpu_custom_call" | custom-call | flops 1 | bytes 1 | tf_op jit(solution)/shard_map/merge/pallas_call | solution.py:396
  (15 shorter events, 0.0 us)
Async XLA Ops:
  0.0 13.6 %collective-permute-start = (bf16[256,896]{1,0:T(8,128)(2,1)}, bf16[256,896]{1,0:T(8,128)(2,1)S(1)}, u32[]{:S(2)}, u32[]{:S(2)}) collective-permute-start(bf16[256,896]{1,0:T(8,128)(2,1)} %refs_0_.1), channel_id=1, source_target_pairs={{0,4},{4,0},{1,5},{5,1},{2,6},{6,2},{3,7},{7,3},{8,12},{12,8},{9,1... | collective-permute-start | bytes 1376264 | tf_op jit(solution)/shard_map/ppermute | solution.py:74
  0.1 17.0 %collective-permute-start.3 = (bf16[256,896]{1,0:T(8,128)(2,1)}, bf16[256,896]{1,0:T(8,128)(2,1)S(1)}, u32[]{:S(2)}, u32[]{:S(2)}) collective-permute-start(bf16[256,896]{1,0:T(8,128)(2,1)} %refs_0_.1), channel_id=1, source_target_pairs={{0,1},{1,2},{2,3},{3,0},{8,11},{9,8},{10,9},{11,10},{4,5},{5,6},{6... | collective-permute-start | bytes 1376264 | tf_op jit(solution)/shard_map/ppermute | solution.py:51
  1.6 13.6 %collective-permute-start.5 = (bf16[256,896]{1,0:T(8,128)(2,1)}, bf16[256,896]{1,0:T(8,128)(2,1)S(1)}, u32[]{:S(2)}, u32[]{:S(2)}) collective-permute-start(bf16[256,896]{1,0:T(8,128)(2,1)} %refs_0_.1), channel_id=1, source_target_pairs={{0,3},{1,0},{2,1},{3,2},{8,9},{9,10},{10,11},{11,8},{4,7},{5,4},{6... | collective-permute-start | bytes 1376264 | tf_op jit(solution)/shard_map/ppermute | solution.py:56
  2.4 17.8 %collective-permute-start.7 = (bf16[2048,128]{1,0:T(8,128)(2,1)}, bf16[2048,128]{1,0:T(8,128)(2,1)S(1)}, u32[]{:S(2)}, u32[]{:S(2)}) collective-permute-start(bf16[2048,128]{1,0:T(8,128)(2,1)} %k0.1), channel_id=1, source_target_pairs={{0,32},{32,0},{1,33},{33,1},{2,34},{34,2},{3,35},{35,3},{4,36},{36... | collective-permute-start | bytes 1572872 | tf_op jit(solution)/shard_map/ppermute | solution.py:78
  6.9 0.7 copy-start
  7.6 0.7 copy-start.4
  8.3 0.7 copy-start.5
  8.9 0.7 copy-start.6
  9.6 1.5 %copy-start.3 = (bf16[256,896]{1,0:T(8,128)(2,1)S(1)}, bf16[256,896]{1,0:T(8,128)(2,1)}, u32[]{:S(2)}) copy-start(bf16[256,896]{1,0:T(8,128)(2,1)} %refs_0_.1) | copy-start | bytes 1376260
  13.6 6.6 %copy-start.2 = (bf16[2048,128]{1,0:T(8,128)(2,1)S(1)}, bf16[2048,128]{1,0:T(8,128)(2,1)}, u32[]{:S(2)}) copy-start(bf16[2048,128]{1,0:T(8,128)(2,1)} %v0.1) | copy-start | bytes 1572868
  13.6 8.6 %collective-permute-start.1 = (bf16[256,896]{1,0:T(8,128)(2,1)S(1)}, bf16[256,896]{1,0:T(8,128)(2,1)S(1)}, u32[]{:S(2)}, u32[]{:S(2)}) collective-permute-start(bf16[256,896]{1,0:T(8,128)(2,1)S(1)} %collective-permute-done.refs_0_), channel_id=1, source_target_pairs={{0,1},{1,2},{2,3},{3,0},{8,11},{9,8},{10,9},{11,10},{4,5},{5,6},{6... | collective-permute-start | bytes 1376264 | tf_op jit(solution)/shard_map/ppermute | solution.py:51
  15.2 12.8 %collective-permute-start.6 = (bf16[256,896]{1,0:T(8,128)(2,1)S(1)}, bf16[256,896]{1,0:T(8,128)(2,1)S(1)}, u32[]{:S(2)}, u32[]{:S(2)}) collective-permute-start(bf16[256,896]{1,0:T(8,128)(2,1)S(1)} %collective-permute-done.5.refs_1_), channel_id=1, source_target_pairs={{0,4},{4,0},{1,5},{5,1},{2,6},{6,2},{3,7},{7,3},{8,12},{12,8},{9,1... | collective-permute-start | bytes 1376264 | tf_op jit(solution)/shard_map/ppermute | solution.py:74
  20.2 13.6 %collective-permute-start.8 = (bf16[2048,128]{1,0:T(8,128)(2,1)S(1)}, bf16[2048,128]{1,0:T(8,128)(2,1)S(1)}, u32[]{:S(2)}, u32[]{:S(2)}) collective-permute-start(bf16[2048,128]{1,0:T(8,128)(2,1)S(1)} %copy-done.2), channel_id=1, source_target_pairs={{0,32},{32,0},{1,33},{33,1},{2,34},{34,2},{3,35},{35,3},{4,36},{36... | collective-permute-start | bytes 1572872 | tf_op jit(solution)/shard_map/ppermute | solution.py:78
  22.2 14.3 %collective-permute-start.4 = (bf16[256,896]{1,0:T(8,128)(2,1)S(1)}, bf16[256,896]{1,0:T(8,128)(2,1)S(1)}, u32[]{:S(2)}, u32[]{:S(2)}) collective-permute-start(bf16[256,896]{1,0:T(8,128)(2,1)S(1)} %collective-permute-done.3.refs_0_), channel_id=1, source_target_pairs={{0,1},{1,2},{2,3},{3,0},{8,11},{9,8},{10,9},{11,10},{4,5},{5,6},{6... | collective-permute-start | bytes 1376264 | tf_op jit(solution)/shard_map/ppermute | solution.py:51
  23.7 12.8 %collective-permute-start.2 = (bf16[256,896]{1,0:T(8,128)(2,1)S(1)}, bf16[256,896]{1,0:T(8,128)(2,1)S(1)}, u32[]{:S(2)}, u32[]{:S(2)}) collective-permute-start(bf16[256,896]{1,0:T(8,128)(2,1)S(1)} %collective-permute-done.1.refs_1_), channel_id=1, source_target_pairs={{0,1},{1,2},{2,3},{3,0},{8,11},{9,8},{10,9},{11,10},{4,5},{5,6},{6... | collective-permute-start | bytes 1376264 | tf_op jit(solution)/shard_map/ppermute | solution.py:51
  30.7 26.3 %copy-start.1 = (bf16[2048,128]{1,0:T(8,128)(2,1)S(1)}, bf16[2048,128]{1,0:T(8,128)(2,1)}, u32[]{:S(2)}) copy-start(bf16[2048,128]{1,0:T(8,128)(2,1)} %k0.1) | copy-start | bytes 1572868
  30.7 26.3 %copy-start.7 = (f32[2,128]{1,0:T(2,128)S(1)}, f32[2,128]{1,0:T(2,128)}, u32[]{:S(2)}) copy-start(f32[2,128]{1,0:T(2,128)} %constant.66.clone.freq_ref) | copy-start | bytes 3076
  37.6 18.4 %collective-permute-start.10 = (bf16[256,512]{1,0:T(8,128)(2,1)S(1)}, bf16[256,512]{1,0:T(8,128)(2,1)S(1)}, u32[]{:S(2)}, u32[]{:S(2)}) collective-permute-start(bf16[256,512]{1,0:T(8,128)(2,1)S(1)} %get-tuple-element.28.q_ref), channel_id=1, source_target_pairs={{0,64},{8,200},{64,128},{72,8},{128,192},{136,72},{192,0},{200,136... | collective-permute-start | bytes 786440 | tf_op jit(solution)/shard_map/ppermute | solution.py:61
  40.9 16.1 %collective-permute-start.9 = (bf16[528,128]{1,0:T(8,128)(2,1)S(1)}, bf16[528,128]{1,0:T(8,128)(2,1)S(1)}, u32[]{:S(2)}, u32[]{:S(2)}) collective-permute-start(bf16[528,128]{1,0:T(8,128)(2,1)S(1)} %get-tuple-element.30.n0), channel_id=1, source_target_pairs={{0,32},{32,0},{1,33},{33,1},{2,34},{34,2},{3,35},{35,3},{4,36},{36... | collective-permute-start | bytes 405512 | tf_op jit(solution)/shard_map/ppermute | solution.py:78
  42.0 20.9 %collective-permute-start.12 = (bf16[256,512]{1,0:T(8,128)(2,1)S(1)}, bf16[256,512]{1,0:T(8,128)(2,1)S(1)}, u32[]{:S(2)}, u32[]{:S(2)}) collective-permute-start(bf16[256,512]{1,0:T(8,128)(2,1)S(1)} %get-tuple-element.28.q_ref), channel_id=1, source_target_pairs={{0,192},{8,72},{64,0},{72,136},{128,64},{136,200},{192,128},{200,8... | collective-permute-start | bytes 786440 | tf_op jit(solution)/shard_map/ppermute | solution.py:66
  56.0 30.7 %collective-permute-start.14 = (bf16[256,512]{1,0:T(8,128)(2,1)S(1)}, bf16[256,512]{1,0:T(8,128)(2,1)S(1)}, u32[]{:S(2)}, u32[]{:S(2)}) collective-permute-start(bf16[256,512]{1,0:T(8,128)(2,1)S(1)} %collective-permute-done.10.q_ref), channel_id=1, source_target_pairs={{0,64},{8,200},{64,128},{72,8},{128,192},{136,72},{192,0},{200,136... | collective-permute-start | bytes 786440 | tf_op jit(solution)/shard_map/ppermute | solution.py:61
  59.7 35.7 %collective-permute-start.11 = (bf16[2,144,512]{2,1,0:T(8,128)(2,1)S(1)}, bf16[2,144,512]{2,1,0:T(8,128)(2,1)S(1)}, u32[]{:S(2)}, u32[]{:S(2)}) collective-permute-start(bf16[2,144,512]{2,1,0:T(8,128)(2,1)S(1)} %attend.5), channel_id=1, source_target_pairs={{0,192},{8,72},{64,0},{72,136},{128,64},{136,200},{192,128},{200,8... | collective-permute-start | bytes 884744 | tf_op jit(solution)/shard_map/ppermute | solution.py:66
  65.9 29.6 %collective-permute-start.13 = (bf16[2,144,512]{2,1,0:T(8,128)(2,1)S(1)}, bf16[2,144,512]{2,1,0:T(8,128)(2,1)S(1)}, u32[]{:S(2)}, u32[]{:S(2)}) collective-permute-start(bf16[2,144,512]{2,1,0:T(8,128)(2,1)S(1)} %attend.6), channel_id=1, source_target_pairs={{0,64},{8,200},{64,128},{72,8},{128,192},{136,72},{192,0},{200,136... | collective-permute-start | bytes 884744 | tf_op jit(solution)/shard_map/ppermute | solution.py:61
  89.6 10.8 %collective-permute-start.15 = (bf16[2,144,512]{2,1,0:T(8,128)(2,1)S(1)}, bf16[2,144,512]{2,1,0:T(8,128)(2,1)S(1)}, u32[]{:S(2)}, u32[]{:S(2)}) collective-permute-start(bf16[2,144,512]{2,1,0:T(8,128)(2,1)S(1)} %attend.7), channel_id=1, source_target_pairs={{0,128},{64,192},{128,0},{192,64},{1,129},{65,193},{129,1},{193,65... | collective-permute-start | bytes 884744 | tf_op jit(solution)/shard_map/ppermute | solution.py:70

commit v8 on v7

--- a/solution.py
+++ b/solution.py
@@ -440,7 +440,7 @@
     h2 = ring_x(after(h1, z1))
     acc = project((Z_AT, Z_AT + 1), (z0, z1), weights, acc)
     acc, kept = project((Z_AT + 3, Z_AT + 2, H_AT + 2), (z3,), weights, acc, ahead=2)
-    acc = after(acc, k1, v1)
+    acc = after(acc, k1)
     query, fresh = last_project(z2, h2, kept, acc, cosine, sine, mine)
     near, behind = ring_z(query), back_z(query)
     far = ring_z(near)

time: 102 us -> 96.6 us (0.947)
  the two profiles are of different devices: /device:TPU:34 before, /device:TPU:32 now
where the time goes in v8:
time: 96.6 us; the launch traced here: 94.9 us
  waiting for transfers between devices  35.2 us (36%)
  starting transfers between devices  31.1 us (32%)
  Pallas kernels  24.1 us (25%)
  local copies, waits for them, and re-layouts  3.53 us (4%)
    ppermute x1, waiting for transfers between devices, far_z(): return lax.ppermute(v, 'zh', [(i, (i + 2) % 4) for i in range(4)])  15.2 us
    pallas_call x4, Pallas kernels, partial_project(): pl.pallas_call(functools.partial(partial_kernel, which, ahead, acc is not...  11.3 us
    ppermute x3, waiting for transfers between devices, ring_z(): return lax.ppermute(v, ('zh', 'c'), pairs)  10 us
    ppermute x4, waiting for transfers between devices, ring_x(): return lax.ppermute(v, ('c', 'x'), opposite_ways(4))  9.83 us
    ppermute x3, starting transfers between devices, ring_z(): return lax.ppermute(v, ('zh', 'c'), pairs)  8.1 us
    pallas_call x4, Pallas kernels, attend(): pl.pallas_call(functools.partial(attend_kernel, shift), out_shape=packed_...  6.8 us
    ppermute x3, starting transfers between devices, py(): return lax.ppermute(v, 'yh', [(0, 1), (1, 0)])  6.58 us
    ppermute x1, starting transfers between devices, far_z(): return lax.ppermute(v, 'zh', [(i, (i + 2) % 4) for i in range(4)])  5.44 us
  transfers between devices with their start and end apart: 16, of which 7 were waited for; matrix products, arithmetic and copies ran while one was open for 2% of the time, Pallas kernels for 24%

profile of v8, /device:TPU:32, one launch (start us, length us, event | category | flops | bytes accessed | tf_op | source)
XLA Modules:
  0.0 94.9 jit_solution(12419898480976009799)
XLA Ops:
  0.0 1.5 %collective-permute-start.3 = (bf16[256,896]{1,0:T(8,128)(2,1)}, bf16[256,896]{1,0:T(8,128)(2,1)S(1)}, u32[]{:S(2)}, u32[]{:S(2)}) collective-permute-start(bf16[256,896]{1,0:T(8,128)(2,1)} %refs_0_.1), channel_id=1, source_target_pairs={{0,1},{1,2},{2,3},{3,0},{8,11},{9,8},{10,9},{11,10},{4,5},{5,6},{6... | collective-permute-start | bytes 1376264 | tf_op jit(solution)/shard_map/ppermute | solution.py:51
  1.5 1.7 %collective-permute-start.5 = (bf16[256,896]{1,0:T(8,128)(2,1)}, bf16[256,896]{1,0:T(8,128)(2,1)S(1)}, u32[]{:S(2)}, u32[]{:S(2)}) collective-permute-start(bf16[256,896]{1,0:T(8,128)(2,1)} %refs_0_.1), channel_id=1, source_target_pairs={{0,3},{1,0},{2,1},{3,2},{8,9},{9,10},{10,11},{11,8},{4,7},{5,4},{6... | collective-permute-start | bytes 1376264 | tf_op jit(solution)/shard_map/ppermute | solution.py:56
  3.2 1.8 %collective-permute-start = (bf16[256,896]{1,0:T(8,128)(2,1)}, bf16[256,896]{1,0:T(8,128)(2,1)S(1)}, u32[]{:S(2)}, u32[]{:S(2)}) collective-permute-start(bf16[256,896]{1,0:T(8,128)(2,1)} %refs_0_.1), channel_id=1, source_target_pairs={{0,4},{4,0},{1,5},{5,1},{2,6},{6,2},{3,7},{7,3},{8,12},{12,8},{9,1... | collective-permute-start | bytes 1376264 | tf_op jit(solution)/shard_map/ppermute | solution.py:74
  5.1 1.5 %collective-permute-start.7 = (bf16[2048,128]{1,0:T(8,128)(2,1)}, bf16[2048,128]{1,0:T(8,128)(2,1)S(1)}, u32[]{:S(2)}, u32[]{:S(2)}) collective-permute-start(bf16[2048,128]{1,0:T(8,128)(2,1)} %k0.1), channel_id=1, source_target_pairs={{0,32},{32,0},{1,33},{33,1},{2,34},{34,2},{3,35},{35,3},{4,36},{36... | collective-permute-start | bytes 1572872 | tf_op jit(solution)/shard_map/ppermute | solution.py:78
  6.5 0.7 pad.1.clone
  7.3 0.7 pad_add_fusion.mine_ref.refs_0_
  8.0 0.1 stack.51.place
  8.1 0.0 copy-start
  8.1 0.7 copy-done
  8.8 0.7 copy-done.4
  9.5 0.7 copy-done.5
  10.1 0.7 copy-done.6
  10.8 1.5 %prepare.1 = (f32[256,128]{1,0:T(8,128)S(1)}, f32[256,128]{1,0:T(8,128)S(1)}, s32[4]{0:T(128)S(1)}, s32[16]{0:T(128)S(1)}) custom-call(s32[12]{0:T(128)S(1)} %stack.51.place, s32[8]{0:T(128)S(1)} %copy-done.5, s32[8,8]{1,0:T(8,128)S(1)} %copy-done.4, s32[2,128]{1,0:T(2,128)S(1)} %copy-done, f32[2,128]{1,0:T(2,128)S(1)} %copy-done.6), custom_call_target="tpu_custom_call" | custom-call | flops 2000000000 | bytes 1 | tf_op jit(solution)/shard_map/prepare/pallas_call | solution.py:118
  12.4 2.4 %project.4.refs_5_ = f32[256,768]{1,0:T(8,128)S(1)} custom-call(s32[12]{0:T(128)S(1)} %stack.51.place, bf16[256,896]{1,0:T(8,128)(2,1)S(1)} %copy-done.3, bf16[7168,512]{1,0:T(8,128)(2,1)} %refs_1_.3, bf16[7168,128]{1,0:T(8,128)(2,1)} %refs_2_.7, bf16[7168,128]{1,0:T(8,128)(2,1)} %refs_3_.7), custom_call_target="tpu_custom_call" | custom-call | flops 6000000000 | bytes 1 | tf_op jit(solution)/shard_map/project/pallas_call | solution.py:179
  14.8 0.1 collective-permute-done.refs_0_
  15.0 0.5 collective-permute-start.1
  15.4 0.0 collective-permute-done.5.refs_1_
  15.4 1.7 %collective-permute-start.6 = (bf16[256,896]{1,0:T(8,128)(2,1)S(1)}, bf16[256,896]{1,0:T(8,128)(2,1)S(1)}, u32[]{:S(2)}, u32[]{:S(2)}) collective-permute-start(bf16[256,896]{1,0:T(8,128)(2,1)S(1)} %collective-permute-done.5.refs_1_), channel_id=1, source_target_pairs={{0,4},{4,0},{1,5},{5,1},{2,6},{6,2},{3,7},{7,3},{8,12},{12,8},{9,1... | collective-permute-start | bytes 1376264 | tf_op jit(solution)/shard_map/ppermute | solution.py:74
  17.1 3.1 %project.5.refs_5_ = f32[256,768]{1,0:T(8,128)S(1)} custom-call(s32[12]{0:T(128)S(1)} %stack.51.place, bf16[256,896]{1,0:T(8,128)(2,1)S(1)} %collective-permute-done.3.refs_0_, bf16[256,896]{1,0:T(8,128)(2,1)S(1)} %collective-permute-done.5.refs_1_, bf16[7168,512]{1,0:T(8,128)(2,1)} %refs_1_.3, bf16[7168,128]{1,0:T(8,128)(2,1)} %refs_2_.7, ...), custom_call_target="tpu_custom_call" | custom-call | flops 6000000000 | bytes 1 | tf_op jit(solution)/shard_map/project/pallas_call | solution.py:179
  20.2 0.0 collective-permute-done.7.k1
  20.2 1.9 %collective-permute-start.8 = (bf16[2048,128]{1,0:T(8,128)(2,1)S(1)}, bf16[2048,128]{1,0:T(8,128)(2,1)S(1)}, u32[]{:S(2)}, u32[]{:S(2)}) collective-permute-start(bf16[2048,128]{1,0:T(8,128)(2,1)S(1)} %copy-done.2), channel_id=1, source_target_pairs={{0,32},{32,0},{1,33},{33,1},{2,34},{34,2},{3,35},{35,3},{4,36},{36... | collective-permute-start | bytes 1572872 | tf_op jit(solution)/shard_map/ppermute | solution.py:78
  22.1 2.5 %collective-permute-done.1.refs_1_ = bf16[256,896]{1,0:T(8,128)(2,1)S(1)} collective-permute-done((bf16[256,896]{1,0:T(8,128)(2,1)S(1)}, bf16[256,896]{1,0:T(8,128)(2,1)S(1)}, u32[]{:S(2)}, u32[]{:S(2)}) %collective-permute-start.1) | collective-permute-done | bytes 458784 | tf_op jit(solution)/shard_map/ppermute | solution.py:51
  24.6 1.4 %collective-permute-start.2 = (bf16[256,896]{1,0:T(8,128)(2,1)S(1)}, bf16[256,896]{1,0:T(8,128)(2,1)S(1)}, u32[]{:S(2)}, u32[]{:S(2)}) collective-permute-start(bf16[256,896]{1,0:T(8,128)(2,1)S(1)} %collective-permute-done.1.refs_1_), channel_id=1, source_target_pairs={{0,1},{1,2},{2,3},{3,0},{8,11},{9,8},{10,9},{11,10},{4,5},{5,6},{6... | collective-permute-start | bytes 1376264 | tf_op jit(solution)/shard_map/ppermute | solution.py:51
  26.1 3.1 %project.6.refs_4_ = f32[256,768]{1,0:T(8,128)S(1)} custom-call(s32[12]{0:T(128)S(1)} %stack.51.place, bf16[256,896]{1,0:T(8,128)(2,1)S(1)} %collective-permute-done.refs_0_, bf16[256,896]{1,0:T(8,128)(2,1)S(1)} %collective-permute-done.1.refs_1_, bf16[7168,512]{1,0:T(8,128)(2,1)} %refs_1_.3, bf16[7168,128]{1,0:T(8,128)(2,1)} %refs_2_.7, ...), custom_call_target="tpu_custom_call" | custom-call | flops 6000000000 | bytes 1 | tf_op jit(solution)/shard_map/project/pallas_call | solution.py:179
  29.1 0.0 collective-permute-done.6.refs_0_
  29.1 2.7 %project.7 = (f32[256,768]{1,0:T(8,128)S(1)}, bf16[2,896,768]{2,1,0:T(8,128)(2,1)S(1)}) custom-call(s32[12]{0:T(128)S(1)} %stack.51.place, bf16[256,896]{1,0:T(8,128)(2,1)S(1)} %collective-permute-done.6.refs_0_, bf16[7168,512]{1,0:T(8,128)(2,1)} %refs_1_.3, bf16[7168,128]{1,0:T(8,128)(2,1)} %refs_2_.7, bf16[7168,128]{1,0:T(8,128)(2,1)} %refs_3_.7, ...), custom_call_target="tpu_custom_call" | custom-call | flops 6000000000 | bytes 1 | tf_op jit(solution)/shard_map/project/pallas_call | solution.py:179
  31.9 0.0 copy-start.1
  31.9 0.0 copy-start.7
  31.9 2.4 %collective-permute-done.4.second_ref = bf16[256,896]{1,0:T(8,128)(2,1)S(1)} collective-permute-done((bf16[256,896]{1,0:T(8,128)(2,1)S(1)}, bf16[256,896]{1,0:T(8,128)(2,1)S(1)}, u32[]{:S(2)}, u32[]{:S(2)}) %collective-permute-start.4) | collective-permute-done | bytes 458784 | tf_op jit(solution)/shard_map/ppermute | solution.py:51
  34.3 4.9 %collective-permute-done.2.first_ref = bf16[256,896]{1,0:T(8,128)(2,1)S(1)} collective-permute-done((bf16[256,896]{1,0:T(8,128)(2,1)S(1)}, bf16[256,896]{1,0:T(8,128)(2,1)S(1)}, u32[]{:S(2)}, u32[]{:S(2)}) %collective-permute-start.2) | collective-permute-done | bytes 458784 | tf_op jit(solution)/shard_map/ppermute | solution.py:51
  39.2 1.1 %project_last.1 = (bf16[256,512]{1,0:T(8,128)(2,1)S(1)}, bf16[528,128]{1,0:T(8,128)(2,1)S(1)}) custom-call(bf16[256,896]{1,0:T(8,128)(2,1)S(1)} %collective-permute-done.2.first_ref, bf16[256,896]{1,0:T(8,128)(2,1)S(1)} %collective-permute-done.4.second_ref, bf16[2,896,768]{2,1,0:T(8,128)(2,1)S(1)} %get-tuple-element.23.weight_ref, ...), custom_call_target="tpu_custom_call" | custom-call | flops 1 | bytes 1 | tf_op jit(solution)/shard_map/project_last/pallas_call | solution.py:213
  40.3 3.3 %collective-permute-start.10 = (bf16[256,512]{1,0:T(8,128)(2,1)S(1)}, bf16[256,512]{1,0:T(8,128)(2,1)S(1)}, u32[]{:S(2)}, u32[]{:S(2)}) collective-permute-start(bf16[256,512]{1,0:T(8,128)(2,1)S(1)} %get-tuple-element.27.q_ref), channel_id=1, source_target_pairs={{0,64},{8,200},{64,128},{72,8},{128,192},{136,72},{192,0},{200,136... | collective-permute-start | bytes 786440 | tf_op jit(solution)/shard_map/ppermute | solution.py:61
  43.7 3.2 %collective-permute-start.9 = (bf16[528,128]{1,0:T(8,128)(2,1)S(1)}, bf16[528,128]{1,0:T(8,128)(2,1)S(1)}, u32[]{:S(2)}, u32[]{:S(2)}) collective-permute-start(bf16[528,128]{1,0:T(8,128)(2,1)S(1)} %get-tuple-element.30.n0), channel_id=1, source_target_pairs={{0,32},{32,0},{1,33},{33,1},{2,34},{34,2},{3,35},{35,3},{4,36},{36... | collective-permute-start | bytes 405512 | tf_op jit(solution)/shard_map/ppermute | solution.py:78
  46.9 2.2 %collective-permute-start.12 = (bf16[256,512]{1,0:T(8,128)(2,1)S(1)}, bf16[256,512]{1,0:T(8,128)(2,1)S(1)}, u32[]{:S(2)}, u32[]{:S(2)}) collective-permute-start(bf16[256,512]{1,0:T(8,128)(2,1)S(1)} %get-tuple-element.27.q_ref), channel_id=1, source_target_pairs={{0,192},{8,72},{64,0},{72,136},{128,64},{136,200},{192,128},{200,8... | collective-permute-start | bytes 786440 | tf_op jit(solution)/shard_map/ppermute | solution.py:66
  49.1 9.5 %collective-permute-done.10.q_ref = bf16[256,512]{1,0:T(8,128)(2,1)S(1)} collective-permute-done((bf16[256,512]{1,0:T(8,128)(2,1)S(1)}, bf16[256,512]{1,0:T(8,128)(2,1)S(1)}, u32[]{:S(2)}, u32[]{:S(2)}) %collective-permute-start.10) | collective-permute-done | bytes 262176 | tf_op jit(solution)/shard_map/ppermute | solution.py:61
  58.7 0.1 collective-permute-start.14
  58.8 0.0 collective-permute-done.8.v1
  58.8 1.8 %join.1 = (bf16[4,1024,128]{2,1,0:T(8,128)(2,1)S(1)}, bf16[4,1024,128]{2,1,0:T(8,128)(2,1)S(1)}) custom-call(s32[4]{0:T(128)S(1)} %get-tuple-element.28.rank_ref, bf16[2048,128]{1,0:T(8,128)(2,1)S(1)} %copy-done.1, bf16[2048,128]{1,0:T(8,128)(2,1)S(1)} %copy-done.2, bf16[2048,128]{1,0:T(8,128)(2,1)S(1)} %collective-permute-done.7.k1, ...), custom_call_target="tpu_custom_call" | custom-call | flops 3000000000 | bytes 1 | tf_op jit(solution)/shard_map/join/pallas_call | solution.py:337
  60.6 0.9 attend.6
  61.5 4.6 %collective-permute-start.13 = (bf16[2,144,512]{2,1,0:T(8,128)(2,1)S(1)}, bf16[2,144,512]{2,1,0:T(8,128)(2,1)S(1)}, u32[]{:S(2)}, u32[]{:S(2)}) collective-permute-start(bf16[2,144,512]{2,1,0:T(8,128)(2,1)S(1)} %attend.6), channel_id=1, source_target_pairs={{0,64},{8,200},{64,128},{72,8},{128,192},{136,72},{192,0},{200,136... | collective-permute-start | bytes 884744 | tf_op jit(solution)/shard_map/ppermute | solution.py:61
  66.1 0.9 attend.5
  67.0 0.1 collective-permute-start.11
  67.1 0.5 collective-permute-done.14.q_ref
  67.6 0.9 attend.7
  68.4 5.4 %collective-permute-start.15 = (bf16[2,144,512]{2,1,0:T(8,128)(2,1)S(1)}, bf16[2,144,512]{2,1,0:T(8,128)(2,1)S(1)}, u32[]{:S(2)}, u32[]{:S(2)}) collective-permute-start(bf16[2,144,512]{2,1,0:T(8,128)(2,1)S(1)} %attend.7), channel_id=1, source_target_pairs={{0,128},{64,192},{128,0},{192,64},{1,129},{65,193},{129,1},{193,65... | collective-permute-start | bytes 884744 | tf_op jit(solution)/shard_map/ppermute | solution.py:70
  73.9 4.2 %attend.4.refs_0_ = bf16[2,144,512]{2,1,0:T(8,128)(2,1)S(1)} custom-call(s32[16]{0:T(128)S(1)} %get-tuple-element.19.valid_ref, bf16[256,512]{1,0:T(8,128)(2,1)S(1)} %get-tuple-element.27.q_ref, bf16[4,1024,128]{2,1,0:T(8,128)(2,1)S(1)} %get-tuple-element.31.jk_ref, bf16[4,1024,128]{2,1,0:T(8,128)(2,1)S(1)} %get-tuple-element.32.jv_ref, ...), custom_call_target="tpu_custom_call" | custom-call | flops 1000000000 | bytes 1 | tf_op jit(solution)/shard_map/attend/pallas_call | solution.py:349
  78.1 15.2 %collective-permute-done.15.refs_3_ = bf16[2,144,512]{2,1,0:T(8,128)(2,1)S(1)} collective-permute-done((bf16[2,144,512]{2,1,0:T(8,128)(2,1)S(1)}, bf16[2,144,512]{2,1,0:T(8,128)(2,1)S(1)}, u32[]{:S(2)}, u32[]{:S(2)}) %collective-permute-start.15) | collective-permute-done | bytes 294944 | tf_op jit(solution)/shard_map/ppermute | solution.py:70
  93.3 1.5 %merge.1 = bf16[256,512]{1,0:T(8,128)(2,1)} custom-call(bf16[2,144,512]{2,1,0:T(8,128)(2,1)S(1)} %attend.4.refs_0_, bf16[2,144,512]{2,1,0:T(8,128)(2,1)S(1)} %collective-permute-done.11.refs_1_, bf16[2,144,512]{2,1,0:T(8,128)(2,1)S(1)} %collective-permute-done.13.refs_2_, bf16[2,144,512]{2,1,0:T(8,128)(2,1)S(1)} %collective-permute-done.15.refs_3_), custom_call_target="tpu_custom_call" | custom-call | flops 1 | bytes 1 | tf_op jit(solution)/shard_map/merge/pallas_call | solution.py:396
  (15 shorter events, 0.0 us)
Async XLA Ops:
  0.0 17.1 %collective-permute-start.3 = (bf16[256,896]{1,0:T(8,128)(2,1)}, bf16[256,896]{1,0:T(8,128)(2,1)S(1)}, u32[]{:S(2)}, u32[]{:S(2)}) collective-permute-start(bf16[256,896]{1,0:T(8,128)(2,1)} %refs_0_.1), channel_id=1, source_target_pairs={{0,1},{1,2},{2,3},{3,0},{8,11},{9,8},{10,9},{11,10},{4,5},{5,6},{6... | collective-permute-start | bytes 1376264 | tf_op jit(solution)/shard_map/ppermute | solution.py:51
  1.5 13.9 %collective-permute-start.5 = (bf16[256,896]{1,0:T(8,128)(2,1)}, bf16[256,896]{1,0:T(8,128)(2,1)S(1)}, u32[]{:S(2)}, u32[]{:S(2)}) collective-permute-start(bf16[256,896]{1,0:T(8,128)(2,1)} %refs_0_.1), channel_id=1, source_target_pairs={{0,3},{1,0},{2,1},{3,2},{8,9},{9,10},{10,11},{11,8},{4,7},{5,4},{6... | collective-permute-start | bytes 1376264 | tf_op jit(solution)/shard_map/ppermute | solution.py:56
  3.2 11.7 %collective-permute-start = (bf16[256,896]{1,0:T(8,128)(2,1)}, bf16[256,896]{1,0:T(8,128)(2,1)S(1)}, u32[]{:S(2)}, u32[]{:S(2)}) collective-permute-start(bf16[256,896]{1,0:T(8,128)(2,1)} %refs_0_.1), channel_id=1, source_target_pairs={{0,4},{4,0},{1,5},{5,1},{2,6},{6,2},{3,7},{7,3},{8,12},{12,8},{9,1... | collective-permute-start | bytes 1376264 | tf_op jit(solution)/shard_map/ppermute | solution.py:74
  5.1 15.1 %collective-permute-start.7 = (bf16[2048,128]{1,0:T(8,128)(2,1)}, bf16[2048,128]{1,0:T(8,128)(2,1)S(1)}, u32[]{:S(2)}, u32[]{:S(2)}) collective-permute-start(bf16[2048,128]{1,0:T(8,128)(2,1)} %k0.1), channel_id=1, source_target_pairs={{0,32},{32,0},{1,33},{33,1},{2,34},{34,2},{3,35},{35,3},{4,36},{36... | collective-permute-start | bytes 1572872 | tf_op jit(solution)/shard_map/ppermute | solution.py:78
  8.1 0.7 copy-start
  8.8 0.7 copy-start.4
  9.5 0.7 copy-start.5
  10.1 0.7 copy-start.6
  10.8 1.5 %copy-start.3 = (bf16[256,896]{1,0:T(8,128)(2,1)S(1)}, bf16[256,896]{1,0:T(8,128)(2,1)}, u32[]{:S(2)}) copy-start(bf16[256,896]{1,0:T(8,128)(2,1)} %refs_0_.1) | copy-start | bytes 1376260
  15.0 5.3 %copy-start.2 = (bf16[2048,128]{1,0:T(8,128)(2,1)S(1)}, bf16[2048,128]{1,0:T(8,128)(2,1)}, u32[]{:S(2)}) copy-start(bf16[2048,128]{1,0:T(8,128)(2,1)} %v0.1) | copy-start | bytes 1572868
  15.0 9.7 %collective-permute-start.1 = (bf16[256,896]{1,0:T(8,128)(2,1)S(1)}, bf16[256,896]{1,0:T(8,128)(2,1)S(1)}, u32[]{:S(2)}, u32[]{:S(2)}) collective-permute-start(bf16[256,896]{1,0:T(8,128)(2,1)S(1)} %collective-permute-done.refs_0_), channel_id=1, source_target_pairs={{0,1},{1,2},{2,3},{3,0},{8,11},{9,8},{10,9},{11,10},{4,5},{5,6},{6... | collective-permute-start | bytes 1376264 | tf_op jit(solution)/shard_map/ppermute | solution.py:51
  15.4 13.7 %collective-permute-start.6 = (bf16[256,896]{1,0:T(8,128)(2,1)S(1)}, bf16[256,896]{1,0:T(8,128)(2,1)S(1)}, u32[]{:S(2)}, u32[]{:S(2)}) collective-permute-start(bf16[256,896]{1,0:T(8,128)(2,1)S(1)} %collective-permute-done.5.refs_1_), channel_id=1, source_target_pairs={{0,4},{4,0},{1,5},{5,1},{2,6},{6,2},{3,7},{7,3},{8,12},{12,8},{9,1... | collective-permute-start | bytes 1376264 | tf_op jit(solution)/shard_map/ppermute | solution.py:74
  20.2 38.5 %collective-permute-start.8 = (bf16[2048,128]{1,0:T(8,128)(2,1)S(1)}, bf16[2048,128]{1,0:T(8,128)(2,1)S(1)}, u32[]{:S(2)}, u32[]{:S(2)}) collective-permute-start(bf16[2048,128]{1,0:T(8,128)(2,1)S(1)} %copy-done.2), channel_id=1, source_target_pairs={{0,32},{32,0},{1,33},{33,1},{2,34},{34,2},{3,35},{35,3},{4,36},{36... | collective-permute-start | bytes 1572872 | tf_op jit(solution)/shard_map/ppermute | solution.py:78
  24.6 9.7 %collective-permute-start.4 = (bf16[256,896]{1,0:T(8,128)(2,1)S(1)}, bf16[256,896]{1,0:T(8,128)(2,1)S(1)}, u32[]{:S(2)}, u32[]{:S(2)}) collective-permute-start(bf16[256,896]{1,0:T(8,128)(2,1)S(1)} %collective-permute-done.3.refs_0_), channel_id=1, source_target_pairs={{0,1},{1,2},{2,3},{3,0},{8,11},{9,8},{10,9},{11,10},{4,5},{5,6},{6... | collective-permute-start | bytes 1376264 | tf_op jit(solution)/shard_map/ppermute | solution.py:51
  24.6 14.6 %collective-permute-start.2 = (bf16[256,896]{1,0:T(8,128)(2,1)S(1)}, bf16[256,896]{1,0:T(8,128)(2,1)S(1)}, u32[]{:S(2)}, u32[]{:S(2)}) collective-permute-start(bf16[256,896]{1,0:T(8,128)(2,1)S(1)} %collective-permute-done.1.refs_1_), channel_id=1, source_target_pairs={{0,1},{1,2},{2,3},{3,0},{8,11},{9,8},{10,9},{11,10},{4,5},{5,6},{6... | collective-permute-start | bytes 1376264 | tf_op jit(solution)/shard_map/ppermute | solution.py:51
  31.9 26.9 %copy-start.1 = (bf16[2048,128]{1,0:T(8,128)(2,1)S(1)}, bf16[2048,128]{1,0:T(8,128)(2,1)}, u32[]{:S(2)}) copy-start(bf16[2048,128]{1,0:T(8,128)(2,1)} %k0.1) | copy-start | bytes 1572868
  31.9 26.9 %copy-start.7 = (f32[2,128]{1,0:T(2,128)S(1)}, f32[2,128]{1,0:T(2,128)}, u32[]{:S(2)}) copy-start(f32[2,128]{1,0:T(2,128)} %constant.66.clone.freq_ref) | copy-start | bytes 3076
  40.3 18.3 %collective-permute-start.10 = (bf16[256,512]{1,0:T(8,128)(2,1)S(1)}, bf16[256,512]{1,0:T(8,128)(2,1)S(1)}, u32[]{:S(2)}, u32[]{:S(2)}) collective-permute-start(bf16[256,512]{1,0:T(8,128)(2,1)S(1)} %get-tuple-element.27.q_ref), channel_id=1, source_target_pairs={{0,64},{8,200},{64,128},{72,8},{128,192},{136,72},{192,0},{200,136... | collective-permute-start | bytes 786440 | tf_op jit(solution)/shard_map/ppermute | solution.py:61
  43.7 15.1 %collective-permute-start.9 = (bf16[528,128]{1,0:T(8,128)(2,1)S(1)}, bf16[528,128]{1,0:T(8,128)(2,1)S(1)}, u32[]{:S(2)}, u32[]{:S(2)}) collective-permute-start(bf16[528,128]{1,0:T(8,128)(2,1)S(1)} %get-tuple-element.30.n0), channel_id=1, source_target_pairs={{0,32},{32,0},{1,33},{33,1},{2,34},{34,2},{3,35},{35,3},{4,36},{36... | collective-permute-start | bytes 405512 | tf_op jit(solution)/shard_map/ppermute | solution.py:78
  46.9 13.7 %collective-permute-start.12 = (bf16[256,512]{1,0:T(8,128)(2,1)S(1)}, bf16[256,512]{1,0:T(8,128)(2,1)S(1)}, u32[]{:S(2)}, u32[]{:S(2)}) collective-permute-start(bf16[256,512]{1,0:T(8,128)(2,1)S(1)} %get-tuple-element.27.q_ref), channel_id=1, source_target_pairs={{0,192},{8,72},{64,0},{72,136},{128,64},{136,200},{192,128},{200,8... | collective-permute-start | bytes 786440 | tf_op jit(solution)/shard_map/ppermute | solution.py:66
  58.7 8.9 %collective-permute-start.14 = (bf16[256,512]{1,0:T(8,128)(2,1)S(1)}, bf16[256,512]{1,0:T(8,128)(2,1)S(1)}, u32[]{:S(2)}, u32[]{:S(2)}) collective-permute-start(bf16[256,512]{1,0:T(8,128)(2,1)S(1)} %collective-permute-done.10.q_ref), channel_id=1, source_target_pairs={{0,64},{8,200},{64,128},{72,8},{128,192},{136,72},{192,0},{200,136... | collective-permute-start | bytes 786440 | tf_op jit(solution)/shard_map/ppermute | solution.py:61
  61.5 16.6 %collective-permute-start.13 = (bf16[2,144,512]{2,1,0:T(8,128)(2,1)S(1)}, bf16[2,144,512]{2,1,0:T(8,128)(2,1)S(1)}, u32[]{:S(2)}, u32[]{:S(2)}) collective-permute-start(bf16[2,144,512]{2,1,0:T(8,128)(2,1)S(1)} %attend.6), channel_id=1, source_target_pairs={{0,64},{8,200},{64,128},{72,8},{128,192},{136,72},{192,0},{200,136... | collective-permute-start | bytes 884744 | tf_op jit(solution)/shard_map/ppermute | solution.py:61
  67.0 11.1 %collective-permute-start.11 = (bf16[2,144,512]{2,1,0:T(8,128)(2,1)S(1)}, bf16[2,144,512]{2,1,0:T(8,128)(2,1)S(1)}, u32[]{:S(2)}, u32[]{:S(2)}) collective-permute-start(bf16[2,144,512]{2,1,0:T(8,128)(2,1)S(1)} %attend.5), channel_id=1, source_target_pairs={{0,192},{8,72},{64,0},{72,136},{128,64},{136,200},{192,128},{200,8... | collective-permute-start | bytes 884744 | tf_op jit(solution)/shard_map/ppermute | solution.py:66
  68.4 24.9 %collective-permute-start.15 = (bf16[2,144,512]{2,1,0:T(8,128)(2,1)S(1)}, bf16[2,144,512]{2,1,0:T(8,128)(2,1)S(1)}, u32[]{:S(2)}, u32[]{:S(2)}) collective-permute-start(bf16[2,144,512]{2,1,0:T(8,128)(2,1)S(1)} %attend.7), channel_id=1, source_target_pairs={{0,128},{64,192},{128,0},{192,64},{1,129},{65,193},{129,1},{193,65... | collective-permute-start | bytes 884744 | tf_op jit(solution)/shard_map/ppermute | solution.py:70

commit v9 on v6

--- a/solution.py
+++ b/solution.py
@@ -440,7 +440,7 @@
     acc, kept = project(
         (Z_AT + 3, Z_AT + 1, Z_AT + 2), (z3, z1), weights, acc, ahead=1
     )
-    acc = after(acc, k1, v1)
+    acc = after(acc, k1)
     query, fresh = last_project(z2, kept, acc, cosine, sine, mine)
     near, behind = ring_z(query), back_z(query)
     far = ring_z(near)

time: 97.3 us -> 95.1 us (0.977)
  the two profiles are of different devices: /device:TPU:36 before, /device:TPU:72 now
where the time goes in v9:
time: 95.1 us; the launch traced here: 94.9 us
  waiting for transfers between devices  42.6 us (45%)
  Pallas kernels  24.1 us (25%)
  starting transfers between devices  23.8 us (25%)
  local copies, waits for them, and re-layouts  3.53 us (4%)
    ppermute x3, waiting for transfers between devices, ring_z(): return lax.ppermute(v, ('zh', 'c'), pairs)  24.4 us
    pallas_call x4, Pallas kernels, partial_project(): pl.pallas_call(functools.partial(partial_kernel, which, ahead, acc is not...  11.7 us
    ppermute x4, waiting for transfers between devices, ring_x(): return lax.ppermute(v, ('c', 'x'), opposite_ways(4))  10.5 us
    ppermute x3, starting transfers between devices, ring_z(): return lax.ppermute(v, ('zh', 'c'), pairs)  8.82 us
    pallas_call x4, Pallas kernels, attend(): pl.pallas_call(functools.partial(attend_kernel, shift), out_shape=packed_...  6.81 us
    ppermute x3, starting transfers between devices, py(): return lax.ppermute(v, 'yh', [(0, 1), (1, 0)])  5.89 us
    ppermute x1, waiting for transfers between devices, far_z(): return lax.ppermute(v, 'zh', [(i, (i + 2) % 4) for i in range(4)])  4.3 us
    ppermute x2, waiting for transfers between devices, back_z(): return lax.ppermute(v, ('zh', 'c'), pairs)  3.39 us
  transfers between devices with their start and end apart: 16, of which 8 were waited for; matrix products, arithmetic and copies ran while one was open for 2% of the time, Pallas kernels for 24%

profile of v9, /device:TPU:72, one launch (start us, length us, event | category | flops | bytes accessed | tf_op | source)
XLA Modules:
  0.0 94.9 jit_solution(14086518704538673014)
XLA Ops:
  0.0 2.8 %collective-permute-start.3 = (bf16[256,896]{1,0:T(8,128)(2,1)}, bf16[256,896]{1,0:T(8,128)(2,1)S(1)}, u32[]{:S(2)}, u32[]{:S(2)}) collective-permute-start(bf16[256,896]{1,0:T(8,128)(2,1)} %refs_0_.1), channel_id=1, source_target_pairs={{0,3},{1,0},{2,1},{3,2},{8,9},{9,10},{10,11},{11,8},{4,7},{5,4},{6... | collective-permute-start | bytes 1376264 | tf_op jit(solution)/shard_map/ppermute | solution.py:56
  2.8 0.0 collective-permute-start.5
  2.8 1.9 %collective-permute-start = (bf16[256,896]{1,0:T(8,128)(2,1)}, bf16[256,896]{1,0:T(8,128)(2,1)S(1)}, u32[]{:S(2)}, u32[]{:S(2)}) collective-permute-start(bf16[256,896]{1,0:T(8,128)(2,1)} %refs_0_.1), channel_id=1, source_target_pairs={{0,4},{4,0},{1,5},{5,1},{2,6},{6,2},{3,7},{7,3},{8,12},{12,8},{9,1... | collective-permute-start | bytes 1376264 | tf_op jit(solution)/shard_map/ppermute | solution.py:74
  4.7 2.3 %collective-permute-start.7 = (bf16[2048,128]{1,0:T(8,128)(2,1)}, bf16[2048,128]{1,0:T(8,128)(2,1)S(1)}, u32[]{:S(2)}, u32[]{:S(2)}) collective-permute-start(bf16[2048,128]{1,0:T(8,128)(2,1)} %k0.1), channel_id=1, source_target_pairs={{0,32},{32,0},{1,33},{33,1},{2,34},{34,2},{3,35},{35,3},{4,36},{36... | collective-permute-start | bytes 1572872 | tf_op jit(solution)/shard_map/ppermute | solution.py:78
  7.0 0.7 pad.1.clone
  7.7 0.7 pad_add_fusion.mine_ref.refs_0_
  8.5 0.1 stack.51.place
  8.5 0.0 copy-start
  8.6 0.7 copy-done
  9.2 0.7 copy-done.4
  9.9 0.7 copy-done.5
  10.6 0.7 copy-done.6
  11.3 1.5 %prepare.1 = (f32[256,128]{1,0:T(8,128)S(1)}, f32[256,128]{1,0:T(8,128)S(1)}, s32[4]{0:T(128)S(1)}, s32[16]{0:T(128)S(1)}) custom-call(s32[12]{0:T(128)S(1)} %stack.51.place, s32[8]{0:T(128)S(1)} %copy-done.5, s32[8,8]{1,0:T(8,128)S(1)} %copy-done.4, s32[2,128]{1,0:T(2,128)S(1)} %copy-done, f32[2,128]{1,0:T(2,128)S(1)} %copy-done.6), custom_call_target="tpu_custom_call" | custom-call | flops 2000000000 | bytes 1 | tf_op jit(solution)/shard_map/prepare/pallas_call | solution.py:118
  12.8 2.4 %project.4.refs_5_ = f32[256,768]{1,0:T(8,128)S(1)} custom-call(s32[12]{0:T(128)S(1)} %stack.51.place, bf16[256,896]{1,0:T(8,128)(2,1)S(1)} %copy-done.3, bf16[7168,512]{1,0:T(8,128)(2,1)} %refs_2_.7, bf16[7168,128]{1,0:T(8,128)(2,1)} %refs_3_.7, bf16[7168,128]{1,0:T(8,128)(2,1)} %refs_4_.5), custom_call_target="tpu_custom_call" | custom-call | flops 6000000000 | bytes 1 | tf_op jit(solution)/shard_map/project/pallas_call | solution.py:179
  15.2 0.0 copy-start.2
  15.3 0.8 collective-permute-start.6
  16.1 1.5 %collective-permute-start.1 = (bf16[256,896]{1,0:T(8,128)(2,1)S(1)}, bf16[256,896]{1,0:T(8,128)(2,1)S(1)}, u32[]{:S(2)}, u32[]{:S(2)}) collective-permute-start(bf16[256,896]{1,0:T(8,128)(2,1)S(1)} %collective-permute-done.refs_0_), channel_id=1, source_target_pairs={{0,1},{1,2},{2,3},{3,0},{8,11},{9,8},{10,9},{11,10},{4,5},{5,6},{6... | collective-permute-start | bytes 1376264 | tf_op jit(solution)/shard_map/ppermute | solution.py:51
  17.6 0.0 collective-permute-done.3.refs_1_
  17.6 0.1 collective-permute-start.4
  17.7 3.1 %project.5.refs_5_ = f32[256,768]{1,0:T(8,128)S(1)} custom-call(s32[12]{0:T(128)S(1)} %stack.51.place, bf16[256,896]{1,0:T(8,128)(2,1)S(1)} %collective-permute-done.5.refs_0_, bf16[256,896]{1,0:T(8,128)(2,1)S(1)} %collective-permute-done.3.refs_1_, bf16[7168,512]{1,0:T(8,128)(2,1)} %refs_2_.7, bf16[7168,128]{1,0:T(8,128)(2,1)} %refs_3_.7, ...), custom_call_target="tpu_custom_call" | custom-call | flops 6000000000 | bytes 1 | tf_op jit(solution)/shard_map/project/pallas_call | solution.py:179
  20.8 2.1 %collective-permute-start.8 = (bf16[2048,128]{1,0:T(8,128)(2,1)S(1)}, bf16[2048,128]{1,0:T(8,128)(2,1)S(1)}, u32[]{:S(2)}, u32[]{:S(2)}) collective-permute-start(bf16[2048,128]{1,0:T(8,128)(2,1)S(1)} %copy-done.2), channel_id=1, source_target_pairs={{0,32},{32,0},{1,33},{33,1},{2,34},{34,2},{3,35},{35,3},{4,36},{36... | collective-permute-start | bytes 1572872 | tf_op jit(solution)/shard_map/ppermute | solution.py:78
  22.9 7.1 %collective-permute-done.1.refs_1_ = bf16[256,896]{1,0:T(8,128)(2,1)S(1)} collective-permute-done((bf16[256,896]{1,0:T(8,128)(2,1)S(1)}, bf16[256,896]{1,0:T(8,128)(2,1)S(1)}, u32[]{:S(2)}, u32[]{:S(2)}) %collective-permute-start.1) | collective-permute-done | bytes 458784 | tf_op jit(solution)/shard_map/ppermute | solution.py:51
  30.0 3.1 %project.6.refs_5_ = f32[256,768]{1,0:T(8,128)S(1)} custom-call(s32[12]{0:T(128)S(1)} %stack.51.place, bf16[256,896]{1,0:T(8,128)(2,1)S(1)} %collective-permute-done.refs_0_, bf16[256,896]{1,0:T(8,128)(2,1)S(1)} %collective-permute-done.6.refs_1_, bf16[7168,512]{1,0:T(8,128)(2,1)} %refs_2_.7, bf16[7168,128]{1,0:T(8,128)(2,1)} %refs_3_.7, ...), custom_call_target="tpu_custom_call" | custom-call | flops 6000000000 | bytes 1 | tf_op jit(solution)/shard_map/project/pallas_call | solution.py:179
  33.0 3.1 %project.7 = (f32[256,768]{1,0:T(8,128)S(1)}, bf16[1,896,768]{2,1,0:T(8,128)(2,1)S(1)}) custom-call(s32[12]{0:T(128)S(1)} %stack.51.place, bf16[256,896]{1,0:T(8,128)(2,1)S(1)} %collective-permute-done.4.refs_0_, bf16[256,896]{1,0:T(8,128)(2,1)S(1)} %collective-permute-done.1.refs_1_, bf16[7168,512]{1,0:T(8,128)(2,1)} %refs_2_.7, bf16[7168,128]{1,0:T(8,128)(2,1)} %refs_3_.7, ...), custom_call_target="tpu_custom_call" | custom-call | flops 6000000000 | bytes 1 | tf_op jit(solution)/shard_map/project/pallas_call | solution.py:179
  36.2 0.0 copy-start.1
  36.2 0.0 copy-start.7
  36.2 3.5 %collective-permute-done.2.piece_ref = bf16[256,896]{1,0:T(8,128)(2,1)S(1)} collective-permute-done((bf16[256,896]{1,0:T(8,128)(2,1)S(1)}, bf16[256,896]{1,0:T(8,128)(2,1)S(1)}, u32[]{:S(2)}, u32[]{:S(2)}) %collective-permute-start.2) | collective-permute-done | bytes 458784 | tf_op jit(solution)/shard_map/ppermute | solution.py:51
  39.6 0.7 project_last.1
  40.3 3.7 %collective-permute-start.10 = (bf16[256,512]{1,0:T(8,128)(2,1)S(1)}, bf16[256,512]{1,0:T(8,128)(2,1)S(1)}, u32[]{:S(2)}, u32[]{:S(2)}) collective-permute-start(bf16[256,512]{1,0:T(8,128)(2,1)S(1)} %get-tuple-element.25.q_ref), channel_id=1, source_target_pairs={{0,64},{8,200},{64,128},{72,8},{128,192},{136,72},{192,0},{200,136... | collective-permute-start | bytes 786440 | tf_op jit(solution)/shard_map/ppermute | solution.py:61
  44.0 1.5 %collective-permute-start.9 = (bf16[528,128]{1,0:T(8,128)(2,1)S(1)}, bf16[528,128]{1,0:T(8,128)(2,1)S(1)}, u32[]{:S(2)}, u32[]{:S(2)}) collective-permute-start(bf16[528,128]{1,0:T(8,128)(2,1)S(1)} %get-tuple-element.28.n0), channel_id=1, source_target_pairs={{0,32},{32,0},{1,33},{33,1},{2,34},{34,2},{3,35},{35,3},{4,36},{36... | collective-permute-start | bytes 405512 | tf_op jit(solution)/shard_map/ppermute | solution.py:78
  45.5 0.0 collective-permute-start.12
  45.5 8.1 %collective-permute-done.10.q_ref = bf16[256,512]{1,0:T(8,128)(2,1)S(1)} collective-permute-done((bf16[256,512]{1,0:T(8,128)(2,1)S(1)}, bf16[256,512]{1,0:T(8,128)(2,1)S(1)}, u32[]{:S(2)}, u32[]{:S(2)}) %collective-permute-start.10) | collective-permute-done | bytes 262176 | tf_op jit(solution)/shard_map/ppermute | solution.py:61
  53.6 5.0 %collective-permute-start.14 = (bf16[256,512]{1,0:T(8,128)(2,1)S(1)}, bf16[256,512]{1,0:T(8,128)(2,1)S(1)}, u32[]{:S(2)}, u32[]{:S(2)}) collective-permute-start(bf16[256,512]{1,0:T(8,128)(2,1)S(1)} %collective-permute-done.10.q_ref), channel_id=1, source_target_pairs={{0,64},{8,200},{64,128},{72,8},{128,192},{136,72},{192,0},{200,136... | collective-permute-start | bytes 786440 | tf_op jit(solution)/shard_map/ppermute | solution.py:61
  58.6 0.0 collective-permute-done.8.v1
  58.6 1.8 %join.1 = (bf16[4,1024,128]{2,1,0:T(8,128)(2,1)S(1)}, bf16[4,1024,128]{2,1,0:T(8,128)(2,1)S(1)}) custom-call(s32[4]{0:T(128)S(1)} %get-tuple-element.26.rank_ref, bf16[2048,128]{1,0:T(8,128)(2,1)S(1)} %copy-done.1, bf16[2048,128]{1,0:T(8,128)(2,1)S(1)} %copy-done.2, bf16[2048,128]{1,0:T(8,128)(2,1)S(1)} %collective-permute-done.7.k1, ...), custom_call_target="tpu_custom_call" | custom-call | flops 3000000000 | bytes 1 | tf_op jit(solution)/shard_map/join/pallas_call | solution.py:335
  60.4 1.0 %collective-permute-done.12.q_ref = bf16[256,512]{1,0:T(8,128)(2,1)S(1)} collective-permute-done((bf16[256,512]{1,0:T(8,128)(2,1)S(1)}, bf16[256,512]{1,0:T(8,128)(2,1)S(1)}, u32[]{:S(2)}, u32[]{:S(2)}) %collective-permute-start.12) | collective-permute-done | bytes 262176 | tf_op jit(solution)/shard_map/ppermute | solution.py:66
  61.4 0.9 attend.6
  62.3 0.2 collective-permute-start.13
  62.4 1.9 %attend.5 = bf16[2,144,512]{2,1,0:T(8,128)(2,1)S(1)} custom-call(s32[16]{0:T(128)S(1)} %get-tuple-element.18.valid_ref, bf16[256,512]{1,0:T(8,128)(2,1)S(1)} %collective-permute-done.10.q_ref, bf16[4,1024,128]{2,1,0:T(8,128)(2,1)S(1)} %get-tuple-element.29.jk_ref, bf16[4,1024,128]{2,1,0:T(8,128)(2,1)S(1)} %get-tuple-element.30.jv_ref), custom_call_target="tpu_custom_call" | custom-call | flops 1000000000 | bytes 1 | tf_op jit(solution)/shard_map/attend/pallas_call | solution.py:347
  64.4 1.9 %collective-permute-start.11 = (bf16[2,144,512]{2,1,0:T(8,128)(2,1)S(1)}, bf16[2,144,512]{2,1,0:T(8,128)(2,1)S(1)}, u32[]{:S(2)}, u32[]{:S(2)}) collective-permute-start(bf16[2,144,512]{2,1,0:T(8,128)(2,1)S(1)} %attend.5), channel_id=1, source_target_pairs={{0,192},{8,72},{64,0},{72,136},{128,64},{136,200},{192,128},{200,8... | collective-permute-start | bytes 884744 | tf_op jit(solution)/shard_map/ppermute | solution.py:66
  66.2 4.0 %collective-permute-done.14.q_ref = bf16[256,512]{1,0:T(8,128)(2,1)S(1)} collective-permute-done((bf16[256,512]{1,0:T(8,128)(2,1)S(1)}, bf16[256,512]{1,0:T(8,128)(2,1)S(1)}, u32[]{:S(2)}, u32[]{:S(2)}) %collective-permute-start.14) | collective-permute-done | bytes 262176 | tf_op jit(solution)/shard_map/ppermute | solution.py:61
  70.3 0.9 attend.7
  71.1 0.1 collective-permute-start.15
  71.2 3.1 %attend.4.refs_0_ = bf16[2,144,512]{2,1,0:T(8,128)(2,1)S(1)} custom-call(s32[16]{0:T(128)S(1)} %get-tuple-element.18.valid_ref, bf16[256,512]{1,0:T(8,128)(2,1)S(1)} %get-tuple-element.25.q_ref, bf16[4,1024,128]{2,1,0:T(8,128)(2,1)S(1)} %get-tuple-element.29.jk_ref, bf16[4,1024,128]{2,1,0:T(8,128)(2,1)S(1)} %get-tuple-element.30.jv_ref, ...), custom_call_target="tpu_custom_call" | custom-call | flops 1000000000 | bytes 1 | tf_op jit(solution)/shard_map/attend/pallas_call | solution.py:347
  74.4 12.3 %collective-permute-done.13.refs_2_ = bf16[2,144,512]{2,1,0:T(8,128)(2,1)S(1)} collective-permute-done((bf16[2,144,512]{2,1,0:T(8,128)(2,1)S(1)}, bf16[2,144,512]{2,1,0:T(8,128)(2,1)S(1)}, u32[]{:S(2)}, u32[]{:S(2)}) %collective-permute-start.13) | collective-permute-done | bytes 294944 | tf_op jit(solution)/shard_map/ppermute | solution.py:61
  86.6 2.4 %collective-permute-done.11.refs_1_ = bf16[2,144,512]{2,1,0:T(8,128)(2,1)S(1)} collective-permute-done((bf16[2,144,512]{2,1,0:T(8,128)(2,1)S(1)}, bf16[2,144,512]{2,1,0:T(8,128)(2,1)S(1)}, u32[]{:S(2)}, u32[]{:S(2)}) %collective-permute-start.11) | collective-permute-done | bytes 294944 | tf_op jit(solution)/shard_map/ppermute | solution.py:66
  89.1 4.3 %collective-permute-done.15.refs_3_ = bf16[2,144,512]{2,1,0:T(8,128)(2,1)S(1)} collective-permute-done((bf16[2,144,512]{2,1,0:T(8,128)(2,1)S(1)}, bf16[2,144,512]{2,1,0:T(8,128)(2,1)S(1)}, u32[]{:S(2)}, u32[]{:S(2)}) %collective-permute-start.15) | collective-permute-done | bytes 294944 | tf_op jit(solution)/shard_map/ppermute | solution.py:70
  93.4 1.5 %merge.1 = bf16[256,512]{1,0:T(8,128)(2,1)} custom-call(bf16[2,144,512]{2,1,0:T(8,128)(2,1)S(1)} %attend.4.refs_0_, bf16[2,144,512]{2,1,0:T(8,128)(2,1)S(1)} %collective-permute-done.11.refs_1_, bf16[2,144,512]{2,1,0:T(8,128)(2,1)S(1)} %collective-permute-done.13.refs_2_, bf16[2,144,512]{2,1,0:T(8,128)(2,1)S(1)} %collective-permute-done.15.refs_3_), custom_call_target="tpu_custom_call" | custom-call | flops 1 | bytes 1 | tf_op jit(solution)/shard_map/merge/pallas_call | solution.py:394
  (15 shorter events, 0.0 us)
Async XLA Ops:
  0.0 17.6 %collective-permute-start.3 = (bf16[256,896]{1,0:T(8,128)(2,1)}, bf16[256,896]{1,0:T(8,128)(2,1)S(1)}, u32[]{:S(2)}, u32[]{:S(2)}) collective-permute-start(bf16[256,896]{1,0:T(8,128)(2,1)} %refs_0_.1), channel_id=1, source_target_pairs={{0,3},{1,0},{2,1},{3,2},{8,9},{9,10},{10,11},{11,8},{4,7},{5,4},{6... | collective-permute-start | bytes 1376264 | tf_op jit(solution)/shard_map/ppermute | solution.py:56
  2.8 12.5 %collective-permute-start.5 = (bf16[256,896]{1,0:T(8,128)(2,1)}, bf16[256,896]{1,0:T(8,128)(2,1)S(1)}, u32[]{:S(2)}, u32[]{:S(2)}) collective-permute-start(bf16[256,896]{1,0:T(8,128)(2,1)} %refs_0_.1), channel_id=1, source_target_pairs={{0,1},{1,2},{2,3},{3,0},{8,11},{9,8},{10,9},{11,10},{4,5},{5,6},{6... | collective-permute-start | bytes 1376264 | tf_op jit(solution)/shard_map/ppermute | solution.py:51
  2.8 13.3 %collective-permute-start = (bf16[256,896]{1,0:T(8,128)(2,1)}, bf16[256,896]{1,0:T(8,128)(2,1)S(1)}, u32[]{:S(2)}, u32[]{:S(2)}) collective-permute-start(bf16[256,896]{1,0:T(8,128)(2,1)} %refs_0_.1), channel_id=1, source_target_pairs={{0,4},{4,0},{1,5},{5,1},{2,6},{6,2},{3,7},{7,3},{8,12},{12,8},{9,1... | collective-permute-start | bytes 1376264 | tf_op jit(solution)/shard_map/ppermute | solution.py:74
  4.7 16.1 %collective-permute-start.7 = (bf16[2048,128]{1,0:T(8,128)(2,1)}, bf16[2048,128]{1,0:T(8,128)(2,1)S(1)}, u32[]{:S(2)}, u32[]{:S(2)}) collective-permute-start(bf16[2048,128]{1,0:T(8,128)(2,1)} %k0.1), channel_id=1, source_target_pairs={{0,32},{32,0},{1,33},{33,1},{2,34},{34,2},{3,35},{35,3},{4,36},{36... | collective-permute-start | bytes 1572872 | tf_op jit(solution)/shard_map/ppermute | solution.py:78
  8.5 0.7 copy-start
  9.2 0.7 copy-start.4
  9.9 0.7 copy-start.5
  10.6 0.7 copy-start.6
  11.2 1.5 %copy-start.3 = (bf16[256,896]{1,0:T(8,128)(2,1)S(1)}, bf16[256,896]{1,0:T(8,128)(2,1)}, u32[]{:S(2)}) copy-start(bf16[256,896]{1,0:T(8,128)(2,1)} %refs_0_.1) | copy-start | bytes 1376260
  15.2 5.6 %copy-start.2 = (bf16[2048,128]{1,0:T(8,128)(2,1)S(1)}, bf16[2048,128]{1,0:T(8,128)(2,1)}, u32[]{:S(2)}) copy-start(bf16[2048,128]{1,0:T(8,128)(2,1)} %v0.1) | copy-start | bytes 1572868
  15.3 14.7 %collective-permute-start.6 = (bf16[256,896]{1,0:T(8,128)(2,1)S(1)}, bf16[256,896]{1,0:T(8,128)(2,1)S(1)}, u32[]{:S(2)}, u32[]{:S(2)}) collective-permute-start(bf16[256,896]{1,0:T(8,128)(2,1)S(1)} %collective-permute-done.5.refs_0_), channel_id=1, source_target_pairs={{0,1},{1,2},{2,3},{3,0},{8,11},{9,8},{10,9},{11,10},{4,5},{5,6},{6... | collective-permute-start | bytes 1376264 | tf_op jit(solution)/shard_map/ppermute | solution.py:51
  16.1 13.8 %collective-permute-start.1 = (bf16[256,896]{1,0:T(8,128)(2,1)S(1)}, bf16[256,896]{1,0:T(8,128)(2,1)S(1)}, u32[]{:S(2)}, u32[]{:S(2)}) collective-permute-start(bf16[256,896]{1,0:T(8,128)(2,1)S(1)} %collective-permute-done.refs_0_), channel_id=1, source_target_pairs={{0,1},{1,2},{2,3},{3,0},{8,11},{9,8},{10,9},{11,10},{4,5},{5,6},{6... | collective-permute-start | bytes 1376264 | tf_op jit(solution)/shard_map/ppermute | solution.py:51
  17.6 15.4 %collective-permute-start.4 = (bf16[256,896]{1,0:T(8,128)(2,1)S(1)}, bf16[256,896]{1,0:T(8,128)(2,1)S(1)}, u32[]{:S(2)}, u32[]{:S(2)}) collective-permute-start(bf16[256,896]{1,0:T(8,128)(2,1)S(1)} %collective-permute-done.3.refs_1_), channel_id=1, source_target_pairs={{0,4},{4,0},{1,5},{5,1},{2,6},{6,2},{3,7},{7,3},{8,12},{12,8},{9,1... | collective-permute-start | bytes 1376264 | tf_op jit(solution)/shard_map/ppermute | solution.py:74
  20.8 37.8 %collective-permute-start.8 = (bf16[2048,128]{1,0:T(8,128)(2,1)S(1)}, bf16[2048,128]{1,0:T(8,128)(2,1)S(1)}, u32[]{:S(2)}, u32[]{:S(2)}) collective-permute-start(bf16[2048,128]{1,0:T(8,128)(2,1)S(1)} %copy-done.2), channel_id=1, source_target_pairs={{0,32},{32,0},{1,33},{33,1},{2,34},{34,2},{3,35},{35,3},{4,36},{36... | collective-permute-start | bytes 1572872 | tf_op jit(solution)/shard_map/ppermute | solution.py:78
  29.9 9.7 %collective-permute-start.2 = (bf16[256,896]{1,0:T(8,128)(2,1)S(1)}, bf16[256,896]{1,0:T(8,128)(2,1)S(1)}, u32[]{:S(2)}, u32[]{:S(2)}) collective-permute-start(bf16[256,896]{1,0:T(8,128)(2,1)S(1)} %collective-permute-done.1.refs_1_), channel_id=1, source_target_pairs={{0,1},{1,2},{2,3},{3,0},{8,11},{9,8},{10,9},{11,10},{4,5},{5,6},{6... | collective-permute-start | bytes 1376264 | tf_op jit(solution)/shard_map/ppermute | solution.py:51
  36.2 22.4 %copy-start.1 = (bf16[2048,128]{1,0:T(8,128)(2,1)S(1)}, bf16[2048,128]{1,0:T(8,128)(2,1)}, u32[]{:S(2)}) copy-start(bf16[2048,128]{1,0:T(8,128)(2,1)} %k0.1) | copy-start | bytes 1572868
  36.2 22.4 %copy-start.7 = (f32[2,128]{1,0:T(2,128)S(1)}, f32[2,128]{1,0:T(2,128)}, u32[]{:S(2)}) copy-start(f32[2,128]{1,0:T(2,128)} %constant.66.clone.freq_ref) | copy-start | bytes 3076
  40.3 13.3 %collective-permute-start.10 = (bf16[256,512]{1,0:T(8,128)(2,1)S(1)}, bf16[256,512]{1,0:T(8,128)(2,1)S(1)}, u32[]{:S(2)}, u32[]{:S(2)}) collective-permute-start(bf16[256,512]{1,0:T(8,128)(2,1)S(1)} %get-tuple-element.25.q_ref), channel_id=1, source_target_pairs={{0,64},{8,200},{64,128},{72,8},{128,192},{136,72},{192,0},{200,136... | collective-permute-start | bytes 786440 | tf_op jit(solution)/shard_map/ppermute | solution.py:61
  44.0 14.6 %collective-permute-start.9 = (bf16[528,128]{1,0:T(8,128)(2,1)S(1)}, bf16[528,128]{1,0:T(8,128)(2,1)S(1)}, u32[]{:S(2)}, u32[]{:S(2)}) collective-permute-start(bf16[528,128]{1,0:T(8,128)(2,1)S(1)} %get-tuple-element.28.n0), channel_id=1, source_target_pairs={{0,32},{32,0},{1,33},{33,1},{2,34},{34,2},{3,35},{35,3},{4,36},{36... | collective-permute-start | bytes 405512 | tf_op jit(solution)/shard_map/ppermute | solution.py:78
  45.5 15.8 %collective-permute-start.12 = (bf16[256,512]{1,0:T(8,128)(2,1)S(1)}, bf16[256,512]{1,0:T(8,128)(2,1)S(1)}, u32[]{:S(2)}, u32[]{:S(2)}) collective-permute-start(bf16[256,512]{1,0:T(8,128)(2,1)S(1)} %get-tuple-element.25.q_ref), channel_id=1, source_target_pairs={{0,192},{8,72},{64,0},{72,136},{128,64},{136,200},{192,128},{200,8... | collective-permute-start | bytes 786440 | tf_op jit(solution)/shard_map/ppermute | solution.py:66
  53.6 16.7 %collective-permute-start.14 = (bf16[256,512]{1,0:T(8,128)(2,1)S(1)}, bf16[256,512]{1,0:T(8,128)(2,1)S(1)}, u32[]{:S(2)}, u32[]{:S(2)}) collective-permute-start(bf16[256,512]{1,0:T(8,128)(2,1)S(1)} %collective-permute-done.10.q_ref), channel_id=1, source_target_pairs={{0,64},{8,200},{64,128},{72,8},{128,192},{136,72},{192,0},{200,136... | collective-permute-start | bytes 786440 | tf_op jit(solution)/shard_map/ppermute | solution.py:61
  62.3 24.4 %collective-permute-start.13 = (bf16[2,144,512]{2,1,0:T(8,128)(2,1)S(1)}, bf16[2,144,512]{2,1,0:T(8,128)(2,1)S(1)}, u32[]{:S(2)}, u32[]{:S(2)}) collective-permute-start(bf16[2,144,512]{2,1,0:T(8,128)(2,1)S(1)} %attend.6), channel_id=1, source_target_pairs={{0,64},{8,200},{64,128},{72,8},{128,192},{136,72},{192,0},{200,136... | collective-permute-start | bytes 884744 | tf_op jit(solution)/shard_map/ppermute | solution.py:61
  64.4 24.7 %collective-permute-start.11 = (bf16[2,144,512]{2,1,0:T(8,128)(2,1)S(1)}, bf16[2,144,512]{2,1,0:T(8,128)(2,1)S(1)}, u32[]{:S(2)}, u32[]{:S(2)}) collective-permute-start(bf16[2,144,512]{2,1,0:T(8,128)(2,1)S(1)} %attend.5), channel_id=1, source_target_pairs={{0,192},{8,72},{64,0},{72,136},{128,64},{136,200},{192,128},{200,8... | collective-permute-start | bytes 884744 | tf_op jit(solution)/shard_map/ppermute | solution.py:66
  71.1 22.2 %collective-permute-start.15 = (bf16[2,144,512]{2,1,0:T(8,128)(2,1)S(1)}, bf16[2,144,512]{2,1,0:T(8,128)(2,1)S(1)}, u32[]{:S(2)}, u32[]{:S(2)}) collective-permute-start(bf16[2,144,512]{2,1,0:T(8,128)(2,1)S(1)} %attend.7), channel_id=1, source_target_pairs={{0,128},{64,192},{128,0},{192,64},{1,129},{65,193},{129,1},{193,65... | collective-permute-start | bytes 884744 | tf_op jit(solution)/shard_map/ppermute | solution.py:70
